TPU v7x, 32 devices: a whole 2x2x4 slice. The times are simulated.
32 devices in a mesh: seq: 8 (over z, x), tensor: 4 (over y, core).
Axes of the slice: x: 2, y: 2, z: 4, core: 2. Of those that a mesh axis runs over, the one named last changes fastest.
Arguments:
- latents: bfloat16 [4096, 1024], P('seq')
- sources: bfloat16 [8192, 1024], P('seq'), may hold values from -6 to 6
- source_index: int32 [32, 256], P('seq'), may hold values from 0 to 8191, as said below
- block_clip: int32 [32], replicated, may hold values from 0 to 2, as said below
- clip_frames: int32 [3], replicated, may hold values from 1 to 2, as said below
- norm_src: float32 [1024], replicated, may hold values from 0.5 to 1.5
- norm_cross: float32 [1024], replicated, may hold values from 0.5 to 1.5
- norm_self: float32 [1024], replicated, may hold values from 0.5 to 1.5
- norm_mlp: float32 [1024], replicated, may hold values from 0.5 to 1.5
- cross_q: bfloat16 [1024, 1024], P(None, 'tensor'), may hold values from -0.1875 to 0.1875
- cross_k: bfloat16 [1024, 1024], P(None, 'tensor'), may hold values from -0.1875 to 0.1875
- cross_v: bfloat16 [1024, 1024], P(None, 'tensor'), may hold values from -0.1875 to 0.1875
- cross_o: bfloat16 [1024, 1024], P('tensor'), may hold values from -0.5 to 0.5
- self_q: bfloat16 [1024, 1024], P(None, 'tensor'), may hold values from -0.1875 to 0.1875
- self_k: bfloat16 [1024, 1024], P(None, 'tensor'), may hold values from -0.1875 to 0.1875
- self_v: bfloat16 [1024, 1024], P(None, 'tensor'), may hold values from -0.1875 to 0.1875
- self_o: bfloat16 [1024, 1024], P('tensor'), may hold values from -0.75 to 0.75
- mlp_in: bfloat16 [1024, 4096], P(None, 'tensor'), may hold values from -0.1875 to 0.1875
- mlp_out: bfloat16 [4096, 1024], P('tensor'), may hold values from -0.09375 to 0.09375
- out_grad: bfloat16 [4096, 1024], P('seq'), may hold values from -6 to 6
Outputs:
- output: bfloat16 [4096, 1024], P('seq')
- latents_grad: bfloat16 [4096, 1024], P('seq')
- sources_grad: bfloat16 [8192, 1024], P('seq')
- norm_src_grad: float32 [1024], replicated
- norm_cross_grad: float32 [1024], replicated
- norm_self_grad: float32 [1024], replicated
- norm_mlp_grad: float32 [1024], replicated
- cross_q_grad: float32 [1024, 1024], P('seq', 'tensor')
- cross_k_grad: float32 [1024, 1024], P('seq', 'tensor')
- cross_v_grad: float32 [1024, 1024], P('seq', 'tensor')
- cross_o_grad: float32 [1024, 1024], P('tensor', 'seq')
- self_q_grad: float32 [1024, 1024], P('seq', 'tensor')
- self_k_grad: float32 [1024, 1024], P('seq', 'tensor')
- self_v_grad: float32 [1024, 1024], P('seq', 'tensor')
- self_o_grad: float32 [1024, 1024], P('tensor', 'seq')
- mlp_in_grad: float32 [1024, 4096], P('seq', 'tensor')
- mlp_out_grad: float32 [4096, 1024], P('tensor', 'seq')
- penalty: float32 [], replicated
Inputs may be any that keep to these rules, and one draw needn't show every extreme that they name: `clip_frames`: the entries sum to 4 and the largest is exactly 2. block_clip[b] depends only on b % 4, and clip c is named by exactly clip_frames[c] of the 4 residues. `source_index`: over the groups b with b // 4 == j the entries are a permutation of the rows j * 4 * 256 to (j + 1) * 4 * 256 - 1.
All inputs are finite; a program needn't handle non-finite values.
Results may differ from a plain program's by a relative error of at most 0.03.
Values may be sent and summed in bfloat16 or wider, within the bound.
No kernel may reach another device: no remote copies, remote signals or barrier semaphores. Data moves between devices by JAX's collectives and lax.ppermute only.
A program may use at most 128 MiB of HBM per device.

v0:
```python
import jax
import jax.numpy as jnp
from jax import lax
from jax.sharding import PartitionSpec as P

HEAD = 128
GROUP = 128
SRC = 256
GROUPS_FRAME = 8


epsilon = 1e-05
masked_value = -1e30


def layer_norm(values):
    centred = values - jnp.mean(values, axis=-1, keepdims=True)
    variance = jnp.mean(centred * centred, axis=-1, keepdims=True)
    return centred * lax.rsqrt(variance + epsilon)


def normed(values, gain_vec):
    return layer_norm(values) * gain_vec


def norm_back(values, gain_vec, grad_rows):
    ignored, pullback = jax.vjp(normed, values, gain_vec)
    return pullback(grad_rows)


def exact_gelu(values):
    return jax.nn.gelu(values, approximate=False)


def row_clips(block_clip, first_row, row_count):
    row_blocks = (first_row + jnp.arange(row_count, dtype=jnp.int32)) // GROUP
    block_ids = jnp.arange(block_clip.shape[0], dtype=jnp.int32)
    hit_table = row_blocks[:, None] == block_ids[None, :]
    return jnp.sum(jnp.where(hit_table, block_clip[None, :], 0), axis=1)


def scores(queries, key_rows, query_clip, key_clip):
    raw_scores = jnp.einsum("qhd,khd->hqk", queries, key_rows, preferred_element_type=jnp.float32)
    key_mask = (query_clip[:, None] == key_clip[None, :])[None]
    return (raw_scores * queries.shape[-1] ** (-0.5), key_mask)


def key_terms(queries, out_grads, log_totals, deltas, query_clip, key_rows, value_rows, key_clip):
    scaled, key_mask = scores(queries, key_rows, query_clip, key_clip)
    attn_probs = jnp.where(key_mask, jnp.exp(scaled - log_totals[:, :, None]), 0.0)
    prob_grads = jnp.einsum(
        "qhd,khd->hqk", out_grads, value_rows, preferred_element_type=jnp.float32
    )
    score_grads = (
        attn_probs * (prob_grads - deltas[:, :, None]) * queries.shape[-1] ** (-0.5)
    ).astype(jnp.bfloat16)
    key_grads = jnp.einsum("hqk,qhd->khd", score_grads, queries, preferred_element_type=jnp.float32)
    value_grads = jnp.einsum(
        "hqk,qhd->khd",
        attn_probs.astype(jnp.bfloat16),
        out_grads,
        preferred_element_type=jnp.float32,
    )
    return (key_grads, value_grads)


def local(
    latents,
    sources,
    source_index,
    block_clip,
    clip_frames,
    norm_src,
    norm_cross,
    norm_self,
    norm_mlp,
    cross_q,
    cross_k,
    cross_v,
    cross_o,
    self_q,
    self_k,
    self_v,
    self_o,
    mlp_in,
    mlp_out,
    out_grad,
):
    seq_rows = latents.shape[0]
    source_count = sources.shape[0]
    blocks_here = seq_rows // GROUP
    head_cols = cross_q.shape[1]
    heads_here = head_cols // HEAD
    scaling = HEAD ** (-0.5)
    seq_index = lax.axis_index("seq")
    inputs = latents.astype(jnp.float32)
    source_rows = sources.astype(jnp.float32)
    normed_src = normed(source_rows, norm_src).astype(jnp.bfloat16)
    normed_one = normed(inputs, norm_cross).astype(jnp.bfloat16)
    cross_query = jnp.dot(normed_one, cross_q, preferred_element_type=jnp.float32).astype(
        jnp.bfloat16
    )
    cross_key = jnp.dot(normed_src, cross_k, preferred_element_type=jnp.float32).astype(
        jnp.bfloat16
    )
    cross_value = jnp.dot(normed_src, cross_v, preferred_element_type=jnp.float32).astype(
        jnp.bfloat16
    )
    local_index = source_index - seq_index * source_count
    block_query = cross_query.reshape(blocks_here, GROUP, heads_here, HEAD)
    block_key = cross_key[local_index].reshape(blocks_here, SRC, heads_here, HEAD)
    block_value = cross_value[local_index].reshape(blocks_here, SRC, heads_here, HEAD)
    cross_scores = (
        jnp.einsum("bqhd,bkhd->bhqk", block_query, block_key, preferred_element_type=jnp.float32)
        * scaling
    )
    cross_probs = jax.nn.softmax(cross_scores, axis=-1)
    cross_weights = cross_probs.astype(jnp.bfloat16)
    cross_mixed = jnp.einsum(
        "bhqk,bkhd->bqhd", cross_weights, block_value, preferred_element_type=jnp.float32
    )
    cross_mixed = cross_mixed.astype(jnp.bfloat16).reshape(seq_rows, head_cols)
    cross_part = jnp.dot(cross_mixed, cross_o, preferred_element_type=jnp.float32)
    own_first = seq_index * seq_rows
    after_cross = inputs + lax.psum(cross_part.astype(jnp.bfloat16), "tensor").astype(jnp.float32)
    normed_two = normed(after_cross, norm_self).astype(jnp.bfloat16)
    self_query = (
        jnp.dot(normed_two, self_q, preferred_element_type=jnp.float32)
        .astype(jnp.bfloat16)
        .reshape(seq_rows, heads_here, HEAD)
    )
    self_key = jnp.dot(normed_two, self_k, preferred_element_type=jnp.float32).astype(jnp.bfloat16)
    self_value = jnp.dot(normed_two, self_v, preferred_element_type=jnp.float32).astype(
        jnp.bfloat16
    )
    key_all, value_all = (
        lax.all_gather(self_key, "seq", axis=0, tiled=True),
        lax.all_gather(self_value, "seq", axis=0, tiled=True),
    )
    total_rows = key_all.shape[0]
    key_width = total_rows // 16
    key_blocks = key_all.reshape(16, key_width, heads_here, HEAD)
    value_blocks = value_all.reshape(16, key_width, heads_here, HEAD)
    block_starts = jnp.arange(16, dtype=jnp.int32) * key_width
    query_clip = row_clips(block_clip, seq_index * seq_rows, seq_rows)

    def block_scores(key_rows, first_row):
        return scores(self_query, key_rows, query_clip, row_clips(block_clip, first_row, key_width))

    def max_step(carried, block_in):
        running_max, running_sum = carried
        key_rows, first_row = block_in
        scaled, key_mask = block_scores(key_rows, first_row)
        scaled = jnp.where(key_mask, scaled, masked_value)
        new_max = jnp.maximum(running_max, jnp.max(scaled, axis=-1))
        kept_terms = jnp.where(key_mask, jnp.exp(scaled - new_max[:, :, None]), 0.0)
        running_sum = running_sum * jnp.exp(running_max - new_max) + jnp.sum(kept_terms, axis=-1)
        return ((new_max, running_sum), None)

    empty_rows = jnp.zeros((heads_here, seq_rows), jnp.float32)
    (running_max, running_sum), ignored = lax.scan(
        max_step, (empty_rows + masked_value, empty_rows), (key_blocks, block_starts)
    )
    log_totals = running_max + jnp.log(running_sum)

    def self_probs(key_rows, first_row):
        scaled, key_mask = block_scores(key_rows, first_row)
        return jnp.where(key_mask, jnp.exp(scaled - log_totals[:, :, None]), 0.0)

    def value_step(summed, block_in):
        key_rows, value_rows, first_row = block_in
        attn_probs = self_probs(key_rows, first_row)
        return (
            summed
            + jnp.einsum(
                "hqk,khd->qhd",
                attn_probs.astype(jnp.bfloat16),
                value_rows,
                preferred_element_type=jnp.float32,
            ),
            None,
        )

    empty_out = jnp.zeros((seq_rows, heads_here, HEAD), jnp.float32)
    self_summed, ignored = lax.scan(value_step, empty_out, (key_blocks, value_blocks, block_starts))
    self_mixed = self_summed.astype(jnp.bfloat16).reshape(seq_rows, head_cols)
    self_part = jnp.dot(self_mixed, self_o, preferred_element_type=jnp.float32)
    after_self = after_cross + lax.psum(self_part.astype(jnp.bfloat16), "tensor").astype(
        jnp.float32
    )
    normed_three = normed(after_self, norm_mlp).astype(jnp.bfloat16)
    hidden = jnp.dot(normed_three, mlp_in, preferred_element_type=jnp.float32)
    activated = exact_gelu(hidden).astype(jnp.bfloat16)
    mlp_part = jnp.dot(activated, mlp_out, preferred_element_type=jnp.float32)
    result = after_self + lax.psum(mlp_part.astype(jnp.bfloat16), "tensor").astype(jnp.float32)
    held_rows = result.shape[0]
    row_blocks = (own_first + jnp.arange(held_rows, dtype=jnp.int32)) // GROUP
    all_blocks = jnp.arange(block_clip.shape[0], dtype=jnp.int32)
    row_squares = jnp.sum(jnp.square(result), axis=1)
    block_squares = jnp.sum(
        jnp.where(row_blocks[:, None] == all_blocks[None, :], row_squares[:, None], 0.0), axis=0
    )
    out_rows = out_grad.astype(jnp.float32)
    mlp_out_grad = jnp.einsum("rf,rd->fd", activated, out_grad, preferred_element_type=jnp.float32)
    act_grad = jnp.einsum("rd,fd->rf", out_grad, mlp_out, preferred_element_type=jnp.float32)
    ignored, gelu_back = jax.vjp(exact_gelu, hidden)
    hidden_grad = gelu_back(act_grad)[0].astype(jnp.bfloat16)
    mlp_in_grad = jnp.einsum(
        "rd,rf->df", normed_three, hidden_grad, preferred_element_type=jnp.float32
    )
    normed_three_part = jnp.einsum(
        "rf,df->rd", hidden_grad, mlp_in, preferred_element_type=jnp.float32
    )
    normed_three_grad = lax.psum(normed_three_part.astype(jnp.bfloat16), "tensor").astype(
        jnp.float32
    )
    self_grad_in, mlp_gain_grad = norm_back(after_self, norm_mlp, normed_three_grad)
    after_self_grad = out_rows + self_grad_in
    self_branch_grad = after_self_grad.astype(jnp.bfloat16)
    self_o_grad = jnp.einsum(
        "rk,rd->kd", self_mixed, self_branch_grad, preferred_element_type=jnp.float32
    )
    self_out_grad = jnp.einsum(
        "rd,kd->rk", self_branch_grad, self_o, preferred_element_type=jnp.float32
    )
    self_out_grad = self_out_grad.astype(jnp.bfloat16).reshape(seq_rows, heads_here, HEAD)

    def delta_step(summed, block_in):
        key_rows, value_rows, first_row = block_in
        attn_probs = self_probs(key_rows, first_row)
        prob_grads = jnp.einsum(
            "qhd,khd->hqk", self_out_grad, value_rows, preferred_element_type=jnp.float32
        )
        return (summed + jnp.sum(attn_probs * prob_grads, axis=-1), None)

    deltas, ignored = lax.scan(delta_step, empty_rows, (key_blocks, value_blocks, block_starts))

    def query_step(summed, block_in):
        key_rows, value_rows, first_row = block_in
        attn_probs = self_probs(key_rows, first_row)
        prob_grads = jnp.einsum(
            "qhd,khd->hqk", self_out_grad, value_rows, preferred_element_type=jnp.float32
        )
        score_grads = (attn_probs * (prob_grads - deltas[:, :, None]) * scaling).astype(
            jnp.bfloat16
        )
        return (
            summed
            + jnp.einsum("hqk,khd->qhd", score_grads, key_rows, preferred_element_type=jnp.float32),
            None,
        )

    query_summed, ignored = lax.scan(
        query_step, empty_out, (key_blocks, value_blocks, block_starts)
    )
    self_query_grad = query_summed.astype(jnp.bfloat16).reshape(seq_rows, head_cols)
    key_table = key_all.reshape(total_rows, heads_here, HEAD)
    value_table = value_all.reshape(total_rows, heads_here, HEAD)

    def sub_block(row_offset):
        key_rows = lax.dynamic_slice_in_dim(key_table, row_offset, key_width, 0)
        value_rows = lax.dynamic_slice_in_dim(value_table, row_offset, key_width, 0)
        key_grads, value_grads = key_terms(
            self_query,
            self_out_grad,
            log_totals,
            deltas,
            query_clip,
            key_rows,
            value_rows,
            row_clips(block_clip, row_offset, key_width),
        )
        return jnp.concatenate((key_grads, value_grads), axis=-1).reshape(key_width, 2 * head_cols)

    row_offsets = (
        jnp.arange(seq_rows * lax.axis_size("seq") // key_width, dtype=jnp.int32) * key_width
    )
    key_sums = (
        lax.psum_scatter(
            lax.map(sub_block, row_offsets)
            .reshape(seq_rows * lax.axis_size("seq"), 2 * head_cols)
            .astype(jnp.bfloat16),
            "seq",
            scatter_dimension=0,
            tiled=True,
        )
        .astype(jnp.float32)
        .reshape(seq_rows, heads_here, 2 * HEAD)
    )
    key_summed = key_sums[:, :, :HEAD]
    value_summed = key_sums[:, :, HEAD:]
    self_key_grad = key_summed.astype(jnp.bfloat16).reshape(seq_rows, head_cols)
    self_value_grad = value_summed.astype(jnp.bfloat16).reshape(seq_rows, head_cols)
    self_q_grad = jnp.einsum(
        "rd,rk->dk", normed_two, self_query_grad, preferred_element_type=jnp.float32
    )
    self_k_grad = jnp.einsum(
        "rd,rk->dk", normed_two, self_key_grad, preferred_element_type=jnp.float32
    )
    self_v_grad = jnp.einsum(
        "rd,rk->dk", normed_two, self_value_grad, preferred_element_type=jnp.float32
    )
    normed_two_part = jnp.einsum(
        "rk,dk->rd", self_query_grad, self_q, preferred_element_type=jnp.float32
    )
    normed_two_part = normed_two_part + jnp.einsum(
        "rk,dk->rd", self_key_grad, self_k, preferred_element_type=jnp.float32
    )
    normed_two_part = normed_two_part + jnp.einsum(
        "rk,dk->rd", self_value_grad, self_v, preferred_element_type=jnp.float32
    )
    normed_two_grad = lax.psum(normed_two_part.astype(jnp.bfloat16), "tensor").astype(jnp.float32)
    cross_grad_in, self_gain_grad = norm_back(after_cross, norm_self, normed_two_grad)
    after_cross_grad = after_self_grad + cross_grad_in
    cross_branch_grad = after_cross_grad.astype(jnp.bfloat16)
    cross_o_grad = jnp.einsum(
        "rk,rd->kd", cross_mixed, cross_branch_grad, preferred_element_type=jnp.float32
    )
    cross_out_grad = jnp.einsum(
        "rd,kd->rk", cross_branch_grad, cross_o, preferred_element_type=jnp.float32
    )
    cross_out_grad = cross_out_grad.astype(jnp.bfloat16).reshape(
        blocks_here, GROUP, heads_here, HEAD
    )
    cross_prob_grads = jnp.einsum(
        "bqhd,bkhd->bhqk", cross_out_grad, block_value, preferred_element_type=jnp.float32
    )
    cross_deltas = jnp.sum(cross_probs * cross_prob_grads, axis=-1, keepdims=True)
    cross_score_grads = (cross_probs * (cross_prob_grads - cross_deltas) * scaling).astype(
        jnp.bfloat16
    )
    cross_query_grad = jnp.einsum(
        "bhqk,bkhd->bqhd", cross_score_grads, block_key, preferred_element_type=jnp.float32
    )
    cross_query_grad = cross_query_grad.astype(jnp.bfloat16).reshape(seq_rows, head_cols)
    key_pieces = jnp.einsum(
        "bhqk,bqhd->bkhd", cross_score_grads, block_query, preferred_element_type=jnp.float32
    ).reshape(blocks_here * SRC, head_cols)
    value_pieces = jnp.einsum(
        "bhqk,bqhd->bkhd", cross_weights, cross_out_grad, preferred_element_type=jnp.float32
    ).reshape(blocks_here * SRC, head_cols)
    flat_index = local_index.reshape(-1)
    cross_key_grad = (
        jnp.zeros((source_count, head_cols), jnp.float32)
        .at[flat_index]
        .add(key_pieces)
        .astype(jnp.bfloat16)
    )
    cross_value_grad = (
        jnp.zeros((source_count, head_cols), jnp.float32)
        .at[flat_index]
        .add(value_pieces)
        .astype(jnp.bfloat16)
    )
    cross_q_grad = jnp.einsum(
        "rd,rk->dk", normed_one, cross_query_grad, preferred_element_type=jnp.float32
    )
    cross_k_grad = jnp.einsum(
        "sd,sk->dk", normed_src, cross_key_grad, preferred_element_type=jnp.float32
    )
    cross_v_grad = jnp.einsum(
        "sd,sk->dk", normed_src, cross_value_grad, preferred_element_type=jnp.float32
    )
    normed_one_part = jnp.einsum(
        "rk,dk->rd", cross_query_grad, cross_q, preferred_element_type=jnp.float32
    )
    normed_src_part = jnp.einsum(
        "sk,dk->sd", cross_key_grad, cross_k, preferred_element_type=jnp.float32
    )
    normed_src_part = normed_src_part + jnp.einsum(
        "sk,dk->sd", cross_value_grad, cross_v, preferred_element_type=jnp.float32
    )
    row_parts = (
        cross_q_grad,
        cross_k_grad,
        cross_v_grad,
        self_q_grad,
        self_k_grad,
        self_v_grad,
        mlp_in_grad,
    )
    cq_out, ck_out, cv_out, sq_out, sk_out, sv_out, mlp_in_out = (
        lax.psum_scatter(
            row_parts[0].astype(jnp.bfloat16), "seq", scatter_dimension=0, tiled=True
        ).astype(jnp.float32),
        lax.psum_scatter(
            row_parts[1].astype(jnp.bfloat16), "seq", scatter_dimension=0, tiled=True
        ).astype(jnp.float32),
        lax.psum_scatter(
            row_parts[2].astype(jnp.bfloat16), "seq", scatter_dimension=0, tiled=True
        ).astype(jnp.float32),
        lax.psum_scatter(
            row_parts[3].astype(jnp.bfloat16), "seq", scatter_dimension=0, tiled=True
        ).astype(jnp.float32),
        lax.psum_scatter(
            row_parts[4].astype(jnp.bfloat16), "seq", scatter_dimension=0, tiled=True
        ).astype(jnp.float32),
        lax.psum_scatter(
            row_parts[5].astype(jnp.bfloat16), "seq", scatter_dimension=0, tiled=True
        ).astype(jnp.float32),
        lax.psum_scatter(
            row_parts[6].astype(jnp.bfloat16), "seq", scatter_dimension=0, tiled=True
        ).astype(jnp.float32),
    )
    col_parts = (cross_o_grad, self_o_grad, mlp_out_grad)
    co_out, so_out, mlp_out_out = (
        lax.psum_scatter(
            col_parts[0].astype(jnp.bfloat16), "seq", scatter_dimension=1, tiled=True
        ).astype(jnp.float32),
        lax.psum_scatter(
            col_parts[1].astype(jnp.bfloat16), "seq", scatter_dimension=1, tiled=True
        ).astype(jnp.float32),
        lax.psum_scatter(
            col_parts[2].astype(jnp.bfloat16), "seq", scatter_dimension=1, tiled=True
        ).astype(jnp.float32),
    )
    normed_one_grad, normed_src_grad = (
        lax.psum(normed_one_part.astype(jnp.bfloat16), "tensor").astype(jnp.float32),
        lax.psum(normed_src_part.astype(jnp.bfloat16), "tensor").astype(jnp.float32),
    )
    input_grad_part, cross_gain_grad = norm_back(inputs, norm_cross, normed_one_grad)
    source_grad, src_gain_grad = norm_back(source_rows, norm_src, normed_src_grad)
    output_rows = result.astype(jnp.bfloat16)
    latents_grad = (after_cross_grad + input_grad_part).astype(jnp.bfloat16)
    sources_grad = source_grad.astype(jnp.bfloat16)
    small_parts = (src_gain_grad, cross_gain_grad, self_gain_grad, mlp_gain_grad, block_squares)
    src_gain_out, cross_gain_out, self_gain_out, mlp_gain_out, block_totals = lax.psum(
        (small_parts[0], small_parts[1], small_parts[2], small_parts[3], small_parts[4]), "seq"
    )
    block_norms = jnp.sqrt(block_totals / (GROUP * result.shape[1]) + 1e-06)
    clip_ids = jnp.arange(clip_frames.shape[0], dtype=jnp.int32)
    member = block_clip[None, :] == clip_ids[:, None]
    per_clip = jnp.sum(jnp.where(member, block_norms[None, :], 0.0), axis=1)
    penalty = jnp.mean(per_clip / (GROUPS_FRAME * clip_frames.astype(jnp.float32)))
    return (
        output_rows,
        latents_grad,
        sources_grad,
        src_gain_out,
        cross_gain_out,
        self_gain_out,
        mlp_gain_out,
        cq_out,
        ck_out,
        cv_out,
        co_out,
        sq_out,
        sk_out,
        sv_out,
        so_out,
        mlp_in_out,
        mlp_out_out,
        penalty,
    )


def solution(mesh):
    in_specs = (
        P("seq", None),
        P("seq", None),
        P("seq", None),
        P(),
        P(),
        P(),
        P(),
        P(),
        P(),
        P(None, "tensor"),
        P(None, "tensor"),
        P(None, "tensor"),
        P("tensor", None),
        P(None, "tensor"),
        P(None, "tensor"),
        P(None, "tensor"),
        P("tensor", None),
        P(None, "tensor"),
        P("tensor", None),
        P("seq", None),
    )
    out_specs = (
        P("seq", None),
        P("seq", None),
        P("seq", None),
        P(),
        P(),
        P(),
        P(),
        P("seq", "tensor"),
        P("seq", "tensor"),
        P("seq", "tensor"),
        P("tensor", "seq"),
        P("seq", "tensor"),
        P("seq", "tensor"),
        P("seq", "tensor"),
        P("tensor", "seq"),
        P("seq", "tensor"),
        P("tensor", "seq"),
        P(),
    )
    return jax.shard_map(local, mesh=mesh, in_specs=in_specs, out_specs=out_specs, check_vma=False)
```

profile of v0, /device:TPU:0, one launch (start us, length us, event | category | flops | bytes accessed | tf_op | source)
XLA Modules:
  0.0 1523.5 jit_solution(14639181916310513819)
XLA Ops:
  21.6 5.7 gather_fusion.1
  34.4 5.7 gather_fusion
  51.3 38.9 %all-reduce.9.cloned.1.call-done = bf16[512,1024]{1,0:T(8,128)(2,1)} async-done(((bf16[512,1024]{1,0:T(8,128)(2,1)}), bf16[512,1024]{1,0:T(8,128)(2,1)}) %all-reduce.9.cloned.1.call-update) | async-done | bytes 1048592 | tf_op jit(solution)/shard_map/psum | solution.py:125
  100.8 44.1 %all-gather.5.cloned.1.call-done = bf16[4096,256]{1,0:T(8,128)(2,1)} async-done(((bf16[512,256]{1,0:T(8,128)(2,1)}), bf16[4096,256]{1,0:T(8,128)(2,1)}) %all-gather.5.cloned.1.call-update) | async-done | bytes 2097168 | tf_op jit(solution)/shard_map/all_gather | solution.py:137
  152.4 50.7 %while.67 = (s32[]{:T(128)}, f32[2,512]{1,0:T(2,128)S(1)}, f32[2,512]{1,0:T(2,128)S(1)}, s32[512]{0:T(512)S(1)}, s32[16]{0:T(128)S(1)}, /*index=5*/s32[32]{0:T(1...) while((s32[]{:T(128)}, f32[2,512]{1,0:T(2,128)S(1)}, ...), condition=%wide.region_14.15_spmd.clone, body=%wide.region_10.14_spmd.clone.sunk | while | flops 68846336 | bytes 2943244 | solution.py:161
  207.8 105.5 %while.68 = (s32[]{:T(128)}, f32[512,2,128]{0,2,1:T(8,128)}, bf16[16,256,2,128]{3,2,1,0:T(2,128)(2,1)}, s32[512]{0:T(512)S(1)}, s32[16]{0:T(128)S(1)}, /*index=5...) while((s32[]{:T(128)}, f32[512,2,128]{0,2,1:T(8,128)}, ...), condition=%wide.region_17.18_spmd.clone, body=%wide.region_15.17_spmd.clone.sunk | while | flops 135687936 | bytes 2370383 | solution.py:185
  317.5 34.7 %all-reduce.11.cloned.1.call-done = bf16[512,1024]{1,0:T(8,128)(2,1)} async-done(((bf16[512,1024]{1,0:T(8,128)(2,1)}), bf16[512,1024]{1,0:T(8,128)(2,1)}) %all-reduce.11.cloned.1.call-update) | async-done | bytes 1048592 | tf_op jit(solution)/shard_map/psum | solution.py:188
  358.0 6.1 add_convert_fusion.4
  380.8 40.5 %all-reduce.17.cloned.1.call-done = (bf16[512,1024]{1,0:T(8,128)(2,1)}, bf16[512,1024]{1,0:T(8,128)(2,1)}) async-done(((bf16[512,1024]{1,0:T(8,128)(2,1)}, bf16[512,1024]{1,0:T(8,128)(2,1)}), (bf16[512,1024]{1,0:T(8,128)(2,1)}, bf16[512,1024]{1,0:T(8,128)(2,1)})) %all-reduce.17.cloned.1.call-update) | async-done | bytes 2097168 | tf_op jit(solution)/shard_map/psum | solution.py:195
  421.4 4.2 fusion.106
  429.3 65.2 %while.69 = (s32[]{:T(128)}, f32[2,512]{1,0:T(2,128)S(1)}, s32[512]{0:T(512)S(1)}, s32[16]{0:T(128)S(1)}, s32[32]{0:T(128)S(1)}, /*index=5*/bf16[16,256,2,128]{3...) while((s32[]{:T(128)}, f32[2,512]{1,0:T(2,128)S(1)}, ...), condition=%wide.region_28.29_spmd.clone, body=%wide.region_25.28_spmd.clone.sunk | while | flops 135688960 | bytes 3172639 | solution.py:236
  494.5 107.7 %while.66 = (s32[]{:T(128)}, bf16[16,256,512]{2,1,0:T(8,128)(2,1)}, s32[512]{0:T(512)S(1)}, s32[16]{0:T(128)S(1)}, s32[32]{0:T(128)S(1)}, /*index=5*/bf16[4096,2...) while((s32[]{:T(128)}, bf16[16,256,512]{2,1,0:T(8,128)(2,1)}, ...), condition=%wide.region_34.35_spmd, body=%wide.region_32.34_spmd.sunk | while | flops 271216384 | bytes 7092551 | solution.py:280
  603.4 69.4 %while.70 = (s32[]{:T(128)}, f32[512,2,128]{0,2,1:T(8,128)S(1)}, bf16[16,256,2,128]{3,1,2,0:T(8,128)(2,1)}, s32[512]{0:T(512)S(1)}, s32[16]{0:T(128)S(1)}, /*ind...) while((s32[]{:T(128)}, f32[512,2,128]{0,2,1:T(8,128)S(1)}, ...), condition=%wide.region_31.32_spmd.clone, body=%wide.region_29.31_spmd.clone.sunk | while | flops 203583232 | bytes 4341538 | solution.py:253
  675.0 15.5 %reduce-scatter.18.cloned.1.call-done = bf16[512,512]{1,0:T(8,128)(2,1)} async-done(((bf16[4096,512]{1,0:T(8,128)(2,1)}), bf16[512,512]{1,0:T(8,128)(2,1)}) %reduce-scatter.18.cloned.1.call-update) | async-done | bytes 524304 | tf_op jit(solution)/shard_map/reduce_scatter | solution.py:279
  721.9 11.3 all-reduce.13.cloned.1.call-done
  744.4 7.0 fusion.129
  753.5 8.0 convolution_bitcast_fusion.4
  763.1 6.0 scatter_custom_fusion
  776.1 6.0 scatter_custom_fusion.1
  792.2 7.8 reduce-scatter.36.cloned.1.call-done
  801.5 63.2 %reduce-scatter.26.cloned.1.call-done = bf16[128,256]{1,0:T(8,128)(2,1)} async-done(((bf16[1024,256]{1,0:T(8,128)(2,1)}), bf16[128,256]{1,0:T(8,128)(2,1)}) %reduce-scatter.26.cloned.1.call-update) | async-done | bytes 65552 | tf_op jit(solution)/shard_map/reduce_scatter | solution.py:392
  866.3 69.0 %reduce-scatter.38.cloned.1.call-done = bf16[128,1024]{1,0:T(8,128)(2,1)} async-done(((bf16[1024,1024]{1,0:T(8,128)(2,1)}), bf16[128,1024]{1,0:T(8,128)(2,1)}) %reduce-scatter.38.cloned.1.call-update) | async-done | bytes 262160
  937.2 68.6 %reduce-scatter.32.cloned.1.call-done = bf16[128,1024]{1,0:T(8,128)(2,1)} async-done(((bf16[1024,1024]{1,0:T(8,128)(2,1)}), bf16[128,1024]{1,0:T(8,128)(2,1)}) %reduce-scatter.32.cloned.1.call-update) | async-done | bytes 262160 | tf_op jit(solution)/shard_map/reduce_scatter | solution.py:401
  1007.7 62.7 %reduce-scatter.28.cloned.1.call-done = bf16[128,256]{1,0:T(8,128)(2,1)} async-done(((bf16[1024,256]{1,0:T(8,128)(2,1)}), bf16[128,256]{1,0:T(8,128)(2,1)}) %reduce-scatter.28.cloned.1.call-update) | async-done | bytes 65552 | tf_op jit(solution)/shard_map/reduce_scatter | solution.py:395
  1071.9 62.9 %reduce-scatter.30.cloned.1.call-done = bf16[128,256]{1,0:T(8,128)(2,1)} async-done(((bf16[1024,256]{1,0:T(8,128)(2,1)}), bf16[128,256]{1,0:T(8,128)(2,1)}) %reduce-scatter.30.cloned.1.call-update) | async-done | bytes 65552 | tf_op jit(solution)/shard_map/reduce_scatter | solution.py:398
  1136.3 63.0 %reduce-scatter.34.cloned.1.call-done = bf16[128,256]{1,0:T(8,128)(2,1)} async-done(((bf16[1024,256]{1,0:T(8,128)(2,1)}), bf16[128,256]{1,0:T(8,128)(2,1)}) %reduce-scatter.34.cloned.1.call-update) | async-done | bytes 65552
  1200.9 62.5 %reduce-scatter.20.cloned.1.call-done = bf16[128,256]{1,0:T(8,128)(2,1)} async-done(((bf16[1024,256]{1,0:T(8,128)(2,1)}), bf16[128,256]{1,0:T(8,128)(2,1)}) %reduce-scatter.20.cloned.1.call-update) | async-done | bytes 65552 | tf_op jit(solution)/shard_map/reduce_scatter | solution.py:383
  1264.9 63.0 %reduce-scatter.22.cloned.1.call-done = bf16[128,256]{1,0:T(8,128)(2,1)} async-done(((bf16[1024,256]{1,0:T(8,128)(2,1)}), bf16[128,256]{1,0:T(8,128)(2,1)}) %reduce-scatter.22.cloned.1.call-update) | async-done | bytes 65552 | tf_op jit(solution)/shard_map/reduce_scatter | solution.py:386
  1329.4 62.6 %reduce-scatter.24.cloned.1.call-done = bf16[128,256]{1,0:T(8,128)(2,1)} async-done(((bf16[1024,256]{1,0:T(8,128)(2,1)}), bf16[128,256]{1,0:T(8,128)(2,1)}) %reduce-scatter.24.cloned.1.call-update) | async-done | bytes 65552 | tf_op jit(solution)/shard_map/reduce_scatter | solution.py:389
  1393.6 69.2 %all-reduce.15.cloned.1.call-done = (bf16[512,1024]{1,0:T(8,128)(2,1)}, bf16[1024,1024]{1,0:T(8,128)(2,1)}) async-done(((bf16[512,1024]{1,0:T(8,128)(2,1)}, bf16[1024,1024]{1,0:T(8,128)(2,1)}), (bf16[512,1024]{1,0:T(8,128)(2,1)}, bf16[1024,1024]{1,0:T(8,128)(2,1)})) %all-reduce.15.cloned.1.call-update) | async-done | bytes 3145744 | tf_op jit(solution)/shard_map/psum | solution.py:418
  1471.8 37.7 %all-reduce = (f32[1024]{0:T(1024)}, f32[1024]{0:T(1024)}, f32[1024]{0:T(1024)}, f32[1024]{0:T(1024)}, f32[32]{0:T(128)S(1)}) all-reduce(f32[1024]{0:T(1024)S(1)} %get-tuple-element.965, f32[1024]{0:T(1024)S(1)} %get-tuple-element.971, f32[1024]{0:T(1024)S(1)} %get-tuple-element.967, ...), channel_id=1, replica_groups=mesh['seq'=8,'tensor'=4] {'seq'}, use_global_device_ids=true, to_apply=%region_49.50 | all-reduce | flops 4128 | bytes 33024 | tf_op jit(solution)/shard_map/psum | solution.py:427
  1509.7 4.2 add_convert_fusion
  (1073 shorter events, 540.8 us)
Async XLA Ops:
  7.2 350.8 %copy-start = (bf16[1024,1024]{1,0:T(8,128)(2,1)S(1)}, bf16[1024,1024]{1,0:T(8,128)(2,1)}, u32[]{:S(2)}) copy-start(bf16[1024,1024]{1,0:T(8,128)(2,1)} %param.48) | copy-start | bytes 6291460
  7.2 83.0 %all-reduce.9.cloned.1.call-start = ((), (), s32[]{:S(2)}) async-start(), calls=%async_computation.11 | async-start | bytes 2097152 | tf_op jit(solution)/shard_map/psum | solution.py:125
  16.4 28.3 %copy-start.43 = (bf16[4,128,2,128]{1,3,2,0:T(8,128)(2,1)}, bf16[4,128,2,128]{1,3,2,0:T(8,128)(2,1)S(1)}, u32[]{:S(2)}) copy-start(bf16[4,128,2,128]{1,3,2,0:T(8,128)(2,1)S(1)} %copy.155) | copy-start | bytes 786436
  48.6 43.2 %copy-start.35 = (bf16[4,128,2,128]{3,2,1,0:T(2,128)(2,1)}, bf16[4,128,2,128]{3,2,1,0:T(2,128)(2,1)S(1)}, u32[]{:S(2)}) copy-start(bf16[4,128,2,128]{3,2,1,0:T(2,128)(2,1)S(1)} %copy.134) | copy-start | bytes 786436
  51.2 41.2 %copy-start.60 = (f32[1024]{0:T(1024)S(1)}, f32[1024]{0:T(1024)}, u32[]{:S(2)}) copy-start(f32[1024]{0:T(1024)} %param.37) | copy-start | bytes 12292
  51.2 93.7 %all-gather.5.cloned.1.call-start = ((), (), s32[]{:S(2)}) async-start(), calls=%async_computation.13 | async-start | bytes 2359296 | tf_op jit(solution)/shard_map/all_gather | solution.py:137
  95.1 108.6 %all-gather.3.cloned.1.call-start = ((), (), s32[]{:S(2)}) async-start(), calls=%async_computation.12 | async-start | bytes 2359296 | tf_op jit(solution)/shard_map/all_gather | solution.py:138
  100.6 251.7 %all-reduce.11.cloned.1.call-start = ((), (), s32[]{:S(2)}) async-start(), calls=%async_computation.14 | async-start | bytes 2097152 | tf_op jit(solution)/shard_map/psum | solution.py:188
  313.2 39.0 %copy-start.101 = (s32[16]{0:T(128)}, s32[16]{0:T(128)S(1)}, u32[]{:S(2)}) copy-start(s32[16]{0:T(128)S(1)} %get-tuple-element.1692) | copy-start | bytes 196
  317.5 103.9 %all-reduce.17.cloned.1.call-start = ((), (), s32[]{:S(2)}) async-start(), calls=%async_computation.28 | async-start | bytes 4194304 | tf_op jit(solution)/shard_map/psum | solution.py:195
  354.3 71.3 %copy-start.72 = (f32[512]{0:T(512)}, f32[512]{0:T(512)S(1)}, u32[]{:S(2)}) copy-start(f32[512]{0:T(512)S(1)} %broadcast_multiply_fusion.1) | copy-start | bytes 6148
  356.6 69.0 %copy-start.76 = (f32[512]{0:T(512)}, f32[512]{0:T(512)S(1)}, u32[]{:S(2)}) copy-start(f32[512]{0:T(512)S(1)} %fusion.180) | copy-start | bytes 6148
  369.3 321.3 %reduce-scatter.18.cloned.1.call-start = ((), (), s32[]{:S(2)}) async-start(), calls=%async_computation.15 | async-start | bytes 4718592 | tf_op jit(solution)/shard_map/reduce_scatter | solution.py:279
  376.7 44.7 %copy-start.8 = (f32[512,1024]{1,0:T(8,128)S(1)}, f32[512,1024]{1,0:T(8,128)}, u32[]{:S(2)}) copy-start(f32[512,1024]{1,0:T(8,128)} %copy-done.7) | copy-start | bytes 6291460
  602.3 131.0 %all-reduce.13.cloned.1.call-start = ((), (), s32[]{:S(2)}) async-start(), calls=%async_computation.16 | async-start | bytes 2097152 | tf_op jit(solution)/shard_map/psum | solution.py:312
  697.3 102.6 %reduce-scatter.36.cloned.1.call-start = ((), (), s32[]{:S(2)}) async-start(), calls=%async_computation.25 | async-start | bytes 589824
  702.0 162.8 %reduce-scatter.26.cloned.1.call-start = ((), (), s32[]{:S(2)}) async-start(), calls=%async_computation.20 | async-start | bytes 589824 | tf_op jit(solution)/shard_map/reduce_scatter | solution.py:392
  704.3 230.9 %reduce-scatter.38.cloned.1.call-start = ((), (), s32[]{:S(2)}) async-start(), calls=%async_computation.26 | async-start | bytes 2359296
  712.3 293.6 %reduce-scatter.32.cloned.1.call-start = ((), (), s32[]{:S(2)}) async-start(), calls=%async_computation.23 | async-start | bytes 2359296 | tf_op jit(solution)/shard_map/reduce_scatter | solution.py:401
  717.9 352.5 %reduce-scatter.28.cloned.1.call-start = ((), (), s32[]{:S(2)}) async-start(), calls=%async_computation.21 | async-start | bytes 589824 | tf_op jit(solution)/shard_map/reduce_scatter | solution.py:395
  720.5 12.8 copy-start.61
  720.5 414.3 %reduce-scatter.30.cloned.1.call-start = ((), (), s32[]{:S(2)}) async-start(), calls=%async_computation.22 | async-start | bytes 589824 | tf_op jit(solution)/shard_map/reduce_scatter | solution.py:398
  721.8 13.4 copy-start.87
  721.8 13.4 copy-start.75
  721.9 477.4 %reduce-scatter.34.cloned.1.call-start = ((), (), s32[]{:S(2)}) async-start(), calls=%async_computation.24 | async-start | bytes 589824
  741.2 522.3 %reduce-scatter.20.cloned.1.call-start = ((), (), s32[]{:S(2)}) async-start(), calls=%async_computation.17 | async-start | bytes 589824 | tf_op jit(solution)/shard_map/reduce_scatter | solution.py:383
  753.2 574.7 %reduce-scatter.22.cloned.1.call-start = ((), (), s32[]{:S(2)}) async-start(), calls=%async_computation.18 | async-start | bytes 589824 | tf_op jit(solution)/shard_map/reduce_scatter | solution.py:386
  772.6 619.4 %reduce-scatter.24.cloned.1.call-start = ((), (), s32[]{:S(2)}) async-start(), calls=%async_computation.19 | async-start | bytes 589824 | tf_op jit(solution)/shard_map/reduce_scatter | solution.py:389
  785.3 677.4 %all-reduce.15.cloned.1.call-start = ((), (), s32[]{:S(2)}) async-start(), calls=%async_computation.27 | async-start | bytes 6291456 | tf_op jit(solution)/shard_map/psum | solution.py:418
  937.2 527.4 %copy-start.81 = (f32[512]{0:T(512)S(1)}, f32[512]{0:T(512)}, u32[]{:S(2)}) copy-start(f32[512]{0:T(512)} %copy-done.80) | copy-start | bytes 6148
  937.2 527.4 %copy-start.4 = (bf16[1024,1024]{1,0:T(8,128)(2,1)S(1)}, bf16[1024,1024]{1,0:T(8,128)(2,1)}, u32[]{:S(2)}) copy-start(bf16[1024,1024]{1,0:T(8,128)(2,1)} %param.31) | copy-start | bytes 6291460
  937.2 527.4 %copy-start.63 = (f32[1024]{0:T(1024)S(1)}, f32[1024]{0:T(1024)}, u32[]{:S(2)}) copy-start(f32[1024]{0:T(1024)} %param.35) | copy-start | bytes 12292
  (120 other events, 287.9 us)
Sparse Core Ops, SparseCore 0:
  51.3 38.8 all-reduce.8
  95.2 49.6 all-gather.4
  147.9 48.0 all-gather.2
  317.6 34.5 all-reduce.10
  369.4 51.9 all-reduce.16
  602.4 88.1 reduce-scatter.17
  697.4 35.7 all-reduce.12
  737.5 62.3 reduce-scatter.35
  803.8 60.8 reduce-scatter.25
  868.6 66.6 reduce-scatter.37
  939.2 66.5 reduce-scatter.31
  1009.4 60.9 reduce-scatter.27
  1073.7 61.0 reduce-scatter.29
  1138.3 60.8 reduce-scatter.33
  1202.4 60.9 reduce-scatter.19
  1267.0 60.9 reduce-scatter.21
  1331.1 60.9 reduce-scatter.23
  1395.1 67.6 all-reduce.14
where the time goes:
time: 1540 us; the launch traced here: 1520 us
  waiting for transfers between devices  840 us (55%)
  matrix products  258 us (17%)
  local copies, waits for them, and re-layouts  184 us (12%)
  other arithmetic  149 us (10%)
  blocking collectives  37.7 us (2%)
  loops' own time  34.6 us (2%)
  between operations  17.8 us (1%)
    unnamed x21, waiting for transfers between devices  140 us
    dynamic_slice x112, local copies, waits for them, and re-layouts, local(): lax.scan(max_step, (empty_rows + masked_value, empty_rows), (key_blocks,...  75 us
    dot_general x64, matrix products, scores(): jnp.einsum('qhd,khd->hqk', queries, key_rows, preferred_element_type=jnp....  71 us
    psum x1, waiting for transfers between devices, local(): lax.psum(normed_one_part.astype(jnp.bfloat16), 'tensor').astype(jnp.float32)  69.2 us
    reduce_scatter x1, waiting for transfers between devices, local(): lax.psum_scatter(row_parts[6].astype(jnp.bfloat16), 'seq', scatter_dimens...  68.6 us
    reduce_scatter x1, waiting for transfers between devices, local(): lax.psum_scatter(row_parts[3].astype(jnp.bfloat16), 'seq', scatter_dimens...  63.2 us
    reduce_scatter x1, waiting for transfers between devices, local(): lax.psum_scatter(row_parts[1].astype(jnp.bfloat16), 'seq', scatter_dimens...  63 us
    reduce_scatter x1, waiting for transfers between devices, local(): lax.psum_scatter(row_parts[5].astype(jnp.bfloat16), 'seq', scatter_dimens...  62.9 us
  transfers between devices with their start and end apart: 18, of which 17 were waited for; matrix products, arithmetic and copies ran while one was open for 15% of the time, Pallas kernels for 0%

commit v1 on v0

v1 whole, which is shorter than its diff:
```python
import functools

import jax
import jax.numpy as jnp
from jax import lax
from jax.experimental import pallas as pl
from jax.experimental.pallas import tpu as pltpu
from jax.sharding import PartitionSpec as P

HEAD = 128
GROUP = 128
SRC = 256
GROUPS_FRAME = 8
LOG2E = 1.4426950408889634
epsilon = 1e-05
masked_value = -1e30
bf16 = jnp.bfloat16
f32 = jnp.float32
EXTRA = 16

VMEM = pl.BlockSpec(memory_space=pltpu.VMEM)
SMEM = pl.BlockSpec(memory_space=pltpu.SMEM)


def sds(shape, dtype):
    return jax.ShapeDtypeStruct(shape, dtype)


def dot(a, b):
    return lax.dot_general(a, b, (((1,), (0,)), ((), ())), preferred_element_type=f32)


def dot_t(a, b):
    return lax.dot_general(a, b, (((1,), (1,)), ((), ())), preferred_element_type=f32)


def dot_ta(a, b):
    return lax.dot_general(a, b, (((0,), (0,)), ((), ())), preferred_element_type=f32)


def centre(values):
    centred = values - jnp.mean(values, axis=-1, keepdims=True)
    variance = jnp.mean(centred * centred, axis=-1, keepdims=True)
    inverse = lax.rsqrt(variance + epsilon)
    return centred * inverse, inverse


def call(body, outs, ins, args, name, scratch=(), grid=None, prefetch=0, flops=0, nbytes=0, trans=0):
    out_specs = [spec for ignored, spec in outs]
    out_shape = [shape for shape, ignored in outs]
    return pl.pallas_call(
        body,
        out_shape=out_shape,
        grid_spec=pltpu.PrefetchScalarGridSpec(
            num_scalar_prefetch=prefetch,
            grid=() if grid is None else grid,
            in_specs=ins,
            out_specs=out_specs,
            scratch_shapes=list(scratch),
        ),
        compiler_params=pltpu.CompilerParams(vmem_limit_bytes=56 * 2**20),
        cost_estimate=pl.CostEstimate(
            flops=int(flops), bytes_accessed=int(nbytes), transcendentals=int(trans)
        ),
        name=name,
    )(*args)


def cross_forward_body(
    core_ref, idx_ref, lat_ref, src_ref, gain_one_ref, gain_src_ref, wq_ref, wk_ref, wv_ref,
    n1_ref, ns_ref, q_ref, kvp_ref, keep_ref, send_ref, kv_s, *, steps,
):
    i = pl.program_id(0)
    width = wq_ref.shape[1]
    heads = width // HEAD
    rows_src = src_ref.shape[0]
    normed_src = (centre(src_ref[...].astype(f32))[0] * gain_src_ref[...]).astype(bf16)
    ns_ref[...] = normed_src
    row0 = pl.multiple_of(i * rows_src, rows_src)
    kv_s[pl.ds(row0, rows_src), 0:width] = dot(normed_src, wk_ref[...]).astype(bf16)
    kv_s[pl.ds(row0, rows_src), width:] = dot(normed_src, wv_ref[...]).astype(bf16)
    normed_one = (centre(lat_ref[...].astype(f32))[0] * gain_one_ref[...]).astype(bf16)
    n1_ref[...] = normed_one
    grp0 = pl.multiple_of(i * GROUP, GROUP)
    q_ref[pl.ds(grp0, GROUP), :] = dot(normed_one, wq_ref[...]).astype(bf16)

    @pl.when(i == steps - 1)
    def _():
        count = kv_s.shape[0]
        lanes = lax.broadcasted_iota(jnp.int32, (128, count), 1).astype(f32)
        for b in range(steps):
            for part in range(SRC // 128):
                row = idx_ref[b : b + 1, part * 128 : (part + 1) * 128]
                column = jnp.transpose(jnp.broadcast_to(row, (128, 128)))
                picks = jnp.where(jnp.tile(column, (1, count // 128)) == lanes, 1.0, 0.0).astype(bf16)
                r0 = b * SRC + part * 128
                kvp_ref[r0 : r0 + 128, :] = dot(picks, kv_s[...]).astype(bf16)
        for b in range(steps):
            for h in range(heads):
                cols = slice(h * HEAD, (h + 1) * HEAD)
                q = q_ref[b * GROUP : (b + 1) * GROUP, cols]
                k = kvp_ref[b * SRC : (b + 1) * SRC, cols]
                v = kvp_ref[b * SRC : (b + 1) * SRC, width + h * HEAD : width + (h + 1) * HEAD]
                s = dot_t(q, k) * (HEAD ** (-0.5) * LOG2E)
                p = jnp.exp2(s - jnp.max(s, axis=-1, keepdims=True))
                total = jnp.sum(p, axis=-1, keepdims=True)
                mixed = (dot(p.astype(bf16), v) / total).astype(bf16)
                if b < steps // 2:
                    keep_ref[b * GROUP : (b + 1) * GROUP, cols] = mixed
                else:
                    r0 = (b - steps // 2) * GROUP
                    send_ref[r0 : r0 + GROUP, cols] = mixed


def cross_forward(core, idx, latents, sources, gain_one, gain_src, wq, wk, wv):
    rows, width_d = latents.shape
    steps = rows // GROUP
    count = sources.shape[0]
    blk = count // steps
    width = wq.shape[1]
    whole = lambda shape: pl.BlockSpec(shape, lambda i, c: (0,) * len(shape))
    return call(
        functools.partial(cross_forward_body, steps=steps),
        [
            (sds((rows, width_d), bf16), pl.BlockSpec((GROUP, width_d), lambda i, c: (i, 0))),
            (sds((count, width_d), bf16), pl.BlockSpec((blk, width_d), lambda i, c: (i, 0))),
            (sds((rows, width), bf16), whole((rows, width))),
            (sds((count, 2 * width), bf16), whole((count, 2 * width))),
            (sds((rows // 2, width), bf16), whole((rows // 2, width))),
            (sds((rows // 2, width), bf16), whole((rows // 2, width))),
        ],
        [
            whole(idx.shape),
            pl.BlockSpec((GROUP, width_d), lambda i, c: ((i + c[0] * (steps // 2)) % steps, 0)),
            pl.BlockSpec((blk, width_d), lambda i, c: (i, 0)),
            whole((1, width_d)),
            whole((1, width_d)),
            whole(wq.shape),
            whole(wk.shape),
            whole(wv.shape),
        ],
        (core, idx, latents, sources, gain_one, gain_src, wq, wk, wv),
        "cross_forward",
        scratch=[pltpu.VMEM((count, 2 * width), bf16)],
        grid=(steps,),
        prefetch=1,
        flops=4e9,
        nbytes=12e6,
    )


def project_body(core_ref, *refs, parts):
    pieces, weights = refs[:parts], refs[parts : 2 * parts]
    base_ref, gain_ref, after_ref, normed_ref = refs[2 * parts :]
    sums = [dot(pieces[k][...], weights[k][...]) for k in range(parts)]
    even, odd = sums[0::2], sums[1::2]
    while len(even) > 1:
        even = [even[k] + even[k + 1] for k in range(0, len(even), 2)]
        odd = [odd[k] + odd[k + 1] for k in range(0, len(odd), 2)]
    after = base_ref[...].astype(f32) + (even[0] + odd[0])
    after_ref[...] = after
    normed_ref[...] = (centre(after)[0] * gain_ref[...]).astype(bf16)


def project(core, pieces, weights, base, gain, own_half):
    parts = len(pieces)
    half, width = pieces[0].shape
    width_d = weights[0].shape[1]
    whole = lambda shape: pl.BlockSpec(shape, lambda i, c: (0,) * len(shape))
    base_spec = (
        pl.BlockSpec((half, width_d), lambda i, c: (c[0], 0)) if own_half else whole((half, width_d))
    )
    return call(
        functools.partial(project_body, parts=parts),
        [(sds((half, width_d), f32), whole((half, width_d))), (sds((half, width_d), bf16), whole((half, width_d)))],
        [whole((half, width))] * parts
        + [whole((width, width_d))] * parts
        + [base_spec, whole((1, width_d))],
        (core, *pieces, *weights, base, gain),
        "project",
        grid=(1,),
        prefetch=1,
        flops=2 * half * width * parts * width_d,
        nbytes=5e6,
    )


def qkv_body(mine_ref, other_ref, wq_ref, wk_ref, wv_ref, q_ref, kv_ref):
    half = mine_ref.shape[0]
    width = wq_ref.shape[1]
    for part, ref in enumerate((mine_ref, other_ref)):
        rows = slice(part * half, (part + 1) * half)
        x = ref[...]
        kv_ref[rows, 0:width] = dot(x, wk_ref[...]).astype(bf16)
        kv_ref[rows, width:] = dot(x, wv_ref[...]).astype(bf16)
        q_ref[rows, :] = dot(x, wq_ref[...]).astype(bf16)


def qkv(mine, other, wq, wk, wv):
    half, width_d = mine.shape
    width = wq.shape[1]
    return call(
        qkv_body,
        [(sds((2 * half, width), bf16), VMEM), (sds((2 * half, 2 * width), bf16), VMEM)],
        [VMEM] * 5,
        (mine, other, wq, wk, wv),
        "qkv",
        flops=2 * 2 * half * width_d * 3 * width,
        nbytes=4e6,
    )


def assemble(refs, entries, dst, rows_blocks):
    for ri, base, p, k in entries:
        for j in range(rows_blocks):
            dst[p * rows_blocks + j, k * GROUP : (k + 1) * GROUP, :] = refs[ri][
                base + j * GROUP : base + (j + 1) * GROUP, :
            ]


def split_rows(rows_value):
    high = rows_value.astype(bf16)
    rest = rows_value - high.astype(f32)
    middle = rest.astype(bf16)
    low = (rest - middle.astype(f32)).astype(bf16)
    return high, middle, low


def pack_extra(row_tiles, heads, blocks, width):
    per_row = width // 128
    out = []
    for h in range(heads):
        flat = [
            jnp.concatenate(row_tiles[h][r * per_row : (r + 1) * per_row], axis=1)
            for r in range(blocks // per_row)
        ]
        rows_value = jnp.concatenate(flat, axis=0)
        out += [part.astype(f32) for part in split_rows(rows_value)]
    used = heads * 3 * (blocks // per_row)
    if used < EXTRA:
        out.append(jnp.zeros((EXTRA - used, width), f32))
    return jnp.concatenate(out, axis=0).astype(bf16)


def unpack_extra(extra, h, j, blocks, width):
    per_row = width // 128
    rows_per = blocks // per_row
    row, lane = j // per_row, (j % per_row) * 128
    parts = [
        extra[(h * 3 + t) * rows_per + row : (h * 3 + t) * rows_per + row + 1, lane : lane + 128]
        for t in range(3)
    ]
    return (parts[0] + parts[1]) + parts[2]


def attend_body(
    clip_q, clip_k, *refs, pieces, entries, heads, blocks, period,
):
    q_ref = refs[0]
    kv_refs = refs[1 : 1 + pieces]
    keep_ref, send_ref, qx_ref, lsec_ref, kv_s, m_s, l_s, acc_s, row_s, o_s = refs[1 + pieces :]
    width = heads * HEAD
    assemble(kv_refs, entries, kv_s, blocks)

    def per_block(i, carry):
        r0 = pl.multiple_of(i * GROUP, GROUP)
        m_s[...] = jnp.full(m_s.shape, masked_value, f32)
        l_s[...] = jnp.zeros(l_s.shape, f32)
        acc_s[...] = jnp.zeros(acc_s.shape, f32)

        def per_keys(g, inner):
            @pl.when(clip_q[i] == clip_k[g])
            def _():
                for h in range(heads):
                    cols = slice(h * HEAD, (h + 1) * HEAD)
                    q = q_ref[pl.ds(r0, GROUP), cols]
                    k = kv_s[g, :, cols]
                    v = kv_s[g, :, width + h * HEAD : width + (h + 1) * HEAD]
                    s = dot_t(q, k) * (HEAD ** (-0.5) * LOG2E)
                    m_old = m_s[h][:, 0:1]
                    m_new = jnp.maximum(m_old, jnp.max(s, axis=-1, keepdims=True))
                    p = jnp.exp2(s - m_new)
                    alpha = jnp.exp2(m_old - m_new)
                    l_new = l_s[h][:, 0:1] * alpha + jnp.sum(p, axis=-1, keepdims=True)
                    acc_s[h] = acc_s[h] * alpha + dot(p.astype(bf16), v)
                    m_s[h] = jnp.broadcast_to(m_new, (GROUP, 128))
                    l_s[h] = jnp.broadcast_to(l_new, (GROUP, 128))

            return inner

        lax.fori_loop(0, period, per_keys, 0)
        for h in range(heads):
            total = l_s[h]
            o_s[pl.ds(r0, GROUP), h * HEAD : (h + 1) * HEAD] = (acc_s[h] / total).astype(bf16)
            lse = m_s[h] + jnp.log2(total)
            lsec_ref[h, pl.ds(r0, GROUP), :] = lse
            row_s[h, i] = jnp.transpose(lse)[0:8]
        return carry

    lax.fori_loop(0, blocks, per_block, 0)
    half = blocks // 2 * GROUP
    keep_ref[...] = o_s[0:half, :]
    send_ref[...] = o_s[half:, :]
    rows = blocks * GROUP
    qx_ref[0:rows, :] = q_ref[...]
    tiles = [[row_s[h, j][0:1] for j in range(blocks)] for h in range(heads)]
    qx_ref[rows : rows + EXTRA, :] = pack_extra(tiles, heads, blocks, width)


def attend(clip_q, clip_k, q, kv_pieces, entries):
    rows, width = q.shape
    heads, blocks, period = width // HEAD, rows // GROUP, clip_k.shape[0]
    pieces = len(kv_pieces)
    body = functools.partial(
        attend_body, pieces=pieces, entries=entries, heads=heads, blocks=blocks, period=period
    )
    return call(
        body,
        [
            (sds((rows // 2, width), bf16), VMEM),
            (sds((rows // 2, width), bf16), VMEM),
            (sds((rows + EXTRA, width), bf16), VMEM),
            (sds((heads, rows, 128), f32), VMEM),
        ],
        [SMEM, SMEM] + [VMEM] * (1 + pieces),
        (clip_q, clip_k, q, *kv_pieces),
        "attend",
        scratch=[
            pltpu.VMEM((period, GROUPS_FRAME * GROUP, 2 * width), bf16),
            pltpu.VMEM((heads, GROUP, 128), f32),
            pltpu.VMEM((heads, GROUP, 128), f32),
            pltpu.VMEM((heads, GROUP, HEAD), f32),
            pltpu.VMEM((heads, blocks, 8, 128), f32),
            pltpu.VMEM((rows, width), bf16),
        ],
        flops=2e9,
        nbytes=7e6,
        trans=2e6,
    )


def out_back_body(mine_ref, other_ref, wo_ref, okeep_ref, osend_ref, dox_ref, dc_ref, *, heads, blocks):
    half = mine_ref.shape[0]
    rows = 2 * half
    tiles = [[] for h in range(heads)]
    for part, (ref, o_ref) in enumerate(((mine_ref, okeep_ref), (other_ref, osend_ref))):
        grad = dot_t(ref[...], wo_ref[...]).astype(bf16)
        dox_ref[part * half : (part + 1) * half, :] = grad
        product = grad.astype(f32) * o_ref[...].astype(f32)
        for h in range(heads):
            delta = jnp.sum(product[:, h * HEAD : (h + 1) * HEAD], axis=-1, keepdims=True)
            delta = jnp.broadcast_to(delta, (half, 128))
            dc_ref[h, part * half : (part + 1) * half, :] = delta
            for j in range(half // GROUP):
                tiles[h].append(jnp.transpose(delta[j * GROUP : (j + 1) * GROUP])[0:1])
    dox_ref[rows : rows + EXTRA, :] = pack_extra(tiles, heads, blocks, heads * HEAD)


def out_back(mine, other, wo, okeep, osend):
    half, width_d = mine.shape
    width = wo.shape[0]
    heads, blocks = width // HEAD, 2 * half // GROUP
    return call(
        functools.partial(out_back_body, heads=heads, blocks=blocks),
        [(sds((2 * half + EXTRA, width), bf16), VMEM), (sds((heads, 2 * half, 128), f32), VMEM)],
        [VMEM] * 5,
        (mine, other, wo, okeep, osend),
        "out_back",
        flops=2 * 2 * half * width * width_d,
        nbytes=4e6,
    )


def query_back_body(clip_q, clip_k, *refs, pieces, entries, heads, blocks, period):
    qx_ref, dox_ref, lsec_ref, dc_ref = refs[0:4]
    kv_refs = refs[4 : 4 + pieces]
    dq_ref, kv_s, acc_s = refs[4 + pieces :]
    width = heads * HEAD
    assemble(kv_refs, entries, kv_s, blocks)

    def per_block(i, carry):
        r0 = pl.multiple_of(i * GROUP, GROUP)
        acc_s[...] = jnp.zeros(acc_s.shape, f32)

        def per_keys(g, inner):
            @pl.when(clip_q[i] == clip_k[g])
            def _():
                for h in range(heads):
                    cols = slice(h * HEAD, (h + 1) * HEAD)
                    k = kv_s[g, :, cols]
                    v = kv_s[g, :, width + h * HEAD : width + (h + 1) * HEAD]
                    s = dot_t(qx_ref[pl.ds(r0, GROUP), cols], k) * (HEAD ** (-0.5) * LOG2E)
                    p = jnp.exp2(s - lsec_ref[h, pl.ds(r0, GROUP), :][:, 0:1])
                    dp = dot_t(dox_ref[pl.ds(r0, GROUP), cols], v)
                    delta = dc_ref[h, pl.ds(r0, GROUP), :][:, 0:1]
                    ds = (p * (dp - delta) * (HEAD ** (-0.5))).astype(bf16)
                    acc_s[h] = acc_s[h] + dot(ds, k)

            return inner

        lax.fori_loop(0, period, per_keys, 0)
        for h in range(heads):
            dq_ref[pl.ds(r0, GROUP), h * HEAD : (h + 1) * HEAD] = acc_s[h].astype(bf16)
        return carry

    lax.fori_loop(0, blocks, per_block, 0)


def query_back(clip_q, clip_k, qx, dox, lsec, dc, kv_pieces, entries):
    rows, width = qx.shape[0] - EXTRA, qx.shape[1]
    heads, blocks, period = width // HEAD, rows // GROUP, clip_k.shape[0]
    pieces = len(kv_pieces)
    return call(
        functools.partial(
            query_back_body, pieces=pieces, entries=entries, heads=heads, blocks=blocks, period=period
        ),
        [(sds((rows, width), bf16), VMEM)],
        [SMEM, SMEM] + [VMEM] * (4 + pieces),
        (clip_q, clip_k, qx, dox, lsec, dc, *kv_pieces),
        "query_back",
        scratch=[
            pltpu.VMEM((period, GROUPS_FRAME * GROUP, 2 * width), bf16),
            pltpu.VMEM((heads, GROUP, HEAD), f32),
        ],
        flops=2e9,
        nbytes=7e6,
        trans=2e6,
    )[0]


def key_back_body(clip_q, clip_k, *refs, pieces, entries, heads, blocks, period):
    kv_ref, dq_ref, wq_ref, wk_ref, wv_ref = refs[0:5]
    qx_refs = refs[5 : 5 + pieces]
    dox_refs = refs[5 + pieces : 5 + 2 * pieces]
    dqkv_ref, keep_ref, send_ref, q_s, do_s, lse_s, delta_s, dk_s, dv_s = refs[5 + 2 * pieces :]
    width = heads * HEAD
    rows = blocks * GROUP
    assemble(qx_refs, entries, q_s, blocks)
    assemble(dox_refs, entries, do_s, blocks)
    for ri, base, p, k in entries:
        for source, target in ((qx_refs, lse_s), (dox_refs, delta_s)):
            extra = source[ri][base + rows : base + rows + EXTRA, :].astype(f32)
            for h in range(heads):
                for j in range(blocks):
                    line = unpack_extra(extra, h, j, blocks, width)
                    target[p * blocks + j, h, :, k * GROUP : (k + 1) * GROUP] = jnp.broadcast_to(
                        line, (8, 128)
                    )
    dqkv_ref[:, 0:width] = dq_ref[...]

    def per_block(j, carry):
        r0 = pl.multiple_of(j * GROUP, GROUP)
        dk_s[...] = jnp.zeros(dk_s.shape, f32)
        dv_s[...] = jnp.zeros(dv_s.shape, f32)

        def per_queries(g, inner):
            @pl.when(clip_q[j] == clip_k[g])
            def _():
                for h in range(heads):
                    cols = slice(h * HEAD, (h + 1) * HEAD)
                    k = kv_ref[pl.ds(r0, GROUP), cols]
                    v = kv_ref[pl.ds(r0, GROUP), width + h * HEAD : width + (h + 1) * HEAD]
                    q = q_s[g, :, cols]
                    do = do_s[g, :, cols]
                    st = dot_t(k, q) * (HEAD ** (-0.5) * LOG2E)
                    pt = jnp.exp2(st - lse_s[g, h, 0:1, :])
                    dv_s[h] = dv_s[h] + dot(pt.astype(bf16), do)
                    dpt = dot_t(v, do)
                    dst = (pt * (dpt - delta_s[g, h, 0:1, :]) * (HEAD ** (-0.5))).astype(bf16)
                    dk_s[h] = dk_s[h] + dot(dst, q)

            return inner

        lax.fori_loop(0, period, per_queries, 0)
        for h in range(heads):
            dqkv_ref[pl.ds(r0, GROUP), width + h * HEAD : width + (h + 1) * HEAD] = dk_s[h].astype(bf16)
            dqkv_ref[pl.ds(r0, GROUP), 2 * width + h * HEAD : 2 * width + (h + 1) * HEAD] = dv_s[
                h
            ].astype(bf16)
        return carry

    lax.fori_loop(0, blocks, per_block, 0)
    half = rows // 2
    for part, ref in enumerate((keep_ref, send_ref)):
        r = slice(part * half, (part + 1) * half)
        total = dot_t(dqkv_ref[r, 0:width], wq_ref[...])
        total = total + dot_t(dqkv_ref[r, width : 2 * width], wk_ref[...])
        total = total + dot_t(dqkv_ref[r, 2 * width :], wv_ref[...])
        ref[...] = total.astype(bf16)


def key_back(clip_q, clip_k, kv, dq, wq, wk, wv, qx_pieces, dox_pieces, entries):
    rows, width = dq.shape
    width_d = wq.shape[0]
    heads, blocks, period = width // HEAD, rows // GROUP, clip_k.shape[0]
    pieces = len(qx_pieces)
    tall = GROUPS_FRAME * GROUP
    return call(
        functools.partial(
            key_back_body, pieces=pieces, entries=entries, heads=heads, blocks=blocks, period=period
        ),
        [
            (sds((rows, 3 * width), bf16), VMEM),
            (sds((rows // 2, width_d), bf16), VMEM),
            (sds((rows // 2, width_d), bf16), VMEM),
        ],
        [SMEM, SMEM] + [VMEM] * (5 + 2 * pieces),
        (clip_q, clip_k, kv, dq, wq, wk, wv, *qx_pieces, *dox_pieces),
        "key_back",
        scratch=[
            pltpu.VMEM((period, tall, width), bf16),
            pltpu.VMEM((period, tall, width), bf16),
            pltpu.VMEM((period, heads, 8, tall), f32),
            pltpu.VMEM((period, heads, 8, tall), f32),
            pltpu.VMEM((heads, GROUP, HEAD), f32),
            pltpu.VMEM((heads, GROUP, HEAD), f32),
        ],
        flops=4e9,
        nbytes=9e6,
        trans=2e6,
    )


def mlp_body(mine_ref, other_ref, win_ref, ag_ref, act_ref, hg_ref, keep_ref, send_ref, *, steps):
    i = pl.program_id(0)
    x = jnp.where(i < steps // 2, mine_ref[...], other_ref[...])
    units = win_ref.shape[1]
    chunk = 256
    total = None
    for n in range(units // chunk):
        cols = slice(n * chunk, (n + 1) * chunk)
        w = win_ref[:, cols]
        hidden = dot(x, w)
        cdf = 0.5 * (1.0 + lax.erf(hidden * 0.7071067811865476))
        act_ref[:, cols] = (hidden * cdf).astype(bf16)
        density = jnp.exp2(hidden * hidden * (-0.5 * LOG2E)) * 0.3989422804014327
        grad = (ag_ref[:, cols] * (cdf + hidden * density)).astype(bf16)
        hg_ref[:, cols] = grad
        term = dot_t(grad, w)
        total = term if total is None else total + term
    total = total.astype(bf16)

    @pl.when(i < steps // 2)
    def _():
        keep_ref[...] = total

    @pl.when(i >= steps // 2)
    def _():
        send_ref[...] = total


def mlp(mine, other, w_in, act_grad):
    half, width_d = mine.shape
    units = w_in.shape[1]
    steps = 2 * half // GROUP
    rows = 2 * half
    low = lambda i: (jnp.minimum(i, steps // 2 - 1), 0)
    high = lambda i: (jnp.maximum(i - steps // 2, 0), 0)
    return call(
        functools.partial(mlp_body, steps=steps),
        [
            (sds((rows, units), bf16), pl.BlockSpec((GROUP, units), lambda i: (i, 0))),
            (sds((rows, units), bf16), pl.BlockSpec((GROUP, units), lambda i: (i, 0))),
            (sds((half, width_d), bf16), pl.BlockSpec((GROUP, width_d), low)),
            (sds((half, width_d), bf16), pl.BlockSpec((GROUP, width_d), high)),
        ],
        [
            pl.BlockSpec((GROUP, width_d), low),
            pl.BlockSpec((GROUP, width_d), high),
            pl.BlockSpec((width_d, units), lambda i: (0, 0)),
            pl.BlockSpec((GROUP, units), lambda i: (i, 0)),
        ],
        (mine, other, w_in, act_grad),
        "mlp",
        grid=(steps,),
        flops=4 * rows * width_d * units,
        nbytes=9e6,
        trans=2 * rows * units,
    )


def norm_back_body(core_ref, s_ref, r_ref, v_ref, gain_ref, base_ref, after_ref, branch_ref, gg_ref):
    n = s_ref[...].astype(f32) + r_ref[...].astype(f32)
    unit, inverse = centre(v_ref[...].astype(f32))
    t = n * gain_ref[...]
    back = inverse * (
        t - jnp.mean(t, axis=-1, keepdims=True) - unit * jnp.mean(t * unit, axis=-1, keepdims=True)
    )
    after = base_ref[...].astype(f32) + back
    after_ref[...] = after
    branch_ref[...] = after.astype(bf16)
    gg_ref[...] = jnp.sum(n * unit, axis=0, keepdims=True)


def norm_back(core, s, r, v, gain, base, own_half):
    half, width_d = s.shape
    whole = lambda shape: pl.BlockSpec(shape, lambda i, c: (0,) * len(shape))
    own = pl.BlockSpec((half, width_d), lambda i, c: (c[0], 0))
    full = whole((half, width_d))
    return call(
        norm_back_body,
        [
            (sds((half, width_d), f32), full),
            (sds((half, width_d), bf16), full),
            (sds((1, width_d), f32), whole((1, width_d))),
        ],
        [full, full, full, whole((1, width_d)), own if own_half else full],
        (core, s, r, v, gain, base),
        "norm_back",
        grid=(1,),
        prefetch=1,
        flops=20 * half * width_d,
        nbytes=5e6,
    )


def final_body(core_ref, s_ref, r_ref, v_ref, gain_ref, base_ref, out_ref, *, with_base):
    n = s_ref[...].astype(f32) + r_ref[...].astype(f32)
    unit, inverse = centre(v_ref[...].astype(f32))
    t = n * gain_ref[...]
    back = inverse * (
        t - jnp.mean(t, axis=-1, keepdims=True) - unit * jnp.mean(t * unit, axis=-1, keepdims=True)
    )
    if with_base:
        back = base_ref[...] + back
    out_ref[...] = back.astype(bf16)


def final_norm(core, s, r, v, gain, base):
    half, width_d = s.shape
    steps = half // 256
    with_base = base is not None
    blk = pl.BlockSpec((256, width_d), lambda i, c: (i, 0))
    own = pl.BlockSpec((256, width_d), lambda i, c: (c[0] * steps + i, 0))
    gain_spec = pl.BlockSpec((1, width_d), lambda i, c: (0, 0))
    if base is None:
        base = gain
    return call(
        functools.partial(final_body, with_base=with_base),
        [(sds((half, width_d), bf16), blk)],
        [blk, blk, own, gain_spec, blk if with_base else gain_spec],
        (core, s, r, v, gain, base),
        "final_norm",
        grid=(steps,),
        prefetch=1,
        flops=20 * half * width_d,
        nbytes=5e6,
    )[0]


def gains_body(core_ref, keep_ref, send_ref, v_ref, out_ref, *, steps):
    i = pl.program_id(0)
    n = jnp.where(i < steps // 2, keep_ref[...], send_ref[...]).astype(f32)
    unit = centre(v_ref[...].astype(f32))[0]
    part = jnp.sum(n * unit, axis=0, keepdims=True)

    @pl.when(i == 0)
    def _():
        out_ref[...] = part

    @pl.when(i > 0)
    def _():
        out_ref[...] = out_ref[...] + part


def gains(core, keep, send, v):
    half, width_d = keep.shape
    blk = 256
    steps = 2 * half // blk
    return call(
        functools.partial(gains_body, steps=steps),
        [(sds((1, width_d), f32), pl.BlockSpec((1, width_d), lambda i, c: (0, 0)))],
        [
            pl.BlockSpec((blk, width_d), lambda i, c: (jnp.minimum(i, steps // 2 - 1), 0)),
            pl.BlockSpec((blk, width_d), lambda i, c: (jnp.maximum(i - steps // 2, 0), 0)),
            pl.BlockSpec((blk, width_d), lambda i, c: ((i + c[0] * (steps // 2)) % steps, 0)),
        ],
        (core, keep, send, v),
        "gains",
        grid=(steps,),
        prefetch=1,
        flops=20 * half * width_d,
        nbytes=8 * half * width_d,
    )[0]


def result_body(s_ref, r_ref, after_ref, out_ref, squares_ref):
    result = after_ref[...] + (s_ref[...].astype(f32) + r_ref[...].astype(f32))
    out_ref[...] = result.astype(bf16)
    for b in range(result.shape[0] // GROUP):
        rows = result[b * GROUP : (b + 1) * GROUP]
        squares_ref[b : b + 1, :] = jnp.sum(rows * rows, axis=0, keepdims=True)


def result_half(s, r, after):
    half, width_d = s.shape
    return call(
        result_body,
        [(sds((half, width_d), bf16), VMEM), (sds((half // GROUP, width_d), f32), VMEM)],
        [VMEM] * 3,
        (s, r, after),
        "result",
        flops=6 * half * width_d,
        nbytes=5e6,
    )


def cross_back_body(
    core_ref, mine_ref, other_ref, wo_ref, q_ref, kvp_ref, row_ref, wq_ref, wk_ref, wv_ref,
    dq_ref, dkv_ref, one_keep_ref, one_send_ref, src_keep_ref, src_send_ref, dkvp_s, *, blocks,
):
    width = wq_ref.shape[1]
    heads = width // HEAD
    count = kvp_ref.shape[0]
    scale = HEAD ** (-0.5)
    for b in range(blocks):
        ref = mine_ref if b < blocks // 2 else other_ref
        part = (b % (blocks // 2)) * GROUP
        grad = dot_t(ref[part : part + GROUP, :], wo_ref[...]).astype(bf16)
        for h in range(heads):
            cols = slice(h * HEAD, (h + 1) * HEAD)
            vcols = slice(width + h * HEAD, width + (h + 1) * HEAD)
            q = q_ref[b * GROUP : (b + 1) * GROUP, cols]
            k = kvp_ref[b * SRC : (b + 1) * SRC, cols]
            v = kvp_ref[b * SRC : (b + 1) * SRC, vcols]
            do = grad[:, cols]
            s = dot_t(q, k) * (scale * LOG2E)
            p = jnp.exp2(s - jnp.max(s, axis=-1, keepdims=True))
            p = p / jnp.sum(p, axis=-1, keepdims=True)
            dp = dot_t(do, v)
            delta = jnp.sum(p * dp, axis=-1, keepdims=True)
            ds = (p * (dp - delta) * scale).astype(bf16)
            dq_ref[b * GROUP : (b + 1) * GROUP, cols] = dot(ds, k).astype(bf16)
            dkvp_s[b * SRC : (b + 1) * SRC, cols] = dot_ta(ds, q).astype(bf16)
            dkvp_s[b * SRC : (b + 1) * SRC, vcols] = dot_ta(p.astype(bf16), do).astype(bf16)
        one = dot_t(dq_ref[b * GROUP : (b + 1) * GROUP, :], wq_ref[...]).astype(bf16)
        if b < blocks // 2:
            one_keep_ref[part : part + GROUP, :] = one
        else:
            one_send_ref[part : part + GROUP, :] = one
    half = count // 2
    blk = 256
    for n in range(count // blk):
        r0 = pl.multiple_of(
            jnp.where(n * blk < half, core_ref[0], 1 - core_ref[0]) * half + (n * blk) % half, blk
        )
        wanted = lax.broadcasted_iota(jnp.int32, (blk, count), 0).astype(f32) + r0.astype(f32)
        picks = jnp.where(row_ref[...] == wanted, 1.0, 0.0).astype(bf16)
        dkv = dot(picks, dkvp_s[...]).astype(bf16)
        dkv_ref[pl.ds(r0, blk), :] = dkv
        total = (dot_t(dkv[:, 0:width], wk_ref[...]) + dot_t(dkv[:, width:], wv_ref[...])).astype(bf16)
        at = (n * blk) % half
        if n * blk < half:
            src_keep_ref[at : at + blk, :] = total
        else:
            src_send_ref[at : at + blk, :] = total


def cross_back(core, mine, other, wo, q, kvp, row, wq, wk, wv):
    rows, width = q.shape
    width_d = wq.shape[0]
    count = kvp.shape[0]
    blocks = rows // GROUP
    return call(
        functools.partial(cross_back_body, blocks=blocks),
        [
            (sds((rows, width), bf16), VMEM),
            (sds((count, 2 * width), bf16), VMEM),
            (sds((rows // 2, width_d), bf16), VMEM),
            (sds((rows // 2, width_d), bf16), VMEM),
            (sds((count // 2, width_d), bf16), VMEM),
            (sds((count // 2, width_d), bf16), VMEM),
        ],
        [SMEM] + [VMEM] * 9,
        (core, mine, other, wo, q, kvp, row, wq, wk, wv),
        "cross_back",
        scratch=[pltpu.VMEM((count, 2 * width), bf16)],
        flops=4e9,
        nbytes=12e6,
    )


def xor_pairs(bit, size):
    return [(i, i ^ bit) for i in range(size)]


def tensor_swap(x, bit):
    return lax.ppermute(x, "tensor", xor_pairs(bit, lax.axis_size("tensor")))


def seq_gather(x):
    size = lax.axis_size("seq")
    if size == 8:
        ring = lambda d: [(s, ((s // 2 + d) % 4) * 2 + s % 2) for s in range(8)]
        move = lambda v, pairs: lax.ppermute(v, "seq", pairs)
        flip = xor_pairs(1, 8)
        beside = move(x, flip)
        up = move(x, ring(1))
        down = move(x, ring(-1))
        far = move(up, ring(1))
        up_beside = move(up, flip)
        down_beside = move(beside, ring(-1))
        far_beside = move(far, flip)
        return [x, beside, up, down, far, up_beside, down_beside, far_beside]
    return [lax.all_gather(x, "seq", axis=0, tiled=True)]


def gather_entries(size, rows, sets):
    if size == 8:
        return tuple((k, 0, 0, k) for k in range(8))
    return tuple((0, s * rows, s % sets, s // sets) for s in range(size))


def half_sum(keep, send):
    size = lax.axis_size("tensor")
    got = tensor_swap(send, 1)
    own = (keep.astype(f32) + got.astype(f32)).astype(bf16)
    bit = 2
    while True:
        other = tensor_swap(own, bit)
        if bit * 2 >= size:
            return own, other
        own = (own.astype(f32) + other.astype(f32)).astype(bf16)
        bit *= 2


def tensor_pieces(keep, send):
    size = lax.axis_size("tensor")
    return [keep if k == 0 else tensor_swap(send if k % 2 else keep, k) for k in range(size)]


def weight_pieces(weight):
    size = lax.axis_size("tensor")
    pieces = {0: weight}
    bit = size // 2
    while bit >= 1:
        pieces.update({k + bit: tensor_swap(v, bit) for k, v in list(pieces.items())})
        bit //= 2
    return [pieces[k] for k in range(size)]


def scatter_rows(parts):
    size = lax.axis_size("seq")
    if size != 8:
        return lax.psum_scatter(parts, "seq", scatter_dimension=0, tiled=True).astype(f32)
    index = lax.axis_index("seq")
    z, x = index // 2, index % 2
    features, columns = parts.shape
    view = parts.reshape(4, 2, features // 8, columns)
    keep = lax.dynamic_index_in_dim(view, x, 1, keepdims=False)
    send = lax.dynamic_index_in_dim(view, 1 - x, 1, keepdims=False)
    both = keep.astype(f32) + lax.ppermute(send, "seq", xor_pairs(1, 8)).astype(f32)
    short = both.astype(bf16)
    total = lax.dynamic_index_in_dim(both, z, 0, keepdims=False)
    for d in (1, 2, 3):
        pairs = [(s, ((s // 2 + d) % 4) * 2 + s % 2) for s in range(8)]
        piece = lax.dynamic_index_in_dim(short, (z + d) % 4, 0, keepdims=False)
        total = total + lax.ppermute(piece, "seq", pairs).astype(f32)
    return total


def sum_everywhere(v):
    for axis in ("tensor", "seq"):
        bit = 1
        while bit < lax.axis_size(axis):
            v = v + lax.ppermute(v, axis, xor_pairs(bit, lax.axis_size(axis)))
            bit *= 2
    return v


def local(
    latents, sources, source_index, block_clip, clip_frames, norm_src, norm_cross, norm_self, norm_mlp,
    cross_q, cross_k, cross_v, cross_o, self_q, self_k, self_v, self_o, mlp_in, mlp_out, out_grad,
):
    rows, width_d = latents.shape
    half = rows // 2
    blocks = rows // GROUP
    count = sources.shape[0]
    width = cross_q.shape[1]
    tensor_size, seq_size = lax.axis_size("tensor"), lax.axis_size("seq")
    t_index, s_index = lax.axis_index("tensor"), lax.axis_index("seq")
    core_index = t_index % 2
    core = core_index.astype(jnp.int32).reshape(1)
    period = block_clip.shape[0] // GROUPS_FRAME
    sets = period // blocks

    def own_first(v):
        first, second = v[: v.shape[0] // 2], v[v.shape[0] // 2 :]
        return jnp.where(core_index == 0, v, jnp.concatenate((second, first)))

    def in_place(mine, other):
        return jnp.where(
            core_index == 0, jnp.concatenate((mine, other)), jnp.concatenate((other, mine))
        )

    gain = lambda g: g.reshape(1, width_d)
    index = own_first((source_index - s_index * count).astype(f32))
    turned = (jnp.arange(blocks, dtype=jnp.int32) + core_index * (blocks // 2)) % blocks
    clip_q = block_clip[blocks * (s_index % sets) + turned]
    clip_k = block_clip[(blocks * jnp.arange(sets, dtype=jnp.int32)[:, None] + turned[None, :]).reshape(-1)]

    cross_o_all = weight_pieces(cross_o)
    self_o_all = weight_pieces(self_o)
    normed_one, normed_src, cross_query, cross_kv, mixed_keep, mixed_send = cross_forward(
        core, index, latents, sources, gain(norm_cross), gain(norm_src), cross_q, cross_k, cross_v
    )
    after_cross, two_mine = project(
        core, tensor_pieces(mixed_keep, mixed_send), cross_o_all, latents, gain(norm_self), True
    )
    two_other = tensor_swap(two_mine, 1)
    query, key_value = qkv(two_mine, two_other, self_q, self_k, self_v)
    kv_pieces = seq_gather(key_value)
    kv_entries = gather_entries(seq_size, rows, sets)
    out_rel = own_first(out_grad)
    act_grad = dot_t(out_rel, mlp_out)
    self_keep, self_send, query_more, lse_columns = attend(clip_q, clip_k, query, kv_pieces, kv_entries)
    after_self, three_mine = project(
        core, tensor_pieces(self_keep, self_send), self_o_all, after_cross, gain(norm_mlp), False
    )
    three_other = tensor_swap(three_mine, 1)
    activated, hidden_grad, three_keep, three_send = mlp(three_mine, three_other, mlp_in, act_grad)
    query_pieces = seq_gather(query_more)
    more_entries = gather_entries(seq_size, rows + EXTRA, sets)

    three_sum, three_got = half_sum(three_keep, three_send)
    after_self_grad, self_branch, mlp_gain = norm_back(
        core, three_sum, three_got, after_self, gain(norm_mlp), out_grad, True
    )
    self_branch_other = tensor_swap(self_branch, 1)
    mlp_part = dot(activated, mlp_out).astype(bf16)
    result_sum, result_got = half_sum(mlp_part[:half], mlp_part[half:])
    output_half, squares = result_half(result_sum, result_got, after_self)
    output = in_place(output_half, tensor_swap(output_half, 1))
    normed_three = jnp.concatenate((three_mine, three_other))
    mlp_in_out = scatter_rows(dot_ta(normed_three, hidden_grad).astype(bf16))
    mlp_out_out = scatter_rows(dot_ta(out_rel, activated).astype(bf16))

    out_more, delta_columns = out_back(self_branch, self_branch_other, self_o, self_keep, self_send)
    out_pieces = seq_gather(out_more)
    self_query_grad = query_back(
        clip_q, clip_k, query_more, out_more, lse_columns, delta_columns, kv_pieces, kv_entries
    )
    self_grads, two_keep, two_send = key_back(
        clip_q, clip_k, key_value, self_query_grad, self_q, self_k, self_v, query_pieces, out_pieces, more_entries
    )
    two_sum, two_got = half_sum(two_keep, two_send)
    after_cross_grad, cross_branch, self_gain = norm_back(
        core, two_sum, two_got, after_cross, gain(norm_self), after_self_grad, False
    )
    cross_branch_other = tensor_swap(cross_branch, 1)
    normed_two = jnp.concatenate((two_mine, two_other))
    self_branch_all = jnp.concatenate((self_branch, self_branch_other))
    self_mixed = jnp.concatenate((self_keep, self_send))
    self_out = scatter_rows(
        jnp.concatenate(
            (dot_ta(normed_two, self_grads).astype(bf16), dot_ta(self_branch_all, self_mixed).astype(bf16)),
            axis=1,
        )
    )

    cross_query_grad, cross_kv_grad, one_keep, one_send, src_keep, src_send = cross_back(
        core, cross_branch, cross_branch_other, cross_o, cross_query, cross_kv,
        index.reshape(1, -1), cross_q, cross_k, cross_v,
    )
    one_sum, one_got = half_sum(one_keep, one_send)
    src_sum, src_got = half_sum(src_keep, src_send)
    cross_gain = gains(core, one_keep, one_send, latents)
    src_gain = gains(core, src_keep, src_send, sources)
    cross_branch_all = jnp.concatenate((cross_branch, cross_branch_other))
    cross_mixed = jnp.concatenate((mixed_keep, mixed_send))
    cross_out = scatter_rows(
        jnp.concatenate(
            (
                dot_ta(normed_one, cross_query_grad).astype(bf16),
                dot_ta(normed_src, cross_kv_grad).astype(bf16),
                dot_ta(cross_branch_all, cross_mixed).astype(bf16),
            ),
            axis=1,
        )
    )
    lat_half = final_norm(core, one_sum, one_got, latents, gain(norm_cross), after_cross_grad)
    src_half = final_norm(core, src_sum, src_got, sources, gain(norm_src), None)
    latents_grad = in_place(lat_half, tensor_swap(lat_half, 1))
    sources_grad = in_place(src_half, tensor_swap(src_half, 1))

    copies = 1.0 / (tensor_size // 2)
    own_blocks = blocks * s_index + turned[: blocks // 2]
    own_clips = block_clip[own_blocks]
    norms = jnp.sqrt(jnp.sum(squares, axis=1) / (GROUP * width_d) + 1e-06)
    frames = clip_frames[own_clips].astype(f32)
    share = jnp.sum(norms / (GROUPS_FRAME * frames)) / clip_frames.shape[0]
    small = jnp.concatenate(
        (
            src_gain,
            cross_gain,
            self_gain * copies,
            mlp_gain * copies,
            jnp.broadcast_to(share * copies, (1, width_d)),
            jnp.zeros((3, width_d), f32),
        )
    )
    small = sum_everywhere(small)
    units = mlp_in.shape[1]
    return (
        output,
        latents_grad,
        sources_grad,
        small[0],
        small[1],
        small[2],
        small[3],
        cross_out[:, 0:width],
        cross_out[:, width : 2 * width],
        cross_out[:, 2 * width : 3 * width],
        cross_out[:, 3 * width :].T,
        self_out[:, 0:width],
        self_out[:, width : 2 * width],
        self_out[:, 2 * width : 3 * width],
        self_out[:, 3 * width :].T,
        mlp_in_out,
        mlp_out_out.T,
        small[4, 0],
    )


def solution(mesh):
    in_specs = (
        P("seq", None), P("seq", None), P("seq", None), P(), P(), P(), P(), P(), P(),
        P(None, "tensor"), P(None, "tensor"), P(None, "tensor"), P("tensor", None),
        P(None, "tensor"), P(None, "tensor"), P(None, "tensor"), P("tensor", None),
        P(None, "tensor"), P("tensor", None), P("seq", None),
    )
    out_specs = (
        P("seq", None), P("seq", None), P("seq", None), P(), P(), P(), P(),
        P("seq", "tensor"), P("seq", "tensor"), P("seq", "tensor"), P("tensor", "seq"),
        P("seq", "tensor"), P("seq", "tensor"), P("seq", "tensor"), P("tensor", "seq"),
        P("seq", "tensor"), P("tensor", "seq"), P(),
    )
    return jax.shard_map(local, mesh=mesh, in_specs=in_specs, out_specs=out_specs, check_vma=False)
```

time: 1540 us -> 463 us (0.30)
  waiting for transfers between devices: 840 us -> 168 us
  matrix products: 258 us -> 16.2 us
  local copies, waits for them, and re-layouts: 184 us -> 62.4 us
  other arithmetic: 149 us -> 37.7 us
  Pallas kernels: 0 us -> 98.5 us
  starting transfers between devices: 2 us -> 72.4 us
  blocking collectives: 37.7 us -> 0 us
  loops' own time: 34.6 us -> 0 us
    reduce_scatter x8 -> x0, waiting for transfers between devices: 461 us -> none  [the longest x1 68.6 us: local(): lax.psum_scatter(row_parts[6].astype(jnp.bfloat16), 'seq', scatter_dimens...]
    dot_general x179 -> x9, matrix products: 256 us -> 16.2 us  [the longest x7 11 us: dot_ta(): lax.dot_general(a, b, (((0,), (0,)), ((), ())), preferred_element_type=f32)]
    psum x5 -> x0, waiting for transfers between devices: 195 us -> none  [the longest x1 69.2 us: local(): lax.psum(normed_one_part.astype(jnp.bfloat16), 'tensor').astype(jnp.float32)]
    ppermute x0 -> x71, waiting for transfers between devices: none -> 168 us  [the longest x21 77.7 us: seq_gather(): move = lambda v, pairs: lax.ppermute(v, 'seq', pairs)]
    unnamed x21 -> x0, waiting for transfers between devices: 140 us -> none
    pallas_call x0 -> x17, Pallas kernels: none -> 98.5 us  [call(): pl.pallas_call(body, out_shape=out_shape, grid_spec=pltpu.PrefetchScalarG...]
    dynamic_slice x128 -> x7, local copies, waits for them, and re-layouts: 93.5 us -> 16 us  [the longest x1 11.3 us: scatter_rows(): keep = lax.dynamic_index_in_dim(view, x, 1, keepdims=False)]
    ppermute x0 -> x71, starting transfers between devices: none -> 72.4 us  [the longest x21 28.2 us: seq_gather(): move = lambda v, pairs: lax.ppermute(v, 'seq', pairs)]
  transfers between devices with their start and end apart: 18 -> 71, of which waited for: 17 -> 22; matrix products, arithmetic and copies ran while one was open for 15% -> 23% of each run, Pallas kernels for 0% -> 17%
where the time goes in v1:
time: 463 us; the launch traced here: 457 us
  waiting for transfers between devices  168 us (36%)
  Pallas kernels  98.5 us (21%)
  starting transfers between devices  72.4 us (16%)
  local copies, waits for them, and re-layouts  62.4 us (13%)
  other arithmetic  37.7 us (8%)
  matrix products  16.2 us (3%)
    pallas_call x17, Pallas kernels, call(): pl.pallas_call(body, out_shape=out_shape, grid_spec=pltpu.PrefetchScalarG...  98.5 us
    ppermute x21, waiting for transfers between devices, seq_gather(): move = lambda v, pairs: lax.ppermute(v, 'seq', pairs)  77.7 us
    ppermute x29, waiting for transfers between devices, tensor_swap(): return lax.ppermute(x, 'tensor', xor_pairs(bit, lax.axis_size('tensor')))  45.5 us
    ppermute x12, waiting for transfers between devices, scatter_rows(): total = total + lax.ppermute(piece, 'seq', pairs).astype(f32)  32.5 us
    unnamed x147, local copies, waits for them, and re-layouts  30.3 us
    ppermute x21, starting transfers between devices, seq_gather(): move = lambda v, pairs: lax.ppermute(v, 'seq', pairs)  28.2 us
    ppermute x29, starting transfers between devices, tensor_swap(): return lax.ppermute(x, 'tensor', xor_pairs(bit, lax.axis_size('tensor')))  16.8 us
    ppermute x12, starting transfers between devices, scatter_rows(): total = total + lax.ppermute(piece, 'seq', pairs).astype(f32)  14.2 us
  transfers between devices with their start and end apart: 71, of which 22 were waited for; matrix products, arithmetic and copies ran while one was open for 23% of the time, Pallas kernels for 17%

profile of v1, /device:TPU:0, one launch (start us, length us, event | category | flops | bytes accessed | tf_op | source)
XLA Modules:
  0.0 457.4 jit_solution(5673002573051464968)
XLA Ops:
  4.4 11.4 %collective-permute-done.4.refs_6_ = bf16[256,1024]{1,0:T(8,128)(2,1)S(1)} collective-permute-done((bf16[256,1024]{1,0:T(8,128)(2,1)}, bf16[256,1024]{1,0:T(8,128)(2,1)S(1)}, u32[]{:S(2)}, u32[]{:S(2)}) %collective-permute-start.4) | collective-permute-done | bytes 524320 | tf_op jit(solution)/shard_map/ppermute | solution.py:788
  17.2 8.9 %cross_forward.1 = (bf16[512,1024]{1,0:T(8,128)(2,1)}, bf16[1024,1024]{1,0:T(8,128)(2,1)}, bf16[512,256]{1,0:T(8,128)(2,1)}, bf16[1024,512]{1,0:T(8,128)(2,1)}, ...) custom-call(s32[1]{0:T(128)} %bitcast.core_ref, f32[4,256]{1,0:T(4,128)} %maximum_select_fusion.6.idx_ref, ...), custom_call_target="tpu_custom_call" | custom-call | flops 4000000000 | bytes 12000000 | tf_op jit(solution)/shard_map/cross_forward/pallas_call | solution.py:51
  28.3 4.7 %collective-permute-done.1.refs_2_ = bf16[256,256]{1,0:T(8,128)(2,1)S(1)} collective-permute-done((bf16[256,256]{1,0:T(8,128)(2,1)}, bf16[256,256]{1,0:T(8,128)(2,1)S(1)}, u32[]{:S(2)}, u32[]{:S(2)}) %collective-permute-start.1) | collective-permute-done | bytes 131104 | tf_op jit(solution)/shard_map/ppermute | solution.py:788
  49.1 13.2 %collective-permute-done.8.refs_3_.refs_6_ = bf16[512,512]{1,0:T(8,128)(2,1)S(1)} collective-permute-done((bf16[512,512]{1,0:T(8,128)(2,1)}, bf16[512,512]{1,0:T(8,128)(2,1)S(1)}, u32[]{:S(2)}, u32[]{:S(2)}) %collective-permute-start.8) | collective-permute-done | bytes 524320 | tf_op jit(solution)/shard_map/ppermute | solution.py:795
  69.4 9.6 %collective-permute-done.10.refs_5_.refs_8_ = bf16[512,512]{1,0:T(8,128)(2,1)} collective-permute-done((bf16[512,512]{1,0:T(8,128)(2,1)S(1)}, bf16[512,512]{1,0:T(8,128)(2,1)}, u32[]{:S(2)}, u32[]{:S(2)}) %collective-permute-start.10) | collective-permute-done | bytes 524320 | tf_op jit(solution)/shard_map/ppermute | solution.py:795
  80.6 8.7 %collective-permute-done.9.refs_4_.refs_7_ = bf16[512,512]{1,0:T(8,128)(2,1)} collective-permute-done((bf16[512,512]{1,0:T(8,128)(2,1)}, bf16[512,512]{1,0:T(8,128)(2,1)}, u32[]{:S(2)}, u32[]{:S(2)}) %collective-permute-start.9) | collective-permute-done | bytes 524320 | tf_op jit(solution)/shard_map/ppermute | solution.py:795
  90.4 9.3 %collective-permute-done.12.refs_7_.refs_10_ = bf16[512,512]{1,0:T(8,128)(2,1)} collective-permute-done((bf16[512,512]{1,0:T(8,128)(2,1)S(1)}, bf16[512,512]{1,0:T(8,128)(2,1)}, u32[]{:S(2)}, u32[]{:S(2)}) %collective-permute-start.12) | collective-permute-done | bytes 524320 | tf_op jit(solution)/shard_map/ppermute | solution.py:795
  99.8 10.4 %attend.1 = (bf16[256,256]{1,0:T(8,128)(2,1)}, bf16[256,256]{1,0:T(8,128)(2,1)}, bf16[528,256]{1,0:T(8,128)(2,1)}, f32[2,512,128]{2,1,0:T(8,128)}) custom-call(s32[4]{0:T(128)} %gather_fusion, s32[4]{0:T(128)} %gather_fusion, bf16[512,256]{1,0:T(8,128)(2,1)} %get-tuple-element.60.refs_0_, bf16[512,512]{1,0:T(8,128)(2,1)} %get-tuple-element.61.refs_1_.refs_4_.refs_0_, ...), custom_call_target="tpu_custom_call" | custom-call | flops 2000000000 | bytes 7000000 | tf_op jit(solution)/shard_map/attend/pallas_call | solution.py:51
  112.1 4.7 %collective-permute-done.15.refs_2_ = bf16[256,256]{1,0:T(8,128)(2,1)S(1)} collective-permute-done((bf16[256,256]{1,0:T(8,128)(2,1)}, bf16[256,256]{1,0:T(8,128)(2,1)S(1)}, u32[]{:S(2)}, u32[]{:S(2)}) %collective-permute-start.15) | collective-permute-done | bytes 131104 | tf_op jit(solution)/shard_map/ppermute | solution.py:788
  119.4 3.9 project.3
  127.1 9.1 %mlp.1 = (bf16[512,1024]{1,0:T(8,128)(2,1)}, bf16[512,1024]{1,0:T(8,128)(2,1)}, bf16[256,1024]{1,0:T(8,128)(2,1)}, bf16[256,1024]{1,0:T(8,128)(2,1)}) custom-call(bf16[256,1024]{1,0:T(8,128)(2,1)} %get-tuple-element.65.mine_ref, bf16[256,1024]{1,0:T(8,128)(2,1)} %copy-done.58, bf16[1024,1024]{1,0:T(8,128)(2,1)} %win_ref.1, f32[512,1024]{1,0:T(8,128)} %fusion.27.ag_ref), custom_call_target="tpu_custom_call" | custom-call | flops 2147483648 | bytes 9000000 | tf_op jit(solution)/shard_map/mlp/pallas_call | solution.py:51
  147.4 8.4 %collective-permute-done.25.r_ref = bf16[256,1024]{1,0:T(8,128)(2,1)} collective-permute-done((bf16[256,1024]{1,0:T(8,128)(2,1)S(1)}, bf16[256,1024]{1,0:T(8,128)(2,1)}, u32[]{:S(2)}, u32[]{:S(2)}) %collective-permute-start.25) | collective-permute-done | bytes 524320 | tf_op jit(solution)/shard_map/ppermute | solution.py:788
  184.2 11.1 %collective-permute-done.31.refs_10_ = bf16[528,256]{1,0:T(8,128)(2,1)} collective-permute-done((bf16[528,256]{1,0:T(8,128)(2,1)}, bf16[528,256]{1,0:T(8,128)(2,1)}, u32[]{:S(2)}, u32[]{:S(2)}) %collective-permute-start.31) | collective-permute-done | bytes 270368 | tf_op jit(solution)/shard_map/ppermute | solution.py:795
  211.1 8.3 %query_back.1.refs_1_ = bf16[512,256]{1,0:T(8,128)(2,1)} custom-call(s32[4]{0:T(128)} %gather_fusion, s32[4]{0:T(128)} %gather_fusion, bf16[528,256]{1,0:T(8,128)(2,1)} %get-tuple-element.69.refs_0_.refs_5_, bf16[528,256]{1,0:T(8,128)(2,1)} %get-tuple-element.73.refs_1_.refs_13_, f32[2,512,128]{2,1,0:T(8,128)} %get-tuple-element.74.refs_2_, ...), custom_call_target="tpu_custom_call" | custom-call | flops 2000000000 | bytes 7000000 | tf_op jit(solution)/shard_map/query_back/pallas_call | solution.py:51
  219.5 15.5 %collective-permute-done.38.refs_18_ = bf16[528,256]{1,0:T(8,128)(2,1)S(1)} collective-permute-done((bf16[528,256]{1,0:T(8,128)(2,1)}, bf16[528,256]{1,0:T(8,128)(2,1)S(1)}, u32[]{:S(2)}, u32[]{:S(2)}) %collective-permute-start.38) | collective-permute-done | bytes 270368 | tf_op jit(solution)/shard_map/ppermute | solution.py:795
  235.0 5.4 %collective-permute-done.40.refs_20_ = bf16[528,256]{1,0:T(8,128)(2,1)S(1)} collective-permute-done((bf16[528,256]{1,0:T(8,128)(2,1)}, bf16[528,256]{1,0:T(8,128)(2,1)S(1)}, u32[]{:S(2)}, u32[]{:S(2)}) %collective-permute-start.40) | collective-permute-done | bytes 270368 | tf_op jit(solution)/shard_map/ppermute | solution.py:795
  241.1 11.5 %key_back.1 = (bf16[512,768]{1,0:T(8,128)(2,1)}, bf16[256,1024]{1,0:T(8,128)(2,1)}, bf16[256,1024]{1,0:T(8,128)(2,1)}) custom-call(s32[4]{0:T(128)} %gather_fusion, s32[4]{0:T(128)} %gather_fusion, bf16[512,512]{1,0:T(8,128)(2,1)} %get-tuple-element.61.refs_1_.refs_4_.refs_0_, bf16[512,256]{1,0:T(8,128)(2,1)} %query_back.1.refs_1_, ...), custom_call_target="tpu_custom_call" | custom-call | flops 4000000000 | bytes 9000000 | tf_op jit(solution)/shard_map/key_back/pallas_call | solution.py:51
  268.8 21.8 %collective-permute-done.69 = bf16[128,1024]{0,1:T(8,128)(2,1)S(1)} collective-permute-done((bf16[128,1024]{0,1:T(8,128)(2,1)}, bf16[128,1024]{0,1:T(8,128)(2,1)S(1)}, u32[]{:S(2)}, u32[]{:S(2)}) %collective-permute-start.69) | collective-permute-done | bytes 262176 | tf_op jit(solution)/shard_map/ppermute | solution.py:858
  292.9 3.8 norm_back.3
  302.8 11.5 %cross_back.1 = (bf16[512,256]{1,0:T(8,128)(2,1)}, bf16[1024,512]{1,0:T(8,128)(2,1)}, bf16[256,1024]{1,0:T(8,128)(2,1)}, bf16[256,1024]{1,0:T(8,128)(2,1)}, bf16...) custom-call(s32[1]{0:T(128)} %bitcast.core_ref, bf16[256,1024]{1,0:T(8,128)(2,1)} %get-tuple-element.79.mine_ref, ...), custom_call_target="tpu_custom_call" | custom-call | flops 4000000000 | bytes 12000000 | tf_op jit(solution)/shard_map/cross_back/pallas_call | solution.py:51
  314.2 4.5 gains.2
  335.1 4.5 reshape.150
  339.5 11.3 %constant_dynamic-slice_fusion.5 = (bf16[4,1,128,1024]{2,1,0,3:T(2,128)(2,1)}, bf16[4,1,128,1024]{2,1,0,3:T(2,128)(2,1)}, bf16[4,1,128,1024]{2,1,0,3:T(2,128)(2,1)}, bf16[4,1,128,1024]{2,1,0,3:T(2,128)(2,1)}) fusion(bf16[4,2,128,1024]{2,1,0,3:T(2,128)(2,1)S(1)} %reshape.151, s32[]{:T(128)S(6)} %select_n.186, s32[]{:T(128)S(6)} %select_n.187, ...), kind=kLoop, calls=%fused_computation.76 | loop fusion | bytes 8388616 | tf_op jit(solution)/shard_map/jit(dynamic_index_in_dim)/dynamic_slice | solution.py:850
  350.9 6.0 %copy.59 = bf16[4,1,128,1024]{3,2,0,1:T(8,128)(2,1)} copy(bf16[4,1,128,1024]{2,1,0,3:T(2,128)(2,1)} %get-tuple-element.172) | data formatting | bytes 2097152
  366.3 4.3 copy.58
  370.6 6.0 %copy.61 = bf16[4,1,128,1024]{3,2,0,1:T(8,128)(2,1)} copy(bf16[4,1,128,1024]{2,1,0,3:T(2,128)(2,1)} %get-tuple-element.139) | data formatting | bytes 2097152
  378.1 4.2 copy.60
  393.6 11.7 %collective-permute-done.59 = bf16[4,128,1024]{2,1,0:T(8,128)(2,1)} collective-permute-done((bf16[4,128,1024]{2,1,0:T(8,128)(2,1)}, bf16[4,128,1024]{2,1,0:T(8,128)(2,1)}, u32[]{:S(2)}, u32[]{:S(2)}) %collective-permute-start.59) | collective-permute-done | bytes 1048608 | tf_op jit(solution)/shard_map/ppermute | solution.py:852
  410.8 11.2 %collective-permute-done.45.r_ref = bf16[256,1024]{1,0:T(8,128)(2,1)S(1)} collective-permute-done((bf16[256,1024]{1,0:T(8,128)(2,1)S(1)}, bf16[256,1024]{1,0:T(8,128)(2,1)S(1)}, u32[]{:S(2)}, u32[]{:S(2)}) %collective-permute-start.45) | collective-permute-done | bytes 524320 | tf_op jit(solution)/shard_map/ppermute | solution.py:788
  429.2 3.9 final_norm.3
  436.8 10.7 %collective-permute-done.61 = bf16[128,1024]{1,0:T(8,128)(2,1)S(1)} collective-permute-done((bf16[128,1024]{1,0:T(8,128)(2,1)S(1)}, bf16[128,1024]{1,0:T(8,128)(2,1)S(1)}, u32[]{:S(2)}, u32[]{:S(2)}) %collective-permute-start.61) | collective-permute-done | bytes 262176 | tf_op jit(solution)/shard_map/ppermute | solution.py:858
  453.3 3.9 maximum_select_fusion
  (346 shorter events, 181.6 us)
Async XLA Ops:
  3.7 30.8 %collective-permute-start.3 = (bf16[256,1024]{1,0:T(8,128)(2,1)}, bf16[256,1024]{1,0:T(8,128)(2,1)S(1)}, u32[]{:S(2)}, u32[]{:S(2)}) collective-permute-start(bf16[256,1024]{1,0:T(8,128)(2,1)} %wo_ref.3), channel_id=1, source_target_pairs={{0,1},{1,0},{2,3},{3,2},{4,5},{5,4},{6,7},{7,6},{8,9},{9,8},{10,11... | collective-permute-start | bytes 1572872 | tf_op jit(solution)/shard_map/ppermute | solution.py:788
  47.6 21.5 %collective-permute-start.7 = (bf16[512,512]{1,0:T(8,128)(2,1)}, bf16[512,512]{1,0:T(8,128)(2,1)S(1)}, u32[]{:S(2)}, u32[]{:S(2)}) collective-permute-start(bf16[512,512]{1,0:T(8,128)(2,1)} %get-tuple-element.61.refs_1_.refs_4_.refs_0_), channel_id=1, source_target_pairs={{0,4},{4,0},{8,12},{12,8},{16,20},{20,16},{24,28},{28,24},{1,5},{5... | collective-permute-start | bytes 1572872 | tf_op jit(solution)/shard_map/ppermute | solution.py:795
  63.8 25.4 %collective-permute-start.9 = (bf16[512,512]{1,0:T(8,128)(2,1)}, bf16[512,512]{1,0:T(8,128)(2,1)}, u32[]{:S(2)}, u32[]{:S(2)}) collective-permute-start(bf16[512,512]{1,0:T(8,128)(2,1)} %get-tuple-element.61.refs_1_.refs_4_.refs_0_), channel_id=1, source_target_pairs={{0,24},{4,28},{8,0},{12,4},{16,8},{20,12},{24,16},{28,20},{1,25},{... | collective-permute-start | bytes 1572872 | tf_op jit(solution)/shard_map/ppermute | solution.py:795
  67.6 22.8 %collective-permute-start.11 = (bf16[512,512]{1,0:T(8,128)(2,1)S(1)}, bf16[512,512]{1,0:T(8,128)(2,1)}, u32[]{:S(2)}, u32[]{:S(2)}) collective-permute-start(bf16[512,512]{1,0:T(8,128)(2,1)S(1)} %collective-permute-done.8.refs_3_.refs_6_), channel_id=1, source_target_pairs={{0,4},{4,0},{8,12},{12,8},{16,20},{20,16},{24,28},{28,24},{1,5},{5... | collective-permute-start | bytes 1572872 | tf_op jit(solution)/shard_map/ppermute | solution.py:795
  69.1 30.6 %collective-permute-start.12 = (bf16[512,512]{1,0:T(8,128)(2,1)S(1)}, bf16[512,512]{1,0:T(8,128)(2,1)}, u32[]{:S(2)}, u32[]{:S(2)}) collective-permute-start(bf16[512,512]{1,0:T(8,128)(2,1)S(1)} %collective-permute-done.7.refs_2_.refs_5_), channel_id=1, source_target_pairs={{0,24},{4,28},{8,0},{12,4},{16,8},{20,12},{24,16},{28,20},{1,25},{... | collective-permute-start | bytes 1572872 | tf_op jit(solution)/shard_map/ppermute | solution.py:795
  80.6 31.5 %collective-permute-start.17 = (bf16[256,1024]{1,0:T(8,128)(2,1)}, bf16[256,1024]{1,0:T(8,128)(2,1)}, u32[]{:S(2)}, u32[]{:S(2)}) collective-permute-start(bf16[256,1024]{1,0:T(8,128)(2,1)} %wo_ref.2), channel_id=1, source_target_pairs={{0,1},{1,0},{2,3},{3,2},{4,5},{5,4},{6,7},{7,6},{8,9},{9,8},{10,11... | collective-permute-start | bytes 1572872 | tf_op jit(solution)/shard_map/ppermute | solution.py:788
  89.2 22.8 %collective-permute-start.19 = (bf16[256,1024]{1,0:T(8,128)(2,1)}, bf16[256,1024]{1,0:T(8,128)(2,1)}, u32[]{:S(2)}, u32[]{:S(2)}) collective-permute-start(bf16[256,1024]{1,0:T(8,128)(2,1)} %collective-permute-done.18.refs_6_), channel_id=1, source_target_pairs={{0,1},{1,0},{2,3},{3,2},{4,5},{5,4},{6,7},{7,6},{8,9},{9,8},{10,11... | collective-permute-start | bytes 1572872 | tf_op jit(solution)/shard_map/ppermute | solution.py:788
  142.3 28.1 %collective-permute-start.27 = (bf16[528,256]{1,0:T(8,128)(2,1)S(1)}, bf16[528,256]{1,0:T(8,128)(2,1)}, u32[]{:S(2)}, u32[]{:S(2)}) collective-permute-start(bf16[528,256]{1,0:T(8,128)(2,1)S(1)} %copy-done.60), channel_id=1, source_target_pairs={{0,4},{4,0},{8,12},{12,8},{16,20},{20,16},{24,28},{28,24},{1,5},{5... | collective-permute-start | bytes 811016 | tf_op jit(solution)/shard_map/ppermute | solution.py:795
  143.7 21.7 %collective-permute-start.28 = (bf16[528,256]{1,0:T(8,128)(2,1)S(1)}, bf16[528,256]{1,0:T(8,128)(2,1)}, u32[]{:S(2)}, u32[]{:S(2)}) collective-permute-start(bf16[528,256]{1,0:T(8,128)(2,1)S(1)} %copy-done.60), channel_id=1, source_target_pairs={{0,8},{4,12},{8,16},{12,20},{16,24},{20,28},{24,0},{28,4},{1,9},{5... | collective-permute-start | bytes 811016 | tf_op jit(solution)/shard_map/ppermute | solution.py:795
  145.9 25.0 %collective-permute-start.22 = (bf16[256,1024]{1,0:T(8,128)(2,1)S(1)}, bf16[256,1024]{1,0:T(8,128)(2,1)S(1)}, u32[]{:S(2)}, u32[]{:S(2)}) collective-permute-start(bf16[256,1024]{1,0:T(8,128)(2,1)S(1)} %add_convert_fusion.4.s_ref), channel_id=1, source_target_pairs={{0,2},{1,3},{2,0},{3,1},{4,6},{5,7},{6,4},{7,5},{8,10},{9,11},{10,... | collective-permute-start | bytes 1572872 | tf_op jit(solution)/shard_map/ppermute | solution.py:788
  163.2 39.3 %collective-permute-start.67 = (bf16[4,128,1024]{2,1,0:T(8,128)(2,1)}, bf16[4,128,1024]{2,1,0:T(8,128)(2,1)}, u32[]{:S(2)}, u32[]{:S(2)}) collective-permute-start(bf16[4,128,1024]{2,1,0:T(8,128)(2,1)} %dynamic-slice_bitcast_fusion), channel_id=1, source_target_pairs={{0,4},{4,0},{8,12},{12,8},{16,20},{20,16},{24,28},{28,24},{1,5},{5... | collective-permute-start | bytes 3145736 | tf_op jit(solution)/shard_map/ppermute | solution.py:852
  170.3 24.9 %collective-permute-start.31 = (bf16[528,256]{1,0:T(8,128)(2,1)}, bf16[528,256]{1,0:T(8,128)(2,1)}, u32[]{:S(2)}, u32[]{:S(2)}) collective-permute-start(bf16[528,256]{1,0:T(8,128)(2,1)} %collective-permute-done.28.refs_7_), channel_id=1, source_target_pairs={{0,4},{4,0},{8,12},{12,8},{16,20},{20,16},{24,28},{28,24},{1,5},{5... | collective-permute-start | bytes 811016 | tf_op jit(solution)/shard_map/ppermute | solution.py:795
  170.9 25.9 %collective-permute-start.35 = (bf16[528,256]{1,0:T(8,128)(2,1)}, bf16[528,256]{1,0:T(8,128)(2,1)}, u32[]{:S(2)}, u32[]{:S(2)}) collective-permute-start(bf16[528,256]{1,0:T(8,128)(2,1)} %get-tuple-element.73.refs_1_.refs_13_), channel_id=1, source_target_pairs={{0,8},{4,12},{8,16},{12,20},{16,24},{20,28},{24,0},{28,4},{1,9},{5... | collective-permute-start | bytes 811016 | tf_op jit(solution)/shard_map/ppermute | solution.py:795
  199.0 60.7 %collective-permute-start.63 = (bf16[4,128,1024]{2,1,0:T(8,128)(2,1)}, bf16[4,128,1024]{2,1,0:T(8,128)(2,1)}, u32[]{:S(2)}, u32[]{:S(2)}) collective-permute-start(bf16[4,128,1024]{2,1,0:T(8,128)(2,1)} %dynamic-slice_bitcast_fusion.1), channel_id=1, source_target_pairs={{0,4},{4,0},{8,12},{12,8},{16,20},{20,16},{24,28},{28,24},{1,5},{5... | collective-permute-start | bytes 3145736 | tf_op jit(solution)/shard_map/ppermute | solution.py:852
  202.5 32.5 %collective-permute-start.38 = (bf16[528,256]{1,0:T(8,128)(2,1)}, bf16[528,256]{1,0:T(8,128)(2,1)S(1)}, u32[]{:S(2)}, u32[]{:S(2)}) collective-permute-start(bf16[528,256]{1,0:T(8,128)(2,1)} %collective-permute-done.35.refs_15_), channel_id=1, source_target_pairs={{0,4},{4,0},{8,12},{12,8},{16,20},{20,16},{24,28},{28,24},{1,5},{5... | collective-permute-start | bytes 811016 | tf_op jit(solution)/shard_map/ppermute | solution.py:795
  206.8 28.2 %collective-permute-start.39 = (bf16[528,256]{1,0:T(8,128)(2,1)}, bf16[528,256]{1,0:T(8,128)(2,1)S(1)}, u32[]{:S(2)}, u32[]{:S(2)}) collective-permute-start(bf16[528,256]{1,0:T(8,128)(2,1)} %collective-permute-done.34.refs_14_), channel_id=1, source_target_pairs={{0,24},{4,28},{8,0},{12,4},{16,8},{20,12},{24,16},{28,20},{1,25},{... | collective-permute-start | bytes 811016 | tf_op jit(solution)/shard_map/ppermute | solution.py:795
  208.3 32.1 %collective-permute-start.40 = (bf16[528,256]{1,0:T(8,128)(2,1)}, bf16[528,256]{1,0:T(8,128)(2,1)S(1)}, u32[]{:S(2)}, u32[]{:S(2)}) collective-permute-start(bf16[528,256]{1,0:T(8,128)(2,1)} %collective-permute-done.37.refs_17_), channel_id=1, source_target_pairs={{0,4},{4,0},{8,12},{12,8},{16,20},{20,16},{24,28},{28,24},{1,5},{5... | collective-permute-start | bytes 811016 | tf_op jit(solution)/shard_map/ppermute | solution.py:795
  219.4 143.9 %collective-permute-start.23 = (bf16[256,1024]{1,0:T(8,128)(2,1)}, bf16[256,1024]{1,0:T(8,128)(2,1)}, u32[]{:S(2)}, u32[]{:S(2)}) collective-permute-start(bf16[256,1024]{1,0:T(8,128)(2,1)} %get-tuple-element.68), channel_id=1, source_target_pairs={{0,1},{1,0},{2,3},{3,2},{4,5},{5,4},{6,7},{7,6},{8,9},{9,8},{10,11... | collective-permute-start | bytes 1572872 | tf_op jit(solution)/shard_map/ppermute | solution.py:788
  257.2 33.4 %collective-permute-start.69 = (bf16[128,1024]{0,1:T(8,128)(2,1)}, bf16[128,1024]{0,1:T(8,128)(2,1)S(1)}, u32[]{:S(2)}, u32[]{:S(2)}) collective-permute-start(bf16[128,1024]{0,1:T(8,128)(2,1)} %bitcast.38), channel_id=1, source_target_pairs={{0,16},{4,20},{8,24},{12,28},{16,0},{20,4},{24,8},{28,12},{1,17},{... | collective-permute-start | bytes 786440 | tf_op jit(solution)/shard_map/ppermute | solution.py:858
  259.7 30.9 %collective-permute-start.68 = (bf16[128,1024]{0,1:T(8,128)(2,1)}, bf16[128,1024]{0,1:T(8,128)(2,1)S(1)}, u32[]{:S(2)}, u32[]{:S(2)}) collective-permute-start(bf16[128,1024]{0,1:T(8,128)(2,1)} %bitcast.37), channel_id=1, source_target_pairs={{0,8},{4,12},{8,16},{12,20},{16,24},{20,28},{24,0},{28,4},{1,9},{5... | collective-permute-start | bytes 786440 | tf_op jit(solution)/shard_map/ppermute | solution.py:858
  265.0 27.0 %collective-permute-start.42 = (bf16[256,1024]{1,0:T(8,128)(2,1)S(1)}, bf16[256,1024]{1,0:T(8,128)(2,1)S(1)}, u32[]{:S(2)}, u32[]{:S(2)}) collective-permute-start(bf16[256,1024]{1,0:T(8,128)(2,1)S(1)} %add_convert_fusion.2.s_ref), channel_id=1, source_target_pairs={{0,2},{1,3},{2,0},{3,1},{4,6},{5,7},{6,4},{7,5},{8,10},{9,11},{10,... | collective-permute-start | bytes 1572872 | tf_op jit(solution)/shard_map/ppermute | solution.py:788
  266.5 90.4 %collective-permute-start.66 = (bf16[128,1024]{1,0:T(8,128)(2,1)S(1)}, bf16[128,1024]{1,0:T(8,128)(2,1)}, u32[]{:S(2)}, u32[]{:S(2)}) collective-permute-start(bf16[128,1024]{1,0:T(8,128)(2,1)S(1)} %get-tuple-element.148), channel_id=1, source_target_pairs={{0,24},{4,28},{8,0},{12,4},{16,8},{20,12},{24,16},{28,20},{1,25},{... | collective-permute-start | bytes 786440 | tf_op jit(solution)/shard_map/ppermute | solution.py:858
  290.6 66.9 %collective-permute-start.65 = (bf16[128,1024]{1,0:T(8,128)(2,1)S(1)}, bf16[128,1024]{1,0:T(8,128)(2,1)}, u32[]{:S(2)}, u32[]{:S(2)}) collective-permute-start(bf16[128,1024]{1,0:T(8,128)(2,1)S(1)} %get-tuple-element.149), channel_id=1, source_target_pairs={{0,16},{4,20},{8,24},{12,28},{16,0},{20,4},{24,8},{28,12},{1,17},{... | collective-permute-start | bytes 786440 | tf_op jit(solution)/shard_map/ppermute | solution.py:858
  290.6 69.3 %collective-permute-start.64 = (bf16[128,1024]{1,0:T(8,128)(2,1)S(1)}, bf16[128,1024]{1,0:T(8,128)(2,1)}, u32[]{:S(2)}, u32[]{:S(2)}) collective-permute-start(bf16[128,1024]{1,0:T(8,128)(2,1)S(1)} %get-tuple-element.147), channel_id=1, source_target_pairs={{0,8},{4,12},{8,16},{12,20},{16,24},{20,28},{24,0},{28,4},{1,9},{5... | collective-permute-start | bytes 786440 | tf_op jit(solution)/shard_map/ppermute | solution.py:858
  339.5 43.9 %collective-permute-start.47 = (bf16[512,1024]{1,0:T(8,128)(2,1)}, bf16[512,1024]{1,0:T(8,128)(2,1)}, u32[]{:S(2)}, u32[]{:S(2)}) collective-permute-start(bf16[512,1024]{1,0:T(8,128)(2,1)} %get-tuple-element.86.send_ref), channel_id=1, source_target_pairs={{0,1},{1,0},{2,3},{3,2},{4,5},{5,4},{6,7},{7,6},{8,9},{9,8},{10,11... | collective-permute-start | bytes 3145736 | tf_op jit(solution)/shard_map/ppermute | solution.py:788
  356.9 31.9 %collective-permute-start.55 = (bf16[4,128,1024]{2,1,0:T(8,128)(2,1)}, bf16[4,128,1024]{2,1,0:T(8,128)(2,1)}, u32[]{:S(2)}, u32[]{:S(2)}) collective-permute-start(bf16[4,128,1024]{2,1,0:T(8,128)(2,1)} %bitcast.13), channel_id=1, source_target_pairs={{0,4},{4,0},{8,12},{12,8},{16,20},{20,16},{24,28},{28,24},{1,5},{5... | collective-permute-start | bytes 3145736 | tf_op jit(solution)/shard_map/ppermute | solution.py:852
  376.6 28.8 %collective-permute-start.59 = (bf16[4,128,1024]{2,1,0:T(8,128)(2,1)}, bf16[4,128,1024]{2,1,0:T(8,128)(2,1)}, u32[]{:S(2)}, u32[]{:S(2)}) collective-permute-start(bf16[4,128,1024]{2,1,0:T(8,128)(2,1)} %bitcast.116), channel_id=1, source_target_pairs={{0,4},{4,0},{8,12},{12,8},{16,20},{20,16},{24,28},{28,24},{1,5},{5... | collective-permute-start | bytes 3145736 | tf_op jit(solution)/shard_map/ppermute | solution.py:852
  385.2 43.1 %collective-permute-start.48 = (bf16[512,1024]{1,0:T(8,128)(2,1)S(1)}, bf16[512,1024]{1,0:T(8,128)(2,1)S(1)}, u32[]{:S(2)}, u32[]{:S(2)}) collective-permute-start(bf16[512,1024]{1,0:T(8,128)(2,1)S(1)} %add_convert_fusion.s_ref), channel_id=1, source_target_pairs={{0,2},{1,3},{2,0},{3,1},{4,6},{5,7},{6,4},{7,5},{8,10},{9,11},{10,... | collective-permute-start | bytes 3145736 | tf_op jit(solution)/shard_map/ppermute | solution.py:788
  388.5 33.5 %collective-permute-start.45 = (bf16[256,1024]{1,0:T(8,128)(2,1)S(1)}, bf16[256,1024]{1,0:T(8,128)(2,1)S(1)}, u32[]{:S(2)}, u32[]{:S(2)}) collective-permute-start(bf16[256,1024]{1,0:T(8,128)(2,1)S(1)} %add_convert_fusion.1.s_ref), channel_id=1, source_target_pairs={{0,2},{1,3},{2,0},{3,1},{4,6},{5,7},{6,4},{7,5},{8,10},{9,11},{10,... | collective-permute-start | bytes 1572872 | tf_op jit(solution)/shard_map/ppermute | solution.py:788
  390.7 42.5 %collective-permute-start.58 = (bf16[128,1024]{1,0:T(8,128)(2,1)S(1)}, bf16[128,1024]{1,0:T(8,128)(2,1)S(1)}, u32[]{:S(2)}, u32[]{:S(2)}) collective-permute-start(bf16[128,1024]{1,0:T(8,128)(2,1)S(1)} %get-tuple-element.154), channel_id=1, source_target_pairs={{0,24},{4,28},{8,0},{12,4},{16,8},{20,12},{24,16},{28,20},{1,25},{... | collective-permute-start | bytes 786440 | tf_op jit(solution)/shard_map/ppermute | solution.py:858
  393.6 40.0 %collective-permute-start.57 = (bf16[128,1024]{1,0:T(8,128)(2,1)S(1)}, bf16[128,1024]{1,0:T(8,128)(2,1)}, u32[]{:S(2)}, u32[]{:S(2)}) collective-permute-start(bf16[128,1024]{1,0:T(8,128)(2,1)S(1)} %get-tuple-element.155), channel_id=1, source_target_pairs={{0,16},{4,20},{8,24},{12,28},{16,0},{20,4},{24,8},{28,12},{1,17},{... | collective-permute-start | bytes 786440 | tf_op jit(solution)/shard_map/ppermute | solution.py:858
  405.4 28.2 %collective-permute-start.56 = (bf16[128,1024]{1,0:T(8,128)(2,1)S(1)}, bf16[128,1024]{1,0:T(8,128)(2,1)}, u32[]{:S(2)}, u32[]{:S(2)}) collective-permute-start(bf16[128,1024]{1,0:T(8,128)(2,1)S(1)} %get-tuple-element.153), channel_id=1, source_target_pairs={{0,8},{4,12},{8,16},{12,20},{16,24},{20,28},{24,0},{28,4},{1,9},{5... | collective-permute-start | bytes 786440 | tf_op jit(solution)/shard_map/ppermute | solution.py:858
  (109 other events, 1219.3 us)

commit v2 on v1

v2 whole, which is shorter than its diff:
```python
import functools
import math

import jax
import jax.numpy as jnp
from jax import lax
from jax.experimental import pallas as pl
from jax.experimental.pallas import tpu as pltpu
from jax.sharding import PartitionSpec as P

HEAD = 128
GROUP = 128
SRC = 256
GROUPS_FRAME = 8
LOG2E = 1.4426950408889634
epsilon = 1e-05
masked_value = -1e30
bf16 = jnp.bfloat16
f32 = jnp.float32
EXTRA = 16
WEIGHT = 1

VMEM = pl.BlockSpec(memory_space=pltpu.VMEM)
SMEM = pl.BlockSpec(memory_space=pltpu.SMEM)


def sds(shape, dtype):
    return jax.ShapeDtypeStruct(shape, dtype)


def dot(a, b):
    return lax.dot_general(a, b, (((1,), (0,)), ((), ())), preferred_element_type=f32)


def dot_t(a, b):
    return lax.dot_general(a, b, (((1,), (1,)), ((), ())), preferred_element_type=f32)


def dot_ta(a, b):
    return lax.dot_general(a, b, (((0,), (0,)), ((), ())), preferred_element_type=f32)


def centre(values):
    centred = values - jnp.mean(values, axis=-1, keepdims=True)
    variance = jnp.mean(centred * centred, axis=-1, keepdims=True)
    inverse = lax.rsqrt(variance + epsilon)
    return centred * inverse, inverse


ANY = pl.BlockSpec(memory_space=pl.ANY)
CHUNK = 64


def by_chunks(rows, step, carry=0):
    for first in range(0, rows, CHUNK):
        carry = step(slice(first, first + CHUNK), carry)
    return carry


def norm_into(out_ref, in_ref, gain_ref):
    gain_vec = gain_ref[...]

    def step(r, held):
        out_ref[r, :] = (centre(in_ref[r, :].astype(f32))[0] * gain_vec).astype(bf16)
        return held

    by_chunks(in_ref.shape[0], step)


def folded(rows_value):
    parts = [rows_value[k : k + 8] for k in range(0, CHUNK, 8)]
    while len(parts) > 1:
        parts = [parts[k] + parts[k + 1] for k in range(0, len(parts), 2)]
    return parts[0]


def call(
    body, outs, ins, args, name, scratch=(), grid=None, prefetch=0, flops=0, nbytes=0, trans=0, ties=(), aliases=None,
    spare=6,
):
    given = prefetch + len(ins)
    room = 0
    for spec, v in [*zip(ins, args[prefetch:]), *[(spec, shape) for shape, spec in outs]]:
        if spec.block_shape is not None:
            room += 2 * math.prod(spec.block_shape) * v.dtype.itemsize
        elif spec is VMEM:
            room += math.prod(v.shape) * v.dtype.itemsize
    room += sum(math.prod(v.shape) * jnp.dtype(v.dtype).itemsize for v in scratch)

    def run(*refs):
        body(*refs[:given], *refs[given + len(ties) :])

    return pl.pallas_call(
        run,
        out_shape=[shape for shape, ignored in outs],
        grid_spec=pltpu.PrefetchScalarGridSpec(
            num_scalar_prefetch=prefetch,
            grid=() if grid is None else grid,
            in_specs=list(ins) + [ANY] * len(ties),
            out_specs=[spec for ignored, spec in outs],
            scratch_shapes=list(scratch),
        ),
        compiler_params=pltpu.CompilerParams(vmem_limit_bytes=room + spare * 2**20),
        cost_estimate=pl.CostEstimate(
            flops=int(flops * WEIGHT), bytes_accessed=int(nbytes * WEIGHT), transcendentals=int(trans * WEIGHT)
        ),
        input_output_aliases=aliases or {},
        name=name,
    )(*args, *ties)


def index_row(idx_ref, pos_ref, b, blocks, count):
    at = (b + pos_ref[0] * (blocks // 2)) % blocks
    return (idx_ref[pl.ds(at, 1), :] - pos_ref[1] * count).astype(f32)


def clip_of(clip_ref, pos_ref, b, blocks, sets, own):
    half = blocks // 2
    if own:
        return clip_ref[blocks * (pos_ref[1] % sets) + (b + pos_ref[0] * half) % blocks]
    return clip_ref[blocks * (b // blocks) + (b % blocks + pos_ref[0] * half) % blocks]


def cross_forward_body(
    pos_ref, idx_ref, lat_ref, src_ref, gain_one_ref, gain_src_ref, wq_ref, wk_ref, wv_ref,
    n1_ref, ns_ref, q_ref, kvp_ref, keep_ref, send_ref, kv_s, *, steps,
):
    i = pl.program_id(0)
    width = wq_ref.shape[1]
    heads = width // HEAD
    rows_src = src_ref.shape[0]
    norm_into(ns_ref, src_ref, gain_src_ref)
    normed_src = ns_ref[...]
    row0 = pl.multiple_of(i * rows_src, rows_src)
    kv_s[pl.ds(row0, rows_src), 0:width] = dot(normed_src, wk_ref[...]).astype(bf16)
    kv_s[pl.ds(row0, rows_src), width:] = dot(normed_src, wv_ref[...]).astype(bf16)
    norm_into(n1_ref, lat_ref, gain_one_ref)
    normed_one = n1_ref[...]
    grp0 = pl.multiple_of(i * GROUP, GROUP)
    q_ref[pl.ds(grp0, GROUP), :] = dot(normed_one, wq_ref[...]).astype(bf16)

    @pl.when(i == steps - 1)
    def _():
        count = kv_s.shape[0]
        lanes = lax.broadcasted_iota(jnp.int32, (128, count), 1).astype(f32)
        for b in range(steps):
            for part in range(SRC // 128):
                row = index_row(idx_ref, pos_ref, b, steps, count)[:, part * 128 : (part + 1) * 128]
                column = jnp.transpose(jnp.broadcast_to(row, (128, 128)))
                picks = jnp.where(jnp.tile(column, (1, count // 128)) == lanes, 1.0, 0.0).astype(bf16)
                r0 = b * SRC + part * 128
                kvp_ref[r0 : r0 + 128, :] = dot(picks, kv_s[...]).astype(bf16)
        for b in range(steps):
            for h in range(heads):
                cols = slice(h * HEAD, (h + 1) * HEAD)
                q = q_ref[b * GROUP : (b + 1) * GROUP, cols]
                k = kvp_ref[b * SRC : (b + 1) * SRC, cols]
                v = kvp_ref[b * SRC : (b + 1) * SRC, width + h * HEAD : width + (h + 1) * HEAD]
                s = dot_t(q, k) * (HEAD ** (-0.5) * LOG2E)
                p = jnp.exp2(s - jnp.max(s, axis=-1, keepdims=True))
                total = jnp.sum(p, axis=-1, keepdims=True)
                mixed = (dot(p.astype(bf16), v) / total).astype(bf16)
                if b < steps // 2:
                    keep_ref[b * GROUP : (b + 1) * GROUP, cols] = mixed
                else:
                    r0 = (b - steps // 2) * GROUP
                    send_ref[r0 : r0 + GROUP, cols] = mixed


def cross_forward(pos, idx, latents, sources, gain_one, gain_src, wq, wk, wv):
    rows, width_d = latents.shape
    steps = rows // GROUP
    count = sources.shape[0]
    blk = count // steps
    width = wq.shape[1]
    whole = lambda shape: pl.BlockSpec(shape, lambda i, c: (0,) * len(shape))
    return call(
        functools.partial(cross_forward_body, steps=steps),
        [
            (sds((rows, width_d), bf16), pl.BlockSpec((GROUP, width_d), lambda i, c: (i, 0))),
            (sds((count, width_d), bf16), pl.BlockSpec((blk, width_d), lambda i, c: (i, 0))),
            (sds((rows, width), bf16), whole((rows, width))),
            (sds((count, 2 * width), bf16), whole((count, 2 * width))),
            (sds((rows // 2, width), bf16), whole((rows // 2, width))),
            (sds((rows // 2, width), bf16), whole((rows // 2, width))),
        ],
        [
            whole(idx.shape),
            pl.BlockSpec((GROUP, width_d), lambda i, c: ((i + c[0] * (steps // 2)) % steps, 0)),
            pl.BlockSpec((blk, width_d), lambda i, c: (i, 0)),
            whole((1, width_d)),
            whole((1, width_d)),
            whole(wq.shape),
            whole(wk.shape),
            whole(wv.shape),
        ],
        (pos, idx, latents, sources, gain_one, gain_src, wq, wk, wv),
        "cross_forward",
        scratch=[pltpu.VMEM((count, 2 * width), bf16)],
        grid=(steps,),
        prefetch=1,
        flops=4e9,
        nbytes=12e6,
        spare=44,
    )


def project_body(pos_ref, *refs, parts, own_half):
    pieces, weights = refs[:parts], refs[parts : 2 * parts]
    base_ref, gain_ref, after_ref, normed_ref, left_s, right_s = refs[2 * parts :]
    half = after_ref.shape[0]
    width = pieces[0].shape[1]
    for k in range(parts):
        at = pl.multiple_of((pos_ref[2] ^ k) * width, width)
        left_s[:, pl.ds(at, width)] = pieces[k][...]
        right_s[pl.ds(at, width), :] = weights[k][...]
    after_ref[...] = dot(left_s[...], right_s[...])
    first = pos_ref[0] * half if own_half else 0
    gain_vec = gain_ref[...]

    def step(r, held):
        base = base_ref[pl.ds(pl.multiple_of(first + r.start, CHUNK), CHUNK), :]
        after = base.astype(f32) + after_ref[r, :]
        after_ref[r, :] = after
        normed_ref[r, :] = (centre(after)[0] * gain_vec).astype(bf16)
        return held

    by_chunks(half, step)


def project(pos, pieces, weights, base, gain, own_half, ties=()):
    parts = len(pieces)
    half, width = pieces[0].shape
    width_d = weights[0].shape[1]
    return call(
        functools.partial(project_body, parts=parts, own_half=own_half),
        [(sds((half, width_d), f32), VMEM), (sds((half, width_d), bf16), VMEM)],
        [SMEM] + [VMEM] * (2 * parts + 2),
        (pos, *pieces, *weights, base, gain),
        "project",
        scratch=[pltpu.VMEM((half, parts * width), bf16), pltpu.VMEM((parts * width, width_d), bf16)],
        flops=2 * half * width * parts * width_d,
        nbytes=5e6,
        ties=ties,
    )


def qkv_body(mine_ref, other_ref, wq_ref, wk_ref, wv_ref, q_ref, kv_ref):
    half = mine_ref.shape[0]
    width = wq_ref.shape[1]
    for part, ref in enumerate((mine_ref, other_ref)):
        rows = slice(part * half, (part + 1) * half)
        x = ref[...]
        kv_ref[rows, 0:width] = dot(x, wk_ref[...]).astype(bf16)
        kv_ref[rows, width:] = dot(x, wv_ref[...]).astype(bf16)
        q_ref[rows, :] = dot(x, wq_ref[...]).astype(bf16)


def qkv(mine, other, wq, wk, wv):
    half, width_d = mine.shape
    width = wq.shape[1]
    return call(
        qkv_body,
        [(sds((2 * half, width), bf16), VMEM), (sds((2 * half, 2 * width), bf16), VMEM)],
        [VMEM] * 5,
        (mine, other, wq, wk, wv),
        "qkv",
        flops=2 * 2 * half * width_d * 3 * width,
        nbytes=4e6,
    )


def assemble(refs, entries, dst, rows_blocks):
    for ri, base, p, k in entries:
        for j in range(rows_blocks):
            dst[p * rows_blocks + j, pl.ds(place_start(k), GROUP), :] = refs[ri][
                base + j * GROUP : base + (j + 1) * GROUP, :
            ]


def place_start(k):
    return k * GROUP if isinstance(k, int) else pl.multiple_of(k * GROUP, GROUP)


def split_rows(rows_value):
    high = rows_value.astype(bf16)
    rest = rows_value - high.astype(f32)
    middle = rest.astype(bf16)
    low = (rest - middle.astype(f32)).astype(bf16)
    return high, middle, low


def pack_extra(row_tiles, heads, blocks, width):
    per_row = width // 128
    out = []
    for h in range(heads):
        flat = [
            jnp.concatenate(row_tiles[h][r * per_row : (r + 1) * per_row], axis=1)
            for r in range(blocks // per_row)
        ]
        rows_value = jnp.concatenate(flat, axis=0)
        out += [part.astype(f32) for part in split_rows(rows_value)]
    used = heads * 3 * (blocks // per_row)
    if used < EXTRA:
        out.append(jnp.zeros((EXTRA - used, width), f32))
    return jnp.concatenate(out, axis=0).astype(bf16)


def unpack_extra(extra, h, j, blocks, width):
    per_row = width // 128
    rows_per = blocks // per_row
    row, lane = j // per_row, (j % per_row) * 128
    parts = [
        extra[(h * 3 + t) * rows_per + row : (h * 3 + t) * rows_per + row + 1, lane : lane + 128]
        for t in range(3)
    ]
    return (parts[0] + parts[1]) + parts[2]


def attend_body(
    pos_ref, clip_ref, *refs, pieces, entries, heads, blocks, period,
):
    q_ref = refs[0]
    kv_refs = refs[1 : 1 + pieces]
    keep_ref, send_ref, lsex_ref, lsec_ref, kv_s, m_s, l_s, acc_s, row_s, o_s = refs[1 + pieces :]
    width = heads * HEAD
    sets = period // blocks
    assemble(kv_refs, entries, kv_s, blocks)

    def per_block(i, carry):
        r0 = pl.multiple_of(i * GROUP, GROUP)
        own_clip = clip_of(clip_ref, pos_ref, i, blocks, sets, True)
        m_s[...] = jnp.full(m_s.shape, masked_value, f32)
        l_s[...] = jnp.zeros(l_s.shape, f32)
        acc_s[...] = jnp.zeros(acc_s.shape, f32)

        def per_keys(g, inner):
            @pl.when(own_clip == clip_of(clip_ref, pos_ref, g, blocks, sets, False))
            def _():
                for h in range(heads):
                    cols = slice(h * HEAD, (h + 1) * HEAD)
                    q = q_ref[pl.ds(r0, GROUP), cols]
                    k = kv_s[g, :, cols]
                    v = kv_s[g, :, width + h * HEAD : width + (h + 1) * HEAD]
                    s = dot_t(q, k) * (HEAD ** (-0.5) * LOG2E)
                    m_old = m_s[h][:, 0:1]
                    m_new = jnp.maximum(m_old, jnp.max(s, axis=-1, keepdims=True))
                    p = jnp.exp2(s - m_new)
                    alpha = jnp.exp2(m_old - m_new)
                    l_new = l_s[h][:, 0:1] * alpha + jnp.sum(p, axis=-1, keepdims=True)
                    acc_s[h] = acc_s[h] * alpha + dot(p.astype(bf16), v)
                    m_s[h] = jnp.broadcast_to(m_new, (GROUP, 128))
                    l_s[h] = jnp.broadcast_to(l_new, (GROUP, 128))

            return inner

        lax.fori_loop(0, period, per_keys, 0)
        for h in range(heads):
            total = l_s[h]
            o_s[pl.ds(r0, GROUP), h * HEAD : (h + 1) * HEAD] = (acc_s[h] / total).astype(bf16)
            lse = m_s[h] + jnp.log2(total)
            lsec_ref[h, pl.ds(r0, GROUP), :] = lse
            row_s[h, i] = jnp.transpose(lse)[0:8]
        return carry

    lax.fori_loop(0, blocks, per_block, 0)
    half = blocks // 2 * GROUP
    keep_ref[...] = o_s[0:half, :]
    send_ref[...] = o_s[half:, :]
    tiles = [[row_s[h, j][0:1] for j in range(blocks)] for h in range(heads)]
    lsex_ref[...] = pack_extra(tiles, heads, blocks, width)


def attend(pos, clips, q, kv_pieces, entries, ties):
    rows, width = q.shape
    heads, blocks, period = width // HEAD, rows // GROUP, clips.shape[0] // GROUPS_FRAME
    pieces = len(kv_pieces)
    body = functools.partial(
        attend_body, pieces=pieces, entries=entries, heads=heads, blocks=blocks, period=period
    )
    return call(
        body,
        [
            (sds((rows // 2, width), bf16), VMEM),
            (sds((rows // 2, width), bf16), VMEM),
            (sds((EXTRA, width), bf16), VMEM),
            (sds((heads, rows, 128), f32), VMEM),
        ],
        [SMEM, SMEM] + [VMEM] * (1 + pieces),
        (pos, clips, q, *kv_pieces),
        "attend",
        ties=ties,
        scratch=[
            pltpu.VMEM((period, GROUPS_FRAME * GROUP, 2 * width), bf16),
            pltpu.VMEM((heads, GROUP, 128), f32),
            pltpu.VMEM((heads, GROUP, 128), f32),
            pltpu.VMEM((heads, GROUP, HEAD), f32),
            pltpu.VMEM((heads, blocks, 8, 128), f32),
            pltpu.VMEM((rows, width), bf16),
        ],
        flops=2e9,
        nbytes=7e6,
        trans=2e6,
    )


def out_back_body(mine_ref, other_ref, wo_ref, okeep_ref, osend_ref, lsex_ref, dox_ref, dc_ref, *, heads, blocks):
    half = mine_ref.shape[0]
    rows = 2 * half
    tiles = [[] for h in range(heads)]
    for part, (ref, o_ref) in enumerate(((mine_ref, okeep_ref), (other_ref, osend_ref))):
        grad = dot_t(ref[...], wo_ref[...]).astype(bf16)
        dox_ref[part * half : (part + 1) * half, :] = grad
        product = grad.astype(f32) * o_ref[...].astype(f32)
        for h in range(heads):
            delta = jnp.sum(product[:, h * HEAD : (h + 1) * HEAD], axis=-1, keepdims=True)
            delta = jnp.broadcast_to(delta, (half, 128))
            dc_ref[h, part * half : (part + 1) * half, :] = delta
            for j in range(half // GROUP):
                tiles[h].append(jnp.transpose(delta[j * GROUP : (j + 1) * GROUP])[0:1])
    dox_ref[rows : rows + EXTRA, :] = pack_extra(tiles, heads, blocks, heads * HEAD)
    dox_ref[rows + EXTRA :, :] = lsex_ref[...]


def out_back(mine, other, wo, okeep, osend, lsex):
    half, width_d = mine.shape
    width = wo.shape[0]
    heads, blocks = width // HEAD, 2 * half // GROUP
    return call(
        functools.partial(out_back_body, heads=heads, blocks=blocks),
        [(sds((2 * half + 2 * EXTRA, width), bf16), VMEM), (sds((heads, 2 * half, 128), f32), VMEM)],
        [VMEM] * 6,
        (mine, other, wo, okeep, osend, lsex),
        "out_back",
        flops=2 * 2 * half * width * width_d,
        nbytes=4e6,
    )


def query_back_body(pos_ref, clip_ref, *refs, pieces, entries, heads, blocks, period):
    qx_ref, dox_ref, lsec_ref, dc_ref = refs[0:4]
    kv_refs = refs[4 : 4 + pieces]
    dq_ref, kv_s, acc_s = refs[4 + pieces :]
    width = heads * HEAD
    sets = period // blocks
    assemble(kv_refs, entries, kv_s, blocks)

    def per_block(i, carry):
        r0 = pl.multiple_of(i * GROUP, GROUP)
        own_clip = clip_of(clip_ref, pos_ref, i, blocks, sets, True)
        acc_s[...] = jnp.zeros(acc_s.shape, f32)

        def per_keys(g, inner):
            @pl.when(own_clip == clip_of(clip_ref, pos_ref, g, blocks, sets, False))
            def _():
                for h in range(heads):
                    cols = slice(h * HEAD, (h + 1) * HEAD)
                    k = kv_s[g, :, cols]
                    v = kv_s[g, :, width + h * HEAD : width + (h + 1) * HEAD]
                    s = dot_t(qx_ref[pl.ds(r0, GROUP), cols], k) * (HEAD ** (-0.5) * LOG2E)
                    p = jnp.exp2(s - lsec_ref[h, pl.ds(r0, GROUP), :][:, 0:1])
                    dp = dot_t(dox_ref[pl.ds(r0, GROUP), cols], v)
                    delta = dc_ref[h, pl.ds(r0, GROUP), :][:, 0:1]
                    ds = (p * (dp - delta) * (HEAD ** (-0.5))).astype(bf16)
                    acc_s[h] = acc_s[h] + dot(ds, k)

            return inner

        lax.fori_loop(0, period, per_keys, 0)
        for h in range(heads):
            dq_ref[pl.ds(r0, GROUP), h * HEAD : (h + 1) * HEAD] = acc_s[h].astype(bf16)
        return carry

    lax.fori_loop(0, blocks, per_block, 0)


def query_back(pos, clips, qx, dox, lsec, dc, kv_pieces, entries):
    rows, width = qx.shape
    heads, blocks, period = width // HEAD, rows // GROUP, clips.shape[0] // GROUPS_FRAME
    pieces = len(kv_pieces)
    return call(
        functools.partial(
            query_back_body, pieces=pieces, entries=entries, heads=heads, blocks=blocks, period=period
        ),
        [(sds((rows, width), bf16), VMEM)],
        [SMEM, SMEM] + [VMEM] * (4 + pieces),
        (pos, clips, qx, dox, lsec, dc, *kv_pieces),
        "query_back",
        scratch=[
            pltpu.VMEM((period, GROUPS_FRAME * GROUP, 2 * width), bf16),
            pltpu.VMEM((heads, GROUP, HEAD), f32),
        ],
        flops=2e9,
        nbytes=7e6,
        trans=2e6,
    )[0]


def key_back_body(
    pos_ref, clip_ref, *refs, q_pieces, do_pieces, q_entries, do_entries, heads, blocks, period
):
    kv_ref, dq_ref, wq_ref, wk_ref, wv_ref = refs[0:5]
    qx_refs = refs[5 : 5 + q_pieces]
    dox_refs = refs[5 + q_pieces : 5 + q_pieces + do_pieces]
    dqkv_ref, keep_ref, send_ref, q_s, do_s, lse_s, delta_s, dk_s, dv_s = refs[5 + q_pieces + do_pieces :]
    width = heads * HEAD
    rows = blocks * GROUP
    sets = period // blocks
    assemble(qx_refs, q_entries, q_s, blocks)
    assemble(dox_refs, do_entries, do_s, blocks)
    for first, target in ((rows, delta_s), (rows + EXTRA, lse_s)):
        for ri, base, p, k in do_entries:
            extra = dox_refs[ri][base + first : base + first + EXTRA, :].astype(f32)
            for h in range(heads):
                for j in range(blocks):
                    line = unpack_extra(extra, h, j, blocks, width)
                    target[p * blocks + j, h, :, pl.ds(place_start(k), GROUP)] = jnp.broadcast_to(
                        line, (8, 128)
                    )
    dqkv_ref[:, 0:width] = dq_ref[...]

    def per_block(j, carry):
        r0 = pl.multiple_of(j * GROUP, GROUP)
        own_clip = clip_of(clip_ref, pos_ref, j, blocks, sets, True)
        dk_s[...] = jnp.zeros(dk_s.shape, f32)
        dv_s[...] = jnp.zeros(dv_s.shape, f32)

        def per_queries(g, inner):
            @pl.when(own_clip == clip_of(clip_ref, pos_ref, g, blocks, sets, False))
            def _():
                for h in range(heads):
                    cols = slice(h * HEAD, (h + 1) * HEAD)
                    k = kv_ref[pl.ds(r0, GROUP), cols]
                    v = kv_ref[pl.ds(r0, GROUP), width + h * HEAD : width + (h + 1) * HEAD]
                    q = q_s[g, :, cols]
                    do = do_s[g, :, cols]
                    st = dot_t(k, q) * (HEAD ** (-0.5) * LOG2E)
                    pt = jnp.exp2(st - lse_s[g, h, 0:1, :])
                    dv_s[h] = dv_s[h] + dot(pt.astype(bf16), do)
                    dpt = dot_t(v, do)
                    dst = (pt * (dpt - delta_s[g, h, 0:1, :]) * (HEAD ** (-0.5))).astype(bf16)
                    dk_s[h] = dk_s[h] + dot(dst, q)

            return inner

        lax.fori_loop(0, period, per_queries, 0)
        for h in range(heads):
            dqkv_ref[pl.ds(r0, GROUP), width + h * HEAD : width + (h + 1) * HEAD] = dk_s[h].astype(bf16)
            dqkv_ref[pl.ds(r0, GROUP), 2 * width + h * HEAD : 2 * width + (h + 1) * HEAD] = dv_s[
                h
            ].astype(bf16)
        return carry

    lax.fori_loop(0, blocks, per_block, 0)
    half = rows // 2
    for part, ref in enumerate((keep_ref, send_ref)):
        r = slice(part * half, (part + 1) * half)
        total = dot_t(dqkv_ref[r, 0:width], wq_ref[...])
        total = total + dot_t(dqkv_ref[r, width : 2 * width], wk_ref[...])
        total = total + dot_t(dqkv_ref[r, 2 * width :], wv_ref[...])
        ref[...] = total.astype(bf16)


def key_back(pos, clips, kv, dq, wq, wk, wv, qx_pieces, q_entries, dox_pieces, do_entries, ties):
    rows, width = dq.shape
    width_d = wq.shape[0]
    heads, blocks, period = width // HEAD, rows // GROUP, clips.shape[0] // GROUPS_FRAME
    tall = GROUPS_FRAME * GROUP
    return call(
        functools.partial(
            key_back_body, q_pieces=len(qx_pieces), do_pieces=len(dox_pieces), q_entries=q_entries,
            do_entries=do_entries, heads=heads, blocks=blocks, period=period,
        ),
        [
            (sds((rows, 3 * width), bf16), VMEM),
            (sds((rows // 2, width_d), bf16), VMEM),
            (sds((rows // 2, width_d), bf16), VMEM),
        ],
        [SMEM, SMEM] + [VMEM] * (5 + len(qx_pieces) + len(dox_pieces)),
        (pos, clips, kv, dq, wq, wk, wv, *qx_pieces, *dox_pieces),
        "key_back",
        ties=ties,
        scratch=[
            pltpu.VMEM((period, tall, width), bf16),
            pltpu.VMEM((period, tall, width), bf16),
            pltpu.VMEM((period, heads, 8, tall), f32),
            pltpu.VMEM((period, heads, 8, tall), f32),
            pltpu.VMEM((heads, GROUP, HEAD), f32),
            pltpu.VMEM((heads, GROUP, HEAD), f32),
        ],
        flops=4e9,
        nbytes=9e6,
        trans=2e6,
    )


def mlp_body(mine_ref, other_ref, win_ref, ag_ref, act_ref, hg_ref, keep_ref, send_ref, *, steps):
    i = pl.program_id(0)
    x = jnp.where(i < steps // 2, mine_ref[...], other_ref[...])
    units = win_ref.shape[1]
    chunk = 256
    total = None
    for n in range(units // chunk):
        cols = slice(n * chunk, (n + 1) * chunk)
        w = win_ref[:, cols]
        hidden = dot(x, w)
        cdf = 0.5 * (1.0 + lax.erf(hidden * 0.7071067811865476))
        act_ref[:, cols] = (hidden * cdf).astype(bf16)
        density = jnp.exp2(hidden * hidden * (-0.5 * LOG2E)) * 0.3989422804014327
        grad = (ag_ref[:, cols] * (cdf + hidden * density)).astype(bf16)
        hg_ref[:, cols] = grad
        term = dot_t(grad, w)
        total = term if total is None else total + term
    total = total.astype(bf16)

    @pl.when(i < steps // 2)
    def _():
        keep_ref[...] = total

    @pl.when(i >= steps // 2)
    def _():
        send_ref[...] = total


def mlp(mine, other, w_in, act_grad):
    half, width_d = mine.shape
    units = w_in.shape[1]
    steps = 2 * half // GROUP
    rows = 2 * half
    low = lambda i: (jnp.minimum(i, steps // 2 - 1), 0)
    high = lambda i: (jnp.maximum(i - steps // 2, 0), 0)
    return call(
        functools.partial(mlp_body, steps=steps),
        [
            (sds((rows, units), bf16), pl.BlockSpec((GROUP, units), lambda i: (i, 0))),
            (sds((rows, units), bf16), pl.BlockSpec((GROUP, units), lambda i: (i, 0))),
            (sds((half, width_d), bf16), pl.BlockSpec((GROUP, width_d), low)),
            (sds((half, width_d), bf16), pl.BlockSpec((GROUP, width_d), high)),
        ],
        [
            pl.BlockSpec((GROUP, width_d), low),
            pl.BlockSpec((GROUP, width_d), high),
            pl.BlockSpec((width_d, units), lambda i: (0, 0)),
            pl.BlockSpec((GROUP, units), lambda i: (i, 0)),
        ],
        (mine, other, w_in, act_grad),
        "mlp",
        grid=(steps,),
        flops=4 * rows * width_d * units,
        nbytes=9e6,
        trans=2 * rows * units,
    )


def mlp_down_body(act_ref, w_ref, keep_ref, send_ref, *, steps):
    i = pl.program_id(0)
    total = dot(act_ref[...], w_ref[...]).astype(bf16)

    @pl.when(i < steps // 2)
    def _():
        keep_ref[...] = total

    @pl.when(i >= steps // 2)
    def _():
        send_ref[...] = total


def mlp_down(activated, w_out, ties):
    rows, units = activated.shape
    width_d = w_out.shape[1]
    steps = rows // GROUP
    half = sds((rows // 2, width_d), bf16)
    return call(
        functools.partial(mlp_down_body, steps=steps),
        [
            (half, pl.BlockSpec((GROUP, width_d), lambda i: (jnp.minimum(i, steps // 2 - 1), 0))),
            (half, pl.BlockSpec((GROUP, width_d), lambda i: (jnp.maximum(i - steps // 2, 0), 0))),
        ],
        [
            pl.BlockSpec((GROUP, units), lambda i: (i, 0)),
            pl.BlockSpec((units, width_d), lambda i: (0, 0)),
        ],
        (activated, w_out),
        "mlp_down",
        grid=(steps,),
        flops=2 * rows * units * width_d,
        nbytes=4e6,
        ties=ties,
    )


def act_back_body(pos_ref, og_ref, w_ref, rel_ref, ag_ref):
    rel_ref[...] = og_ref[...]
    ag_ref[...] = dot_t(og_ref[...], w_ref[...])


def act_back(pos, out_grad, w_out):
    rows, width_d = out_grad.shape
    units = w_out.shape[0]
    steps = rows // GROUP
    blk = pl.BlockSpec((GROUP, width_d), lambda i, c: (i, 0))
    return call(
        act_back_body,
        [
            (sds((rows, width_d), bf16), blk),
            (sds((rows, units), f32), pl.BlockSpec((GROUP, units), lambda i, c: (i, 0))),
        ],
        [
            pl.BlockSpec((GROUP, width_d), lambda i, c: ((i + c[0] * (steps // 2)) % steps, 0)),
            pl.BlockSpec((units, width_d), lambda i, c: (0, 0)),
        ],
        (pos, out_grad, w_out),
        "act_back",
        grid=(steps,),
        prefetch=1,
        flops=2 * rows * width_d * units,
        nbytes=6e6,
    )


def through_norm(n, v, gain_vec):
    unit, inverse = centre(v)
    t = n * gain_vec
    back = inverse * (
        t - jnp.mean(t, axis=-1, keepdims=True) - unit * jnp.mean(t * unit, axis=-1, keepdims=True)
    )
    return back, unit


def norm_back_body(s_ref, r_ref, v_ref, gain_ref, base_ref, after_ref, branch_ref, gg_ref):
    gain_vec = gain_ref[...]

    def step(r, held):
        n = s_ref[r, :].astype(f32) + r_ref[r, :].astype(f32)
        back, unit = through_norm(n, v_ref[r, :], gain_vec)
        after = base_ref[r, :].astype(f32) + back
        after_ref[r, :] = after
        branch_ref[r, :] = after.astype(bf16)
        return held + folded(n * unit)

    total = by_chunks(s_ref.shape[0], step, jnp.zeros((8, s_ref.shape[1]), f32))
    gg_ref[...] = jnp.sum(total, axis=0, keepdims=True)


def norm_back(s, r, v, gain, base, ties):
    half, width_d = s.shape
    return call(
        norm_back_body,
        [
            (sds((half, width_d), f32), VMEM),
            (sds((half, width_d), bf16), VMEM),
            (sds((1, width_d), f32), VMEM),
        ],
        [VMEM] * 5,
        (s, r, v, gain, base),
        "norm_back",
        ties=ties,
        flops=20 * half * width_d,
        nbytes=5e6,
    )


def final_body(pos_ref, s_ref, r_ref, v_ref, gain_ref, *refs, with_base):
    gain_vec = gain_ref[...]

    def step(r, held):
        n = s_ref[r, :].astype(f32) + r_ref[r, :].astype(f32)
        back = through_norm(n, v_ref[r, :].astype(f32), gain_vec)[0]
        if with_base:
            back = refs[0][r, :] + back
        refs[-2][r, :] = back.astype(bf16)
        refs[-1][r, :] = back.astype(bf16)
        return held

    by_chunks(s_ref.shape[0], step)


def final_norm(pos, s, r, v, gain, base, ties):
    half, width_d = s.shape
    rows = 128
    steps = half // rows
    blk = pl.BlockSpec((rows, width_d), lambda i, c: (i, 0))
    own = pl.BlockSpec((rows, width_d), lambda i, c: (c[0] * steps + i, 0))
    more = () if base is None else (base,)
    return call(
        functools.partial(final_body, with_base=base is not None),
        [(sds((half, width_d), bf16), blk), (sds((2 * half, width_d), bf16), own)],
        [blk, blk, own, pl.BlockSpec((1, width_d), lambda i, c: (0, 0))] + [blk] * len(more),
        (pos, s, r, v, gain, *more),
        "final_norm",
        ties=ties,
        grid=(steps,),
        prefetch=1,
        flops=20 * half * width_d,
        nbytes=8 * half * width_d,
    )


def place_body(pos_ref, other_ref, whole_ref, out_ref):
    out_ref[...] = other_ref[...]


def place_other(pos, whole, other):
    half, width_d = other.shape
    rows = 256
    steps = half // rows
    return call(
        place_body,
        [(sds(whole.shape, bf16), pl.BlockSpec((rows, width_d), lambda i, c: ((1 - c[0]) * steps + i, 0)))],
        [pl.BlockSpec((rows, width_d), lambda i, c: (i, 0)), ANY],
        (pos, other, whole),
        "place_other",
        grid=(steps,),
        prefetch=1,
        nbytes=4 * half * width_d,
        aliases={2: 0},
    )[0]


def result_body(pos_ref, s_ref, r_ref, after_ref, half_ref, whole_ref, squares_ref):
    def step(r, held):
        result = after_ref[r, :] + (s_ref[r, :].astype(f32) + r_ref[r, :].astype(f32))
        half_ref[r, :] = result.astype(bf16)
        whole_ref[r, :] = result.astype(bf16)
        return held + folded(result * result)

    total = by_chunks(s_ref.shape[0], step, jnp.zeros((8, s_ref.shape[1]), f32))
    squares_ref[pl.ds(pl.program_id(0), 1), :] = jnp.sum(total, axis=0, keepdims=True)


def result_half(pos, s, r, after):
    half, width_d = s.shape
    steps = half // GROUP
    blk = pl.BlockSpec((GROUP, width_d), lambda i, c: (i, 0))
    own = pl.BlockSpec((GROUP, width_d), lambda i, c: (c[0] * steps + i, 0))
    return call(
        result_body,
        [
            (sds((half, width_d), bf16), blk),
            (sds((2 * half, width_d), bf16), own),
            (sds((steps, width_d), f32), pl.BlockSpec((steps, width_d), lambda i, c: (0, 0))),
        ],
        [blk] * 3,
        (pos, s, r, after),
        "result",
        grid=(steps,),
        prefetch=1,
        flops=6 * half * width_d,
        nbytes=5e6,
    )


def gains_body(
    pos_ref, clip_ref, frames_ref, one_keep, one_send, src_keep, src_send, lat_ref, src_ref,
    self_ref, mlp_ref, squares_ref, out_ref, *, one_steps, src_steps, blocks, sets, copies, clips,
):
    i = pl.program_id(0)

    @pl.when(i == 0)
    def _():
        width_d = out_ref.shape[1]
        share = jnp.zeros((1, 1), f32)
        for b in range(blocks // 2):
            total = jnp.sum(squares_ref[b : b + 1, :], axis=1, keepdims=True)
            frames = frames_ref[clip_of(clip_ref, pos_ref, b, blocks, sets, True)].astype(f32)
            norm = jnp.sqrt(total / (GROUP * width_d) + 1e-06)
            share = share + norm / (jnp.broadcast_to(frames, (1, 1)) * (GROUPS_FRAME * clips))
        out_ref[0:2, :] = jnp.zeros((2, width_d), f32)
        out_ref[2:3, :] = self_ref[...] * copies
        out_ref[3:4, :] = mlp_ref[...] * copies
        out_ref[4:8, :] = jnp.broadcast_to(share * copies, (4, width_d))

    def add(row, v_ref, keep_ref, send_ref, kept):
        def step(r, held):
            n = jnp.where(kept, keep_ref[r, :].astype(f32), send_ref[r, :].astype(f32))
            return held + folded(n * centre(v_ref[r, :].astype(f32))[0])

        total = by_chunks(v_ref.shape[0], step, jnp.zeros((8, v_ref.shape[1]), f32))
        out_ref[row : row + 1, :] = out_ref[row : row + 1, :] + jnp.sum(total, axis=0, keepdims=True)

    pl.when(i < one_steps)(lambda: add(1, lat_ref, one_keep, one_send, i < one_steps // 2))
    pl.when(i >= one_steps)(lambda: add(0, src_ref, src_keep, src_send, i - one_steps < src_steps // 2))


def gains(pos, clips, frames, one_keep, one_send, src_keep, src_send, latents, sources, self_gain, mlp_gain,
          squares, copies, ties):
    half, width_d = one_keep.shape
    count = sources.shape[0]
    blk = 256
    one_steps, src_steps = 2 * half // blk, count // blk
    blocks = 2 * half // GROUP
    sets = clips.shape[0] // GROUPS_FRAME // blocks
    clamp = lambda v, top: jnp.minimum(jnp.maximum(v, 0), top)
    spec = lambda f: pl.BlockSpec((blk, width_d), lambda i, *c: (f(i, c[0]), 0))
    fixed = lambda n: pl.BlockSpec((n, width_d), lambda i, *c: (0, 0))
    turn = lambda i, c, steps: (clamp(i, steps - 1) + c[0] * (steps // 2)) % steps
    return call(
        functools.partial(
            gains_body, one_steps=one_steps, src_steps=src_steps, blocks=blocks, sets=sets, copies=copies,
            clips=frames.shape[0],
        ),
        [(sds((8, width_d), f32), fixed(8))],
        [
            spec(lambda i, c: clamp(i, one_steps // 2 - 1)),
            spec(lambda i, c: clamp(i - one_steps // 2, one_steps // 2 - 1)),
            spec(lambda i, c: clamp(i - one_steps, src_steps // 2 - 1)),
            spec(lambda i, c: clamp(i - one_steps - src_steps // 2, src_steps // 2 - 1)),
            spec(lambda i, c: turn(i, c, one_steps)),
            spec(lambda i, c: turn(i - one_steps, c, src_steps)),
            fixed(1), fixed(1), fixed(blocks // 2),
        ],
        (pos, clips, frames, one_keep, one_send, src_keep, src_send, latents, sources, self_gain, mlp_gain, squares),
        "gains",
        grid=(one_steps + src_steps,),
        prefetch=3,
        flops=20 * (2 * half + count) * width_d,
        nbytes=4 * (2 * half + count) * width_d,
        ties=ties,
    )[0]


def feature_grads_body(pos_ref, *refs, items, split, blk):
    given = sum(a + b for a, b in items)
    outs = refs[given:]
    at, column = 0, 0
    for lefts, rights in items:
        total, row = None, 0
        for k in range(lefts):
            left = refs[at + k]
            rows = left.shape[0]
            if rights == 1:
                right = refs[at + lefts][row : row + rows, :]
            else:
                right = refs[at + lefts + k][...]
            term = dot_ta(left[...], right)
            total = term if total is None else total + term
            row += rows
        at += lefts + rights
        cols = slice(column, column + total.shape[1])
        column += total.shape[1]
        total = total.astype(bf16)
        for j in range(blk // 128):
            part = total[j * 128 : (j + 1) * 128]
            if split:
                mine = (pos_ref[1] + j) % 2 == 0

                @pl.when(mine)
                def _():
                    outs[0][j // 2, :, cols] = part

                @pl.when(jnp.logical_not(mine))
                def _():
                    outs[1][j // 2, :, cols] = part
            else:
                outs[0][j, :, cols] = part


def feature_grads(pos, items, split, ties=()):
    arrays, specs, counts, columns, flops = [], [], [], 0, 0
    features = items[0][0][0].shape[1]
    blk = 512
    for lefts, rights in items:
        counts.append((len(lefts), len(rights)))
        for v in lefts:
            arrays.append(v)
            specs.append(pl.BlockSpec((v.shape[0], blk), lambda i, c: (0, i)))
            flops += 2 * v.shape[0] * v.shape[1] * rights[0].shape[1]
        for v in rights:
            arrays.append(v)
            specs.append(pl.BlockSpec(v.shape, lambda i, c: (0, 0)))
        columns += rights[0].shape[1]
    steps = features // blk
    sets = features // 256 if split else features // 128
    count = 2 if split else 1
    outs = [
        (sds((sets, 128, columns), bf16), pl.BlockSpec((sets // steps, 128, columns), lambda i, c: (i, 0, 0)))
    ] * count
    return call(
        functools.partial(feature_grads_body, items=tuple(counts), split=split, blk=blk),
        outs,
        specs,
        (pos, *arrays),
        "feature_grads",
        grid=(steps,),
        prefetch=1,
        flops=flops,
        nbytes=2 * features * columns + sum(2 * v.size for v in arrays),
        ties=ties,
    )


def middle_body(pos_ref, keep_ref, got_ref, own_ref, one_ref, two_ref, three_ref):
    z = pos_ref[1] // 2
    own_ref[...] = keep_ref[z].astype(f32) + got_ref[z].astype(f32)
    for d, ref in ((1, one_ref), (2, two_ref), (3, three_ref)):
        at = (z + d) % 4
        ref[...] = (keep_ref[at].astype(f32) + got_ref[at].astype(f32)).astype(bf16)


def ended_body(own_ref, one_ref, two_ref, three_ref, *outs, turned):
    total = own_ref[...] + (one_ref[...].astype(f32) + (two_ref[...].astype(f32) + three_ref[...].astype(f32)))
    width = total.shape[1] // len(outs)
    for k, ref in enumerate(outs):
        part = total[:, k * width : (k + 1) * width]
        ref[...] = part.T if k in turned else part


def scatter_middle(pos, keep, got, ties=()):
    blk = keep.shape[1:]
    return call(
        middle_body,
        [(sds(blk, f32), VMEM)] + [(sds(blk, bf16), VMEM)] * 3,
        [SMEM, VMEM, VMEM],
        (pos, keep, got),
        "middle",
        nbytes=4 * keep.size,
        ties=ties,
    )


def scatter_end(own, moved, parts, turned, ties=()):
    blk = own.shape
    width = blk[1] // parts
    return call(
        functools.partial(ended_body, turned=turned),
        [(sds((width, blk[0]) if k in turned else (blk[0], width), f32), VMEM) for k in range(parts)],
        [VMEM] * 4,
        (own, *moved),
        "ended",
        nbytes=10 * blk[0] * blk[1],
        ties=ties,
    )


def flip_x(v):
    return lax.ppermute(v, "seq", xor_pairs(1, 8))


def spread_z(pieces):
    return [lax.ppermute(pieces[d - 1], "seq", ring_pairs(d)) for d in (1, 2, 3)]


def scatter_whole(pos, items, parts, turned, ties):
    whole = feature_grads(pos, items, False, ties)[0]
    whole = whole.reshape(-1, whole.shape[2])
    total = lax.psum_scatter(whole, "seq", scatter_dimension=0, tiled=True).astype(f32)
    width = total.shape[1] // parts
    pieces = [total[:, k * width : (k + 1) * width] for k in range(parts)]
    return [piece.T if k in turned else piece for k, piece in enumerate(pieces)]


def tied(values, other):
    out = lax.optimization_barrier((other, *values))
    return list(out[1:]), out[0]


def cross_back_body(
    pos_ref, mine_ref, other_ref, wo_ref, q_ref, kvp_ref, idx_ref, wq_ref, wk_ref, wv_ref,
    dq_ref, dkv_ref, one_keep_ref, one_send_ref, src_keep_ref, src_send_ref, dkvp_s, *, blocks,
):
    width = wq_ref.shape[1]
    heads = width // HEAD
    count = kvp_ref.shape[0]
    scale = HEAD ** (-0.5)
    for b in range(blocks):
        ref = mine_ref if b < blocks // 2 else other_ref
        part = (b % (blocks // 2)) * GROUP
        grad = dot_t(ref[part : part + GROUP, :], wo_ref[...]).astype(bf16)
        for h in range(heads):
            cols = slice(h * HEAD, (h + 1) * HEAD)
            vcols = slice(width + h * HEAD, width + (h + 1) * HEAD)
            q = q_ref[b * GROUP : (b + 1) * GROUP, cols]
            k = kvp_ref[b * SRC : (b + 1) * SRC, cols]
            v = kvp_ref[b * SRC : (b + 1) * SRC, vcols]
            do = grad[:, cols]
            s = dot_t(q, k) * (scale * LOG2E)
            p = jnp.exp2(s - jnp.max(s, axis=-1, keepdims=True))
            p = p / jnp.sum(p, axis=-1, keepdims=True)
            dp = dot_t(do, v)
            delta = jnp.sum(p * dp, axis=-1, keepdims=True)
            ds = (p * (dp - delta) * scale).astype(bf16)
            dq_ref[b * GROUP : (b + 1) * GROUP, cols] = dot(ds, k).astype(bf16)
            dkvp_s[b * SRC : (b + 1) * SRC, cols] = dot_ta(ds, q).astype(bf16)
            dkvp_s[b * SRC : (b + 1) * SRC, vcols] = dot_ta(p.astype(bf16), do).astype(bf16)
        one = dot_t(dq_ref[b * GROUP : (b + 1) * GROUP, :], wq_ref[...]).astype(bf16)
        if b < blocks // 2:
            one_keep_ref[part : part + GROUP, :] = one
        else:
            one_send_ref[part : part + GROUP, :] = one
    half = count // 2
    blk = 256
    row = jnp.concatenate([index_row(idx_ref, pos_ref, b, blocks, count) for b in range(blocks)], axis=1)
    for n in range(count // blk):
        r0 = pl.multiple_of(
            (pos_ref[0] if n * blk < half else 1 - pos_ref[0]) * half + (n * blk) % half, blk
        )
        wanted = lax.broadcasted_iota(jnp.int32, (blk, count), 0).astype(f32) + r0.astype(f32)
        picks = jnp.where(row == wanted, 1.0, 0.0).astype(bf16)
        dkv = dot(picks, dkvp_s[...]).astype(bf16)
        dkv_ref[pl.ds(r0, blk), :] = dkv
        total = (dot_t(dkv[:, 0:width], wk_ref[...]) + dot_t(dkv[:, width:], wv_ref[...])).astype(bf16)
        at = (n * blk) % half
        if n * blk < half:
            src_keep_ref[at : at + blk, :] = total
        else:
            src_send_ref[at : at + blk, :] = total


def cross_back(pos, mine, other, wo, q, kvp, idx, wq, wk, wv, ties):
    rows, width = q.shape
    width_d = wq.shape[0]
    count = kvp.shape[0]
    blocks = rows // GROUP
    return call(
        functools.partial(cross_back_body, blocks=blocks),
        [
            (sds((rows, width), bf16), VMEM),
            (sds((count, 2 * width), bf16), VMEM),
            (sds((rows // 2, width_d), bf16), VMEM),
            (sds((rows // 2, width_d), bf16), VMEM),
            (sds((count // 2, width_d), bf16), VMEM),
            (sds((count // 2, width_d), bf16), VMEM),
        ],
        [SMEM] + [VMEM] * 9,
        (pos, mine, other, wo, q, kvp, idx, wq, wk, wv),
        "cross_back",
        ties=ties,
        scratch=[pltpu.VMEM((count, 2 * width), bf16)],
        flops=4e9,
        nbytes=12e6,
    )


def xor_pairs(bit, size):
    return [(i, i ^ bit) for i in range(size)]


def ring_pairs(d):
    return [(s, ((s // 2 + d) % 4) * 2 + s % 2) for s in range(8)]


def tensor_swap(x, bit):
    return lax.ppermute(x, "tensor", xor_pairs(bit, lax.axis_size("tensor")))


def seq_gather(x):
    size = lax.axis_size("seq")
    if size == 8:
        move = lambda v, pairs: lax.ppermute(v, "seq", pairs)
        flip = xor_pairs(1, 8)
        beside = move(x, flip)
        up = move(x, ring_pairs(1))
        down = move(x, ring_pairs(-1))
        far = move(up, ring_pairs(1))
        up_beside = move(up, flip)
        down_beside = move(beside, ring_pairs(-1))
        far_beside = move(far, flip)
        return [x, beside, up, down, far, up_beside, down_beside, far_beside]
    return gather_whole(x)


def gather_whole(x):
    return [lax.all_gather(x, "seq", axis=0, tiled=True)]


def gather_entries(size, rows, sets):
    if size == 8:
        return tuple((k, 0, 0, k) for k in range(8))
    return whole_entries(size, rows, sets)


def whole_entries(size, rows, sets):
    return tuple((0, s * rows, s % sets, s // sets) for s in range(size))


def half_sum(keep, send):
    size = lax.axis_size("tensor")
    got = tensor_swap(send, 1)
    own = (keep.astype(f32) + got.astype(f32)).astype(bf16)
    bit = 2
    while True:
        other = tensor_swap(own, bit)
        if bit * 2 >= size:
            return own, other
        own = (own.astype(f32) + other.astype(f32)).astype(bf16)
        bit *= 2


def tensor_pieces(keep, send):
    size = lax.axis_size("tensor")
    return [keep if k == 0 else tensor_swap(send if k % 2 else keep, k) for k in range(size)]


def weight_far(weight):
    pieces = {0: weight}
    bit = lax.axis_size("tensor") // 2
    while bit >= 2:
        pieces.update({k + bit: tensor_swap(v, bit) for k, v in list(pieces.items())})
        bit //= 2
    return pieces


def weight_pieces(pieces):
    pieces = dict(pieces)
    pieces.update({k + 1: tensor_swap(v, 1) for k, v in list(pieces.items())})
    return [pieces[k] for k in range(len(pieces))]


def tie_all(pieces, other):
    keys = sorted(pieces)
    tied = lax.optimization_barrier((other, *[pieces[k] for k in keys]))
    return dict(zip(keys, tied[1:])), tied[0]


def sum_everywhere(v):
    for axis in ("tensor", "seq"):
        bit = 1
        while bit < lax.axis_size(axis):
            v = v + lax.ppermute(v, axis, xor_pairs(bit, lax.axis_size(axis)))
            bit *= 2
    return v


def local(
    latents, sources, source_index, block_clip, clip_frames, norm_src, norm_cross, norm_self, norm_mlp,
    cross_q, cross_k, cross_v, cross_o, self_q, self_k, self_v, self_o, mlp_in, mlp_out, out_grad,
):
    rows, width_d = latents.shape
    blocks = rows // GROUP
    width = cross_q.shape[1]
    units = mlp_in.shape[1]
    tensor_size, seq_size = lax.axis_size("tensor"), lax.axis_size("seq")
    core = lax.axis_index("tensor") % 2
    pos = jnp.stack((core, lax.axis_index("seq"), lax.axis_index("tensor"))).astype(jnp.int32)
    sets = block_clip.shape[0] // GROUPS_FRAME // blocks
    gain = lambda g: g.reshape(1, width_d)
    kv_entries = gather_entries(seq_size, rows, sets)
    out_entries = gather_entries(seq_size, rows + 2 * EXTRA, sets)

    cross_o_far = weight_far(cross_o)
    normed_one, normed_src, cross_query, cross_kv, mixed_keep, mixed_send = cross_forward(
        pos, source_index, latents, sources, gain(norm_cross), gain(norm_src), cross_q, cross_k, cross_v
    )
    cross_o_far, mixed_keep = tie_all(cross_o_far, mixed_keep)
    after_cross, two_mine = project(
        pos, tensor_pieces(mixed_keep, mixed_send), weight_pieces(cross_o_far), latents, gain(norm_self), True
    )
    two_other = tensor_swap(two_mine, 1)
    query, key_value = qkv(two_mine, two_other, self_q, self_k, self_v)
    kv_pieces = seq_gather(key_value)
    self_o_tied, two_mine = tie_all({0: self_o}, two_mine)
    self_o_all = weight_pieces(weight_far(self_o_tied[0]))
    out_rel, act_grad = act_back(pos, out_grad, mlp_out)
    split = seq_size == 8
    query_pieces = seq_gather(query)
    self_keep, self_send, lse_rows, lse_columns = attend(
        pos, block_clip, query, kv_pieces, kv_entries, (act_grad, *self_o_all[1:], *query_pieces[2:4])
    )
    after_self, three_mine = project(
        pos, tensor_pieces(self_keep, self_send), self_o_all, after_cross, gain(norm_mlp), False,
        (query_pieces[1], query_pieces[4]) if split else (),
    )
    three_other = tensor_swap(three_mine, 1)
    activated, hidden_grad, three_keep, three_send = mlp(three_mine, three_other, mlp_in, act_grad)

    three_sum, three_got = half_sum(three_keep, three_send)
    in_items = (((three_mine, three_other), (hidden_grad,)),)
    out_items = (((out_rel,), (activated,)),)
    early = ()
    if split:
        in_keep, in_send = feature_grads(pos, in_items, True, (three_sum,))
        early = (in_keep, *query_pieces[5:])
    after_self_grad, self_branch, mlp_gain = norm_back(
        three_sum, three_got, after_self, gain(norm_mlp), out_rel, early
    )
    self_branch_other = tensor_swap(self_branch, 1)

    out_more, delta_columns = out_back(self_branch, self_branch_other, self_o, self_keep, self_send, lse_rows)
    if split:
        in_got = flip_x(in_send)
    out_pieces = seq_gather(out_more)
    self_query_grad = query_back(
        pos, block_clip, query, out_more, lse_columns, delta_columns, kv_pieces, kv_entries
    )
    begun = tuple(out_pieces[1:4]) if split else (out_more,)
    down_keep, down_send = mlp_down(activated, mlp_out, begun)
    result_sum, result_got = half_sum(down_keep, down_send)
    output_half, output_whole, squares = result_half(pos, result_sum, result_got, after_self)
    output = place_other(pos, output_whole, tensor_swap(output_half, 1))
    early = ()
    if split:
        out_keep, out_send = feature_grads(pos, out_items, True, begun)
        in_own, *in_parts = scatter_middle(pos, in_keep, in_got)
        (*in_parts, out_send), out_pieces[-1] = tied([*in_parts, out_send], out_pieces[-1])
        out_got = flip_x(out_send)
        in_moved = spread_z(in_parts)
        early = (squares,)
    self_grads, two_keep, two_send = key_back(
        pos, block_clip, key_value, self_query_grad, self_q, self_k, self_v,
        query_pieces, kv_entries, out_pieces, out_entries, early,
    )
    two_sum, two_got = half_sum(two_keep, two_send)
    self_items = (
        ((two_mine, two_other), (self_grads,)),
        ((self_branch, self_branch_other), (self_keep, self_send)),
    )
    early = ()
    if split:
        self_wkeep, self_wsend = feature_grads(pos, self_items, True, (two_sum,))
        early = (self_wkeep, out_got, *in_moved)
    after_cross_grad, cross_branch, self_gain = norm_back(
        two_sum, two_got, after_cross, gain(norm_self), after_self_grad, early
    )
    cross_branch_other = tensor_swap(cross_branch, 1)

    cross_query_grad, cross_kv_grad, one_keep, one_send, src_keep, src_send = cross_back(
        pos, cross_branch, cross_branch_other, cross_o, cross_query, cross_kv, source_index,
        cross_q, cross_k, cross_v, (output,),
    )
    src_sum, src_got = half_sum(src_keep, src_send)
    one_sum, one_got = half_sum(one_keep, one_send)
    cross_items = (
        ((normed_one,), (cross_query_grad,)),
        ((normed_src,), (cross_kv_grad,)),
        ((cross_branch, cross_branch_other), (mixed_keep, mixed_send)),
    )
    early = ()
    if split:
        (self_wsend,), src_sum = tied([self_wsend], src_sum)
        self_wgot = flip_x(self_wsend)
        out_own, *out_parts = scatter_middle(pos, out_keep, out_got, (one_sum, src_sum))
        out_moved = spread_z(out_parts)
        cross_wkeep, cross_wsend = feature_grads(pos, cross_items, True, (src_sum, one_sum, out_own))
        (cross_wsend,), self_wgot = tied([cross_wsend], self_wgot)
        cross_wgot = flip_x(cross_wsend)
        self_own, *self_parts = scatter_middle(pos, self_wkeep, self_wgot, (cross_wkeep,))
        self_moved = spread_z(self_parts)
        early = (cross_wkeep, *out_moved)
    small = gains(
        pos, block_clip, clip_frames, one_keep, one_send, src_keep, src_send, latents, sources,
        self_gain, mlp_gain, squares, 2.0 / tensor_size, (src_sum, one_sum, *early[0:1]),
    )
    early = (*early, small)
    src_half, src_whole = final_norm(pos, src_sum, src_got, sources, gain(norm_src), None, early)
    lat_half, lat_whole = final_norm(pos, one_sum, one_got, latents, gain(norm_cross), after_cross_grad, early)
    (small,), lat_half = tied([small], lat_half)
    small = sum_everywhere(small)
    sources_grad = place_other(pos, src_whole, tensor_swap(src_half, 1))
    latents_grad = place_other(pos, lat_whole, tensor_swap(lat_half, 1))
    if split:
        cross_own, *cross_parts = scatter_middle(pos, cross_wkeep, cross_wgot, self_moved)
        cross_outs = scatter_end(cross_own, spread_z(cross_parts), 4, (3,))
        self_outs = scatter_end(self_own, self_moved, 4, (3,))
        mlp_outs = [
            scatter_end(in_own, in_moved, 1, ())[0],
            scatter_end(out_own, out_moved, 1, (0,))[0],
        ]
    else:
        cross_outs = scatter_whole(pos, cross_items, 4, (3,), ())
        self_outs = scatter_whole(pos, self_items, 4, (3,), ())
        mlp_outs = scatter_whole(pos, in_items, 1, (), ()) + scatter_whole(pos, out_items, 1, (0,), ())
    return (
        output, latents_grad, sources_grad, small[0], small[1], small[2], small[3],
        *cross_outs, *self_outs, *mlp_outs, small[4, 0],
    )


def solution(mesh):
    in_specs = (
        P("seq", None), P("seq", None), P("seq", None), P(), P(), P(), P(), P(), P(),
        P(None, "tensor"), P(None, "tensor"), P(None, "tensor"), P("tensor", None),
        P(None, "tensor"), P(None, "tensor"), P(None, "tensor"), P("tensor", None),
        P(None, "tensor"), P("tensor", None), P("seq", None),
    )
    out_specs = (
        P("seq", None), P("seq", None), P("seq", None), P(), P(), P(), P(),
        P("seq", "tensor"), P("seq", "tensor"), P("seq", "tensor"), P("tensor", "seq"),
        P("seq", "tensor"), P("seq", "tensor"), P("seq", "tensor"), P("tensor", "seq"),
        P("seq", "tensor"), P("tensor", "seq"), P(),
    )
    return jax.shard_map(local, mesh=mesh, in_specs=in_specs, out_specs=out_specs, check_vma=False)
```

time: 463 us -> 350 us (0.76)
  local copies, waits for them, and re-layouts: 62.4 us -> 3.39 us
  other arithmetic: 37.7 us -> 1.77 us
  matrix products: 16.2 us -> 0 us
  starting transfers between devices: 72.4 us -> 80.1 us
  Pallas kernels: 98.5 us -> 93.8 us
    unnamed x147 -> x58, local copies, waits for them, and re-layouts: 30.3 us -> 2.26 us
    ppermute x29, waiting for transfers between devices: 45.5 us -> 24.5 us  [tensor_swap(): return lax.ppermute(x, 'tensor', xor_pairs(bit, lax.axis_size('tensor')))]
    dot_general x9 -> x0, matrix products: 16.2 us -> none  [the longest x7 11 us: dot_ta(): lax.dot_general(a, b, (((0,), (0,)), ((), ())), preferred_element_type=f32)]
    dynamic_slice x7 -> x0, local copies, waits for them, and re-layouts: 16 us -> none  [the longest x1 11.3 us: scatter_rows(): keep = lax.dynamic_index_in_dim(view, x, 1, keepdims=False)]
    ppermute x16, starting transfers between devices: 18.4 us -> 33.6 us  [the longest x12 27 us: spread_z(): lax.ppermute(pieces[d - 1], 'seq', ring_pairs(d))]
    select_n x8 -> x0, other arithmetic: 11.3 us -> none  [the longest x3 9.92 us: in_place(): jnp.where(core_index == 0, jnp.concatenate((mine, other)), jnp.concatenat...]
    add x5 -> x0, other arithmetic: 9.31 us -> none  [the longest x2 4.69 us: scatter_rows(): keep.astype(f32) + lax.ppermute(send, 'seq', xor_pairs(1, 8)).astype(f32)]
    ppermute x5, waiting for transfers between devices: 0.36 us -> 9.35 us  [sum_everywhere(): v = v + lax.ppermute(v, axis, xor_pairs(bit, lax.axis_size(axis)))]
  transfers between devices with their start and end apart: 71 -> 71, of which waited for: 22 -> 39; matrix products, arithmetic and copies ran while one was open for 23% -> 1% of each run, Pallas kernels for 17% -> 18%
where the time goes in v2:
time: 350 us; the launch traced here: 347 us
  waiting for transfers between devices  167 us (48%)
  Pallas kernels  93.8 us (27%)
  starting transfers between devices  80.1 us (23%)
    pallas_call x33, Pallas kernels, call(): pl.pallas_call(run, out_shape=[shape for shape, ignored in outs], grid_sp...  93.8 us
    ppermute x21, waiting for transfers between devices, seq_gather(): move = lambda v, pairs: lax.ppermute(v, 'seq', pairs)  82.9 us
    ppermute x12, waiting for transfers between devices, spread_z(): lax.ppermute(pieces[d - 1], 'seq', ring_pairs(d))  32.9 us
    ppermute x12, starting transfers between devices, spread_z(): lax.ppermute(pieces[d - 1], 'seq', ring_pairs(d))  27 us
    ppermute x21, starting transfers between devices, seq_gather(): move = lambda v, pairs: lax.ppermute(v, 'seq', pairs)  26.4 us
    ppermute x29, waiting for transfers between devices, tensor_swap(): return lax.ppermute(x, 'tensor', xor_pairs(bit, lax.axis_size('tensor')))  24.5 us
    ppermute x4, waiting for transfers between devices, flip_x(): return lax.ppermute(v, 'seq', xor_pairs(1, 8))  17 us
    ppermute x29, starting transfers between devices, tensor_swap(): return lax.ppermute(x, 'tensor', xor_pairs(bit, lax.axis_size('tensor')))  15.3 us
  transfers between devices with their start and end apart: 71, of which 39 were waited for; matrix products, arithmetic and copies ran while one was open for 1% of the time, Pallas kernels for 18%

profile of v2, /device:TPU:0, one launch (start us, length us, event | category | flops | bytes accessed | tf_op | source)
XLA Modules:
  0.0 347.0 jit_solution(4292073246562425480)
XLA Ops:
  4.3 9.8 %cross_forward.1 = (bf16[512,1024]{1,0:T(8,128)(2,1)}, bf16[1024,1024]{1,0:T(8,128)(2,1)}, bf16[512,256]{1,0:T(8,128)(2,1)}, bf16[1024,512]{1,0:T(8,128)(2,1)}, ...) custom-call(s32[3]{0:T(128)} %pad_add_fusion.refs_0_, s32[4,256]{1,0:T(4,128)} %refs_6_.5, bf16[512,1024]{1,0:T(8,128)(2,1)} %refs_3_.8, ...), custom_call_target="tpu_custom_call" | custom-call | flops 4000000000 | bytes 12000000 | tf_op jit(solution)/shard_map/cross_forward/pallas_call | solution.py:93
  35.7 11.2 %collective-permute-done.8.refs_5_.refs_8_ = bf16[512,512]{1,0:T(8,128)(2,1)S(1)} collective-permute-done((bf16[512,512]{1,0:T(8,128)(2,1)S(1)}, bf16[512,512]{1,0:T(8,128)(2,1)S(1)}, u32[]{:S(2)}, u32[]{:S(2)}) %collective-permute-start.8) | collective-permute-done | bytes 524320 | tf_op jit(solution)/shard_map/ppermute | solution.py:1149
  46.9 3.8 %collective-permute-start.18 = (bf16[512,256]{1,0:T(8,128)(2,1)S(1)}, bf16[512,256]{1,0:T(8,128)(2,1)S(1)}, u32[]{:S(2)}, u32[]{:S(2)}) collective-permute-start(bf16[512,256]{1,0:T(8,128)(2,1)S(1)} %get-tuple-element.120.refs_2_.refs_7_), channel_id=1, source_target_pairs={{0,24},{4,28},{8,0},{12,4},{16,8},{20,12},{24,16},{28,20},{1,25},{... | collective-permute-start | bytes 786440 | tf_op jit(solution)/shard_map/ppermute | solution.py:1149
  50.8 3.8 %collective-permute-start.9 = (bf16[512,512]{1,0:T(8,128)(2,1)S(1)}, bf16[512,512]{1,0:T(8,128)(2,1)S(1)}, u32[]{:S(2)}, u32[]{:S(2)}) collective-permute-start(bf16[512,512]{1,0:T(8,128)(2,1)S(1)} %get-tuple-element.121.refs_3_.refs_6_.refs_2_), channel_id=1, source_target_pairs={{0,24},{4,28},{8,0},{12,4},{16,8},{20,12},{24,16},{28,20},{1,25},{... | collective-permute-start | bytes 1572872 | tf_op jit(solution)/shard_map/ppermute | solution.py:1149
  54.6 13.7 %collective-permute-done.18.refs_16_.refs_10_ = bf16[512,256]{1,0:T(8,128)(2,1)S(1)} collective-permute-done((bf16[512,256]{1,0:T(8,128)(2,1)S(1)}, bf16[512,256]{1,0:T(8,128)(2,1)S(1)}, u32[]{:S(2)}, u32[]{:S(2)}) %collective-permute-start.18) | collective-permute-done | bytes 262176 | tf_op jit(solution)/shard_map/ppermute | solution.py:1149
  68.3 6.6 %collective-permute-done.17.refs_15_.refs_9_ = bf16[512,256]{1,0:T(8,128)(2,1)S(1)} collective-permute-done((bf16[512,256]{1,0:T(8,128)(2,1)S(1)}, bf16[512,256]{1,0:T(8,128)(2,1)S(1)}, u32[]{:S(2)}, u32[]{:S(2)}) %collective-permute-start.17) | collective-permute-done | bytes 262176 | tf_op jit(solution)/shard_map/ppermute | solution.py:1149
  76.9 3.9 %act_back.1 = (bf16[512,1024]{1,0:T(8,128)(2,1)S(1)}, f32[512,1024]{1,0:T(8,128)S(1)}) custom-call(s32[3]{0:T(128)S(1)} %copy-done.11, bf16[512,1024]{1,0:T(8,128)(2,1)S(1)} %copy-done.19, bf16[1024,1024]{1,0:T(8,128)(2,1)S(1)} %copy-done.3), custom_call_target="tpu_custom_call" | custom-call | flops 1073741824 | bytes 6000000 | tf_op jit(solution)/shard_map/act_back/pallas_call | solution.py:93
  85.4 4.3 %collective-permute-done.11.refs_8_.refs_11_ = bf16[512,512]{1,0:T(8,128)(2,1)S(1)} collective-permute-done((bf16[512,512]{1,0:T(8,128)(2,1)S(1)}, bf16[512,512]{1,0:T(8,128)(2,1)S(1)}, u32[]{:S(2)}, u32[]{:S(2)}) %collective-permute-start.11) | collective-permute-done | bytes 524320 | tf_op jit(solution)/shard_map/ppermute | solution.py:1149
  89.7 4.4 %collective-permute-done.12.refs_9_.refs_12_ = bf16[512,512]{1,0:T(8,128)(2,1)S(1)} collective-permute-done((bf16[512,512]{1,0:T(8,128)(2,1)S(1)}, bf16[512,512]{1,0:T(8,128)(2,1)S(1)}, u32[]{:S(2)}, u32[]{:S(2)}) %collective-permute-start.12) | collective-permute-done | bytes 524320 | tf_op jit(solution)/shard_map/ppermute | solution.py:1149
  94.1 6.1 %collective-permute-done.13.refs_10_.refs_13_ = bf16[512,512]{1,0:T(8,128)(2,1)S(1)} collective-permute-done((bf16[512,512]{1,0:T(8,128)(2,1)S(1)}, bf16[512,512]{1,0:T(8,128)(2,1)S(1)}, u32[]{:S(2)}, u32[]{:S(2)}) %collective-permute-start.13) | collective-permute-done | bytes 524320 | tf_op jit(solution)/shard_map/ppermute | solution.py:1149
  100.1 7.9 %attend.1 = (bf16[256,256]{1,0:T(8,128)(2,1)S(1)}, bf16[256,256]{1,0:T(8,128)(2,1)S(1)}, bf16[16,256]{1,0:T(8,128)(2,1)S(1)}, f32[2,512,128]{2,1,0:T(8,128)S(1)}) custom-call(s32[3]{0:T(128)S(1)} %copy-done.11, s32[32]{0:T(128)S(1)} %copy-done.16, bf16[512,256]{1,0:T(8,128)(2,1)S(1)} %get-tuple-element.120.refs_2_.refs_7_, ...), custom_call_target="tpu_custom_call" | custom-call | flops 2000000000 | bytes 7000000 | tf_op jit(solution)/shard_map/attend/pallas_call | solution.py:93
  110.3 3.9 %collective-permute-done.20.refs_3_ = bf16[256,256]{1,0:T(8,128)(2,1)S(1)} collective-permute-done((bf16[256,256]{1,0:T(8,128)(2,1)S(1)}, bf16[256,256]{1,0:T(8,128)(2,1)S(1)}, u32[]{:S(2)}, u32[]{:S(2)}) %collective-permute-start.20) | collective-permute-done | bytes 131104 | tf_op jit(solution)/shard_map/ppermute | solution.py:1143
  119.1 6.0 %mlp.1 = (bf16[512,1024]{1,0:T(8,128)(2,1)S(1)}, bf16[512,1024]{1,0:T(8,128)(2,1)S(1)}, bf16[256,1024]{1,0:T(8,128)(2,1)S(1)}, bf16[256,1024]{1,0:T(8,128)(2,1)S(1)}) custom-call(bf16[256,1024]{1,0:T(8,128)(2,1)S(1)} %get-tuple-element.127.refs_0_.refs_1_, bf16[256,1024]{1,0:T(8,128)(2,1)S(1)} %collective-permute-done.24.refs_1_.refs_2_, ...), custom_call_target="tpu_custom_call" | custom-call | flops 2147483648 | bytes 9000000 | tf_op jit(solution)/shard_map/mlp/pallas_call | solution.py:93
  132.8 3.8 %collective-permute-done.28.refs_7_.refs_13_ = bf16[512,256]{1,0:T(8,128)(2,1)S(1)} collective-permute-done((bf16[512,256]{1,0:T(8,128)(2,1)S(1)}, bf16[512,256]{1,0:T(8,128)(2,1)S(1)}, u32[]{:S(2)}, u32[]{:S(2)}) %collective-permute-start.28) | collective-permute-done | bytes 262176 | tf_op jit(solution)/shard_map/ppermute | solution.py:1149
  137.5 4.7 %collective-permute-done.29.refs_8_.refs_14_ = bf16[512,256]{1,0:T(8,128)(2,1)S(1)} collective-permute-done((bf16[512,256]{1,0:T(8,128)(2,1)S(1)}, bf16[512,256]{1,0:T(8,128)(2,1)S(1)}, u32[]{:S(2)}, u32[]{:S(2)}) %collective-permute-start.29) | collective-permute-done | bytes 262176 | tf_op jit(solution)/shard_map/ppermute | solution.py:1149
  149.3 6.1 %collective-permute-done.33.refs_4_.refs_5_.refs_18_ = bf16[544,256]{1,0:T(8,128)(2,1)S(1)} collective-permute-done((bf16[544,256]{1,0:T(8,128)(2,1)S(1)}, bf16[544,256]{1,0:T(8,128)(2,1)S(1)}, u32[]{:S(2)}, u32[]{:S(2)}) %collective-permute-start.33) | collective-permute-done | bytes 278560 | tf_op jit(solution)/shard_map/ppermute | solution.py:1149
  155.4 5.2 %collective-permute-done.32.refs_3_.refs_4_.refs_17_ = bf16[544,256]{1,0:T(8,128)(2,1)S(1)} collective-permute-done((bf16[544,256]{1,0:T(8,128)(2,1)S(1)}, bf16[544,256]{1,0:T(8,128)(2,1)S(1)}, u32[]{:S(2)}, u32[]{:S(2)}) %collective-permute-start.32) | collective-permute-done | bytes 278560 | tf_op jit(solution)/shard_map/ppermute | solution.py:1149
  169.8 5.8 %collective-permute-done.37.refs_19_ = bf16[544,256]{1,0:T(8,128)(2,1)S(1)} collective-permute-done((bf16[544,256]{1,0:T(8,128)(2,1)S(1)}, bf16[544,256]{1,0:T(8,128)(2,1)S(1)}, u32[]{:S(2)}, u32[]{:S(2)}) %collective-permute-start.37) | collective-permute-done | bytes 278560 | tf_op jit(solution)/shard_map/ppermute | solution.py:1149
  176.0 5.8 %query_back.1.refs_3_ = bf16[512,256]{1,0:T(8,128)(2,1)S(1)} custom-call(s32[3]{0:T(128)S(1)} %copy-done.11, s32[32]{0:T(128)S(1)} %copy-done.16, bf16[512,256]{1,0:T(8,128)(2,1)S(1)} %get-tuple-element.120.refs_2_.refs_7_, bf16[544,256]{1,0:T(8,128)(2,1)S(1)} %get-tuple-element.137.refs_3_.refs_15_, f32[2,512,128]{2,1,0:T(8,128)S(1)} %get-tuple-element.142.refs_4_, ...), custom_call_target="tpu_custom_call" | custom-call | flops 2000000000 | bytes 7000000 | tf_op jit(solution)/shard_map/query_back/pallas_call | solution.py:93
  181.8 6.8 %collective-permute-done.41.refs_2_ = bf16[4,128,1024]{2,1,0:T(8,128)(2,1)S(1)} collective-permute-done((bf16[4,128,1024]{2,1,0:T(8,128)(2,1)S(1)}, bf16[4,128,1024]{2,1,0:T(8,128)(2,1)S(1)}, u32[]{:S(2)}, u32[]{:S(2)}) %collective-permute-start.41) | collective-permute-done | bytes 1048608 | tf_op jit(solution)/shard_map/ppermute | solution.py:1036
  191.9 8.3 %collective-permute-done.40.refs_22_ = bf16[544,256]{1,0:T(8,128)(2,1)S(1)} collective-permute-done((bf16[544,256]{1,0:T(8,128)(2,1)S(1)}, bf16[544,256]{1,0:T(8,128)(2,1)S(1)}, u32[]{:S(2)}, u32[]{:S(2)}) %collective-permute-start.40) | collective-permute-done | bytes 278560 | tf_op jit(solution)/shard_map/ppermute | solution.py:1149
  201.7 8.5 %key_back.1 = (bf16[512,768]{1,0:T(8,128)(2,1)S(1)}, bf16[256,1024]{1,0:T(8,128)(2,1)S(1)}, bf16[256,1024]{1,0:T(8,128)(2,1)S(1)}) custom-call(s32[3]{0:T(128)S(1)} %copy-done.11, s32[32]{0:T(128)S(1)} %copy-done.16, bf16[512,512]{1,0:T(8,128)(2,1)S(1)} %get-tuple-element.121.refs_3_.refs_6_.refs_2_, bf16[512,256]{1,0:T(8,128)(2,1)S(1)} %query_back.1.refs_3_, ...), custom_call_target="tpu_custom_call" | custom-call | flops 4000000000 | bytes 9000000 | tf_op jit(solution)/shard_map/key_back/pallas_call | solution.py:93
  224.6 10.1 %collective-permute-done.46.refs_8_.refs_2_ = bf16[128,1024]{1,0:T(8,128)(2,1)S(1)} collective-permute-done((bf16[128,1024]{1,0:T(8,128)(2,1)S(1)}, bf16[128,1024]{1,0:T(8,128)(2,1)S(1)}, u32[]{:S(2)}, u32[]{:S(2)}) %collective-permute-start.46) | collective-permute-done | bytes 262176 | tf_op jit(solution)/shard_map/ppermute | solution.py:1040
  240.0 8.6 %cross_back.1 = (bf16[512,256]{1,0:T(8,128)(2,1)S(1)}, bf16[1024,512]{1,0:T(8,128)(2,1)S(1)}, bf16[256,1024]{1,0:T(8,128)(2,1)S(1)}, bf16[256,1024]{1,0:T(8,128)...) custom-call(s32[3]{0:T(128)S(1)} %copy-done.11, ...), custom_call_target="tpu_custom_call" | custom-call | flops 4000000000 | bytes 12000000 | tf_op jit(solution)/shard_map/cross_back/pallas_call | solution.py:93
  256.3 4.6 %collective-permute-start.52 = (bf16[128,1024]{1,0:T(8,128)(2,1)S(1)}, bf16[128,1024]{1,0:T(8,128)(2,1)S(1)}, u32[]{:S(2)}, u32[]{:S(2)}) collective-permute-start(bf16[128,1024]{1,0:T(8,128)(2,1)S(1)} %get-tuple-element.178), channel_id=1, source_target_pairs={{0,8},{4,12},{8,16},{12,20},{16,24},{20,28},{24,0},{28,4},{1,9},{5... | collective-permute-start | bytes 786440 | tf_op jit(solution)/shard_map/ppermute | solution.py:1040
  263.3 4.6 %feature_grads.7 = (bf16[4,128,1024]{2,1,0:T(8,128)(2,1)S(1)}, bf16[4,128,1024]{2,1,0:T(8,128)(2,1)S(1)}) custom-call(s32[3]{0:T(128)S(1)} %copy-done.11, bf16[512,1024]{1,0:T(8,128)(2,1)S(1)} %copy-done.5, bf16[512,256]{1,0:T(8,128)(2,1)S(1)} %get-tuple-element.168.refs_2_, bf16[1024,1024]{1,0:T(8,128)(2,1)S(1)} %copy-done.4, ...), custom_call_target="tpu_custom_call" | custom-call | flops 1610612736 | bytes 7864320 | tf_op jit(solution)/shard_map/feature_grads/pallas_call | solution.py:93
  267.9 9.0 %collective-permute-done.63.refs_2_ = bf16[4,128,1024]{2,1,0:T(8,128)(2,1)S(1)} collective-permute-done((bf16[4,128,1024]{2,1,0:T(8,128)(2,1)S(1)}, bf16[4,128,1024]{2,1,0:T(8,128)(2,1)S(1)}, u32[]{:S(2)}, u32[]{:S(2)}) %collective-permute-start.63) | collective-permute-done | bytes 1048608 | tf_op jit(solution)/shard_map/ppermute | solution.py:1036
  287.0 5.4 %collective-permute-start.65 = (bf16[128,1024]{1,0:T(8,128)(2,1)S(1)}, bf16[128,1024]{1,0:T(8,128)(2,1)S(1)}, u32[]{:S(2)}, u32[]{:S(2)}) collective-permute-start(bf16[128,1024]{1,0:T(8,128)(2,1)S(1)} %get-tuple-element.193), channel_id=1, source_target_pairs={{0,8},{4,12},{8,16},{12,20},{16,24},{20,28},{24,0},{28,4},{1,9},{5... | collective-permute-start | bytes 786440 | tf_op jit(solution)/shard_map/ppermute | solution.py:1040
  311.2 9.6 %collective-permute-done.66.refs_4_.refs_2_ = bf16[128,1024]{1,0:T(8,128)(2,1)S(1)} collective-permute-done((bf16[128,1024]{1,0:T(8,128)(2,1)S(1)}, bf16[128,1024]{1,0:T(8,128)(2,1)S(1)}, u32[]{:S(2)}, u32[]{:S(2)}) %collective-permute-start.66) | collective-permute-done | bytes 262176 | tf_op jit(solution)/shard_map/ppermute | solution.py:1040
  324.5 4.2 %collective-permute-start.68 = (bf16[128,1024]{1,0:T(8,128)(2,1)S(1)}, bf16[128,1024]{1,0:T(8,128)(2,1)S(1)}, u32[]{:S(2)}, u32[]{:S(2)}) collective-permute-start(bf16[128,1024]{1,0:T(8,128)(2,1)S(1)} %get-tuple-element.197), channel_id=1, source_target_pairs={{0,8},{4,12},{8,16},{12,20},{16,24},{20,28},{24,0},{28,4},{1,9},{5... | collective-permute-start | bytes 786440 | tf_op jit(solution)/shard_map/ppermute | solution.py:1040
  328.7 3.8 %collective-permute-start.70 = (bf16[128,1024]{1,0:T(8,128)(2,1)S(1)}, bf16[128,1024]{1,0:T(8,128)(2,1)S(1)}, u32[]{:S(2)}, u32[]{:S(2)}) collective-permute-start(bf16[128,1024]{1,0:T(8,128)(2,1)S(1)} %get-tuple-element.199), channel_id=1, source_target_pairs={{0,24},{4,28},{8,0},{12,4},{16,8},{20,12},{24,16},{28,20},{1,25},{... | collective-permute-start | bytes 786440 | tf_op jit(solution)/shard_map/ppermute | solution.py:1040
  339.3 6.8 %collective-permute-done.69.refs_2_ = bf16[128,1024]{1,0:T(8,128)(2,1)S(1)} collective-permute-done((bf16[128,1024]{1,0:T(8,128)(2,1)S(1)}, bf16[128,1024]{1,0:T(8,128)(2,1)S(1)}, u32[]{:S(2)}, u32[]{:S(2)}) %collective-permute-start.69) | collective-permute-done | bytes 262176 | tf_op jit(solution)/shard_map/ppermute | solution.py:1040
  (214 shorter events, 138.7 us)
Async XLA Ops:
  30.8 16.1 %collective-permute-start.8 = (bf16[512,512]{1,0:T(8,128)(2,1)S(1)}, bf16[512,512]{1,0:T(8,128)(2,1)S(1)}, u32[]{:S(2)}, u32[]{:S(2)}) collective-permute-start(bf16[512,512]{1,0:T(8,128)(2,1)S(1)} %get-tuple-element.121.refs_3_.refs_6_.refs_2_), channel_id=1, source_target_pairs={{0,8},{4,12},{8,16},{12,20},{16,24},{20,28},{24,0},{28,4},{1,9},{5... | collective-permute-start | bytes 1572872 | tf_op jit(solution)/shard_map/ppermute | solution.py:1149
  32.7 18.1 %collective-permute-start.15 = (bf16[256,1024]{1,0:T(8,128)(2,1)S(1)}, bf16[256,1024]{1,0:T(8,128)(2,1)S(1)}, u32[]{:S(2)}, u32[]{:S(2)}) collective-permute-start(bf16[256,1024]{1,0:T(8,128)(2,1)S(1)} %copy-done.2), channel_id=1, source_target_pairs={{0,2},{1,3},{2,0},{3,1},{4,6},{5,7},{6,4},{7,5},{8,10},{9,11},{10,... | collective-permute-start | bytes 1572872 | tf_op jit(solution)/shard_map/ppermute | solution.py:1143
  34.2 16.6 %collective-permute-start.14 = (bf16[256,1024]{1,0:T(8,128)(2,1)S(1)}, bf16[256,1024]{1,0:T(8,128)(2,1)S(1)}, u32[]{:S(2)}, u32[]{:S(2)}) collective-permute-start(bf16[256,1024]{1,0:T(8,128)(2,1)S(1)} %copy-done.2), channel_id=1, source_target_pairs={{0,1},{1,0},{2,3},{3,2},{4,5},{5,4},{6,7},{7,6},{8,9},{9,8},{10,11... | collective-permute-start | bytes 1572872 | tf_op jit(solution)/shard_map/ppermute | solution.py:1143
  34.2 42.2 %collective-permute-start.7 = (bf16[512,512]{1,0:T(8,128)(2,1)S(1)}, bf16[512,512]{1,0:T(8,128)(2,1)S(1)}, u32[]{:S(2)}, u32[]{:S(2)}) collective-permute-start(bf16[512,512]{1,0:T(8,128)(2,1)S(1)} %get-tuple-element.121.refs_3_.refs_6_.refs_2_), channel_id=1, source_target_pairs={{0,4},{4,0},{8,12},{12,8},{16,20},{20,16},{24,28},{28,24},{1,5},{5... | collective-permute-start | bytes 1572872 | tf_op jit(solution)/shard_map/ppermute | solution.py:1149
  46.9 29.4 %collective-permute-start.10 = (bf16[512,512]{1,0:T(8,128)(2,1)S(1)}, bf16[512,512]{1,0:T(8,128)(2,1)S(1)}, u32[]{:S(2)}, u32[]{:S(2)}) collective-permute-start(bf16[512,512]{1,0:T(8,128)(2,1)S(1)} %collective-permute-done.8.refs_5_.refs_8_), channel_id=1, source_target_pairs={{0,8},{4,12},{8,16},{12,20},{16,24},{20,28},{24,0},{28,4},{1,9},{5... | collective-permute-start | bytes 1572872 | tf_op jit(solution)/shard_map/ppermute | solution.py:1149
  46.9 21.3 %collective-permute-start.18 = (bf16[512,256]{1,0:T(8,128)(2,1)S(1)}, bf16[512,256]{1,0:T(8,128)(2,1)S(1)}, u32[]{:S(2)}, u32[]{:S(2)}) collective-permute-start(bf16[512,256]{1,0:T(8,128)(2,1)S(1)} %get-tuple-element.120.refs_2_.refs_7_), channel_id=1, source_target_pairs={{0,24},{4,28},{8,0},{12,4},{16,8},{20,12},{24,16},{28,20},{1,25},{... | collective-permute-start | bytes 786440 | tf_op jit(solution)/shard_map/ppermute | solution.py:1149
  50.7 24.1 %collective-permute-start.17 = (bf16[512,256]{1,0:T(8,128)(2,1)S(1)}, bf16[512,256]{1,0:T(8,128)(2,1)S(1)}, u32[]{:S(2)}, u32[]{:S(2)}) collective-permute-start(bf16[512,256]{1,0:T(8,128)(2,1)S(1)} %get-tuple-element.120.refs_2_.refs_7_), channel_id=1, source_target_pairs={{0,8},{4,12},{8,16},{12,20},{16,24},{20,28},{24,0},{28,4},{1,9},{5... | collective-permute-start | bytes 786440 | tf_op jit(solution)/shard_map/ppermute | solution.py:1149
  50.8 33.5 %collective-permute-start.9 = (bf16[512,512]{1,0:T(8,128)(2,1)S(1)}, bf16[512,512]{1,0:T(8,128)(2,1)S(1)}, u32[]{:S(2)}, u32[]{:S(2)}) collective-permute-start(bf16[512,512]{1,0:T(8,128)(2,1)S(1)} %get-tuple-element.121.refs_3_.refs_6_.refs_2_), channel_id=1, source_target_pairs={{0,24},{4,28},{8,0},{12,4},{16,8},{20,12},{24,16},{28,20},{1,25},{... | collective-permute-start | bytes 1572872 | tf_op jit(solution)/shard_map/ppermute | solution.py:1149
  76.4 17.7 %collective-permute-start.12 = (bf16[512,512]{1,0:T(8,128)(2,1)S(1)}, bf16[512,512]{1,0:T(8,128)(2,1)S(1)}, u32[]{:S(2)}, u32[]{:S(2)}) collective-permute-start(bf16[512,512]{1,0:T(8,128)(2,1)S(1)} %collective-permute-done.7.refs_4_.refs_7_), channel_id=1, source_target_pairs={{0,24},{4,28},{8,0},{12,4},{16,8},{20,12},{24,16},{28,20},{1,25},{... | collective-permute-start | bytes 1572872 | tf_op jit(solution)/shard_map/ppermute | solution.py:1149
  76.4 23.8 %collective-permute-start.13 = (bf16[512,512]{1,0:T(8,128)(2,1)S(1)}, bf16[512,512]{1,0:T(8,128)(2,1)S(1)}, u32[]{:S(2)}, u32[]{:S(2)}) collective-permute-start(bf16[512,512]{1,0:T(8,128)(2,1)S(1)} %collective-permute-done.10.refs_7_.refs_10_), channel_id=1, source_target_pairs={{0,4},{4,0},{8,12},{12,8},{16,20},{20,16},{24,28},{28,24},{1,5},{5... | collective-permute-start | bytes 1572872 | tf_op jit(solution)/shard_map/ppermute | solution.py:1149
  80.8 29.4 %collective-permute-start.22 = (bf16[512,256]{1,0:T(8,128)(2,1)S(1)}, bf16[512,256]{1,0:T(8,128)(2,1)S(1)}, u32[]{:S(2)}, u32[]{:S(2)}) collective-permute-start(bf16[512,256]{1,0:T(8,128)(2,1)S(1)} %get-tuple-element.120.refs_2_.refs_7_), channel_id=1, source_target_pairs={{0,4},{4,0},{8,12},{12,8},{16,20},{20,16},{24,28},{28,24},{1,5},{5... | collective-permute-start | bytes 786440 | tf_op jit(solution)/shard_map/ppermute | solution.py:1149
  84.2 26.0 %collective-permute-start.23 = (bf16[512,256]{1,0:T(8,128)(2,1)S(1)}, bf16[512,256]{1,0:T(8,128)(2,1)S(1)}, u32[]{:S(2)}, u32[]{:S(2)}) collective-permute-start(bf16[512,256]{1,0:T(8,128)(2,1)S(1)} %collective-permute-done.17.refs_15_.refs_9_), channel_id=1, source_target_pairs={{0,8},{4,12},{8,16},{12,20},{16,24},{20,28},{24,0},{28,4},{1,9},{5... | collective-permute-start | bytes 786440 | tf_op jit(solution)/shard_map/ppermute | solution.py:1149
  162.6 26.0 %collective-permute-start.41 = (bf16[4,128,1024]{2,1,0:T(8,128)(2,1)S(1)}, bf16[4,128,1024]{2,1,0:T(8,128)(2,1)S(1)}, u32[]{:S(2)}, u32[]{:S(2)}) collective-permute-start(bf16[4,128,1024]{2,1,0:T(8,128)(2,1)S(1)} %get-tuple-element.144), channel_id=1, source_target_pairs={{0,4},{4,0},{8,12},{12,8},{16,20},{20,16},{24,28},{28,24},{1,5},{5... | collective-permute-start | bytes 3145736 | tf_op jit(solution)/shard_map/ppermute | solution.py:1036
  166.0 34.1 %collective-permute-start.35 = (bf16[256,1024]{1,0:T(8,128)(2,1)S(1)}, bf16[256,1024]{1,0:T(8,128)(2,1)S(1)}, u32[]{:S(2)}, u32[]{:S(2)}) collective-permute-start(bf16[256,1024]{1,0:T(8,128)(2,1)S(1)} %add_convert_fusion.3.refs_1_), channel_id=1, source_target_pairs={{0,2},{1,3},{2,0},{3,1},{4,6},{5,7},{6,4},{7,5},{8,10},{9,11},{10,... | collective-permute-start | bytes 1572872 | tf_op jit(solution)/shard_map/ppermute | solution.py:1143
  166.6 35.0 %collective-permute-start.38 = (bf16[544,256]{1,0:T(8,128)(2,1)S(1)}, bf16[544,256]{1,0:T(8,128)(2,1)S(1)}, u32[]{:S(2)}, u32[]{:S(2)}) collective-permute-start(bf16[544,256]{1,0:T(8,128)(2,1)S(1)} %collective-permute-done.32.refs_3_.refs_4_.refs_17_), channel_id=1, source_target_pairs={{0,4},{4,0},{8,12},{12,8},{16,20},{20,16},{24,28},{28,24},{1,5},{5... | collective-permute-start | bytes 835592 | tf_op jit(solution)/shard_map/ppermute | solution.py:1149
  167.7 34.0 %collective-permute-start.39 = (bf16[544,256]{1,0:T(8,128)(2,1)S(1)}, bf16[544,256]{1,0:T(8,128)(2,1)S(1)}, u32[]{:S(2)}, u32[]{:S(2)}) collective-permute-start(bf16[544,256]{1,0:T(8,128)(2,1)S(1)} %collective-permute-done.31.refs_2_.refs_3_.refs_16_), channel_id=1, source_target_pairs={{0,24},{4,28},{8,0},{12,4},{16,8},{20,12},{24,16},{28,20},{1,25},{... | collective-permute-start | bytes 835592 | tf_op jit(solution)/shard_map/ppermute | solution.py:1149
  175.6 24.5 %collective-permute-start.40 = (bf16[544,256]{1,0:T(8,128)(2,1)S(1)}, bf16[544,256]{1,0:T(8,128)(2,1)S(1)}, u32[]{:S(2)}, u32[]{:S(2)}) collective-permute-start(bf16[544,256]{1,0:T(8,128)(2,1)S(1)} %collective-permute-done.37.refs_19_), channel_id=1, source_target_pairs={{0,4},{4,0},{8,12},{12,8},{16,20},{20,16},{24,28},{28,24},{1,5},{5... | collective-permute-start | bytes 835592 | tf_op jit(solution)/shard_map/ppermute | solution.py:1149
  210.3 25.6 %collective-permute-start.44 = (bf16[4,128,1024]{2,1,0:T(8,128)(2,1)S(1)}, bf16[4,128,1024]{2,1,0:T(8,128)(2,1)S(1)}, u32[]{:S(2)}, u32[]{:S(2)}) collective-permute-start(bf16[4,128,1024]{2,1,0:T(8,128)(2,1)S(1)} %get-tuple-element.157), channel_id=1, source_target_pairs={{0,4},{4,0},{8,12},{12,8},{16,20},{20,16},{24,28},{28,24},{1,5},{5... | collective-permute-start | bytes 3145736 | tf_op jit(solution)/shard_map/ppermute | solution.py:1036
  212.4 23.5 %collective-permute-start.43 = (bf16[256,1024]{1,0:T(8,128)(2,1)S(1)}, bf16[256,1024]{1,0:T(8,128)(2,1)S(1)}, u32[]{:S(2)}, u32[]{:S(2)}) collective-permute-start(bf16[256,1024]{1,0:T(8,128)(2,1)S(1)} %add_convert_fusion.2.refs_8_.refs_0_), channel_id=1, source_target_pairs={{0,2},{1,3},{2,0},{3,1},{4,6},{5,7},{6,4},{7,5},{8,10},{9,11},{10,... | collective-permute-start | bytes 1572872 | tf_op jit(solution)/shard_map/ppermute | solution.py:1143
  215.2 19.5 %collective-permute-start.46 = (bf16[128,1024]{1,0:T(8,128)(2,1)S(1)}, bf16[128,1024]{1,0:T(8,128)(2,1)S(1)}, u32[]{:S(2)}, u32[]{:S(2)}) collective-permute-start(bf16[128,1024]{1,0:T(8,128)(2,1)S(1)} %get-tuple-element.159), channel_id=1, source_target_pairs={{0,16},{4,20},{8,24},{12,28},{16,0},{20,4},{24,8},{28,12},{1,17},{... | collective-permute-start | bytes 786440 | tf_op jit(solution)/shard_map/ppermute | solution.py:1040
  216.1 18.6 %collective-permute-start.47 = (bf16[128,1024]{1,0:T(8,128)(2,1)S(1)}, bf16[128,1024]{1,0:T(8,128)(2,1)S(1)}, u32[]{:S(2)}, u32[]{:S(2)}) collective-permute-start(bf16[128,1024]{1,0:T(8,128)(2,1)S(1)} %get-tuple-element.160), channel_id=1, source_target_pairs={{0,24},{4,28},{8,0},{12,4},{16,8},{20,12},{24,16},{28,20},{1,25},{... | collective-permute-start | bytes 786440 | tf_op jit(solution)/shard_map/ppermute | solution.py:1040
  251.7 25.3 %collective-permute-start.63 = (bf16[4,128,1024]{2,1,0:T(8,128)(2,1)S(1)}, bf16[4,128,1024]{2,1,0:T(8,128)(2,1)S(1)}, u32[]{:S(2)}, u32[]{:S(2)}) collective-permute-start(bf16[4,128,1024]{2,1,0:T(8,128)(2,1)S(1)} %get-tuple-element.189), channel_id=1, source_target_pairs={{0,4},{4,0},{8,12},{12,8},{16,20},{20,16},{24,28},{28,24},{1,5},{5... | collective-permute-start | bytes 3145736 | tf_op jit(solution)/shard_map/ppermute | solution.py:1036
  253.4 29.6 %collective-permute-start.56 = (bf16[512,1024]{1,0:T(8,128)(2,1)S(1)}, bf16[512,1024]{1,0:T(8,128)(2,1)S(1)}, u32[]{:S(2)}, u32[]{:S(2)}) collective-permute-start(bf16[512,1024]{1,0:T(8,128)(2,1)S(1)} %add_convert_fusion.refs_4_.refs_9_.refs_12_.refs_1_), channel_id=1, source_target_pairs={{0,2},{1,3},{2,0},{3,1},{4,6},{5,7},{6,4},{7,5},{8,10},{9,11},{10,... | collective-permute-start | bytes 3145736 | tf_op jit(solution)/shard_map/ppermute | solution.py:1143
  256.3 22.3 %collective-permute-start.52 = (bf16[128,1024]{1,0:T(8,128)(2,1)S(1)}, bf16[128,1024]{1,0:T(8,128)(2,1)S(1)}, u32[]{:S(2)}, u32[]{:S(2)}) collective-permute-start(bf16[128,1024]{1,0:T(8,128)(2,1)S(1)} %get-tuple-element.178), channel_id=1, source_target_pairs={{0,8},{4,12},{8,16},{12,20},{16,24},{20,28},{24,0},{28,4},{1,9},{5... | collective-permute-start | bytes 786440 | tf_op jit(solution)/shard_map/ppermute | solution.py:1040
  260.9 22.0 %collective-permute-start.53 = (bf16[128,1024]{1,0:T(8,128)(2,1)S(1)}, bf16[128,1024]{1,0:T(8,128)(2,1)S(1)}, u32[]{:S(2)}, u32[]{:S(2)}) collective-permute-start(bf16[128,1024]{1,0:T(8,128)(2,1)S(1)} %get-tuple-element.179), channel_id=1, source_target_pairs={{0,16},{4,20},{8,24},{12,28},{16,0},{20,4},{24,8},{28,12},{1,17},{... | collective-permute-start | bytes 786440 | tf_op jit(solution)/shard_map/ppermute | solution.py:1040
  261.2 21.8 %collective-permute-start.54 = (bf16[128,1024]{1,0:T(8,128)(2,1)S(1)}, bf16[128,1024]{1,0:T(8,128)(2,1)S(1)}, u32[]{:S(2)}, u32[]{:S(2)}) collective-permute-start(bf16[128,1024]{1,0:T(8,128)(2,1)S(1)} %get-tuple-element.180), channel_id=1, source_target_pairs={{0,24},{4,28},{8,0},{12,4},{16,8},{20,12},{24,16},{28,20},{1,25},{... | collective-permute-start | bytes 786440 | tf_op jit(solution)/shard_map/ppermute | solution.py:1040
  277.0 46.7 %collective-permute-start.64 = (bf16[4,128,1024]{2,1,0:T(8,128)(2,1)S(1)}, bf16[4,128,1024]{2,1,0:T(8,128)(2,1)S(1)}, u32[]{:S(2)}, u32[]{:S(2)}) collective-permute-start(bf16[4,128,1024]{2,1,0:T(8,128)(2,1)S(1)} %get-tuple-element.191), channel_id=1, source_target_pairs={{0,4},{4,0},{8,12},{12,8},{16,20},{20,16},{24,28},{28,24},{1,5},{5... | collective-permute-start | bytes 3145736 | tf_op jit(solution)/shard_map/ppermute | solution.py:1036
  286.2 51.5 %collective-permute-start.57 = (bf16[512,1024]{1,0:T(8,128)(2,1)S(1)}, bf16[512,1024]{1,0:T(8,128)(2,1)S(1)}, u32[]{:S(2)}, u32[]{:S(2)}) collective-permute-start(bf16[512,1024]{1,0:T(8,128)(2,1)S(1)} %get-tuple-element.186), channel_id=1, source_target_pairs={{0,1},{1,0},{2,3},{3,2},{4,5},{5,4},{6,7},{7,6},{8,9},{9,8},{10,11... | collective-permute-start | bytes 3145736 | tf_op jit(solution)/shard_map/ppermute | solution.py:1143
  287.0 22.1 %collective-permute-start.65 = (bf16[128,1024]{1,0:T(8,128)(2,1)S(1)}, bf16[128,1024]{1,0:T(8,128)(2,1)S(1)}, u32[]{:S(2)}, u32[]{:S(2)}) collective-permute-start(bf16[128,1024]{1,0:T(8,128)(2,1)S(1)} %get-tuple-element.193), channel_id=1, source_target_pairs={{0,8},{4,12},{8,16},{12,20},{16,24},{20,28},{24,0},{28,4},{1,9},{5... | collective-permute-start | bytes 786440 | tf_op jit(solution)/shard_map/ppermute | solution.py:1040
  309.0 26.4 %collective-permute-start.55 = (bf16[256,1024]{1,0:T(8,128)(2,1)S(1)}, bf16[256,1024]{1,0:T(8,128)(2,1)S(1)}, u32[]{:S(2)}, u32[]{:S(2)}) collective-permute-start(bf16[256,1024]{1,0:T(8,128)(2,1)S(1)} %get-tuple-element.184), channel_id=1, source_target_pairs={{0,1},{1,0},{2,3},{3,2},{4,5},{5,4},{6,7},{7,6},{8,9},{9,8},{10,11... | collective-permute-start | bytes 1572872 | tf_op jit(solution)/shard_map/ppermute | solution.py:1143
  328.7 17.4 %collective-permute-start.69 = (bf16[128,1024]{1,0:T(8,128)(2,1)S(1)}, bf16[128,1024]{1,0:T(8,128)(2,1)S(1)}, u32[]{:S(2)}, u32[]{:S(2)}) collective-permute-start(bf16[128,1024]{1,0:T(8,128)(2,1)S(1)} %get-tuple-element.198), channel_id=1, source_target_pairs={{0,16},{4,20},{8,24},{12,28},{16,0},{20,4},{24,8},{28,12},{1,17},{... | collective-permute-start | bytes 786440 | tf_op jit(solution)/shard_map/ppermute | solution.py:1040
  328.7 17.4 %collective-permute-start.70 = (bf16[128,1024]{1,0:T(8,128)(2,1)S(1)}, bf16[128,1024]{1,0:T(8,128)(2,1)S(1)}, u32[]{:S(2)}, u32[]{:S(2)}) collective-permute-start(bf16[128,1024]{1,0:T(8,128)(2,1)S(1)} %get-tuple-element.199), channel_id=1, source_target_pairs={{0,24},{4,28},{8,0},{12,4},{16,8},{20,12},{24,16},{28,20},{1,25},{... | collective-permute-start | bytes 786440 | tf_op jit(solution)/shard_map/ppermute | solution.py:1040
  (68 other events, 743.9 us)

commit v3 on v2

--- a/solution.py
+++ b/solution.py
@@ -760,39 +760,81 @@
     )
 
 
-def final_body(pos_ref, s_ref, r_ref, v_ref, gain_ref, *refs, with_base):
-    gain_vec = gain_ref[...]
-
-    def step(r, held):
-        n = s_ref[r, :].astype(f32) + r_ref[r, :].astype(f32)
-        back = through_norm(n, v_ref[r, :].astype(f32), gain_vec)[0]
-        if with_base:
-            back = refs[0][r, :] + back
-        refs[-2][r, :] = back.astype(bf16)
-        refs[-1][r, :] = back.astype(bf16)
-        return held
-
-    by_chunks(s_ref.shape[0], step)
-
-
-def final_norm(pos, s, r, v, gain, base, ties):
-    half, width_d = s.shape
-    rows = 128
-    steps = half // rows
-    blk = pl.BlockSpec((rows, width_d), lambda i, c: (i, 0))
-    own = pl.BlockSpec((rows, width_d), lambda i, c: (c[0] * steps + i, 0))
-    more = () if base is None else (base,)
-    return call(
-        functools.partial(final_body, with_base=base is not None),
-        [(sds((half, width_d), bf16), blk), (sds((2 * half, width_d), bf16), own)],
-        [blk, blk, own, pl.BlockSpec((1, width_d), lambda i, c: (0, 0))] + [blk] * len(more),
-        (pos, s, r, v, gain, *more),
+def final_body(
+    pos_ref, s_ref, r_ref, lat_ref, src_ref, gain_one_ref, gain_src_ref, base_ref, half_ref, lat_out, src_out, *, first,
+):
+    def run(v_ref, gain_ref, base, out_ref):
+        gain_vec = gain_ref[...]
+
+        def step(r, held):
+            n = s_ref[r, :].astype(f32) + r_ref[r, :].astype(f32)
+            back = through_norm(n, v_ref[r, :].astype(f32), gain_vec)[0]
+            if base is not None:
+                back = base[r, :] + back
+            half_ref[r, :] = back.astype(bf16)
+            out_ref[r, :] = back.astype(bf16)
+            return held
+
+        by_chunks(s_ref.shape[0], step)
+
+    i = pl.program_id(0)
+    pl.when(i < first)(lambda: run(lat_ref, gain_one_ref, base_ref, lat_out))
+    pl.when(i >= first)(lambda: run(src_ref, gain_src_ref, None, src_out))
+
+
+def final_norm(pos, s, r, latents, sources, gain_one, gain_src, base, ties):
+    width_d = s.shape[1]
+    blk = 128
+    one, src = latents.shape[0] // 2 // blk, sources.shape[0] // 2 // blk
+    at_one = lambda i: jnp.minimum(i, one - 1)
+    at_src = lambda i: jnp.maximum(i - one, 0)
+    spec = lambda f: pl.BlockSpec((blk, width_d), lambda i, c: (f(i, c), 0))
+    gain_spec = pl.BlockSpec((1, width_d), lambda i, c: (0, 0))
+    own_one, own_src = spec(lambda i, c: c[0] * one + at_one(i)), spec(lambda i, c: c[0] * src + at_src(i))
+    each = spec(lambda i, c: i)
+    return call(
+        functools.partial(final_body, first=one),
+        [(sds(s.shape, bf16), each), (sds(latents.shape, bf16), own_one), (sds(sources.shape, bf16), own_src)],
+        [each, each, own_one, own_src, gain_spec, gain_spec, spec(lambda i, c: at_one(i))],
+        (pos, s, r, latents, sources, gain_one, gain_src, base),
         "final_norm",
+        grid=(one + src,),
+        prefetch=1,
+        flops=20 * s.size,
+        nbytes=8 * s.size,
         ties=ties,
+    )
+
+
+def place_both_body(pos_ref, other_ref, lat_in, src_in, lat_out, src_out):
+    i = pl.program_id(0)
+
+    @pl.when(i == 0)
+    def _():
+        lat_out[...] = other_ref[...]
+
+    @pl.when(i > 0)
+    def _():
+        src_out[...] = other_ref[...]
+
+
+def place_both(pos, other, lat_whole, src_whole):
+    blk, width_d = lat_whole.shape[0] // 2, other.shape[1]
+    steps = other.shape[0] // blk
+    spec = lambda f: pl.BlockSpec((blk, width_d), lambda i, c: (f(i, c), 0))
+    return call(
+        place_both_body,
+        [
+            (sds(lat_whole.shape, bf16), spec(lambda i, c: 1 - c[0])),
+            (sds(src_whole.shape, bf16), spec(lambda i, c: (1 - c[0]) * (steps - 1) + jnp.maximum(i - 1, 0))),
+        ],
+        [spec(lambda i, c: i), ANY, ANY],
+        (pos, other, lat_whole, src_whole),
+        "place_both",
         grid=(steps,),
         prefetch=1,
-        flops=20 * half * width_d,
-        nbytes=8 * half * width_d,
+        nbytes=4 * other.size,
+        aliases={2: 0, 3: 1},
     )
 
 
@@ -851,7 +893,7 @@
 
 
 def gains_body(
-    pos_ref, clip_ref, frames_ref, one_keep, one_send, src_keep, src_send, lat_ref, src_ref,
+    pos_ref, clip_ref, frames_ref, keep, send, lat_ref, src_ref,
     self_ref, mlp_ref, squares_ref, out_ref, *, one_steps, src_steps, blocks, sets, copies, clips,
 ):
     i = pl.program_id(0)
@@ -878,22 +920,28 @@
         total = by_chunks(v_ref.shape[0], step, jnp.zeros((8, v_ref.shape[1]), f32))
         out_ref[row : row + 1, :] = out_ref[row : row + 1, :] + jnp.sum(total, axis=0, keepdims=True)
 
-    pl.when(i < one_steps)(lambda: add(1, lat_ref, one_keep, one_send, i < one_steps // 2))
-    pl.when(i >= one_steps)(lambda: add(0, src_ref, src_keep, src_send, i - one_steps < src_steps // 2))
-
-
-def gains(pos, clips, frames, one_keep, one_send, src_keep, src_send, latents, sources, self_gain, mlp_gain,
-          squares, copies, ties):
-    half, width_d = one_keep.shape
+    pl.when(i < one_steps)(lambda: add(1, lat_ref, keep, send, i < one_steps // 2))
+    pl.when(i >= one_steps)(lambda: add(0, src_ref, keep, send, i - one_steps < src_steps // 2))
+
+
+def gains(pos, clips, frames, keep, send, latents, sources, self_gain, mlp_gain, squares, copies, ties):
+    rows, width_d = latents.shape
     count = sources.shape[0]
     blk = 256
-    one_steps, src_steps = 2 * half // blk, count // blk
-    blocks = 2 * half // GROUP
+    one_steps, src_steps = rows // blk, count // blk
+    one_half, src_half = one_steps // 2, src_steps // 2
+    blocks = rows // GROUP
     sets = clips.shape[0] // GROUPS_FRAME // blocks
     clamp = lambda v, top: jnp.minimum(jnp.maximum(v, 0), top)
     spec = lambda f: pl.BlockSpec((blk, width_d), lambda i, *c: (f(i, c[0]), 0))
     fixed = lambda n: pl.BlockSpec((n, width_d), lambda i, *c: (0, 0))
     turn = lambda i, c, steps: (clamp(i, steps - 1) + c[0] * (steps // 2)) % steps
+    kept = lambda i, c: jnp.where(
+        i < one_steps, clamp(i, one_half - 1), one_half + clamp(i - one_steps, src_half - 1)
+    )
+    sent = lambda i, c: jnp.where(
+        i < one_steps, clamp(i - one_half, one_half - 1), one_half + clamp(i - one_steps - src_half, src_half - 1)
+    )
     return call(
         functools.partial(
             gains_body, one_steps=one_steps, src_steps=src_steps, blocks=blocks, sets=sets, copies=copies,
@@ -901,27 +949,25 @@
         ),
         [(sds((8, width_d), f32), fixed(8))],
         [
-            spec(lambda i, c: clamp(i, one_steps // 2 - 1)),
-            spec(lambda i, c: clamp(i - one_steps // 2, one_steps // 2 - 1)),
-            spec(lambda i, c: clamp(i - one_steps, src_steps // 2 - 1)),
-            spec(lambda i, c: clamp(i - one_steps - src_steps // 2, src_steps // 2 - 1)),
+            spec(kept),
+            spec(sent),
             spec(lambda i, c: turn(i, c, one_steps)),
             spec(lambda i, c: turn(i - one_steps, c, src_steps)),
             fixed(1), fixed(1), fixed(blocks // 2),
         ],
-        (pos, clips, frames, one_keep, one_send, src_keep, src_send, latents, sources, self_gain, mlp_gain, squares),
+        (pos, clips, frames, keep, send, latents, sources, self_gain, mlp_gain, squares),
         "gains",
         grid=(one_steps + src_steps,),
         prefetch=3,
-        flops=20 * (2 * half + count) * width_d,
-        nbytes=4 * (2 * half + count) * width_d,
+        flops=20 * (rows + count) * width_d,
+        nbytes=4 * (rows + count) * width_d,
         ties=ties,
     )[0]
 
 
-def feature_grads_body(pos_ref, *refs, items, split, blk):
+def feature_grads_body(pos_ref, *refs, items, sends, blk):
     given = sum(a + b for a, b in items)
-    outs = refs[given:]
+    keep_ref, send_refs = refs[given], refs[given + 1 :]
     at, column = 0, 0
     for lefts, rights in items:
         total, row = None, 0
@@ -936,26 +982,29 @@
             total = term if total is None else total + term
             row += rows
         at += lefts + rights
-        cols = slice(column, column + total.shape[1])
-        column += total.shape[1]
+        first, column = column, column + total.shape[1]
         total = total.astype(bf16)
         for j in range(blk // 128):
             part = total[j * 128 : (j + 1) * 128]
-            if split:
-                mine = (pos_ref[1] + j) % 2 == 0
-
-                @pl.when(mine)
-                def _():
-                    outs[0][j // 2, :, cols] = part
-
-                @pl.when(jnp.logical_not(mine))
-                def _():
-                    outs[1][j // 2, :, cols] = part
-            else:
-                outs[0][j, :, cols] = part
-
-
-def feature_grads(pos, items, split, ties=()):
+            if sends == 0:
+                keep_ref[j, :, first:column] = part
+                continue
+            mine = (pos_ref[1] + j) % 2 == 0
+
+            @pl.when(mine)
+            def _():
+                keep_ref[j // 2, :, first:column] = part
+
+            @pl.when(jnp.logical_not(mine))
+            def _():
+                width = send_refs[0].shape[2]
+                for h, ref in enumerate(send_refs):
+                    low, high = max(first, h * width), min(column, (h + 1) * width)
+                    if low < high:
+                        ref[j // 2, :, low - h * width : high - h * width] = part[:, low - first : high - first]
+
+
+def feature_grads(pos, items, sends, ties=()):
     arrays, specs, counts, columns, flops = [], [], [], 0, 0
     features = items[0][0][0].shape[1]
     blk = 512
@@ -970,14 +1019,11 @@
             specs.append(pl.BlockSpec(v.shape, lambda i, c: (0, 0)))
         columns += rights[0].shape[1]
     steps = features // blk
-    sets = features // 256 if split else features // 128
-    count = 2 if split else 1
-    outs = [
-        (sds((sets, 128, columns), bf16), pl.BlockSpec((sets // steps, 128, columns), lambda i, c: (i, 0, 0)))
-    ] * count
-    return call(
-        functools.partial(feature_grads_body, items=tuple(counts), split=split, blk=blk),
-        outs,
+    sets = features // 256 if sends else features // 128
+    out = lambda n: (sds((sets, 128, n), bf16), pl.BlockSpec((sets // steps, 128, n), lambda i, c: (i, 0, 0)))
+    return call(
+        functools.partial(feature_grads_body, items=tuple(counts), sends=sends, blk=blk),
+        [out(columns)] + [out(columns // sends)] * sends if sends else [out(columns)],
         specs,
         (pos, *arrays),
         "feature_grads",
@@ -989,44 +1035,67 @@
     )
 
 
-def middle_body(pos_ref, keep_ref, got_ref, own_ref, one_ref, two_ref, three_ref):
+def stage_one_body(pos_ref, keep_ref, *refs):
     z = pos_ref[1] // 2
-    own_ref[...] = keep_ref[z].astype(f32) + got_ref[z].astype(f32)
-    for d, ref in ((1, one_ref), (2, two_ref), (3, three_ref)):
-        at = (z + d) % 4
-        ref[...] = (keep_ref[at].astype(f32) + got_ref[at].astype(f32)).astype(bf16)
-
-
-def ended_body(own_ref, one_ref, two_ref, three_ref, *outs, turned):
-    total = own_ref[...] + (one_ref[...].astype(f32) + (two_ref[...].astype(f32) + three_ref[...].astype(f32)))
+    gots, (own_ref, send_ref) = refs[:-2], refs[-2:]
+    width = gots[0].shape[2]
+    for h, got_ref in enumerate(gots):
+        cols = slice(h * width, (h + 1) * width)
+        for k in range(2):
+            at = z ^ (2 * k)
+            own_ref[k, :, cols] = keep_ref[at, :, cols].astype(f32) + got_ref[at].astype(f32)
+            at = z ^ 1 ^ (2 * k)
+            send_ref[k, :, cols] = (keep_ref[at, :, cols].astype(f32) + got_ref[at].astype(f32)).astype(bf16)
+
+
+def stage_one(pos, keep, gots, ties=()):
+    shape = (2, *keep.shape[1:])
+    return call(
+        stage_one_body,
+        [(sds(shape, f32), VMEM), (sds(shape, bf16), VMEM)],
+        [SMEM] + [VMEM] * (1 + len(gots)),
+        (pos, keep, *gots),
+        "stage_one",
+        nbytes=4 * keep.size,
+        ties=ties,
+    )
+
+
+def stage_two_body(keep_ref, got_ref, own_ref, send_ref):
+    own_ref[...] = keep_ref[0] + got_ref[0].astype(f32)
+    send_ref[...] = (keep_ref[1] + got_ref[1].astype(f32)).astype(bf16)
+
+
+def stage_two(keep, got, ties=()):
+    shape = keep.shape[1:]
+    return call(
+        stage_two_body,
+        [(sds(shape, f32), VMEM), (sds(shape, bf16), VMEM)],
+        [VMEM] * 2,
+        (keep, got),
+        "stage_two",
+        nbytes=4 * keep.size,
+        ties=ties,
+    )
+
+
+def stage_end_body(own_ref, got_ref, *outs, turned):
+    total = own_ref[...] + got_ref[...].astype(f32)
     width = total.shape[1] // len(outs)
     for k, ref in enumerate(outs):
         part = total[:, k * width : (k + 1) * width]
         ref[...] = part.T if k in turned else part
 
 
-def scatter_middle(pos, keep, got, ties=()):
-    blk = keep.shape[1:]
-    return call(
-        middle_body,
-        [(sds(blk, f32), VMEM)] + [(sds(blk, bf16), VMEM)] * 3,
-        [SMEM, VMEM, VMEM],
-        (pos, keep, got),
-        "middle",
-        nbytes=4 * keep.size,
-        ties=ties,
-    )
-
-
-def scatter_end(own, moved, parts, turned, ties=()):
+def stage_end(own, got, parts, turned, ties=()):
     blk = own.shape
     width = blk[1] // parts
     return call(
-        functools.partial(ended_body, turned=turned),
+        functools.partial(stage_end_body, turned=turned),
         [(sds((width, blk[0]) if k in turned else (blk[0], width), f32), VMEM) for k in range(parts)],
-        [VMEM] * 4,
-        (own, *moved),
-        "ended",
+        [VMEM] * 2,
+        (own, got),
+        "stage_end",
         nbytes=10 * blk[0] * blk[1],
         ties=ties,
     )
@@ -1036,12 +1105,16 @@
     return lax.ppermute(v, "seq", xor_pairs(1, 8))
 
 
-def spread_z(pieces):
-    return [lax.ppermute(pieces[d - 1], "seq", ring_pairs(d)) for d in (1, 2, 3)]
+def near_z(v):
+    return lax.ppermute(v, "seq", xor_pairs(2, 8))
+
+
+def far_z(v):
+    return lax.ppermute(v, "seq", xor_pairs(4, 8))
 
 
 def scatter_whole(pos, items, parts, turned, ties):
-    whole = feature_grads(pos, items, False, ties)[0]
+    whole = feature_grads(pos, items, 0, ties)[0]
     whole = whole.reshape(-1, whole.shape[2])
     total = lax.psum_scatter(whole, "seq", scatter_dimension=0, tiled=True).astype(f32)
     width = total.shape[1] // parts
@@ -1056,7 +1129,7 @@
 
 def cross_back_body(
     pos_ref, mine_ref, other_ref, wo_ref, q_ref, kvp_ref, idx_ref, wq_ref, wk_ref, wv_ref,
-    dq_ref, dkv_ref, one_keep_ref, one_send_ref, src_keep_ref, src_send_ref, dkvp_s, *, blocks,
+    dq_ref, dk_ref, dv_ref, keep_ref, send_ref, dkvp_s, *, blocks,
 ):
     width = wq_ref.shape[1]
     heads = width // HEAD
@@ -1084,9 +1157,9 @@
             dkvp_s[b * SRC : (b + 1) * SRC, vcols] = dot_ta(p.astype(bf16), do).astype(bf16)
         one = dot_t(dq_ref[b * GROUP : (b + 1) * GROUP, :], wq_ref[...]).astype(bf16)
         if b < blocks // 2:
-            one_keep_ref[part : part + GROUP, :] = one
+            keep_ref[part : part + GROUP, :] = one
         else:
-            one_send_ref[part : part + GROUP, :] = one
+            send_ref[part : part + GROUP, :] = one
     half = count // 2
     blk = 256
     row = jnp.concatenate([index_row(idx_ref, pos_ref, b, blocks, count) for b in range(blocks)], axis=1)
@@ -1097,13 +1170,14 @@
         wanted = lax.broadcasted_iota(jnp.int32, (blk, count), 0).astype(f32) + r0.astype(f32)
         picks = jnp.where(row == wanted, 1.0, 0.0).astype(bf16)
         dkv = dot(picks, dkvp_s[...]).astype(bf16)
-        dkv_ref[pl.ds(r0, blk), :] = dkv
+        dk_ref[pl.ds(r0, blk), :] = dkv[:, 0:width]
+        dv_ref[pl.ds(r0, blk), :] = dkv[:, width:]
         total = (dot_t(dkv[:, 0:width], wk_ref[...]) + dot_t(dkv[:, width:], wv_ref[...])).astype(bf16)
-        at = (n * blk) % half
+        at = blocks // 2 * GROUP + (n * blk) % half
         if n * blk < half:
-            src_keep_ref[at : at + blk, :] = total
+            keep_ref[at : at + blk, :] = total
         else:
-            src_send_ref[at : at + blk, :] = total
+            send_ref[at : at + blk, :] = total
 
 
 def cross_back(pos, mine, other, wo, q, kvp, idx, wq, wk, wv, ties):
@@ -1115,11 +1189,10 @@
         functools.partial(cross_back_body, blocks=blocks),
         [
             (sds((rows, width), bf16), VMEM),
-            (sds((count, 2 * width), bf16), VMEM),
-            (sds((rows // 2, width_d), bf16), VMEM),
-            (sds((rows // 2, width_d), bf16), VMEM),
-            (sds((count // 2, width_d), bf16), VMEM),
-            (sds((count // 2, width_d), bf16), VMEM),
+            (sds((count, width), bf16), VMEM),
+            (sds((count, width), bf16), VMEM),
+            (sds(((rows + count) // 2, width_d), bf16), VMEM),
+            (sds(((rows + count) // 2, width_d), bf16), VMEM),
         ],
         [SMEM] + [VMEM] * 9,
         (pos, mine, other, wo, q, kvp, idx, wq, wk, wv),
@@ -1143,7 +1216,7 @@
     return lax.ppermute(x, "tensor", xor_pairs(bit, lax.axis_size("tensor")))
 
 
-def seq_gather(x):
+def seq_gather(x, between=None):
     size = lax.axis_size("seq")
     if size == 8:
         move = lambda v, pairs: lax.ppermute(v, "seq", pairs)
@@ -1151,12 +1224,16 @@
         beside = move(x, flip)
         up = move(x, ring_pairs(1))
         down = move(x, ring_pairs(-1))
+        if between is not None:
+            (beside, up), between = tied([beside, up], between)
         far = move(up, ring_pairs(1))
         up_beside = move(up, flip)
         down_beside = move(beside, ring_pairs(-1))
         far_beside = move(far, flip)
-        return [x, beside, up, down, far, up_beside, down_beside, far_beside]
-    return gather_whole(x)
+        pieces = [x, beside, up, down, far, up_beside, down_beside, far_beside]
+    else:
+        pieces = gather_whole(x)
+    return pieces if between is None else (pieces, between)
 
 
 def gather_whole(x):
@@ -1212,12 +1289,12 @@
     return dict(zip(keys, tied[1:])), tied[0]
 
 
-def sum_everywhere(v):
-    for axis in ("tensor", "seq"):
-        bit = 1
-        while bit < lax.axis_size(axis):
-            v = v + lax.ppermute(v, axis, xor_pairs(bit, lax.axis_size(axis)))
-            bit *= 2
+def sum_over(v, axis, only):
+    size = lax.axis_size(axis)
+    bit = only or 1
+    while bit < size:
+        v = v + lax.ppermute(v, axis, xor_pairs(bit, size))
+        bit = size if only else bit * 2
     return v
 
 
@@ -1254,11 +1331,11 @@
     split = seq_size == 8
     query_pieces = seq_gather(query)
     self_keep, self_send, lse_rows, lse_columns = attend(
-        pos, block_clip, query, kv_pieces, kv_entries, (act_grad, *self_o_all[1:], *query_pieces[2:4])
+        pos, block_clip, query, kv_pieces, kv_entries, (act_grad, *self_o_all[1:])
     )
     after_self, three_mine = project(
         pos, tensor_pieces(self_keep, self_send), self_o_all, after_cross, gain(norm_mlp), False,
-        (query_pieces[1], query_pieces[4]) if split else (),
+        query_pieces[1:4],
     )
     three_other = tensor_swap(three_mine, 1)
     activated, hidden_grad, three_keep, three_send = mlp(three_mine, three_other, mlp_in, act_grad)
@@ -1268,8 +1345,11 @@
     out_items = (((out_rel,), (activated,)),)
     early = ()
     if split:
-        in_keep, in_send = feature_grads(pos, in_items, True, (three_sum,))
-        early = (in_keep, *query_pieces[5:])
+        in_keep, in_send = feature_grads(pos, in_items, 1, (three_sum,))
+        out_keep, out_send_a, out_send_b = feature_grads(pos, out_items, 2, (in_keep,))
+        early = (out_keep, *query_pieces[4:])
+    down_keep, down_send = mlp_down(activated, mlp_out, (three_sum, *early[0:1]))
+    early = (*early, down_keep)
     after_self_grad, self_branch, mlp_gain = norm_back(
         three_sum, three_got, after_self, gain(norm_mlp), out_rel, early
     )
@@ -1278,27 +1358,27 @@
     out_more, delta_columns = out_back(self_branch, self_branch_other, self_o, self_keep, self_send, lse_rows)
     if split:
         in_got = flip_x(in_send)
-    out_pieces = seq_gather(out_more)
     self_query_grad = query_back(
         pos, block_clip, query, out_more, lse_columns, delta_columns, kv_pieces, kv_entries
     )
-    begun = tuple(out_pieces[1:4]) if split else (out_more,)
-    down_keep, down_send = mlp_down(activated, mlp_out, begun)
+    out_pieces, self_query_grad = seq_gather(out_more, self_query_grad)
     result_sum, result_got = half_sum(down_keep, down_send)
     output_half, output_whole, squares = result_half(pos, result_sum, result_got, after_self)
     output = place_other(pos, output_whole, tensor_swap(output_half, 1))
     early = ()
     if split:
-        out_keep, out_send = feature_grads(pos, out_items, True, begun)
-        in_own, *in_parts = scatter_middle(pos, in_keep, in_got)
-        (*in_parts, out_send), out_pieces[-1] = tied([*in_parts, out_send], out_pieces[-1])
-        out_got = flip_x(out_send)
-        in_moved = spread_z(in_parts)
+        in_keep, in_send = stage_one(pos, in_keep, [in_got])
+        (out_send_a, in_send), out_pieces[-1] = tied([out_send_a, in_send], out_pieces[-1])
+        out_got_a = flip_x(out_send_a)
         early = (squares,)
     self_grads, two_keep, two_send = key_back(
         pos, block_clip, key_value, self_query_grad, self_q, self_k, self_v,
         query_pieces, kv_entries, out_pieces, out_entries, early,
     )
+    if split:
+        (two_send, out_send_b), out_got_a = tied([two_send, out_send_b], out_got_a)
+        out_got_b = flip_x(out_send_b)
+        in_got = near_z(in_send)
     two_sum, two_got = half_sum(two_keep, two_send)
     self_items = (
         ((two_mine, two_other), (self_grads,)),
@@ -1306,57 +1386,94 @@
     )
     early = ()
     if split:
-        self_wkeep, self_wsend = feature_grads(pos, self_items, True, (two_sum,))
-        early = (self_wkeep, out_got, *in_moved)
+        self_wkeep, self_send_a, self_send_b = feature_grads(pos, self_items, 2, (two_sum,))
+        in_own, in_send = stage_two(in_keep, in_got, (two_sum,))
+        out_keep, out_send = stage_one(pos, out_keep, [out_got_a, out_got_b], (in_send,))
+        early = (self_wkeep, in_own, out_keep, output)
     after_cross_grad, cross_branch, self_gain = norm_back(
         two_sum, two_got, after_cross, gain(norm_self), after_self_grad, early
     )
     cross_branch_other = tensor_swap(cross_branch, 1)
 
-    cross_query_grad, cross_kv_grad, one_keep, one_send, src_keep, src_send = cross_back(
+    if split:
+        (self_send_a, in_send), cross_branch_other = tied([self_send_a, in_send], cross_branch_other)
+        self_got_a = flip_x(self_send_a)
+        in_got = far_z(in_send)
+    cross_query_grad, cross_key_grad, cross_value_grad, both_keep, both_send = cross_back(
         pos, cross_branch, cross_branch_other, cross_o, cross_query, cross_kv, source_index,
-        cross_q, cross_k, cross_v, (output,),
-    )
-    src_sum, src_got = half_sum(src_keep, src_send)
-    one_sum, one_got = half_sum(one_keep, one_send)
-    cross_items = (
-        ((normed_one,), (cross_query_grad,)),
-        ((normed_src,), (cross_kv_grad,)),
+        cross_q, cross_k, cross_v, (),
+    )
+    first_items = (((normed_one,), (cross_query_grad,)), ((normed_src,), (cross_key_grad,)))
+    second_items = (
+        ((normed_src,), (cross_value_grad,)),
         ((cross_branch, cross_branch_other), (mixed_keep, mixed_send)),
     )
-    early = ()
+    gains_of = lambda ties: gains(
+        pos, block_clip, clip_frames, both_keep, both_send, latents, sources,
+        self_gain, mlp_gain, squares, 2.0 / tensor_size, ties,
+    )
+    final_of = lambda ties: final_norm(
+        pos, both_sum, both_got, latents, sources, gain(norm_cross), gain(norm_src), after_cross_grad, ties
+    )
     if split:
-        (self_wsend,), src_sum = tied([self_wsend], src_sum)
-        self_wgot = flip_x(self_wsend)
-        out_own, *out_parts = scatter_middle(pos, out_keep, out_got, (one_sum, src_sum))
-        out_moved = spread_z(out_parts)
-        cross_wkeep, cross_wsend = feature_grads(pos, cross_items, True, (src_sum, one_sum, out_own))
-        (cross_wsend,), self_wgot = tied([cross_wsend], self_wgot)
-        cross_wgot = flip_x(cross_wsend)
-        self_own, *self_parts = scatter_middle(pos, self_wkeep, self_wgot, (cross_wkeep,))
-        self_moved = spread_z(self_parts)
-        early = (cross_wkeep, *out_moved)
-    small = gains(
-        pos, block_clip, clip_frames, one_keep, one_send, src_keep, src_send, latents, sources,
-        self_gain, mlp_gain, squares, 2.0 / tensor_size, (src_sum, one_sum, *early[0:1]),
-    )
-    early = (*early, small)
-    src_half, src_whole = final_norm(pos, src_sum, src_got, sources, gain(norm_src), None, early)
-    lat_half, lat_whole = final_norm(pos, one_sum, one_got, latents, gain(norm_cross), after_cross_grad, early)
-    (small,), lat_half = tied([small], lat_half)
-    small = sum_everywhere(small)
-    sources_grad = place_other(pos, src_whole, tensor_swap(src_half, 1))
-    latents_grad = place_other(pos, lat_whole, tensor_swap(lat_half, 1))
-    if split:
-        cross_own, *cross_parts = scatter_middle(pos, cross_wkeep, cross_wgot, self_moved)
-        cross_outs = scatter_end(cross_own, spread_z(cross_parts), 4, (3,))
-        self_outs = scatter_end(self_own, self_moved, 4, (3,))
-        mlp_outs = [
-            scatter_end(in_own, in_moved, 1, ())[0],
-            scatter_end(out_own, out_moved, 1, (0,))[0],
-        ]
+        both_send, self_send_b, out_send, self_got_a, in_got = lax.optimization_barrier(
+            (both_send, self_send_b, out_send, self_got_a, in_got)
+        )
+        self_got_b = flip_x(self_send_b)
+        out_got = near_z(out_send)
+        both_sum, both_got = half_sum(both_keep, both_send)
+        small = gains_of((both_sum,))
+        first_keep, first_send = feature_grads(pos, first_items, 1, (small,))
+        second_keep, second_send = feature_grads(pos, second_items, 1, (first_keep,))
+        out_own, out_send = stage_two(out_keep, out_got, (second_keep,))
+        self_wkeep, self_wsend = stage_one(pos, self_wkeep, [self_got_a, self_got_b], (out_own,))
+
+        first_send, out_send, self_wsend, small = lax.optimization_barrier((first_send, out_send, self_wsend, small))
+        first_got = flip_x(first_send)
+        out_got = far_z(out_send)
+        self_wgot = near_z(self_wsend)
+        small = sum_over(sum_over(small, "tensor", 1), "seq", 1)
+        first_keep, first_send = stage_one(pos, first_keep, [first_got], (out_got, small))
+        self_own, self_wsend = stage_two(self_wkeep, self_wgot, (first_keep,))
+
+        second_send, first_send, self_wsend, small = lax.optimization_barrier(
+            (second_send, first_send, self_wsend, small)
+        )
+        second_got = flip_x(second_send)
+        first_got = near_z(first_send)
+        self_wgot = far_z(self_wsend)
+        small = sum_over(small, "seq", 2)
+        both_half, lat_whole, src_whole = final_of(())
+        second_keep, second_send = stage_one(pos, second_keep, [second_got], (self_wgot, small))
+        first_own, first_send = stage_two(first_keep, first_got, (second_keep,))
+
+        second_send, first_send, small, both_half = lax.optimization_barrier(
+            (second_send, first_send, small, both_half)
+        )
+        second_got = near_z(second_send)
+        first_got = far_z(first_send)
+        small = sum_over(small, "seq", 4)
+        both_other = tensor_swap(both_half, 1)
+        second_own, second_send = stage_two(second_keep, second_got, (first_got, small))
+
+        second_send, both_other, small = lax.optimization_barrier((second_send, both_other, small))
+        second_got = far_z(second_send)
+        bit = 2
+        while bit < tensor_size:
+            small = sum_over(small, "tensor", bit)
+            bit *= 2
+        latents_grad, sources_grad = place_both(pos, both_other, lat_whole, src_whole)
+        mlp_outs = [stage_end(in_own, in_got, 1, ())[0], stage_end(out_own, out_got, 1, (0,))[0]]
+        self_outs = stage_end(self_own, self_wgot, 4, (3,))
+        cross_outs = [*stage_end(first_own, first_got, 2, ()), *stage_end(second_own, second_got, 2, (1,))]
     else:
-        cross_outs = scatter_whole(pos, cross_items, 4, (3,), ())
+        both_sum, both_got = half_sum(both_keep, both_send)
+        small = gains_of((both_sum,))
+        small = sum_over(small, "tensor", 0)
+        small = sum_over(small, "seq", 0)
+        both_half, lat_whole, src_whole = final_of(())
+        latents_grad, sources_grad = place_both(pos, tensor_swap(both_half, 1), lat_whole, src_whole)
+        cross_outs = scatter_whole(pos, first_items, 2, (), ()) + scatter_whole(pos, second_items, 2, (1,), ())
         self_outs = scatter_whole(pos, self_items, 4, (3,), ())
         mlp_outs = scatter_whole(pos, in_items, 1, (), ()) + scatter_whole(pos, out_items, 1, (0,), ())
     return (

time: 350 us -> 318 us (0.909)
  waiting for transfers between devices: 167 us -> 142 us
  starting transfers between devices: 80.1 us -> 75.7 us
    ppermute x4 -> x7, waiting for transfers between devices: 17 us -> 2.04 us  [flip_x(): return lax.ppermute(v, 'seq', xor_pairs(1, 8))]
    ppermute x21, waiting for transfers between devices: 82.9 us -> 71.3 us  [seq_gather(): move = lambda v, pairs: lax.ppermute(v, 'seq', pairs)]
    ppermute x17 -> x15, starting transfers between devices: 31.7 us -> 20.8 us  [the longest x5 12.9 us: far_z(): return lax.ppermute(v, 'seq', xor_pairs(4, 8))]
    ppermute x21, starting transfers between devices: 26.4 us -> 34.1 us  [seq_gather(): move = lambda v, pairs: lax.ppermute(v, 'seq', pairs)]
    ppermute x17 -> x15, waiting for transfers between devices: 42.3 us -> 47.8 us  [the longest x5 25.3 us: sum_over(): v = v + lax.ppermute(v, axis, xor_pairs(bit, size))]
    ppermute x29 -> x26, waiting for transfers between devices: 24.5 us -> 20.8 us  [tensor_swap(): return lax.ppermute(x, 'tensor', xor_pairs(bit, lax.axis_size('tensor')))]
    pallas_call x33 -> x39, Pallas kernels: 93.8 us -> 95.2 us  [call(): pl.pallas_call(run, out_shape=[shape for shape, ignored in outs], grid_sp...]
    ppermute x29 -> x26, starting transfers between devices: 15.3 us -> 15.3 us  [tensor_swap(): return lax.ppermute(x, 'tensor', xor_pairs(bit, lax.axis_size('tensor')))]
  transfers between devices with their start and end apart: 71 -> 69, of which waited for: 39 -> 36; matrix products, arithmetic and copies ran while one was open for 1% -> 1% of each run, Pallas kernels for 18% -> 24%
where the time goes in v3:
time: 318 us
  waiting for transfers between devices  142 us (45%)
  Pallas kernels  95.2 us (30%)
  starting transfers between devices  75.7 us (24%)
    pallas_call x39, Pallas kernels, call(): pl.pallas_call(run, out_shape=[shape for shape, ignored in outs], grid_sp...  95.2 us
    ppermute x21, waiting for transfers between devices, seq_gather(): move = lambda v, pairs: lax.ppermute(v, 'seq', pairs)  71.3 us
    ppermute x21, starting transfers between devices, seq_gather(): move = lambda v, pairs: lax.ppermute(v, 'seq', pairs)  34.1 us
    ppermute x5, waiting for transfers between devices, sum_over(): v = v + lax.ppermute(v, axis, xor_pairs(bit, size))  25.3 us
    ppermute x26, waiting for transfers between devices, tensor_swap(): return lax.ppermute(x, 'tensor', xor_pairs(bit, lax.axis_size('tensor')))  20.8 us
    ppermute x26, starting transfers between devices, tensor_swap(): return lax.ppermute(x, 'tensor', xor_pairs(bit, lax.axis_size('tensor')))  15.3 us
    ppermute x5, starting transfers between devices, far_z(): return lax.ppermute(v, 'seq', xor_pairs(4, 8))  12.9 us
    ppermute x5, waiting for transfers between devices, far_z(): return lax.ppermute(v, 'seq', xor_pairs(4, 8))  11.4 us
  transfers between devices with their start and end apart: 69, of which 36 were waited for; matrix products, arithmetic and copies ran while one was open for 1% of the time, Pallas kernels for 24%

profile of v3, /device:TPU:0, one launch (start us, length us, event | category | flops | bytes accessed | tf_op | source)
XLA Modules:
  0.0 318.2 jit_solution(6860300445828387887)
XLA Ops:
  4.3 9.8 %cross_forward.1 = (bf16[512,1024]{1,0:T(8,128)(2,1)}, bf16[1024,1024]{1,0:T(8,128)(2,1)}, bf16[512,256]{1,0:T(8,128)(2,1)}, bf16[1024,512]{1,0:T(8,128)(2,1)}, ...) custom-call(s32[3]{0:T(128)} %pad_add_fusion.refs_0_, s32[4,256]{1,0:T(4,128)} %refs_6_.6, bf16[512,1024]{1,0:T(8,128)(2,1)} %refs_3_.7, ...), custom_call_target="tpu_custom_call" | custom-call | flops 4000000000 | bytes 12000000 | tf_op jit(solution)/shard_map/cross_forward/pallas_call | solution.py:93
  18.5 3.6 %collective-permute-done.3.refs_4_ = bf16[256,256]{1,0:T(8,128)(2,1)S(1)} collective-permute-done((bf16[256,256]{1,0:T(8,128)(2,1)}, bf16[256,256]{1,0:T(8,128)(2,1)S(1)}, u32[]{:S(2)}, u32[]{:S(2)}) %collective-permute-start.3) | collective-permute-done | bytes 131104 | tf_op jit(solution)/shard_map/ppermute | solution.py:1216
  35.7 11.2 %collective-permute-done.8.refs_5_.refs_8_ = bf16[512,512]{1,0:T(8,128)(2,1)S(1)} collective-permute-done((bf16[512,512]{1,0:T(8,128)(2,1)S(1)}, bf16[512,512]{1,0:T(8,128)(2,1)S(1)}, u32[]{:S(2)}, u32[]{:S(2)}) %collective-permute-start.8) | collective-permute-done | bytes 524320 | tf_op jit(solution)/shard_map/ppermute | solution.py:1222
  46.9 3.8 %collective-permute-start.9 = (bf16[512,512]{1,0:T(8,128)(2,1)S(1)}, bf16[512,512]{1,0:T(8,128)(2,1)S(1)}, u32[]{:S(2)}, u32[]{:S(2)}) collective-permute-start(bf16[512,512]{1,0:T(8,128)(2,1)S(1)} %get-tuple-element.150.refs_3_.refs_6_.refs_2_), channel_id=1, source_target_pairs={{0,24},{4,28},{8,0},{12,4},{16,8},{20,12},{24,16},{28,20},{1,25},{... | collective-permute-start | bytes 1572872 | tf_op jit(solution)/shard_map/ppermute | solution.py:1222
  52.3 11.2 %collective-permute-done.10.refs_7_.refs_10_ = bf16[512,512]{1,0:T(8,128)(2,1)S(1)} collective-permute-done((bf16[512,512]{1,0:T(8,128)(2,1)S(1)}, bf16[512,512]{1,0:T(8,128)(2,1)S(1)}, u32[]{:S(2)}, u32[]{:S(2)}) %collective-permute-start.10) | collective-permute-done | bytes 524320 | tf_op jit(solution)/shard_map/ppermute | solution.py:1222
  65.1 3.9 %act_back.1 = (bf16[512,1024]{1,0:T(8,128)(2,1)S(1)}, f32[512,1024]{1,0:T(8,128)S(1)}) custom-call(s32[3]{0:T(128)S(1)} %copy-done.11, bf16[512,1024]{1,0:T(8,128)(2,1)S(1)} %copy-done.19, bf16[1024,1024]{1,0:T(8,128)(2,1)S(1)} %copy-done.4), custom_call_target="tpu_custom_call" | custom-call | flops 1073741824 | bytes 6000000 | tf_op jit(solution)/shard_map/act_back/pallas_call | solution.py:93
  69.0 3.9 %collective-permute-done.9.refs_6_.refs_9_ = bf16[512,512]{1,0:T(8,128)(2,1)S(1)} collective-permute-done((bf16[512,512]{1,0:T(8,128)(2,1)S(1)}, bf16[512,512]{1,0:T(8,128)(2,1)S(1)}, u32[]{:S(2)}, u32[]{:S(2)}) %collective-permute-start.9) | collective-permute-done | bytes 524320 | tf_op jit(solution)/shard_map/ppermute | solution.py:1222
  75.3 8.9 %collective-permute-done.12.refs_9_.refs_12_ = bf16[512,512]{1,0:T(8,128)(2,1)S(1)} collective-permute-done((bf16[512,512]{1,0:T(8,128)(2,1)S(1)}, bf16[512,512]{1,0:T(8,128)(2,1)S(1)}, u32[]{:S(2)}, u32[]{:S(2)}) %collective-permute-start.12) | collective-permute-done | bytes 524320 | tf_op jit(solution)/shard_map/ppermute | solution.py:1222
  84.2 7.9 %attend.1 = (bf16[256,256]{1,0:T(8,128)(2,1)S(1)}, bf16[256,256]{1,0:T(8,128)(2,1)S(1)}, bf16[16,256]{1,0:T(8,128)(2,1)S(1)}, f32[2,512,128]{2,1,0:T(8,128)S(1)}) custom-call(s32[3]{0:T(128)S(1)} %copy-done.11, s32[32]{0:T(128)S(1)} %copy-done.16, bf16[512,256]{1,0:T(8,128)(2,1)S(1)} %get-tuple-element.149.refs_2_.refs_7_, ...), custom_call_target="tpu_custom_call" | custom-call | flops 2000000000 | bytes 7000000 | tf_op jit(solution)/shard_map/attend/pallas_call | solution.py:93
  103.2 6.0 %mlp.1 = (bf16[512,1024]{1,0:T(8,128)(2,1)S(1)}, bf16[512,1024]{1,0:T(8,128)(2,1)S(1)}, bf16[256,1024]{1,0:T(8,128)(2,1)S(1)}, bf16[256,1024]{1,0:T(8,128)(2,1)S(1)}) custom-call(bf16[256,1024]{1,0:T(8,128)(2,1)S(1)} %get-tuple-element.156.refs_0_.refs_1_, bf16[256,1024]{1,0:T(8,128)(2,1)S(1)} %collective-permute-done.23.refs_1_.refs_2_, ...), custom_call_target="tpu_custom_call" | custom-call | flops 2147483648 | bytes 9000000 | tf_op jit(solution)/shard_map/mlp/pallas_call | solution.py:93
  116.6 3.9 %collective-permute-done.29.refs_6_.refs_11_ = bf16[512,256]{1,0:T(8,128)(2,1)S(1)} collective-permute-done((bf16[512,256]{1,0:T(8,128)(2,1)S(1)}, bf16[512,256]{1,0:T(8,128)(2,1)S(1)}, u32[]{:S(2)}, u32[]{:S(2)}) %collective-permute-start.29) | collective-permute-done | bytes 262176 | tf_op jit(solution)/shard_map/ppermute | solution.py:1222
  132.5 3.7 %collective-permute-start.35 = (bf16[544,256]{1,0:T(8,128)(2,1)S(1)}, bf16[544,256]{1,0:T(8,128)(2,1)S(1)}, u32[]{:S(2)}, u32[]{:S(2)}) collective-permute-start(bf16[544,256]{1,0:T(8,128)(2,1)S(1)} %get-tuple-element.172.refs_3_.refs_15_), channel_id=1, source_target_pairs={{0,8},{4,12},{8,16},{12,20},{16,24},{20,28},{24,0},{28,4},{1,9},{5... | collective-permute-start | bytes 835592 | tf_op jit(solution)/shard_map/ppermute | solution.py:1222
  136.7 5.8 %query_back.1.refs_3_ = bf16[512,256]{1,0:T(8,128)(2,1)S(1)} custom-call(s32[3]{0:T(128)S(1)} %copy-done.11, s32[32]{0:T(128)S(1)} %copy-done.16, bf16[512,256]{1,0:T(8,128)(2,1)S(1)} %get-tuple-element.149.refs_2_.refs_7_, bf16[544,256]{1,0:T(8,128)(2,1)S(1)} %get-tuple-element.172.refs_3_.refs_15_, f32[2,512,128]{2,1,0:T(8,128)S(1)} %get-tuple-element.173.refs_4_, ...), custom_call_target="tpu_custom_call" | custom-call | flops 2000000000 | bytes 7000000 | tf_op jit(solution)/shard_map/query_back/pallas_call | solution.py:93
  143.0 18.3 %collective-permute-done.34.refs_16_ = bf16[544,256]{1,0:T(8,128)(2,1)S(1)} collective-permute-done((bf16[544,256]{1,0:T(8,128)(2,1)S(1)}, bf16[544,256]{1,0:T(8,128)(2,1)S(1)}, u32[]{:S(2)}, u32[]{:S(2)}) %collective-permute-start.34) | collective-permute-done | bytes 278560 | tf_op jit(solution)/shard_map/ppermute | solution.py:1222
  161.4 3.7 %collective-permute-start.37 = (bf16[544,256]{1,0:T(8,128)(2,1)S(1)}, bf16[544,256]{1,0:T(8,128)(2,1)S(1)}, u32[]{:S(2)}, u32[]{:S(2)}) collective-permute-start(bf16[544,256]{1,0:T(8,128)(2,1)S(1)} %collective-permute-done.35.refs_17_), channel_id=1, source_target_pairs={{0,8},{4,12},{8,16},{12,20},{16,24},{20,28},{24,0},{28,4},{1,9},{5... | collective-permute-start | bytes 835592 | tf_op jit(solution)/shard_map/ppermute | solution.py:1222
  165.3 6.1 %collective-permute-done.37.refs_19_ = bf16[544,256]{1,0:T(8,128)(2,1)S(1)} collective-permute-done((bf16[544,256]{1,0:T(8,128)(2,1)S(1)}, bf16[544,256]{1,0:T(8,128)(2,1)S(1)}, u32[]{:S(2)}, u32[]{:S(2)}) %collective-permute-start.37) | collective-permute-done | bytes 278560 | tf_op jit(solution)/shard_map/ppermute | solution.py:1222
  171.9 3.5 %collective-permute-start.36 = (bf16[544,256]{1,0:T(8,128)(2,1)S(1)}, bf16[544,256]{1,0:T(8,128)(2,1)S(1)}, u32[]{:S(2)}, u32[]{:S(2)}) collective-permute-start(bf16[544,256]{1,0:T(8,128)(2,1)S(1)} %get-tuple-element.172.refs_3_.refs_15_), channel_id=1, source_target_pairs={{0,24},{4,28},{8,0},{12,4},{16,8},{20,12},{24,16},{28,20},{1,25},{... | collective-permute-start | bytes 835592 | tf_op jit(solution)/shard_map/ppermute | solution.py:1222
  182.5 3.7 %collective-permute-done.39.refs_21_ = bf16[544,256]{1,0:T(8,128)(2,1)S(1)} collective-permute-done((bf16[544,256]{1,0:T(8,128)(2,1)S(1)}, bf16[544,256]{1,0:T(8,128)(2,1)S(1)}, u32[]{:S(2)}, u32[]{:S(2)}) %collective-permute-start.39) | collective-permute-done | bytes 278560 | tf_op jit(solution)/shard_map/ppermute | solution.py:1222
  186.7 8.5 %key_back.1 = (bf16[512,768]{1,0:T(8,128)(2,1)S(1)}, bf16[256,1024]{1,0:T(8,128)(2,1)S(1)}, bf16[256,1024]{1,0:T(8,128)(2,1)S(1)}) custom-call(s32[3]{0:T(128)S(1)} %copy-done.11, s32[32]{0:T(128)S(1)} %copy-done.16, bf16[512,512]{1,0:T(8,128)(2,1)S(1)} %get-tuple-element.150.refs_3_.refs_6_.refs_2_, bf16[512,256]{1,0:T(8,128)(2,1)S(1)} %query_back.1.refs_3_, ...), custom_call_target="tpu_custom_call" | custom-call | flops 4000000000 | bytes 9000000 | tf_op jit(solution)/shard_map/key_back/pallas_call | solution.py:93
  201.7 8.6 %collective-permute-done.45.refs_1_ = bf16[2,128,1024]{2,1,0:T(8,128)(2,1)S(1)} collective-permute-done((bf16[2,128,1024]{2,1,0:T(8,128)(2,1)S(1)}, bf16[2,128,1024]{2,1,0:T(8,128)(2,1)S(1)}, u32[]{:S(2)}, u32[]{:S(2)}) %collective-permute-start.45) | collective-permute-done | bytes 524320 | tf_op jit(solution)/shard_map/ppermute | solution.py:1109
  212.6 3.5 %feature_grads.7 = (bf16[4,128,1024]{2,1,0:T(8,128)(2,1)S(1)}, bf16[4,128,512]{2,1,0:T(8,128)(2,1)S(1)}, bf16[4,128,512]{2,1,0:T(8,128)(2,1)S(1)}) custom-call(s32[3]{0:T(128)S(1)} %copy-done.11, bf16[256,1024]{1,0:T(8,128)(2,1)S(1)} %get-tuple-element.189.refs_0_.refs_1_, bf16[256,1024]{1,0:T(8,128)(2,1)S(1)} %collective-permute-done.6.refs_1_.refs_2_, ...), custom_call_target="tpu_custom_call" | custom-call | flops 1073741824 | bytes 5242880 | tf_op jit(solution)/shard_map/feature_grads/pallas_call | solution.py:93
  222.5 8.6 %cross_back.1 = (bf16[512,256]{1,0:T(8,128)(2,1)S(1)}, bf16[1024,256]{1,0:T(8,128)(2,1)S(1)}, bf16[1024,256]{1,0:T(8,128)(2,1)S(1)}, bf16[768,1024]{1,0:T(8,128)(2,1)S(1)}, bf16[768,1024]{1,0:T(8,128)(2,1)S(1)}) custom-call(s32[3]{0:T(128)S(1)} %copy-done.11, bf16[256,1024]{1,0:T(8,128)(2,1)S(1)} %get-tuple-element.199.refs_1_.refs_3_, ...), custom_call_target="tpu_custom_call" | custom-call | flops 4000000000 | bytes 12000000 | tf_op jit(solution)/shard_map/cross_back/pallas_call | solution.py:93
  231.1 3.3 %collective-permute-done.49.refs_1_ = bf16[128,1024]{1,0:T(8,128)(2,1)S(1)} collective-permute-done((bf16[128,1024]{1,0:T(8,128)(2,1)S(1)}, bf16[128,1024]{1,0:T(8,128)(2,1)S(1)}, u32[]{:S(2)}, u32[]{:S(2)}) %collective-permute-start.49) | collective-permute-done | bytes 262176 | tf_op jit(solution)/shard_map/ppermute | solution.py:1113
  240.0 4.0 %gains.1.refs_5_ = f32[8,1024]{1,0:T(8,128)S(1)} custom-call(s32[3]{0:T(128)S(1)} %copy-done.11, s32[32]{0:T(128)S(1)} %copy-done.16, s32[3]{0:T(128)S(1)} %copy-done.17, bf16[768,1024]{1,0:T(8,128)(2,1)S(1)} %get-tuple-element.208.refs_3_, bf16[768,1024]{1,0:T(8,128)(2,1)S(1)} %get-tuple-element.214.refs_4_, bf16[512,1024]{1,0:T(8,128)(2,1)S(1)} %copy-done, ...), custom_call_target="tpu_custom_call" | custom-call | flops 31457280 | bytes 6291456 | tf_op jit(solution)/shard_map/gains/pallas_call | solution.py:93
  252.9 3.4 %collective-permute-start.54 = (bf16[128,1024]{1,0:T(8,128)(2,1)S(1)}, bf16[128,1024]{1,0:T(8,128)(2,1)S(1)}, u32[]{:S(2)}, u32[]{:S(2)}) collective-permute-start(bf16[128,1024]{1,0:T(8,128)(2,1)S(1)} %get-tuple-element.228), channel_id=1, source_target_pairs={{0,16},{4,20},{8,24},{12,28},{16,0},{20,4},{24,8},{28,12},{1,17},{... | collective-permute-start | bytes 786440 | tf_op jit(solution)/shard_map/ppermute | solution.py:1113
  258.0 7.6 %collective-permute-done.56 = f32[8,1024]{1,0:T(8,128)S(1)} collective-permute-done((f32[8,1024]{1,0:T(8,128)S(1)}, f32[8,1024]{1,0:T(8,128)S(1)}, u32[]{:S(2)}, u32[]{:S(2)}) %collective-permute-start.56) | collective-permute-done | bytes 32800 | tf_op jit(solution)/shard_map/ppermute | solution.py:1296
  265.6 3.8 %collective-permute-done.54.refs_3_.refs_1_ = bf16[128,1024]{1,0:T(8,128)(2,1)S(1)} collective-permute-done((bf16[128,1024]{1,0:T(8,128)(2,1)S(1)}, bf16[128,1024]{1,0:T(8,128)(2,1)S(1)}, u32[]{:S(2)}, u32[]{:S(2)}) %collective-permute-start.54) | collective-permute-done | bytes 262176 | tf_op jit(solution)/shard_map/ppermute | solution.py:1113
  276.4 9.9 %collective-permute-done.60 = f32[8,1024]{1,0:T(8,128)S(1)} collective-permute-done((f32[8,1024]{1,0:T(8,128)S(1)}, f32[8,1024]{1,0:T(8,128)S(1)}, u32[]{:S(2)}, u32[]{:S(2)}) %collective-permute-start.60) | collective-permute-done | bytes 32800 | tf_op jit(solution)/shard_map/ppermute | solution.py:1296
  287.1 4.5 %final_norm.1 = (bf16[768,1024]{1,0:T(8,128)(2,1)S(1)}, bf16[512,1024]{1,0:T(8,128)(2,1)}, bf16[1024,1024]{1,0:T(8,128)(2,1)}) custom-call(s32[3]{0:T(128)S(1)} %copy-done.11, bf16[768,1024]{1,0:T(8,128)(2,1)S(1)} %add_convert_fusion.refs_10_.refs_1_, bf16[768,1024]{1,0:T(8,128)(2,1)S(1)} %collective-permute-done.62.refs_2_, bf16[512,1024]{1,0:T(8,128)(2,1)S(1)} %copy-done, ...), custom_call_target="tpu_custom_call" | custom-call | flops 15728640 | bytes 6291456 | tf_op jit(solution)/shard_map/final_norm/pallas_call | solution.py:93
  292.8 3.1 collective-permute-start.64
  296.0 6.6 %collective-permute-done.65 = f32[8,1024]{1,0:T(8,128)S(1)} collective-permute-done((f32[8,1024]{1,0:T(8,128)S(1)}, f32[8,1024]{1,0:T(8,128)S(1)}, u32[]{:S(2)}, u32[]{:S(2)}) %collective-permute-start.65) | collective-permute-done | bytes 32800 | tf_op jit(solution)/shard_map/ppermute | solution.py:1296
  313.3 4.2 %collective-permute-done.68.refs_1_ = bf16[128,512]{1,0:T(8,128)(2,1)S(1)} collective-permute-done((bf16[128,512]{1,0:T(8,128)(2,1)S(1)}, bf16[128,512]{1,0:T(8,128)(2,1)S(1)}, u32[]{:S(2)}, u32[]{:S(2)}) %collective-permute-start.68) | collective-permute-done | bytes 131104 | tf_op jit(solution)/shard_map/ppermute | solution.py:1113
  (215 shorter events, 118.3 us)
Async XLA Ops:
  0.7 15.2 %collective-permute-start = (bf16[256,1024]{1,0:T(8,128)(2,1)}, bf16[256,1024]{1,0:T(8,128)(2,1)S(1)}, u32[]{:S(2)}, u32[]{:S(2)}) collective-permute-start(bf16[256,1024]{1,0:T(8,128)(2,1)} %refs_3_.6), channel_id=1, source_target_pairs={{0,2},{1,3},{2,0},{3,1},{4,6},{5,7},{6,4},{7,5},{8,10},{9,11},{10,... | collective-permute-start | bytes 1572872 | tf_op jit(solution)/shard_map/ppermute | solution.py:1216
  30.8 16.1 %collective-permute-start.8 = (bf16[512,512]{1,0:T(8,128)(2,1)S(1)}, bf16[512,512]{1,0:T(8,128)(2,1)S(1)}, u32[]{:S(2)}, u32[]{:S(2)}) collective-permute-start(bf16[512,512]{1,0:T(8,128)(2,1)S(1)} %get-tuple-element.150.refs_3_.refs_6_.refs_2_), channel_id=1, source_target_pairs={{0,8},{4,12},{8,16},{12,20},{16,24},{20,28},{24,0},{28,4},{1,9},{5... | collective-permute-start | bytes 1572872 | tf_op jit(solution)/shard_map/ppermute | solution.py:1222
  32.7 14.2 %collective-permute-start.15 = (bf16[256,1024]{1,0:T(8,128)(2,1)S(1)}, bf16[256,1024]{1,0:T(8,128)(2,1)S(1)}, u32[]{:S(2)}, u32[]{:S(2)}) collective-permute-start(bf16[256,1024]{1,0:T(8,128)(2,1)S(1)} %copy-done.5), channel_id=1, source_target_pairs={{0,2},{1,3},{2,0},{3,1},{4,6},{5,7},{6,4},{7,5},{8,10},{9,11},{10,... | collective-permute-start | bytes 1572872 | tf_op jit(solution)/shard_map/ppermute | solution.py:1216
  34.2 16.6 %collective-permute-start.14 = (bf16[256,1024]{1,0:T(8,128)(2,1)S(1)}, bf16[256,1024]{1,0:T(8,128)(2,1)S(1)}, u32[]{:S(2)}, u32[]{:S(2)}) collective-permute-start(bf16[256,1024]{1,0:T(8,128)(2,1)S(1)} %copy-done.5), channel_id=1, source_target_pairs={{0,1},{1,0},{2,3},{3,2},{4,5},{5,4},{6,7},{7,6},{8,9},{9,8},{10,11... | collective-permute-start | bytes 1572872 | tf_op jit(solution)/shard_map/ppermute | solution.py:1216
  34.2 18.1 %collective-permute-start.7 = (bf16[512,512]{1,0:T(8,128)(2,1)S(1)}, bf16[512,512]{1,0:T(8,128)(2,1)S(1)}, u32[]{:S(2)}, u32[]{:S(2)}) collective-permute-start(bf16[512,512]{1,0:T(8,128)(2,1)S(1)} %get-tuple-element.150.refs_3_.refs_6_.refs_2_), channel_id=1, source_target_pairs={{0,4},{4,0},{8,12},{12,8},{16,20},{20,16},{24,28},{28,24},{1,5},{5... | collective-permute-start | bytes 1572872 | tf_op jit(solution)/shard_map/ppermute | solution.py:1222
  46.9 16.6 %collective-permute-start.10 = (bf16[512,512]{1,0:T(8,128)(2,1)S(1)}, bf16[512,512]{1,0:T(8,128)(2,1)S(1)}, u32[]{:S(2)}, u32[]{:S(2)}) collective-permute-start(bf16[512,512]{1,0:T(8,128)(2,1)S(1)} %collective-permute-done.8.refs_5_.refs_8_), channel_id=1, source_target_pairs={{0,8},{4,12},{8,16},{12,20},{16,24},{20,28},{24,0},{28,4},{1,9},{5... | collective-permute-start | bytes 1572872 | tf_op jit(solution)/shard_map/ppermute | solution.py:1222
  46.9 18.2 %collective-permute-start.16 = (bf16[256,1024]{1,0:T(8,128)(2,1)S(1)}, bf16[256,1024]{1,0:T(8,128)(2,1)S(1)}, u32[]{:S(2)}, u32[]{:S(2)}) collective-permute-start(bf16[256,1024]{1,0:T(8,128)(2,1)S(1)} %collective-permute-done.15.refs_13_.refs_7_), channel_id=1, source_target_pairs={{0,1},{1,0},{2,3},{3,2},{4,5},{5,4},{6,7},{7,6},{8,9},{9,8},{10,11... | collective-permute-start | bytes 1572872 | tf_op jit(solution)/shard_map/ppermute | solution.py:1216
  46.9 26.0 %collective-permute-start.9 = (bf16[512,512]{1,0:T(8,128)(2,1)S(1)}, bf16[512,512]{1,0:T(8,128)(2,1)S(1)}, u32[]{:S(2)}, u32[]{:S(2)}) collective-permute-start(bf16[512,512]{1,0:T(8,128)(2,1)S(1)} %get-tuple-element.150.refs_3_.refs_6_.refs_2_), channel_id=1, source_target_pairs={{0,24},{4,28},{8,0},{12,4},{16,8},{20,12},{24,16},{28,20},{1,25},{... | collective-permute-start | bytes 1572872 | tf_op jit(solution)/shard_map/ppermute | solution.py:1222
  50.8 23.3 %collective-permute-start.11 = (bf16[512,512]{1,0:T(8,128)(2,1)S(1)}, bf16[512,512]{1,0:T(8,128)(2,1)S(1)}, u32[]{:S(2)}, u32[]{:S(2)}) collective-permute-start(bf16[512,512]{1,0:T(8,128)(2,1)S(1)} %collective-permute-done.8.refs_5_.refs_8_), channel_id=1, source_target_pairs={{0,4},{4,0},{8,12},{12,8},{16,20},{20,16},{24,28},{28,24},{1,5},{5... | collective-permute-start | bytes 1572872 | tf_op jit(solution)/shard_map/ppermute | solution.py:1222
  52.2 31.9 %collective-permute-start.12 = (bf16[512,512]{1,0:T(8,128)(2,1)S(1)}, bf16[512,512]{1,0:T(8,128)(2,1)S(1)}, u32[]{:S(2)}, u32[]{:S(2)}) collective-permute-start(bf16[512,512]{1,0:T(8,128)(2,1)S(1)} %collective-permute-done.7.refs_4_.refs_7_), channel_id=1, source_target_pairs={{0,24},{4,28},{8,0},{12,4},{16,8},{20,12},{24,16},{28,20},{1,25},{... | collective-permute-start | bytes 1572872 | tf_op jit(solution)/shard_map/ppermute | solution.py:1222
  63.6 20.6 %collective-permute-start.13 = (bf16[512,512]{1,0:T(8,128)(2,1)S(1)}, bf16[512,512]{1,0:T(8,128)(2,1)S(1)}, u32[]{:S(2)}, u32[]{:S(2)}) collective-permute-start(bf16[512,512]{1,0:T(8,128)(2,1)S(1)} %collective-permute-done.10.refs_7_.refs_10_), channel_id=1, source_target_pairs={{0,4},{4,0},{8,12},{12,8},{16,20},{20,16},{24,28},{28,24},{1,5},{5... | collective-permute-start | bytes 1572872 | tf_op jit(solution)/shard_map/ppermute | solution.py:1222
  65.1 28.6 %collective-permute-start.22 = (bf16[512,256]{1,0:T(8,128)(2,1)S(1)}, bf16[512,256]{1,0:T(8,128)(2,1)S(1)}, u32[]{:S(2)}, u32[]{:S(2)}) collective-permute-start(bf16[512,256]{1,0:T(8,128)(2,1)S(1)} %get-tuple-element.149.refs_2_.refs_7_), channel_id=1, source_target_pairs={{0,24},{4,28},{8,0},{12,4},{16,8},{20,12},{24,16},{28,20},{1,25},{... | collective-permute-start | bytes 786440 | tf_op jit(solution)/shard_map/ppermute | solution.py:1222
  72.9 23.0 %collective-permute-start.21 = (bf16[512,256]{1,0:T(8,128)(2,1)S(1)}, bf16[512,256]{1,0:T(8,128)(2,1)S(1)}, u32[]{:S(2)}, u32[]{:S(2)}) collective-permute-start(bf16[512,256]{1,0:T(8,128)(2,1)S(1)} %get-tuple-element.149.refs_2_.refs_7_), channel_id=1, source_target_pairs={{0,8},{4,12},{8,16},{12,20},{16,24},{20,28},{24,0},{28,4},{1,9},{5... | collective-permute-start | bytes 786440 | tf_op jit(solution)/shard_map/ppermute | solution.py:1222
  74.1 21.9 %collective-permute-start.20 = (bf16[512,256]{1,0:T(8,128)(2,1)S(1)}, bf16[512,256]{1,0:T(8,128)(2,1)S(1)}, u32[]{:S(2)}, u32[]{:S(2)}) collective-permute-start(bf16[512,256]{1,0:T(8,128)(2,1)S(1)} %get-tuple-element.149.refs_2_.refs_7_), channel_id=1, source_target_pairs={{0,4},{4,0},{8,12},{12,8},{16,20},{20,16},{24,28},{28,24},{1,5},{5... | collective-permute-start | bytes 786440 | tf_op jit(solution)/shard_map/ppermute | solution.py:1222
  111.4 17.5 %collective-permute-start.28 = (bf16[256,1024]{1,0:T(8,128)(2,1)S(1)}, bf16[256,1024]{1,0:T(8,128)(2,1)S(1)}, u32[]{:S(2)}, u32[]{:S(2)}) collective-permute-start(bf16[256,1024]{1,0:T(8,128)(2,1)S(1)} %add_convert_fusion.3.refs_4_.refs_2_.refs_0_), channel_id=1, source_target_pairs={{0,2},{1,3},{2,0},{3,1},{4,6},{5,7},{6,4},{7,5},{8,10},{9,11},{10,... | collective-permute-start | bytes 1572872 | tf_op jit(solution)/shard_map/ppermute | solution.py:1216
  112.8 16.0 %collective-permute-start.30 = (bf16[512,256]{1,0:T(8,128)(2,1)S(1)}, bf16[512,256]{1,0:T(8,128)(2,1)S(1)}, u32[]{:S(2)}, u32[]{:S(2)}) collective-permute-start(bf16[512,256]{1,0:T(8,128)(2,1)S(1)} %collective-permute-done.21.refs_12_.refs_9_), channel_id=1, source_target_pairs={{0,4},{4,0},{8,12},{12,8},{16,20},{20,16},{24,28},{28,24},{1,5},{5... | collective-permute-start | bytes 786440 | tf_op jit(solution)/shard_map/ppermute | solution.py:1222
  114.3 14.6 %collective-permute-start.31 = (bf16[512,256]{1,0:T(8,128)(2,1)S(1)}, bf16[512,256]{1,0:T(8,128)(2,1)S(1)}, u32[]{:S(2)}, u32[]{:S(2)}) collective-permute-start(bf16[512,256]{1,0:T(8,128)(2,1)S(1)} %collective-permute-done.20.refs_11_.refs_8_), channel_id=1, source_target_pairs={{0,24},{4,28},{8,0},{12,4},{16,8},{20,12},{24,16},{28,20},{1,25},{... | collective-permute-start | bytes 786440 | tf_op jit(solution)/shard_map/ppermute | solution.py:1222
  129.8 47.3 %collective-permute-start.41 = (bf16[4,128,1024]{2,1,0:T(8,128)(2,1)S(1)}, bf16[4,128,1024]{2,1,0:T(8,128)(2,1)S(1)}, u32[]{:S(2)}, u32[]{:S(2)}) collective-permute-start(bf16[4,128,1024]{2,1,0:T(8,128)(2,1)S(1)} %get-tuple-element.179), channel_id=1, source_target_pairs={{0,4},{4,0},{8,12},{12,8},{16,20},{20,16},{24,28},{28,24},{1,5},{5... | collective-permute-start | bytes 3145736 | tf_op jit(solution)/shard_map/ppermute | solution.py:1105
  130.4 34.6 %collective-permute-start.25 = (bf16[256,1024]{1,0:T(8,128)(2,1)S(1)}, bf16[256,1024]{1,0:T(8,128)(2,1)S(1)}, u32[]{:S(2)}, u32[]{:S(2)}) collective-permute-start(bf16[256,1024]{1,0:T(8,128)(2,1)S(1)} %get-tuple-element.165), channel_id=1, source_target_pairs={{0,1},{1,0},{2,3},{3,2},{4,5},{5,4},{6,7},{7,6},{8,9},{9,8},{10,11... | collective-permute-start | bytes 1572872 | tf_op jit(solution)/shard_map/ppermute | solution.py:1216
  136.2 25.2 %collective-permute-start.34 = (bf16[544,256]{1,0:T(8,128)(2,1)S(1)}, bf16[544,256]{1,0:T(8,128)(2,1)S(1)}, u32[]{:S(2)}, u32[]{:S(2)}) collective-permute-start(bf16[544,256]{1,0:T(8,128)(2,1)S(1)} %get-tuple-element.172.refs_3_.refs_15_), channel_id=1, source_target_pairs={{0,4},{4,0},{8,12},{12,8},{16,20},{20,16},{24,28},{28,24},{1,5},{5... | collective-permute-start | bytes 835592 | tf_op jit(solution)/shard_map/ppermute | solution.py:1222
  165.2 14.8 %collective-permute-start.26 = (bf16[256,1024]{1,0:T(8,128)(2,1)S(1)}, bf16[256,1024]{1,0:T(8,128)(2,1)S(1)}, u32[]{:S(2)}, u32[]{:S(2)}) collective-permute-start(bf16[256,1024]{1,0:T(8,128)(2,1)S(1)} %add_convert_fusion.2.refs_1_), channel_id=1, source_target_pairs={{0,2},{1,3},{2,0},{3,1},{4,6},{5,7},{6,4},{7,5},{8,10},{9,11},{10,... | collective-permute-start | bytes 1572872 | tf_op jit(solution)/shard_map/ppermute | solution.py:1216
  179.7 16.2 %collective-permute-start.42 = (bf16[4,128,512]{2,1,0:T(8,128)(2,1)S(1)}, bf16[4,128,512]{2,1,0:T(8,128)(2,1)S(1)}, u32[]{:S(2)}, u32[]{:S(2)}) collective-permute-start(bf16[4,128,512]{2,1,0:T(8,128)(2,1)S(1)} %get-tuple-element.184), channel_id=1, source_target_pairs={{0,4},{4,0},{8,12},{12,8},{16,20},{20,16},{24,28},{28,24},{1,5},{5... | collective-permute-start | bytes 1572872 | tf_op jit(solution)/shard_map/ppermute | solution.py:1105
  199.0 17.1 %collective-permute-start.44 = (bf16[256,1024]{1,0:T(8,128)(2,1)S(1)}, bf16[256,1024]{1,0:T(8,128)(2,1)S(1)}, u32[]{:S(2)}, u32[]{:S(2)}) collective-permute-start(bf16[256,1024]{1,0:T(8,128)(2,1)S(1)} %add_convert_fusion.1.refs_8_.refs_2_.refs_0_), channel_id=1, source_target_pairs={{0,2},{1,3},{2,0},{3,1},{4,6},{5,7},{6,4},{7,5},{8,10},{9,11},{10,... | collective-permute-start | bytes 1572872 | tf_op jit(solution)/shard_map/ppermute | solution.py:1216
  219.0 15.4 %collective-permute-start.48 = (bf16[4,128,512]{2,1,0:T(8,128)(2,1)S(1)}, bf16[4,128,512]{2,1,0:T(8,128)(2,1)S(1)}, u32[]{:S(2)}, u32[]{:S(2)}) collective-permute-start(bf16[4,128,512]{2,1,0:T(8,128)(2,1)S(1)} %get-tuple-element.212), channel_id=1, source_target_pairs={{0,4},{4,0},{8,12},{12,8},{16,20},{20,16},{24,28},{28,24},{1,5},{5... | collective-permute-start | bytes 1572872 | tf_op jit(solution)/shard_map/ppermute | solution.py:1105
  219.5 14.9 %collective-permute-start.49 = (bf16[128,1024]{1,0:T(8,128)(2,1)S(1)}, bf16[128,1024]{1,0:T(8,128)(2,1)S(1)}, u32[]{:S(2)}, u32[]{:S(2)}) collective-permute-start(bf16[128,1024]{1,0:T(8,128)(2,1)S(1)} %get-tuple-element.213.refs_4_), channel_id=1, source_target_pairs={{0,16},{4,20},{8,24},{12,28},{16,0},{20,4},{24,8},{28,12},{1,17},{... | collective-permute-start | bytes 786440 | tf_op jit(solution)/shard_map/ppermute | solution.py:1113
  234.4 15.8 %collective-permute-start.51 = (bf16[2,128,1024]{2,1,0:T(8,128)(2,1)S(1)}, bf16[2,128,1024]{2,1,0:T(8,128)(2,1)S(1)}, u32[]{:S(2)}, u32[]{:S(2)}) collective-permute-start(bf16[2,128,1024]{2,1,0:T(8,128)(2,1)S(1)} %get-tuple-element.221), channel_id=1, source_target_pairs={{0,8},{4,12},{8,0},{12,4},{16,24},{20,28},{24,16},{28,20},{1,9},{5... | collective-permute-start | bytes 1572872 | tf_op jit(solution)/shard_map/ppermute | solution.py:1109
  234.6 15.7 %collective-permute-start.52 = (bf16[4,128,512]{2,1,0:T(8,128)(2,1)S(1)}, bf16[4,128,512]{2,1,0:T(8,128)(2,1)S(1)}, u32[]{:S(2)}, u32[]{:S(2)}) collective-permute-start(bf16[4,128,512]{2,1,0:T(8,128)(2,1)S(1)} %get-tuple-element.224), channel_id=1, source_target_pairs={{0,4},{4,0},{8,12},{12,8},{16,20},{20,16},{24,28},{28,24},{1,5},{5... | collective-permute-start | bytes 1572872 | tf_op jit(solution)/shard_map/ppermute | solution.py:1105
  238.5 48.5 %collective-permute-start.62 = (bf16[768,1024]{1,0:T(8,128)(2,1)S(1)}, bf16[768,1024]{1,0:T(8,128)(2,1)S(1)}, u32[]{:S(2)}, u32[]{:S(2)}) collective-permute-start(bf16[768,1024]{1,0:T(8,128)(2,1)S(1)} %add_convert_fusion.refs_10_.refs_1_), channel_id=1, source_target_pairs={{0,2},{1,3},{2,0},{3,1},{4,6},{5,7},{6,4},{7,5},{8,10},{9,11},{10,... | collective-permute-start | bytes 4718600 | tf_op jit(solution)/shard_map/ppermute | solution.py:1216
  251.2 18.3 %collective-permute-start.53 = (bf16[4,128,512]{2,1,0:T(8,128)(2,1)S(1)}, bf16[4,128,512]{2,1,0:T(8,128)(2,1)S(1)}, u32[]{:S(2)}, u32[]{:S(2)}) collective-permute-start(bf16[4,128,512]{2,1,0:T(8,128)(2,1)S(1)} %get-tuple-element.227), channel_id=1, source_target_pairs={{0,4},{4,0},{8,12},{12,8},{16,20},{20,16},{24,28},{28,24},{1,5},{5... | collective-permute-start | bytes 1572872 | tf_op jit(solution)/shard_map/ppermute | solution.py:1105
  252.4 19.0 %collective-permute-start.57 = (bf16[2,128,1024]{2,1,0:T(8,128)(2,1)S(1)}, bf16[2,128,1024]{2,1,0:T(8,128)(2,1)S(1)}, u32[]{:S(2)}, u32[]{:S(2)}) collective-permute-start(bf16[2,128,1024]{2,1,0:T(8,128)(2,1)S(1)} %get-tuple-element.232), channel_id=1, source_target_pairs={{0,8},{4,12},{8,0},{12,4},{16,24},{20,28},{24,16},{28,20},{1,9},{5... | collective-permute-start | bytes 1572872 | tf_op jit(solution)/shard_map/ppermute | solution.py:1109
  252.9 16.5 %collective-permute-start.54 = (bf16[128,1024]{1,0:T(8,128)(2,1)S(1)}, bf16[128,1024]{1,0:T(8,128)(2,1)S(1)}, u32[]{:S(2)}, u32[]{:S(2)}) collective-permute-start(bf16[128,1024]{1,0:T(8,128)(2,1)S(1)} %get-tuple-element.228), channel_id=1, source_target_pairs={{0,16},{4,20},{8,24},{12,28},{16,0},{20,4},{24,8},{28,12},{1,17},{... | collective-permute-start | bytes 786440 | tf_op jit(solution)/shard_map/ppermute | solution.py:1113
  271.5 14.8 %collective-permute-start.58 = (bf16[4,128,512]{2,1,0:T(8,128)(2,1)S(1)}, bf16[4,128,512]{2,1,0:T(8,128)(2,1)S(1)}, u32[]{:S(2)}, u32[]{:S(2)}) collective-permute-start(bf16[4,128,512]{2,1,0:T(8,128)(2,1)S(1)} %get-tuple-element.235), channel_id=1, source_target_pairs={{0,4},{4,0},{8,12},{12,8},{16,20},{20,16},{24,28},{28,24},{1,5},{5... | collective-permute-start | bytes 1572872 | tf_op jit(solution)/shard_map/ppermute | solution.py:1105
  (66 other events, 680.6 us)

commit v4 on v3

--- a/solution.py
+++ b/solution.py
@@ -1216,7 +1216,7 @@
     return lax.ppermute(x, "tensor", xor_pairs(bit, lax.axis_size("tensor")))
 
 
-def seq_gather(x, between=None):
+def seq_gather(x, between=None, guest=None):
     size = lax.axis_size("seq")
     if size == 8:
         move = lambda v, pairs: lax.ppermute(v, "seq", pairs)
@@ -1224,16 +1224,22 @@
         beside = move(x, flip)
         up = move(x, ring_pairs(1))
         down = move(x, ring_pairs(-1))
-        if between is not None:
-            (beside, up), between = tied([beside, up], between)
+        if guest is not None:
+            (beside, up, guest), between = tied([beside, up, guest], between)
+            guest = flip_x(guest)
         far = move(up, ring_pairs(1))
-        up_beside = move(up, flip)
         down_beside = move(beside, ring_pairs(-1))
-        far_beside = move(far, flip)
+        if guest is not None:
+            up_beside = move(beside, ring_pairs(1))
+            (far_sent, up_beside), down_beside = tied([far, up_beside], down_beside)
+        else:
+            up_beside = move(up, flip)
+            far_sent = far
+        far_beside = move(far_sent, flip)
         pieces = [x, beside, up, down, far, up_beside, down_beside, far_beside]
     else:
         pieces = gather_whole(x)
-    return pieces if between is None else (pieces, between)
+    return pieces if guest is None else (pieces, between, guest)
 
 
 def gather_whole(x):
@@ -1356,12 +1362,13 @@
     self_branch_other = tensor_swap(self_branch, 1)
 
     out_more, delta_columns = out_back(self_branch, self_branch_other, self_o, self_keep, self_send, lse_rows)
-    if split:
-        in_got = flip_x(in_send)
     self_query_grad = query_back(
         pos, block_clip, query, out_more, lse_columns, delta_columns, kv_pieces, kv_entries
     )
-    out_pieces, self_query_grad = seq_gather(out_more, self_query_grad)
+    if split:
+        out_pieces, self_query_grad, in_got = seq_gather(out_more, self_query_grad, in_send)
+    else:
+        out_pieces = seq_gather(out_more)
     result_sum, result_got = half_sum(down_keep, down_send)
     output_half, output_whole, squares = result_half(pos, result_sum, result_got, after_self)
     output = place_other(pos, output_whole, tensor_swap(output_half, 1))
@@ -1387,7 +1394,7 @@
     early = ()
     if split:
         self_wkeep, self_send_a, self_send_b = feature_grads(pos, self_items, 2, (two_sum,))
-        in_own, in_send = stage_two(in_keep, in_got, (two_sum,))
+        in_own, in_send = stage_two(in_keep, in_got, (self_wkeep,))
         out_keep, out_send = stage_one(pos, out_keep, [out_got_a, out_got_b], (in_send,))
         early = (self_wkeep, in_own, out_keep, output)
     after_cross_grad, cross_branch, self_gain = norm_back(
@@ -1422,17 +1429,18 @@
         self_got_b = flip_x(self_send_b)
         out_got = near_z(out_send)
         both_sum, both_got = half_sum(both_keep, both_send)
-        small = gains_of((both_sum,))
-        first_keep, first_send = feature_grads(pos, first_items, 1, (small,))
+        first_keep, first_send = feature_grads(pos, first_items, 1, (both_sum,))
         second_keep, second_send = feature_grads(pos, second_items, 1, (first_keep,))
         out_own, out_send = stage_two(out_keep, out_got, (second_keep,))
         self_wkeep, self_wsend = stage_one(pos, self_wkeep, [self_got_a, self_got_b], (out_own,))
 
-        first_send, out_send, self_wsend, small = lax.optimization_barrier((first_send, out_send, self_wsend, small))
+        first_send, out_send, self_wsend = lax.optimization_barrier((first_send, out_send, self_wsend))
         first_got = flip_x(first_send)
         out_got = far_z(out_send)
         self_wgot = near_z(self_wsend)
-        small = sum_over(sum_over(small, "tensor", 1), "seq", 1)
+        mlp_outs = stage_end(in_own, in_got, 1, (), (self_wsend,))
+        small = gains_of((first_send, mlp_outs[0]))
+        small = sum_over(small, "tensor", 1)
         first_keep, first_send = stage_one(pos, first_keep, [first_got], (out_got, small))
         self_own, self_wsend = stage_two(self_wkeep, self_wgot, (first_keep,))
 
@@ -1442,9 +1450,11 @@
         second_got = flip_x(second_send)
         first_got = near_z(first_send)
         self_wgot = far_z(self_wsend)
-        small = sum_over(small, "seq", 2)
         both_half, lat_whole, src_whole = final_of(())
-        second_keep, second_send = stage_one(pos, second_keep, [second_got], (self_wgot, small))
+        mlp_outs = [*mlp_outs, stage_end(out_own, out_got, 1, (0,), (both_half,))[0]]
+        small, both_half = lax.optimization_barrier((small, both_half))
+        small = sum_over(small, "seq", 1)
+        second_keep, second_send = stage_one(pos, second_keep, [second_got], (self_wgot, small, mlp_outs[1]))
         first_own, first_send = stage_two(first_keep, first_got, (second_keep,))
 
         second_send, first_send, small, both_half = lax.optimization_barrier(
@@ -1452,19 +1462,19 @@
         )
         second_got = near_z(second_send)
         first_got = far_z(first_send)
-        small = sum_over(small, "seq", 4)
+        small = sum_over(small, "seq", 2)
         both_other = tensor_swap(both_half, 1)
-        second_own, second_send = stage_two(second_keep, second_got, (first_got, small))
+        self_outs = stage_end(self_own, self_wgot, 4, (3,), (first_send,))
+        second_own, second_send = stage_two(second_keep, second_got, (first_got, small, self_outs[0]))
 
         second_send, both_other, small = lax.optimization_barrier((second_send, both_other, small))
         second_got = far_z(second_send)
+        small = sum_over(small, "seq", 4)
         bit = 2
         while bit < tensor_size:
             small = sum_over(small, "tensor", bit)
             bit *= 2
         latents_grad, sources_grad = place_both(pos, both_other, lat_whole, src_whole)
-        mlp_outs = [stage_end(in_own, in_got, 1, ())[0], stage_end(out_own, out_got, 1, (0,))[0]]
-        self_outs = stage_end(self_own, self_wgot, 4, (3,))
         cross_outs = [*stage_end(first_own, first_got, 2, ()), *stage_end(second_own, second_got, 2, (1,))]
     else:
         both_sum, both_got = half_sum(both_keep, both_send)

time: 318 us -> 306 us (0.962)
  waiting for transfers between devices: 142 us -> 133 us
  starting transfers between devices: 75.7 us -> 69.4 us
    ppermute x5, waiting for transfers between devices: 25.3 us -> 14.7 us  [sum_over(): v = v + lax.ppermute(v, axis, xor_pairs(bit, size))]
    ppermute x21, waiting for transfers between devices: 71.3 us -> 62.4 us  [seq_gather(): move = lambda v, pairs: lax.ppermute(v, 'seq', pairs)]
    ppermute x5, starting transfers between devices: 12.9 us -> 7.04 us  [far_z(): return lax.ppermute(v, 'seq', xor_pairs(4, 8))]
    ppermute x5, waiting for transfers between devices: 11.4 us -> 17 us  [far_z(): return lax.ppermute(v, 'seq', xor_pairs(4, 8))]
    ppermute x21, starting transfers between devices: 34.1 us -> 29.5 us  [seq_gather(): move = lambda v, pairs: lax.ppermute(v, 'seq', pairs)]
  transfers between devices with their start and end apart: 69 -> 69, of which waited for: 36 -> 36; matrix products, arithmetic and copies ran while one was open for 1% -> 1% of each run, Pallas kernels for 24% -> 27%
where the time goes in v4:
time: 306 us
  waiting for transfers between devices  133 us (43%)
  Pallas kernels  95.4 us (31%)
  starting transfers between devices  69.4 us (23%)
  local copies, waits for them, and re-layouts  5.14 us (2%)
    pallas_call x39, Pallas kernels, call(): pl.pallas_call(run, out_shape=[shape for shape, ignored in outs], grid_sp...  95.4 us
    ppermute x21, waiting for transfers between devices, seq_gather(): move = lambda v, pairs: lax.ppermute(v, 'seq', pairs)  62.4 us
    ppermute x21, starting transfers between devices, seq_gather(): move = lambda v, pairs: lax.ppermute(v, 'seq', pairs)  29.5 us
    ppermute x26, waiting for transfers between devices, tensor_swap(): return lax.ppermute(x, 'tensor', xor_pairs(bit, lax.axis_size('tensor')))  23.8 us
    ppermute x5, waiting for transfers between devices, far_z(): return lax.ppermute(v, 'seq', xor_pairs(4, 8))  17 us
    ppermute x26, starting transfers between devices, tensor_swap(): return lax.ppermute(x, 'tensor', xor_pairs(bit, lax.axis_size('tensor')))  16.7 us
    ppermute x5, waiting for transfers between devices, sum_over(): v = v + lax.ppermute(v, axis, xor_pairs(bit, size))  14.7 us
    ppermute x5, waiting for transfers between devices, near_z(): return lax.ppermute(v, 'seq', xor_pairs(2, 8))  10.7 us
  transfers between devices with their start and end apart: 69, of which 36 were waited for; matrix products, arithmetic and copies ran while one was open for 1% of the time, Pallas kernels for 27%

profile of v4, /device:TPU:0, one launch (start us, length us, event | category | flops | bytes accessed | tf_op | source)
XLA Modules:
  0.0 305.9 jit_solution(10372678872624002097)
XLA Ops:
  0.7 3.0 collective-permute-start
  4.3 9.8 %cross_forward.1 = (bf16[512,1024]{1,0:T(8,128)(2,1)}, bf16[1024,1024]{1,0:T(8,128)(2,1)}, bf16[512,256]{1,0:T(8,128)(2,1)}, bf16[1024,512]{1,0:T(8,128)(2,1)}, ...) custom-call(s32[3]{0:T(128)} %pad_add_fusion.refs_0_, s32[4,256]{1,0:T(4,128)} %refs_6_.6, bf16[512,1024]{1,0:T(8,128)(2,1)} %refs_3_.7, ...), custom_call_target="tpu_custom_call" | custom-call | flops 4000000000 | bytes 12000000 | tf_op jit(solution)/shard_map/cross_forward/pallas_call | solution.py:93
  18.5 3.6 %collective-permute-done.3.refs_4_ = bf16[256,256]{1,0:T(8,128)(2,1)S(1)} collective-permute-done((bf16[256,256]{1,0:T(8,128)(2,1)}, bf16[256,256]{1,0:T(8,128)(2,1)S(1)}, u32[]{:S(2)}, u32[]{:S(2)}) %collective-permute-start.3) | collective-permute-done | bytes 131104 | tf_op jit(solution)/shard_map/ppermute | solution.py:1216
  22.1 3.1 %collective-permute-done.2.refs_3_ = bf16[256,256]{1,0:T(8,128)(2,1)S(1)} collective-permute-done((bf16[256,256]{1,0:T(8,128)(2,1)}, bf16[256,256]{1,0:T(8,128)(2,1)S(1)}, u32[]{:S(2)}, u32[]{:S(2)}) %collective-permute-start.2) | collective-permute-done | bytes 131104 | tf_op jit(solution)/shard_map/ppermute | solution.py:1216
  35.7 11.2 %collective-permute-done.8.refs_5_.refs_8_ = bf16[512,512]{1,0:T(8,128)(2,1)S(1)} collective-permute-done((bf16[512,512]{1,0:T(8,128)(2,1)S(1)}, bf16[512,512]{1,0:T(8,128)(2,1)S(1)}, u32[]{:S(2)}, u32[]{:S(2)}) %collective-permute-start.8) | collective-permute-done | bytes 524320 | tf_op jit(solution)/shard_map/ppermute | solution.py:1222
  46.9 3.8 %collective-permute-start.9 = (bf16[512,512]{1,0:T(8,128)(2,1)S(1)}, bf16[512,512]{1,0:T(8,128)(2,1)S(1)}, u32[]{:S(2)}, u32[]{:S(2)}) collective-permute-start(bf16[512,512]{1,0:T(8,128)(2,1)S(1)} %get-tuple-element.155.refs_3_.refs_6_.refs_2_), channel_id=1, source_target_pairs={{0,24},{4,28},{8,0},{12,4},{16,8},{20,12},{24,16},{28,20},{1,25},{... | collective-permute-start | bytes 1572872 | tf_op jit(solution)/shard_map/ppermute | solution.py:1222
  52.3 11.2 %collective-permute-done.10.refs_7_.refs_10_ = bf16[512,512]{1,0:T(8,128)(2,1)S(1)} collective-permute-done((bf16[512,512]{1,0:T(8,128)(2,1)S(1)}, bf16[512,512]{1,0:T(8,128)(2,1)S(1)}, u32[]{:S(2)}, u32[]{:S(2)}) %collective-permute-start.10) | collective-permute-done | bytes 524320 | tf_op jit(solution)/shard_map/ppermute | solution.py:1222
  65.1 3.9 %act_back.1 = (bf16[512,1024]{1,0:T(8,128)(2,1)S(1)}, f32[512,1024]{1,0:T(8,128)S(1)}) custom-call(s32[3]{0:T(128)S(1)} %copy-done.14, bf16[512,1024]{1,0:T(8,128)(2,1)S(1)} %copy-done.22, bf16[1024,1024]{1,0:T(8,128)(2,1)S(1)} %copy-done.4), custom_call_target="tpu_custom_call" | custom-call | flops 1073741824 | bytes 6000000 | tf_op jit(solution)/shard_map/act_back/pallas_call | solution.py:93
  69.0 3.9 %collective-permute-done.9.refs_6_.refs_9_ = bf16[512,512]{1,0:T(8,128)(2,1)S(1)} collective-permute-done((bf16[512,512]{1,0:T(8,128)(2,1)S(1)}, bf16[512,512]{1,0:T(8,128)(2,1)S(1)}, u32[]{:S(2)}, u32[]{:S(2)}) %collective-permute-start.9) | collective-permute-done | bytes 524320 | tf_op jit(solution)/shard_map/ppermute | solution.py:1222
  75.3 8.9 %collective-permute-done.12.refs_9_.refs_12_ = bf16[512,512]{1,0:T(8,128)(2,1)S(1)} collective-permute-done((bf16[512,512]{1,0:T(8,128)(2,1)S(1)}, bf16[512,512]{1,0:T(8,128)(2,1)S(1)}, u32[]{:S(2)}, u32[]{:S(2)}) %collective-permute-start.12) | collective-permute-done | bytes 524320 | tf_op jit(solution)/shard_map/ppermute | solution.py:1222
  84.2 7.9 %attend.1 = (bf16[256,256]{1,0:T(8,128)(2,1)S(1)}, bf16[256,256]{1,0:T(8,128)(2,1)S(1)}, bf16[16,256]{1,0:T(8,128)(2,1)S(1)}, f32[2,512,128]{2,1,0:T(8,128)S(1)}) custom-call(s32[3]{0:T(128)S(1)} %copy-done.14, s32[32]{0:T(128)S(1)} %copy-done.19, bf16[512,256]{1,0:T(8,128)(2,1)S(1)} %get-tuple-element.154.refs_2_.refs_7_, ...), custom_call_target="tpu_custom_call" | custom-call | flops 2000000000 | bytes 7000000 | tf_op jit(solution)/shard_map/attend/pallas_call | solution.py:93
  103.2 6.0 %mlp.1 = (bf16[512,1024]{1,0:T(8,128)(2,1)S(1)}, bf16[512,1024]{1,0:T(8,128)(2,1)S(1)}, bf16[256,1024]{1,0:T(8,128)(2,1)S(1)}, bf16[256,1024]{1,0:T(8,128)(2,1)S(1)}) custom-call(bf16[256,1024]{1,0:T(8,128)(2,1)S(1)} %get-tuple-element.161.refs_0_.refs_1_, bf16[256,1024]{1,0:T(8,128)(2,1)S(1)} %collective-permute-done.23.refs_1_.refs_2_, ...), custom_call_target="tpu_custom_call" | custom-call | flops 2147483648 | bytes 9000000 | tf_op jit(solution)/shard_map/mlp/pallas_call | solution.py:93
  116.7 3.9 %collective-permute-done.29.refs_6_.refs_11_ = bf16[512,256]{1,0:T(8,128)(2,1)S(1)} collective-permute-done((bf16[512,256]{1,0:T(8,128)(2,1)S(1)}, bf16[512,256]{1,0:T(8,128)(2,1)S(1)}, u32[]{:S(2)}, u32[]{:S(2)}) %collective-permute-start.29) | collective-permute-done | bytes 262176 | tf_op jit(solution)/shard_map/ppermute | solution.py:1222
  132.5 3.7 %collective-permute-start.35 = (bf16[544,256]{1,0:T(8,128)(2,1)S(1)}, bf16[544,256]{1,0:T(8,128)(2,1)S(1)}, u32[]{:S(2)}, u32[]{:S(2)}) collective-permute-start(bf16[544,256]{1,0:T(8,128)(2,1)S(1)} %get-tuple-element.177.refs_3_.refs_15_), channel_id=1, source_target_pairs={{0,8},{4,12},{8,16},{12,20},{16,24},{20,28},{24,0},{28,4},{1,9},{5... | collective-permute-start | bytes 835592 | tf_op jit(solution)/shard_map/ppermute | solution.py:1222
  136.8 5.7 %query_back.1.refs_3_ = bf16[512,256]{1,0:T(8,128)(2,1)S(1)} custom-call(s32[3]{0:T(128)S(1)} %copy-done.14, s32[32]{0:T(128)S(1)} %copy-done.19, bf16[512,256]{1,0:T(8,128)(2,1)S(1)} %get-tuple-element.154.refs_2_.refs_7_, bf16[544,256]{1,0:T(8,128)(2,1)S(1)} %get-tuple-element.177.refs_3_.refs_15_, f32[2,512,128]{2,1,0:T(8,128)S(1)} %get-tuple-element.178.refs_4_, ...), custom_call_target="tpu_custom_call" | custom-call | flops 2000000000 | bytes 7000000 | tf_op jit(solution)/shard_map/query_back/pallas_call | solution.py:93
  151.3 15.4 %collective-permute-done.37.refs_19_ = bf16[544,256]{1,0:T(8,128)(2,1)S(1)} collective-permute-done((bf16[544,256]{1,0:T(8,128)(2,1)S(1)}, bf16[544,256]{1,0:T(8,128)(2,1)S(1)}, u32[]{:S(2)}, u32[]{:S(2)}) %collective-permute-start.37) | collective-permute-done | bytes 278560 | tf_op jit(solution)/shard_map/ppermute | solution.py:1222
  170.6 4.0 %collective-permute-done.40.refs_22_ = bf16[544,256]{1,0:T(8,128)(2,1)S(1)} collective-permute-done((bf16[544,256]{1,0:T(8,128)(2,1)S(1)}, bf16[544,256]{1,0:T(8,128)(2,1)S(1)}, u32[]{:S(2)}, u32[]{:S(2)}) %collective-permute-start.40) | collective-permute-done | bytes 278560 | tf_op jit(solution)/shard_map/ppermute | solution.py:1222
  177.2 8.5 %key_back.1 = (bf16[512,768]{1,0:T(8,128)(2,1)S(1)}, bf16[256,1024]{1,0:T(8,128)(2,1)S(1)}, bf16[256,1024]{1,0:T(8,128)(2,1)S(1)}) custom-call(s32[3]{0:T(128)S(1)} %copy-done.14, s32[32]{0:T(128)S(1)} %copy-done.19, bf16[512,512]{1,0:T(8,128)(2,1)S(1)} %get-tuple-element.155.refs_3_.refs_6_.refs_2_, bf16[512,256]{1,0:T(8,128)(2,1)S(1)} %query_back.1.refs_3_, ...), custom_call_target="tpu_custom_call" | custom-call | flops 4000000000 | bytes 9000000 | tf_op jit(solution)/shard_map/key_back/pallas_call | solution.py:93
  194.0 3.5 %feature_grads.7 = (bf16[4,128,1024]{2,1,0:T(8,128)(2,1)S(1)}, bf16[4,128,512]{2,1,0:T(8,128)(2,1)S(1)}, bf16[4,128,512]{2,1,0:T(8,128)(2,1)S(1)}) custom-call(s32[3]{0:T(128)S(1)} %copy-done.14, bf16[256,1024]{1,0:T(8,128)(2,1)S(1)} %get-tuple-element.198.refs_0_.refs_1_, bf16[256,1024]{1,0:T(8,128)(2,1)S(1)} %collective-permute-done.6.refs_1_.refs_2_, ...), custom_call_target="tpu_custom_call" | custom-call | flops 1073741824 | bytes 5242880 | tf_op jit(solution)/shard_map/feature_grads/pallas_call | solution.py:93
  197.5 4.2 %collective-permute-done.45.refs_1_ = bf16[2,128,1024]{2,1,0:T(8,128)(2,1)S(1)} collective-permute-done((bf16[2,128,1024]{2,1,0:T(8,128)(2,1)S(1)}, bf16[2,128,1024]{2,1,0:T(8,128)(2,1)S(1)}, u32[]{:S(2)}, u32[]{:S(2)}) %collective-permute-start.45) | collective-permute-done | bytes 524320 | tf_op jit(solution)/shard_map/ppermute | solution.py:1109
  209.3 8.6 %cross_back.1 = (bf16[512,256]{1,0:T(8,128)(2,1)S(1)}, bf16[1024,256]{1,0:T(8,128)(2,1)S(1)}, bf16[1024,256]{1,0:T(8,128)(2,1)S(1)}, bf16[768,1024]{1,0:T(8,128)(2,1)S(1)}, bf16[768,1024]{1,0:T(8,128)(2,1)S(1)}) custom-call(s32[3]{0:T(128)S(1)} %copy-done.14, bf16[256,1024]{1,0:T(8,128)(2,1)S(1)} %get-tuple-element.208.refs_1_.refs_3_, ...), custom_call_target="tpu_custom_call" | custom-call | flops 4000000000 | bytes 12000000 | tf_op jit(solution)/shard_map/cross_back/pallas_call | solution.py:93
  217.9 4.9 %collective-permute-done.49.refs_1_ = bf16[128,1024]{1,0:T(8,128)(2,1)S(1)} collective-permute-done((bf16[128,1024]{1,0:T(8,128)(2,1)S(1)}, bf16[128,1024]{1,0:T(8,128)(2,1)S(1)}, u32[]{:S(2)}, u32[]{:S(2)}) %collective-permute-start.49) | collective-permute-done | bytes 262176 | tf_op jit(solution)/shard_map/ppermute | solution.py:1113
  222.8 3.4 %collective-permute-done.50 = bf16[768,1024]{1,0:T(8,128)(2,1)S(1)} collective-permute-done((bf16[768,1024]{1,0:T(8,128)(2,1)S(1)}, bf16[768,1024]{1,0:T(8,128)(2,1)S(1)}, u32[]{:S(2)}, u32[]{:S(2)}) %collective-permute-start.50) | collective-permute-done | bytes 1572896 | tf_op jit(solution)/shard_map/ppermute | solution.py:1216
  229.6 3.3 %feature_grads.8 = (bf16[4,128,512]{2,1,0:T(8,128)(2,1)S(1)}, bf16[4,128,512]{2,1,0:T(8,128)(2,1)S(1)}) custom-call(s32[3]{0:T(128)S(1)} %copy-done.14, bf16[512,1024]{1,0:T(8,128)(2,1)S(1)} %copy-done.8, bf16[512,256]{1,0:T(8,128)(2,1)S(1)} %get-tuple-element.215.refs_2_, bf16[1024,1024]{1,0:T(8,128)(2,1)S(1)} %copy-done.2, ...), custom_call_target="tpu_custom_call" | custom-call | flops 805306368 | bytes 4980736 | tf_op jit(solution)/shard_map/feature_grads/pallas_call | solution.py:93
  233.0 3.1 %feature_grads.9 = (bf16[4,128,512]{2,1,0:T(8,128)(2,1)S(1)}, bf16[4,128,512]{2,1,0:T(8,128)(2,1)S(1)}) custom-call(s32[3]{0:T(128)S(1)} %copy-done.14, bf16[1024,1024]{1,0:T(8,128)(2,1)S(1)} %copy-done.2, bf16[1024,256]{1,0:T(8,128)(2,1)S(1)} %get-tuple-element.213.refs_2_, bf16[256,1024]{1,0:T(8,128)(2,1)S(1)} %get-tuple-element.208.refs_1_.refs_3_, ...), custom_call_target="tpu_custom_call" | custom-call | flops 805306368 | bytes 4980736 | tf_op jit(solution)/shard_map/feature_grads/pallas_call | solution.py:93
  236.1 6.0 %collective-permute-done.51.refs_1_ = bf16[2,128,1024]{2,1,0:T(8,128)(2,1)S(1)} collective-permute-done((bf16[2,128,1024]{2,1,0:T(8,128)(2,1)S(1)}, bf16[2,128,1024]{2,1,0:T(8,128)(2,1)S(1)}, u32[]{:S(2)}, u32[]{:S(2)}) %collective-permute-start.51) | collective-permute-done | bytes 524320 | tf_op jit(solution)/shard_map/ppermute | solution.py:1109
  248.1 3.8 %gains.1 = f32[8,1024]{1,0:T(8,128)S(1)} custom-call(s32[3]{0:T(128)S(1)} %copy-done.14, s32[32]{0:T(128)S(1)} %copy-done.19, s32[3]{0:T(128)S(1)} %copy-done.20, bf16[768,1024]{1,0:T(8,128)(2,1)S(1)} %get-tuple-element.217.refs_3_, bf16[768,1024]{1,0:T(8,128)(2,1)S(1)} %get-tuple-element.223.refs_4_, bf16[512,1024]{1,0:T(8,128)(2,1)S(1)} %copy-done, ...), custom_call_target="tpu_custom_call" | custom-call | flops 31457280 | bytes 6291456 | tf_op jit(solution)/shard_map/gains/pallas_call | solution.py:93
  253.2 8.0 %collective-permute-done.54.refs_3_.refs_1_ = bf16[128,1024]{1,0:T(8,128)(2,1)S(1)} collective-permute-done((bf16[128,1024]{1,0:T(8,128)(2,1)S(1)}, bf16[128,1024]{1,0:T(8,128)(2,1)S(1)}, u32[]{:S(2)}, u32[]{:S(2)}) %collective-permute-start.54) | collective-permute-done | bytes 262176 | tf_op jit(solution)/shard_map/ppermute | solution.py:1113
  266.4 4.5 %final_norm.1 = (bf16[768,1024]{1,0:T(8,128)(2,1)S(1)}, bf16[512,1024]{1,0:T(8,128)(2,1)}, bf16[1024,1024]{1,0:T(8,128)(2,1)}) custom-call(s32[3]{0:T(128)S(1)} %copy-done.14, bf16[768,1024]{1,0:T(8,128)(2,1)S(1)} %add_convert_fusion.refs_5_.refs_1_, bf16[768,1024]{1,0:T(8,128)(2,1)S(1)} %collective-permute-done.59.refs_2_, bf16[512,1024]{1,0:T(8,128)(2,1)S(1)} %copy-done, ...), custom_call_target="tpu_custom_call" | custom-call | flops 15728640 | bytes 6291456 | tf_op jit(solution)/shard_map/final_norm/pallas_call | solution.py:93
  282.3 7.9 %collective-permute-done.64 = f32[8,1024]{1,0:T(8,128)S(1)} collective-permute-done((f32[8,1024]{1,0:T(8,128)S(1)}, f32[8,1024]{1,0:T(8,128)S(1)}, u32[]{:S(2)}, u32[]{:S(2)}) %collective-permute-start.64) | collective-permute-done | bytes 32800 | tf_op jit(solution)/shard_map/ppermute | solution.py:1302
  292.7 3.4 %collective-permute-done.66 = f32[8,1024]{1,0:T(8,128)S(1)} collective-permute-done((f32[8,1024]{1,0:T(8,128)S(1)}, f32[8,1024]{1,0:T(8,128)S(1)}, u32[]{:S(2)}, u32[]{:S(2)}) %collective-permute-start.66) | collective-permute-done | bytes 32800 | tf_op jit(solution)/shard_map/ppermute | solution.py:1302
  301.8 3.3 %collective-permute-done.68.refs_1_ = bf16[128,512]{1,0:T(8,128)(2,1)S(1)} collective-permute-done((bf16[128,512]{1,0:T(8,128)(2,1)S(1)}, bf16[128,512]{1,0:T(8,128)(2,1)S(1)}, u32[]{:S(2)}, u32[]{:S(2)}) %collective-permute-start.68) | collective-permute-done | bytes 131104 | tf_op jit(solution)/shard_map/ppermute | solution.py:1113
  (221 shorter events, 118.9 us)
Async XLA Ops:
  0.7 15.2 %collective-permute-start = (bf16[256,1024]{1,0:T(8,128)(2,1)}, bf16[256,1024]{1,0:T(8,128)(2,1)S(1)}, u32[]{:S(2)}, u32[]{:S(2)}) collective-permute-start(bf16[256,1024]{1,0:T(8,128)(2,1)} %refs_3_.6), channel_id=1, source_target_pairs={{0,2},{1,3},{2,0},{3,1},{4,6},{5,7},{6,4},{7,5},{8,10},{9,11},{10,... | collective-permute-start | bytes 1572872 | tf_op jit(solution)/shard_map/ppermute | solution.py:1216
  30.8 16.1 %collective-permute-start.8 = (bf16[512,512]{1,0:T(8,128)(2,1)S(1)}, bf16[512,512]{1,0:T(8,128)(2,1)S(1)}, u32[]{:S(2)}, u32[]{:S(2)}) collective-permute-start(bf16[512,512]{1,0:T(8,128)(2,1)S(1)} %get-tuple-element.155.refs_3_.refs_6_.refs_2_), channel_id=1, source_target_pairs={{0,8},{4,12},{8,16},{12,20},{16,24},{20,28},{24,0},{28,4},{1,9},{5... | collective-permute-start | bytes 1572872 | tf_op jit(solution)/shard_map/ppermute | solution.py:1222
  32.7 14.2 %collective-permute-start.15 = (bf16[256,1024]{1,0:T(8,128)(2,1)S(1)}, bf16[256,1024]{1,0:T(8,128)(2,1)S(1)}, u32[]{:S(2)}, u32[]{:S(2)}) collective-permute-start(bf16[256,1024]{1,0:T(8,128)(2,1)S(1)} %copy-done.5), channel_id=1, source_target_pairs={{0,2},{1,3},{2,0},{3,1},{4,6},{5,7},{6,4},{7,5},{8,10},{9,11},{10,... | collective-permute-start | bytes 1572872 | tf_op jit(solution)/shard_map/ppermute | solution.py:1216
  34.2 16.6 %collective-permute-start.14 = (bf16[256,1024]{1,0:T(8,128)(2,1)S(1)}, bf16[256,1024]{1,0:T(8,128)(2,1)S(1)}, u32[]{:S(2)}, u32[]{:S(2)}) collective-permute-start(bf16[256,1024]{1,0:T(8,128)(2,1)S(1)} %copy-done.5), channel_id=1, source_target_pairs={{0,1},{1,0},{2,3},{3,2},{4,5},{5,4},{6,7},{7,6},{8,9},{9,8},{10,11... | collective-permute-start | bytes 1572872 | tf_op jit(solution)/shard_map/ppermute | solution.py:1216
  34.2 18.1 %collective-permute-start.7 = (bf16[512,512]{1,0:T(8,128)(2,1)S(1)}, bf16[512,512]{1,0:T(8,128)(2,1)S(1)}, u32[]{:S(2)}, u32[]{:S(2)}) collective-permute-start(bf16[512,512]{1,0:T(8,128)(2,1)S(1)} %get-tuple-element.155.refs_3_.refs_6_.refs_2_), channel_id=1, source_target_pairs={{0,4},{4,0},{8,12},{12,8},{16,20},{20,16},{24,28},{28,24},{1,5},{5... | collective-permute-start | bytes 1572872 | tf_op jit(solution)/shard_map/ppermute | solution.py:1222
  46.9 16.6 %collective-permute-start.10 = (bf16[512,512]{1,0:T(8,128)(2,1)S(1)}, bf16[512,512]{1,0:T(8,128)(2,1)S(1)}, u32[]{:S(2)}, u32[]{:S(2)}) collective-permute-start(bf16[512,512]{1,0:T(8,128)(2,1)S(1)} %collective-permute-done.8.refs_5_.refs_8_), channel_id=1, source_target_pairs={{0,8},{4,12},{8,16},{12,20},{16,24},{20,28},{24,0},{28,4},{1,9},{5... | collective-permute-start | bytes 1572872 | tf_op jit(solution)/shard_map/ppermute | solution.py:1222
  46.9 18.2 %collective-permute-start.16 = (bf16[256,1024]{1,0:T(8,128)(2,1)S(1)}, bf16[256,1024]{1,0:T(8,128)(2,1)S(1)}, u32[]{:S(2)}, u32[]{:S(2)}) collective-permute-start(bf16[256,1024]{1,0:T(8,128)(2,1)S(1)} %collective-permute-done.15.refs_13_.refs_7_), channel_id=1, source_target_pairs={{0,1},{1,0},{2,3},{3,2},{4,5},{5,4},{6,7},{7,6},{8,9},{9,8},{10,11... | collective-permute-start | bytes 1572872 | tf_op jit(solution)/shard_map/ppermute | solution.py:1216
  46.9 26.0 %collective-permute-start.9 = (bf16[512,512]{1,0:T(8,128)(2,1)S(1)}, bf16[512,512]{1,0:T(8,128)(2,1)S(1)}, u32[]{:S(2)}, u32[]{:S(2)}) collective-permute-start(bf16[512,512]{1,0:T(8,128)(2,1)S(1)} %get-tuple-element.155.refs_3_.refs_6_.refs_2_), channel_id=1, source_target_pairs={{0,24},{4,28},{8,0},{12,4},{16,8},{20,12},{24,16},{28,20},{1,25},{... | collective-permute-start | bytes 1572872 | tf_op jit(solution)/shard_map/ppermute | solution.py:1222
  50.8 23.3 %collective-permute-start.11 = (bf16[512,512]{1,0:T(8,128)(2,1)S(1)}, bf16[512,512]{1,0:T(8,128)(2,1)S(1)}, u32[]{:S(2)}, u32[]{:S(2)}) collective-permute-start(bf16[512,512]{1,0:T(8,128)(2,1)S(1)} %collective-permute-done.8.refs_5_.refs_8_), channel_id=1, source_target_pairs={{0,4},{4,0},{8,12},{12,8},{16,20},{20,16},{24,28},{28,24},{1,5},{5... | collective-permute-start | bytes 1572872 | tf_op jit(solution)/shard_map/ppermute | solution.py:1222
  52.3 31.9 %collective-permute-start.12 = (bf16[512,512]{1,0:T(8,128)(2,1)S(1)}, bf16[512,512]{1,0:T(8,128)(2,1)S(1)}, u32[]{:S(2)}, u32[]{:S(2)}) collective-permute-start(bf16[512,512]{1,0:T(8,128)(2,1)S(1)} %collective-permute-done.7.refs_4_.refs_7_), channel_id=1, source_target_pairs={{0,24},{4,28},{8,0},{12,4},{16,8},{20,12},{24,16},{28,20},{1,25},{... | collective-permute-start | bytes 1572872 | tf_op jit(solution)/shard_map/ppermute | solution.py:1222
  63.6 20.6 %collective-permute-start.13 = (bf16[512,512]{1,0:T(8,128)(2,1)S(1)}, bf16[512,512]{1,0:T(8,128)(2,1)S(1)}, u32[]{:S(2)}, u32[]{:S(2)}) collective-permute-start(bf16[512,512]{1,0:T(8,128)(2,1)S(1)} %collective-permute-done.10.refs_7_.refs_10_), channel_id=1, source_target_pairs={{0,4},{4,0},{8,12},{12,8},{16,20},{20,16},{24,28},{28,24},{1,5},{5... | collective-permute-start | bytes 1572872 | tf_op jit(solution)/shard_map/ppermute | solution.py:1222
  65.1 28.6 %collective-permute-start.22 = (bf16[512,256]{1,0:T(8,128)(2,1)S(1)}, bf16[512,256]{1,0:T(8,128)(2,1)S(1)}, u32[]{:S(2)}, u32[]{:S(2)}) collective-permute-start(bf16[512,256]{1,0:T(8,128)(2,1)S(1)} %get-tuple-element.154.refs_2_.refs_7_), channel_id=1, source_target_pairs={{0,24},{4,28},{8,0},{12,4},{16,8},{20,12},{24,16},{28,20},{1,25},{... | collective-permute-start | bytes 786440 | tf_op jit(solution)/shard_map/ppermute | solution.py:1222
  73.0 23.0 %collective-permute-start.21 = (bf16[512,256]{1,0:T(8,128)(2,1)S(1)}, bf16[512,256]{1,0:T(8,128)(2,1)S(1)}, u32[]{:S(2)}, u32[]{:S(2)}) collective-permute-start(bf16[512,256]{1,0:T(8,128)(2,1)S(1)} %get-tuple-element.154.refs_2_.refs_7_), channel_id=1, source_target_pairs={{0,8},{4,12},{8,16},{12,20},{16,24},{20,28},{24,0},{28,4},{1,9},{5... | collective-permute-start | bytes 786440 | tf_op jit(solution)/shard_map/ppermute | solution.py:1222
  74.1 21.9 %collective-permute-start.20 = (bf16[512,256]{1,0:T(8,128)(2,1)S(1)}, bf16[512,256]{1,0:T(8,128)(2,1)S(1)}, u32[]{:S(2)}, u32[]{:S(2)}) collective-permute-start(bf16[512,256]{1,0:T(8,128)(2,1)S(1)} %get-tuple-element.154.refs_2_.refs_7_), channel_id=1, source_target_pairs={{0,4},{4,0},{8,12},{12,8},{16,20},{20,16},{24,28},{28,24},{1,5},{5... | collective-permute-start | bytes 786440 | tf_op jit(solution)/shard_map/ppermute | solution.py:1222
  111.4 17.5 %collective-permute-start.28 = (bf16[256,1024]{1,0:T(8,128)(2,1)S(1)}, bf16[256,1024]{1,0:T(8,128)(2,1)S(1)}, u32[]{:S(2)}, u32[]{:S(2)}) collective-permute-start(bf16[256,1024]{1,0:T(8,128)(2,1)S(1)} %add_convert_fusion.3.refs_4_.refs_2_.refs_0_), channel_id=1, source_target_pairs={{0,2},{1,3},{2,0},{3,1},{4,6},{5,7},{6,4},{7,5},{8,10},{9,11},{10,... | collective-permute-start | bytes 1572872 | tf_op jit(solution)/shard_map/ppermute | solution.py:1216
  112.9 16.0 %collective-permute-start.30 = (bf16[512,256]{1,0:T(8,128)(2,1)S(1)}, bf16[512,256]{1,0:T(8,128)(2,1)S(1)}, u32[]{:S(2)}, u32[]{:S(2)}) collective-permute-start(bf16[512,256]{1,0:T(8,128)(2,1)S(1)} %collective-permute-done.21.refs_12_.refs_9_), channel_id=1, source_target_pairs={{0,4},{4,0},{8,12},{12,8},{16,20},{20,16},{24,28},{28,24},{1,5},{5... | collective-permute-start | bytes 786440 | tf_op jit(solution)/shard_map/ppermute | solution.py:1222
  114.4 14.6 %collective-permute-start.31 = (bf16[512,256]{1,0:T(8,128)(2,1)S(1)}, bf16[512,256]{1,0:T(8,128)(2,1)S(1)}, u32[]{:S(2)}, u32[]{:S(2)}) collective-permute-start(bf16[512,256]{1,0:T(8,128)(2,1)S(1)} %collective-permute-done.20.refs_11_.refs_8_), channel_id=1, source_target_pairs={{0,24},{4,28},{8,0},{12,4},{16,8},{20,12},{24,16},{28,20},{1,25},{... | collective-permute-start | bytes 786440 | tf_op jit(solution)/shard_map/ppermute | solution.py:1222
  144.7 25.2 %collective-permute-start.41 = (bf16[4,128,1024]{2,1,0:T(8,128)(2,1)S(1)}, bf16[4,128,1024]{2,1,0:T(8,128)(2,1)S(1)}, u32[]{:S(2)}, u32[]{:S(2)}) collective-permute-start(bf16[4,128,1024]{2,1,0:T(8,128)(2,1)S(1)} %get-tuple-element.188), channel_id=1, source_target_pairs={{0,4},{4,0},{8,12},{12,8},{16,20},{20,16},{24,28},{28,24},{1,5},{5... | collective-permute-start | bytes 3145736 | tf_op jit(solution)/shard_map/ppermute | solution.py:1105
  145.2 21.5 %collective-permute-start.39 = (bf16[544,256]{1,0:T(8,128)(2,1)S(1)}, bf16[544,256]{1,0:T(8,128)(2,1)S(1)}, u32[]{:S(2)}, u32[]{:S(2)}) collective-permute-start(bf16[544,256]{1,0:T(8,128)(2,1)S(1)} %collective-permute-done.34.refs_16_), channel_id=1, source_target_pairs={{0,8},{4,12},{8,16},{12,20},{16,24},{20,28},{24,0},{28,4},{1,9},{5... | collective-permute-start | bytes 835592 | tf_op jit(solution)/shard_map/ppermute | solution.py:1222
  147.7 19.0 %collective-permute-start.38 = (bf16[544,256]{1,0:T(8,128)(2,1)S(1)}, bf16[544,256]{1,0:T(8,128)(2,1)S(1)}, u32[]{:S(2)}, u32[]{:S(2)}) collective-permute-start(bf16[544,256]{1,0:T(8,128)(2,1)S(1)} %collective-permute-done.34.refs_16_), channel_id=1, source_target_pairs={{0,24},{4,28},{8,0},{12,4},{16,8},{20,12},{24,16},{28,20},{1,25},{... | collective-permute-start | bytes 835592 | tf_op jit(solution)/shard_map/ppermute | solution.py:1222
  149.0 17.6 %collective-permute-start.37 = (bf16[544,256]{1,0:T(8,128)(2,1)S(1)}, bf16[544,256]{1,0:T(8,128)(2,1)S(1)}, u32[]{:S(2)}, u32[]{:S(2)}) collective-permute-start(bf16[544,256]{1,0:T(8,128)(2,1)S(1)} %collective-permute-done.35.refs_17_), channel_id=1, source_target_pairs={{0,8},{4,12},{8,16},{12,20},{16,24},{20,28},{24,0},{28,4},{1,9},{5... | collective-permute-start | bytes 835592 | tf_op jit(solution)/shard_map/ppermute | solution.py:1222
  149.9 25.8 %collective-permute-start.26 = (bf16[256,1024]{1,0:T(8,128)(2,1)S(1)}, bf16[256,1024]{1,0:T(8,128)(2,1)S(1)}, u32[]{:S(2)}, u32[]{:S(2)}) collective-permute-start(bf16[256,1024]{1,0:T(8,128)(2,1)S(1)} %add_convert_fusion.2.refs_1_), channel_id=1, source_target_pairs={{0,2},{1,3},{2,0},{3,1},{4,6},{5,7},{6,4},{7,5},{8,10},{9,11},{10,... | collective-permute-start | bytes 1572872 | tf_op jit(solution)/shard_map/ppermute | solution.py:1216
  187.6 14.1 %collective-permute-start.45 = (bf16[2,128,1024]{2,1,0:T(8,128)(2,1)S(1)}, bf16[2,128,1024]{2,1,0:T(8,128)(2,1)S(1)}, u32[]{:S(2)}, u32[]{:S(2)}) collective-permute-start(bf16[2,128,1024]{2,1,0:T(8,128)(2,1)S(1)} %get-tuple-element.202), channel_id=1, source_target_pairs={{0,8},{4,12},{8,0},{12,4},{16,24},{20,28},{24,16},{28,20},{1,9},{5... | collective-permute-start | bytes 1572872 | tf_op jit(solution)/shard_map/ppermute | solution.py:1109
  189.6 13.6 %collective-permute-start.46 = (bf16[4,128,512]{2,1,0:T(8,128)(2,1)S(1)}, bf16[4,128,512]{2,1,0:T(8,128)(2,1)S(1)}, u32[]{:S(2)}, u32[]{:S(2)}) collective-permute-start(bf16[4,128,512]{2,1,0:T(8,128)(2,1)S(1)} %get-tuple-element.205), channel_id=1, source_target_pairs={{0,4},{4,0},{8,12},{12,8},{16,20},{20,16},{24,28},{28,24},{1,5},{5... | collective-permute-start | bytes 1572872 | tf_op jit(solution)/shard_map/ppermute | solution.py:1105
  207.4 15.4 %collective-permute-start.48 = (bf16[4,128,512]{2,1,0:T(8,128)(2,1)S(1)}, bf16[4,128,512]{2,1,0:T(8,128)(2,1)S(1)}, u32[]{:S(2)}, u32[]{:S(2)}) collective-permute-start(bf16[4,128,512]{2,1,0:T(8,128)(2,1)S(1)} %get-tuple-element.221), channel_id=1, source_target_pairs={{0,4},{4,0},{8,12},{12,8},{16,20},{20,16},{24,28},{28,24},{1,5},{5... | collective-permute-start | bytes 1572872 | tf_op jit(solution)/shard_map/ppermute | solution.py:1105
  208.2 14.6 %collective-permute-start.49 = (bf16[128,1024]{1,0:T(8,128)(2,1)S(1)}, bf16[128,1024]{1,0:T(8,128)(2,1)S(1)}, u32[]{:S(2)}, u32[]{:S(2)}) collective-permute-start(bf16[128,1024]{1,0:T(8,128)(2,1)S(1)} %get-tuple-element.222.refs_4_), channel_id=1, source_target_pairs={{0,16},{4,20},{8,24},{12,28},{16,0},{20,4},{24,8},{28,12},{1,17},{... | collective-permute-start | bytes 786440 | tf_op jit(solution)/shard_map/ppermute | solution.py:1113
  226.9 39.4 %collective-permute-start.59 = (bf16[768,1024]{1,0:T(8,128)(2,1)S(1)}, bf16[768,1024]{1,0:T(8,128)(2,1)S(1)}, u32[]{:S(2)}, u32[]{:S(2)}) collective-permute-start(bf16[768,1024]{1,0:T(8,128)(2,1)S(1)} %add_convert_fusion.refs_5_.refs_1_), channel_id=1, source_target_pairs={{0,2},{1,3},{2,0},{3,1},{4,6},{5,7},{6,4},{7,5},{8,10},{9,11},{10,... | collective-permute-start | bytes 4718600 | tf_op jit(solution)/shard_map/ppermute | solution.py:1216
  228.4 13.7 %collective-permute-start.51 = (bf16[2,128,1024]{2,1,0:T(8,128)(2,1)S(1)}, bf16[2,128,1024]{2,1,0:T(8,128)(2,1)S(1)}, u32[]{:S(2)}, u32[]{:S(2)}) collective-permute-start(bf16[2,128,1024]{2,1,0:T(8,128)(2,1)S(1)} %get-tuple-element.228), channel_id=1, source_target_pairs={{0,8},{4,12},{8,0},{12,4},{16,24},{20,28},{24,16},{28,20},{1,9},{5... | collective-permute-start | bytes 1572872 | tf_op jit(solution)/shard_map/ppermute | solution.py:1109
  228.4 13.8 %collective-permute-start.52 = (bf16[4,128,512]{2,1,0:T(8,128)(2,1)S(1)}, bf16[4,128,512]{2,1,0:T(8,128)(2,1)S(1)}, u32[]{:S(2)}, u32[]{:S(2)}) collective-permute-start(bf16[4,128,512]{2,1,0:T(8,128)(2,1)S(1)} %get-tuple-element.231), channel_id=1, source_target_pairs={{0,4},{4,0},{8,12},{12,8},{16,20},{20,16},{24,28},{28,24},{1,5},{5... | collective-permute-start | bytes 1572872 | tf_op jit(solution)/shard_map/ppermute | solution.py:1105
  243.1 18.2 %collective-permute-start.53 = (bf16[4,128,512]{2,1,0:T(8,128)(2,1)S(1)}, bf16[4,128,512]{2,1,0:T(8,128)(2,1)S(1)}, u32[]{:S(2)}, u32[]{:S(2)}) collective-permute-start(bf16[4,128,512]{2,1,0:T(8,128)(2,1)S(1)} %get-tuple-element.234.refs_10_), channel_id=1, source_target_pairs={{0,4},{4,0},{8,12},{12,8},{16,20},{20,16},{24,28},{28,24},{1,5},{5... | collective-permute-start | bytes 1572872 | tf_op jit(solution)/shard_map/ppermute | solution.py:1105
  244.3 18.2 %collective-permute-start.56 = (bf16[2,128,1024]{2,1,0:T(8,128)(2,1)S(1)}, bf16[2,128,1024]{2,1,0:T(8,128)(2,1)S(1)}, u32[]{:S(2)}, u32[]{:S(2)}) collective-permute-start(bf16[2,128,1024]{2,1,0:T(8,128)(2,1)S(1)} %get-tuple-element.239.refs_2_), channel_id=1, source_target_pairs={{0,8},{4,12},{8,0},{12,4},{16,24},{20,28},{24,16},{28,20},{1,9},{5... | collective-permute-start | bytes 1572872 | tf_op jit(solution)/shard_map/ppermute | solution.py:1109
  245.9 15.3 %collective-permute-start.54 = (bf16[128,1024]{1,0:T(8,128)(2,1)S(1)}, bf16[128,1024]{1,0:T(8,128)(2,1)S(1)}, u32[]{:S(2)}, u32[]{:S(2)}) collective-permute-start(bf16[128,1024]{1,0:T(8,128)(2,1)S(1)} %get-tuple-element.235), channel_id=1, source_target_pairs={{0,16},{4,20},{8,24},{12,28},{16,0},{20,4},{24,8},{28,12},{1,17},{... | collective-permute-start | bytes 786440 | tf_op jit(solution)/shard_map/ppermute | solution.py:1113
  (69 other events, 669.4 us)

commit v5 on v4

--- a/solution.py
+++ b/solution.py
@@ -123,7 +123,7 @@
 
 def cross_forward_body(
     pos_ref, idx_ref, lat_ref, src_ref, gain_one_ref, gain_src_ref, wq_ref, wk_ref, wv_ref,
-    n1_ref, ns_ref, q_ref, kvp_ref, keep_ref, send_ref, kv_s, *, steps,
+    n1_ref, ns_ref, q_ref, kvp_ref, keep_ref, send_ref, kv_s, picks_s, *, steps,
 ):
     i = pl.program_id(0)
     width = wq_ref.shape[1]
@@ -149,7 +149,8 @@
                 column = jnp.transpose(jnp.broadcast_to(row, (128, 128)))
                 picks = jnp.where(jnp.tile(column, (1, count // 128)) == lanes, 1.0, 0.0).astype(bf16)
                 r0 = b * SRC + part * 128
-                kvp_ref[r0 : r0 + 128, :] = dot(picks, kv_s[...]).astype(bf16)
+                picks_s[r0 : r0 + 128, :] = picks
+        kvp_ref[...] = dot(picks_s[...], kv_s[...]).astype(bf16)
         for b in range(steps):
             for h in range(heads):
                 cols = slice(h * HEAD, (h + 1) * HEAD)
@@ -196,7 +197,7 @@
         ],
         (pos, idx, latents, sources, gain_one, gain_src, wq, wk, wv),
         "cross_forward",
-        scratch=[pltpu.VMEM((count, 2 * width), bf16)],
+        scratch=[pltpu.VMEM((count, 2 * width), bf16), pltpu.VMEM((count, count), bf16)],
         grid=(steps,),
         prefetch=1,
         flops=4e9,
@@ -598,7 +599,7 @@
     i = pl.program_id(0)
     x = jnp.where(i < steps // 2, mine_ref[...], other_ref[...])
     units = win_ref.shape[1]
-    chunk = 256
+    chunk = 512
     total = None
     for n in range(units // chunk):
         cols = slice(n * chunk, (n + 1) * chunk)
@@ -625,26 +626,27 @@
 def mlp(mine, other, w_in, act_grad):
     half, width_d = mine.shape
     units = w_in.shape[1]
-    steps = 2 * half // GROUP
+    steps = 2
     rows = 2 * half
     low = lambda i: (jnp.minimum(i, steps // 2 - 1), 0)
     high = lambda i: (jnp.maximum(i - steps // 2, 0), 0)
     return call(
         functools.partial(mlp_body, steps=steps),
         [
-            (sds((rows, units), bf16), pl.BlockSpec((GROUP, units), lambda i: (i, 0))),
-            (sds((rows, units), bf16), pl.BlockSpec((GROUP, units), lambda i: (i, 0))),
-            (sds((half, width_d), bf16), pl.BlockSpec((GROUP, width_d), low)),
-            (sds((half, width_d), bf16), pl.BlockSpec((GROUP, width_d), high)),
+            (sds((rows, units), bf16), pl.BlockSpec((half, units), lambda i: (i, 0))),
+            (sds((rows, units), bf16), pl.BlockSpec((half, units), lambda i: (i, 0))),
+            (sds((half, width_d), bf16), pl.BlockSpec((half, width_d), low)),
+            (sds((half, width_d), bf16), pl.BlockSpec((half, width_d), high)),
         ],
         [
-            pl.BlockSpec((GROUP, width_d), low),
-            pl.BlockSpec((GROUP, width_d), high),
+            pl.BlockSpec((half, width_d), low),
+            pl.BlockSpec((half, width_d), high),
             pl.BlockSpec((width_d, units), lambda i: (0, 0)),
-            pl.BlockSpec((GROUP, units), lambda i: (i, 0)),
+            pl.BlockSpec((half, units), lambda i: (i, 0)),
         ],
         (mine, other, w_in, act_grad),
         "mlp",
+        spare=10,
         grid=(steps,),
         flops=4 * rows * width_d * units,
         nbytes=9e6,
@@ -668,16 +670,17 @@
 def mlp_down(activated, w_out, ties):
     rows, units = activated.shape
     width_d = w_out.shape[1]
-    steps = rows // GROUP
-    half = sds((rows // 2, width_d), bf16)
+    steps = 2
+    blk = rows // steps
+    half = sds((blk, width_d), bf16)
     return call(
         functools.partial(mlp_down_body, steps=steps),
         [
-            (half, pl.BlockSpec((GROUP, width_d), lambda i: (jnp.minimum(i, steps // 2 - 1), 0))),
-            (half, pl.BlockSpec((GROUP, width_d), lambda i: (jnp.maximum(i - steps // 2, 0), 0))),
+            (half, pl.BlockSpec((blk, width_d), lambda i: (jnp.minimum(i, steps // 2 - 1), 0))),
+            (half, pl.BlockSpec((blk, width_d), lambda i: (jnp.maximum(i - steps // 2, 0), 0))),
         ],
         [
-            pl.BlockSpec((GROUP, units), lambda i: (i, 0)),
+            pl.BlockSpec((blk, units), lambda i: (i, 0)),
             pl.BlockSpec((units, width_d), lambda i: (0, 0)),
         ],
         (activated, w_out),
@@ -1129,23 +1132,23 @@
 
 def cross_back_body(
     pos_ref, mine_ref, other_ref, wo_ref, q_ref, kvp_ref, idx_ref, wq_ref, wk_ref, wv_ref,
-    dq_ref, dk_ref, dv_ref, keep_ref, send_ref, dkvp_s, *, blocks,
+    dq_ref, dk_ref, dv_ref, keep_ref, send_ref, dkvp_s, grad_s, *, blocks,
 ):
     width = wq_ref.shape[1]
     heads = width // HEAD
     count = kvp_ref.shape[0]
     scale = HEAD ** (-0.5)
+    rows = blocks * GROUP
+    for part, ref in enumerate((mine_ref, other_ref)):
+        grad_s[part * rows // 2 : (part + 1) * rows // 2, :] = dot_t(ref[...], wo_ref[...]).astype(bf16)
     for b in range(blocks):
-        ref = mine_ref if b < blocks // 2 else other_ref
-        part = (b % (blocks // 2)) * GROUP
-        grad = dot_t(ref[part : part + GROUP, :], wo_ref[...]).astype(bf16)
         for h in range(heads):
             cols = slice(h * HEAD, (h + 1) * HEAD)
             vcols = slice(width + h * HEAD, width + (h + 1) * HEAD)
             q = q_ref[b * GROUP : (b + 1) * GROUP, cols]
             k = kvp_ref[b * SRC : (b + 1) * SRC, cols]
             v = kvp_ref[b * SRC : (b + 1) * SRC, vcols]
-            do = grad[:, cols]
+            do = grad_s[b * GROUP : (b + 1) * GROUP, cols]
             s = dot_t(q, k) * (scale * LOG2E)
             p = jnp.exp2(s - jnp.max(s, axis=-1, keepdims=True))
             p = p / jnp.sum(p, axis=-1, keepdims=True)
@@ -1155,29 +1158,20 @@
             dq_ref[b * GROUP : (b + 1) * GROUP, cols] = dot(ds, k).astype(bf16)
             dkvp_s[b * SRC : (b + 1) * SRC, cols] = dot_ta(ds, q).astype(bf16)
             dkvp_s[b * SRC : (b + 1) * SRC, vcols] = dot_ta(p.astype(bf16), do).astype(bf16)
-        one = dot_t(dq_ref[b * GROUP : (b + 1) * GROUP, :], wq_ref[...]).astype(bf16)
-        if b < blocks // 2:
-            keep_ref[part : part + GROUP, :] = one
-        else:
-            send_ref[part : part + GROUP, :] = one
+    one = dot_t(dq_ref[...], wq_ref[...]).astype(bf16)
+    keep_ref[0 : rows // 2, :] = one[0 : rows // 2]
+    send_ref[0 : rows // 2, :] = one[rows // 2 :]
     half = count // 2
-    blk = 256
     row = jnp.concatenate([index_row(idx_ref, pos_ref, b, blocks, count) for b in range(blocks)], axis=1)
-    for n in range(count // blk):
-        r0 = pl.multiple_of(
-            (pos_ref[0] if n * blk < half else 1 - pos_ref[0]) * half + (n * blk) % half, blk
-        )
-        wanted = lax.broadcasted_iota(jnp.int32, (blk, count), 0).astype(f32) + r0.astype(f32)
+    for part, ref in enumerate((keep_ref, send_ref)):
+        r0 = pl.multiple_of((pos_ref[0] if part == 0 else 1 - pos_ref[0]) * half, half)
+        wanted = lax.broadcasted_iota(jnp.int32, (half, count), 0).astype(f32) + r0.astype(f32)
         picks = jnp.where(row == wanted, 1.0, 0.0).astype(bf16)
         dkv = dot(picks, dkvp_s[...]).astype(bf16)
-        dk_ref[pl.ds(r0, blk), :] = dkv[:, 0:width]
-        dv_ref[pl.ds(r0, blk), :] = dkv[:, width:]
-        total = (dot_t(dkv[:, 0:width], wk_ref[...]) + dot_t(dkv[:, width:], wv_ref[...])).astype(bf16)
-        at = blocks // 2 * GROUP + (n * blk) % half
-        if n * blk < half:
-            keep_ref[at : at + blk, :] = total
-        else:
-            send_ref[at : at + blk, :] = total
+        dk_ref[pl.ds(r0, half), :] = dkv[:, 0:width]
+        dv_ref[pl.ds(r0, half), :] = dkv[:, width:]
+        total = dot_t(dkv[:, 0:width], wk_ref[...]) + dot_t(dkv[:, width:], wv_ref[...])
+        ref[rows // 2 :, :] = total.astype(bf16)
 
 
 def cross_back(pos, mine, other, wo, q, kvp, idx, wq, wk, wv, ties):
@@ -1198,7 +1192,8 @@
         (pos, mine, other, wo, q, kvp, idx, wq, wk, wv),
         "cross_back",
         ties=ties,
-        scratch=[pltpu.VMEM((count, 2 * width), bf16)],
+        scratch=[pltpu.VMEM((count, 2 * width), bf16), pltpu.VMEM((rows, width), bf16)],
+        spare=14,
         flops=4e9,
         nbytes=12e6,
     )
@@ -1410,8 +1405,9 @@
         pos, cross_branch, cross_branch_other, cross_o, cross_query, cross_kv, source_index,
         cross_q, cross_k, cross_v, (),
     )
-    first_items = (((normed_one,), (cross_query_grad,)), ((normed_src,), (cross_key_grad,)))
-    second_items = (
+    cross_items = (
+        ((normed_one,), (cross_query_grad,)),
+        ((normed_src,), (cross_key_grad,)),
         ((normed_src,), (cross_value_grad,)),
         ((cross_branch, cross_branch_other), (mixed_keep, mixed_send)),
     )
@@ -1429,53 +1425,39 @@
         self_got_b = flip_x(self_send_b)
         out_got = near_z(out_send)
         both_sum, both_got = half_sum(both_keep, both_send)
-        first_keep, first_send = feature_grads(pos, first_items, 1, (both_sum,))
-        second_keep, second_send = feature_grads(pos, second_items, 1, (first_keep,))
-        out_own, out_send = stage_two(out_keep, out_got, (second_keep,))
+        cross_wkeep, cross_wsend = feature_grads(pos, cross_items, 1, (both_sum,))
+        out_own, out_send = stage_two(out_keep, out_got, (cross_wkeep,))
         self_wkeep, self_wsend = stage_one(pos, self_wkeep, [self_got_a, self_got_b], (out_own,))
 
-        first_send, out_send, self_wsend = lax.optimization_barrier((first_send, out_send, self_wsend))
-        first_got = flip_x(first_send)
+        cross_wsend, out_send, self_wsend = lax.optimization_barrier((cross_wsend, out_send, self_wsend))
+        cross_wgot = flip_x(cross_wsend)
         out_got = far_z(out_send)
         self_wgot = near_z(self_wsend)
         mlp_outs = stage_end(in_own, in_got, 1, (), (self_wsend,))
-        small = gains_of((first_send, mlp_outs[0]))
-        small = sum_over(small, "tensor", 1)
-        first_keep, first_send = stage_one(pos, first_keep, [first_got], (out_got, small))
-        self_own, self_wsend = stage_two(self_wkeep, self_wgot, (first_keep,))
-
-        second_send, first_send, self_wsend, small = lax.optimization_barrier(
-            (second_send, first_send, self_wsend, small)
-        )
-        second_got = flip_x(second_send)
-        first_got = near_z(first_send)
+        small = gains_of((cross_wsend, mlp_outs[0]))
+        small = sum_over(sum_over(small, "tensor", 1), "seq", 1)
+        self_own, self_wsend = stage_two(self_wkeep, self_wgot, (out_got, small))
         self_wgot = far_z(self_wsend)
+        cross_wkeep, cross_wsend = stage_one(pos, cross_wkeep, [cross_wgot], (self_wsend,))
+
+        cross_wsend, small = lax.optimization_barrier((cross_wsend, small))
+        cross_wgot = near_z(cross_wsend)
         both_half, lat_whole, src_whole = final_of(())
         mlp_outs = [*mlp_outs, stage_end(out_own, out_got, 1, (0,), (both_half,))[0]]
         small, both_half = lax.optimization_barrier((small, both_half))
-        small = sum_over(small, "seq", 1)
-        second_keep, second_send = stage_one(pos, second_keep, [second_got], (self_wgot, small, mlp_outs[1]))
-        first_own, first_send = stage_two(first_keep, first_got, (second_keep,))
-
-        second_send, first_send, small, both_half = lax.optimization_barrier(
-            (second_send, first_send, small, both_half)
-        )
-        second_got = near_z(second_send)
-        first_got = far_z(first_send)
-        small = sum_over(small, "seq", 2)
-        both_other = tensor_swap(both_half, 1)
-        self_outs = stage_end(self_own, self_wgot, 4, (3,), (first_send,))
-        second_own, second_send = stage_two(second_keep, second_got, (first_got, small, self_outs[0]))
-
-        second_send, both_other, small = lax.optimization_barrier((second_send, both_other, small))
-        second_got = far_z(second_send)
-        small = sum_over(small, "seq", 4)
+        near, far, both = [lax.ppermute(small, "seq", xor_pairs(bit, 8)) for bit in (2, 4, 6)]
+        small = (small + near) + (far + both)
+        cross_own, cross_wsend = stage_two(cross_wkeep, cross_wgot, (self_wgot, small, mlp_outs[1]))
+
+        cross_wsend, small, both_half = lax.optimization_barrier((cross_wsend, small, both_half))
+        cross_wgot = far_z(cross_wsend)
         bit = 2
         while bit < tensor_size:
             small = sum_over(small, "tensor", bit)
             bit *= 2
-        latents_grad, sources_grad = place_both(pos, both_other, lat_whole, src_whole)
-        cross_outs = [*stage_end(first_own, first_got, 2, ()), *stage_end(second_own, second_got, 2, (1,))]
+        self_outs = stage_end(self_own, self_wgot, 4, (3,))
+        latents_grad, sources_grad = place_both(pos, tensor_swap(both_half, 1), lat_whole, src_whole)
+        cross_outs = stage_end(cross_own, cross_wgot, 4, (3,), (latents_grad, self_outs[0]))
     else:
         both_sum, both_got = half_sum(both_keep, both_send)
         small = gains_of((both_sum,))
@@ -1483,7 +1465,7 @@
         small = sum_over(small, "seq", 0)
         both_half, lat_whole, src_whole = final_of(())
         latents_grad, sources_grad = place_both(pos, tensor_swap(both_half, 1), lat_whole, src_whole)
-        cross_outs = scatter_whole(pos, first_items, 2, (), ()) + scatter_whole(pos, second_items, 2, (1,), ())
+        cross_outs = scatter_whole(pos, cross_items, 4, (3,), ())
         self_outs = scatter_whole(pos, self_items, 4, (3,), ())
         mlp_outs = scatter_whole(pos, in_items, 1, (), ()) + scatter_whole(pos, out_items, 1, (0,), ())
     return (

time: 306 us -> 301 us (0.984)
  Pallas kernels: 95.4 us -> 89.6 us
    ppermute x0 -> x3, waiting for transfers between devices: none -> 8.16 us  [local(): lax.ppermute(small, 'seq', xor_pairs(bit, 8))]
    pallas_call x39 -> x35, Pallas kernels: 95.4 us -> 89.6 us  [call(): pl.pallas_call(run, out_shape=[shape for shape, ignored in outs], grid_sp...]
    ppermute x0 -> x3, starting transfers between devices: none -> 4.39 us  [local(): lax.ppermute(small, 'seq', xor_pairs(bit, 8))]
    ppermute x5 -> x4, waiting for transfers between devices: 17 us -> 12.8 us  [far_z(): return lax.ppermute(v, 'seq', xor_pairs(4, 8))]
    ppermute x5 -> x4, waiting for transfers between devices: 10.7 us -> 6.59 us  [near_z(): return lax.ppermute(v, 'seq', xor_pairs(2, 8))]
    ppermute x5 -> x4, starting transfers between devices: 7.04 us -> 4.16 us  [far_z(): return lax.ppermute(v, 'seq', xor_pairs(4, 8))]
    ppermute x5 -> x3, waiting for transfers between devices: 14.7 us -> 17.1 us  [sum_over(): v = v + lax.ppermute(v, axis, xor_pairs(bit, size))]
    ppermute x7 -> x6, starting transfers between devices: 7.07 us -> 6.16 us  [flip_x(): return lax.ppermute(v, 'seq', xor_pairs(1, 8))]
  transfers between devices with their start and end apart: 69 -> 67, of which waited for: 36 -> 33; matrix products, arithmetic and copies ran while one was open for 1% -> 1% of each run, Pallas kernels for 27% -> 26%
where the time goes in v5:
time: 301 us; the launch traced here: 300 us
  waiting for transfers between devices  134 us (45%)
  Pallas kernels  89.6 us (30%)
  starting transfers between devices  68.4 us (23%)
  local copies, waits for them, and re-layouts  5.47 us (2%)
    pallas_call x35, Pallas kernels, call(): pl.pallas_call(run, out_shape=[shape for shape, ignored in outs], grid_sp...  89.6 us
    ppermute x21, waiting for transfers between devices, seq_gather(): move = lambda v, pairs: lax.ppermute(v, 'seq', pairs)  62.4 us
    ppermute x21, starting transfers between devices, seq_gather(): move = lambda v, pairs: lax.ppermute(v, 'seq', pairs)  29.4 us
    ppermute x26, waiting for transfers between devices, tensor_swap(): return lax.ppermute(x, 'tensor', xor_pairs(bit, lax.axis_size('tensor')))  22.5 us
    ppermute x3, waiting for transfers between devices, sum_over(): v = v + lax.ppermute(v, axis, xor_pairs(bit, size))  17.1 us
    ppermute x26, starting transfers between devices, tensor_swap(): return lax.ppermute(x, 'tensor', xor_pairs(bit, lax.axis_size('tensor')))  16.7 us
    ppermute x4, waiting for transfers between devices, far_z(): return lax.ppermute(v, 'seq', xor_pairs(4, 8))  12.8 us
    ppermute x3, waiting for transfers between devices, local(): lax.ppermute(small, 'seq', xor_pairs(bit, 8))  8.16 us
  transfers between devices with their start and end apart: 67, of which 33 were waited for; matrix products, arithmetic and copies ran while one was open for 1% of the time, Pallas kernels for 26%

profile of v5, /device:TPU:0, one launch (start us, length us, event | category | flops | bytes accessed | tf_op | source)
XLA Modules:
  0.0 300.4 jit_solution(1900226865079417247)
XLA Ops:
  0.7 3.0 %collective-permute-start = (bf16[256,1024]{1,0:T(8,128)(2,1)}, bf16[256,1024]{1,0:T(8,128)(2,1)S(1)}, u32[]{:S(2)}, u32[]{:S(2)}) collective-permute-start(bf16[256,1024]{1,0:T(8,128)(2,1)} %refs_3_.6), channel_id=1, source_target_pairs={{0,2},{1,3},{2,0},{3,1},{4,6},{5,7},{6,4},{7,5},{8,10},{9,11},{10,... | collective-permute-start | bytes 1572872 | tf_op jit(solution)/shard_map/ppermute | solution.py:1211
  4.3 9.8 %cross_forward.1 = (bf16[512,1024]{1,0:T(8,128)(2,1)}, bf16[1024,1024]{1,0:T(8,128)(2,1)}, bf16[512,256]{1,0:T(8,128)(2,1)}, bf16[1024,512]{1,0:T(8,128)(2,1)}, ...) custom-call(s32[3]{0:T(128)} %pad_add_fusion.refs_0_, s32[4,256]{1,0:T(4,128)} %refs_6_.6, bf16[512,1024]{1,0:T(8,128)(2,1)} %refs_3_.7, ...), custom_call_target="tpu_custom_call" | custom-call | flops 4000000000 | bytes 12000000 | tf_op jit(solution)/shard_map/cross_forward/pallas_call | solution.py:93
  18.5 3.6 %collective-permute-done.3.refs_4_ = bf16[256,256]{1,0:T(8,128)(2,1)S(1)} collective-permute-done((bf16[256,256]{1,0:T(8,128)(2,1)}, bf16[256,256]{1,0:T(8,128)(2,1)S(1)}, u32[]{:S(2)}, u32[]{:S(2)}) %collective-permute-start.3) | collective-permute-done | bytes 131104 | tf_op jit(solution)/shard_map/ppermute | solution.py:1211
  22.1 3.1 %collective-permute-done.2.refs_3_ = bf16[256,256]{1,0:T(8,128)(2,1)S(1)} collective-permute-done((bf16[256,256]{1,0:T(8,128)(2,1)}, bf16[256,256]{1,0:T(8,128)(2,1)S(1)}, u32[]{:S(2)}, u32[]{:S(2)}) %collective-permute-start.2) | collective-permute-done | bytes 131104 | tf_op jit(solution)/shard_map/ppermute | solution.py:1211
  35.7 11.2 %collective-permute-done.8.refs_5_.refs_8_ = bf16[512,512]{1,0:T(8,128)(2,1)S(1)} collective-permute-done((bf16[512,512]{1,0:T(8,128)(2,1)S(1)}, bf16[512,512]{1,0:T(8,128)(2,1)S(1)}, u32[]{:S(2)}, u32[]{:S(2)}) %collective-permute-start.8) | collective-permute-done | bytes 524320 | tf_op jit(solution)/shard_map/ppermute | solution.py:1217
  46.9 3.8 %collective-permute-start.9 = (bf16[512,512]{1,0:T(8,128)(2,1)S(1)}, bf16[512,512]{1,0:T(8,128)(2,1)S(1)}, u32[]{:S(2)}, u32[]{:S(2)}) collective-permute-start(bf16[512,512]{1,0:T(8,128)(2,1)S(1)} %get-tuple-element.143.refs_3_.refs_6_.refs_2_), channel_id=1, source_target_pairs={{0,24},{4,28},{8,0},{12,4},{16,8},{20,12},{24,16},{28,20},{1,25},{... | collective-permute-start | bytes 1572872 | tf_op jit(solution)/shard_map/ppermute | solution.py:1217
  52.3 11.2 %collective-permute-done.10.refs_7_.refs_10_ = bf16[512,512]{1,0:T(8,128)(2,1)S(1)} collective-permute-done((bf16[512,512]{1,0:T(8,128)(2,1)S(1)}, bf16[512,512]{1,0:T(8,128)(2,1)S(1)}, u32[]{:S(2)}, u32[]{:S(2)}) %collective-permute-start.10) | collective-permute-done | bytes 524320 | tf_op jit(solution)/shard_map/ppermute | solution.py:1217
  65.1 3.9 %act_back.1 = (bf16[512,1024]{1,0:T(8,128)(2,1)S(1)}, f32[512,1024]{1,0:T(8,128)S(1)}) custom-call(s32[3]{0:T(128)S(1)} %copy-done.15, bf16[512,1024]{1,0:T(8,128)(2,1)S(1)} %copy-done.23, bf16[1024,1024]{1,0:T(8,128)(2,1)S(1)} %copy-done.6), custom_call_target="tpu_custom_call" | custom-call | flops 1073741824 | bytes 6000000 | tf_op jit(solution)/shard_map/act_back/pallas_call | solution.py:93
  69.0 3.9 %collective-permute-done.9.refs_6_.refs_9_ = bf16[512,512]{1,0:T(8,128)(2,1)S(1)} collective-permute-done((bf16[512,512]{1,0:T(8,128)(2,1)S(1)}, bf16[512,512]{1,0:T(8,128)(2,1)S(1)}, u32[]{:S(2)}, u32[]{:S(2)}) %collective-permute-start.9) | collective-permute-done | bytes 524320 | tf_op jit(solution)/shard_map/ppermute | solution.py:1217
  75.3 8.9 %collective-permute-done.12.refs_9_.refs_12_ = bf16[512,512]{1,0:T(8,128)(2,1)S(1)} collective-permute-done((bf16[512,512]{1,0:T(8,128)(2,1)S(1)}, bf16[512,512]{1,0:T(8,128)(2,1)S(1)}, u32[]{:S(2)}, u32[]{:S(2)}) %collective-permute-start.12) | collective-permute-done | bytes 524320 | tf_op jit(solution)/shard_map/ppermute | solution.py:1217
  84.2 7.9 %attend.1 = (bf16[256,256]{1,0:T(8,128)(2,1)S(1)}, bf16[256,256]{1,0:T(8,128)(2,1)S(1)}, bf16[16,256]{1,0:T(8,128)(2,1)S(1)}, f32[2,512,128]{2,1,0:T(8,128)S(1)}) custom-call(s32[3]{0:T(128)S(1)} %copy-done.15, s32[32]{0:T(128)S(1)} %copy-done.20, bf16[512,256]{1,0:T(8,128)(2,1)S(1)} %get-tuple-element.142.refs_2_.refs_7_, ...), custom_call_target="tpu_custom_call" | custom-call | flops 2000000000 | bytes 7000000 | tf_op jit(solution)/shard_map/attend/pallas_call | solution.py:93
  103.2 3.4 %mlp.1 = (bf16[512,1024]{1,0:T(8,128)(2,1)S(1)}, bf16[512,1024]{1,0:T(8,128)(2,1)S(1)}, bf16[256,1024]{1,0:T(8,128)(2,1)S(1)}, bf16[256,1024]{1,0:T(8,128)(2,1)S(1)}) custom-call(bf16[256,1024]{1,0:T(8,128)(2,1)S(1)} %get-tuple-element.149.refs_0_.refs_1_, bf16[256,1024]{1,0:T(8,128)(2,1)S(1)} %collective-permute-done.23.refs_1_.refs_2_, ...), custom_call_target="tpu_custom_call" | custom-call | flops 2147483648 | bytes 9000000 | tf_op jit(solution)/shard_map/mlp/pallas_call | solution.py:93
  114.0 3.9 %collective-permute-done.29.refs_6_.refs_11_ = bf16[512,256]{1,0:T(8,128)(2,1)S(1)} collective-permute-done((bf16[512,256]{1,0:T(8,128)(2,1)S(1)}, bf16[512,256]{1,0:T(8,128)(2,1)S(1)}, u32[]{:S(2)}, u32[]{:S(2)}) %collective-permute-start.29) | collective-permute-done | bytes 262176 | tf_op jit(solution)/shard_map/ppermute | solution.py:1217
  119.4 2.4 feature_grads.4
  121.8 2.4 feature_grads.5
  129.4 3.7 %collective-permute-start.35 = (bf16[544,256]{1,0:T(8,128)(2,1)S(1)}, bf16[544,256]{1,0:T(8,128)(2,1)S(1)}, u32[]{:S(2)}, u32[]{:S(2)}) collective-permute-start(bf16[544,256]{1,0:T(8,128)(2,1)S(1)} %get-tuple-element.165.refs_3_.refs_15_), channel_id=1, source_target_pairs={{0,8},{4,12},{8,16},{12,20},{16,24},{20,28},{24,0},{28,4},{1,9},{5... | collective-permute-start | bytes 835592 | tf_op jit(solution)/shard_map/ppermute | solution.py:1217
  133.7 5.7 %query_back.1.refs_3_ = bf16[512,256]{1,0:T(8,128)(2,1)S(1)} custom-call(s32[3]{0:T(128)S(1)} %copy-done.15, s32[32]{0:T(128)S(1)} %copy-done.20, bf16[512,256]{1,0:T(8,128)(2,1)S(1)} %get-tuple-element.142.refs_2_.refs_7_, bf16[544,256]{1,0:T(8,128)(2,1)S(1)} %get-tuple-element.165.refs_3_.refs_15_, f32[2,512,128]{2,1,0:T(8,128)S(1)} %get-tuple-element.166.refs_4_, ...), custom_call_target="tpu_custom_call" | custom-call | flops 2000000000 | bytes 7000000 | tf_op jit(solution)/shard_map/query_back/pallas_call | solution.py:93
  142.1 2.4 collective-permute-start.39
  148.2 15.4 %collective-permute-done.37.refs_19_ = bf16[544,256]{1,0:T(8,128)(2,1)S(1)} collective-permute-done((bf16[544,256]{1,0:T(8,128)(2,1)S(1)}, bf16[544,256]{1,0:T(8,128)(2,1)S(1)}, u32[]{:S(2)}, u32[]{:S(2)}) %collective-permute-start.37) | collective-permute-done | bytes 278560 | tf_op jit(solution)/shard_map/ppermute | solution.py:1217
  167.5 4.0 %collective-permute-done.40.refs_22_ = bf16[544,256]{1,0:T(8,128)(2,1)S(1)} collective-permute-done((bf16[544,256]{1,0:T(8,128)(2,1)S(1)}, bf16[544,256]{1,0:T(8,128)(2,1)S(1)}, u32[]{:S(2)}, u32[]{:S(2)}) %collective-permute-start.40) | collective-permute-done | bytes 278560 | tf_op jit(solution)/shard_map/ppermute | solution.py:1217
  174.0 8.5 %key_back.1 = (bf16[512,768]{1,0:T(8,128)(2,1)S(1)}, bf16[256,1024]{1,0:T(8,128)(2,1)S(1)}, bf16[256,1024]{1,0:T(8,128)(2,1)S(1)}) custom-call(s32[3]{0:T(128)S(1)} %copy-done.15, s32[32]{0:T(128)S(1)} %copy-done.20, bf16[512,512]{1,0:T(8,128)(2,1)S(1)} %get-tuple-element.143.refs_3_.refs_6_.refs_2_, bf16[512,256]{1,0:T(8,128)(2,1)S(1)} %query_back.1.refs_3_, ...), custom_call_target="tpu_custom_call" | custom-call | flops 4000000000 | bytes 9000000 | tf_op jit(solution)/shard_map/key_back/pallas_call | solution.py:93
  190.8 3.5 %feature_grads.6 = (bf16[4,128,1024]{2,1,0:T(8,128)(2,1)S(1)}, bf16[4,128,512]{2,1,0:T(8,128)(2,1)S(1)}, bf16[4,128,512]{2,1,0:T(8,128)(2,1)S(1)}) custom-call(s32[3]{0:T(128)S(1)} %copy-done.15, bf16[256,1024]{1,0:T(8,128)(2,1)S(1)} %get-tuple-element.186.refs_0_.refs_1_, bf16[256,1024]{1,0:T(8,128)(2,1)S(1)} %collective-permute-done.6.refs_1_.refs_2_, ...), custom_call_target="tpu_custom_call" | custom-call | flops 1073741824 | bytes 5242880 | tf_op jit(solution)/shard_map/feature_grads/pallas_call | solution.py:93
  194.3 4.2 %collective-permute-done.45.refs_1_ = bf16[2,128,1024]{2,1,0:T(8,128)(2,1)S(1)} collective-permute-done((bf16[2,128,1024]{2,1,0:T(8,128)(2,1)S(1)}, bf16[2,128,1024]{2,1,0:T(8,128)(2,1)S(1)}, u32[]{:S(2)}, u32[]{:S(2)}) %collective-permute-start.45) | collective-permute-done | bytes 524320 | tf_op jit(solution)/shard_map/ppermute | solution.py:1112
  206.2 7.4 %cross_back.1 = (bf16[512,256]{1,0:T(8,128)(2,1)S(1)}, bf16[1024,256]{1,0:T(8,128)(2,1)S(1)}, bf16[1024,256]{1,0:T(8,128)(2,1)S(1)}, bf16[768,1024]{1,0:T(8,128)(2,1)S(1)}, bf16[768,1024]{1,0:T(8,128)(2,1)S(1)}) custom-call(s32[3]{0:T(128)S(1)} %copy-done.15, bf16[256,1024]{1,0:T(8,128)(2,1)S(1)} %get-tuple-element.196.refs_1_.refs_7_, ...), custom_call_target="tpu_custom_call" | custom-call | flops 4000000000 | bytes 12000000 | tf_op jit(solution)/shard_map/cross_back/pallas_call | solution.py:93
  213.6 6.0 %collective-permute-done.49.refs_1_ = bf16[128,1024]{1,0:T(8,128)(2,1)S(1)} collective-permute-done((bf16[128,1024]{1,0:T(8,128)(2,1)S(1)}, bf16[128,1024]{1,0:T(8,128)(2,1)S(1)}, u32[]{:S(2)}, u32[]{:S(2)}) %collective-permute-start.49) | collective-permute-done | bytes 262176 | tf_op jit(solution)/shard_map/ppermute | solution.py:1116
  225.2 6.4 %feature_grads.7 = (bf16[4,128,1024]{2,1,0:T(8,128)(2,1)S(1)}, bf16[4,128,1024]{2,1,0:T(8,128)(2,1)S(1)}) custom-call(s32[3]{0:T(128)S(1)} %copy-done.15, bf16[512,1024]{1,0:T(8,128)(2,1)S(1)} %copy-done.9, bf16[512,256]{1,0:T(8,128)(2,1)S(1)} %get-tuple-element.201.refs_2_, bf16[1024,1024]{1,0:T(8,128)(2,1)S(1)} %copy-done.1, ...), custom_call_target="tpu_custom_call" | custom-call | flops 1610612736 | bytes 9961472 | tf_op jit(solution)/shard_map/feature_grads/pallas_call | solution.py:93
  231.5 2.4 collective-permute-done.51.refs_1_
  240.0 3.8 %gains.1 = f32[8,1024]{1,0:T(8,128)S(1)} custom-call(s32[3]{0:T(128)S(1)} %copy-done.15, s32[32]{0:T(128)S(1)} %copy-done.20, s32[3]{0:T(128)S(1)} %copy-done.21, bf16[768,1024]{1,0:T(8,128)(2,1)S(1)} %get-tuple-element.205.refs_3_, bf16[768,1024]{1,0:T(8,128)(2,1)S(1)} %get-tuple-element.211.refs_4_, bf16[512,1024]{1,0:T(8,128)(2,1)S(1)} %copy-done, ...), custom_call_target="tpu_custom_call" | custom-call | flops 31457280 | bytes 6291456 | tf_op jit(solution)/shard_map/gains/pallas_call | solution.py:93
  246.2 14.2 %collective-permute-done.57 = f32[8,1024]{1,0:T(8,128)S(1)} collective-permute-done((f32[8,1024]{1,0:T(8,128)S(1)}, f32[8,1024]{1,0:T(8,128)S(1)}, u32[]{:S(2)}, u32[]{:S(2)}) %collective-permute-start.57) | collective-permute-done | bytes 32800 | tf_op jit(solution)/shard_map/ppermute | solution.py:1297
  263.8 4.5 %final_norm.1 = (bf16[768,1024]{1,0:T(8,128)(2,1)S(1)}, bf16[512,1024]{1,0:T(8,128)(2,1)}, bf16[1024,1024]{1,0:T(8,128)(2,1)}) custom-call(s32[3]{0:T(128)S(1)} %copy-done.15, bf16[768,1024]{1,0:T(8,128)(2,1)S(1)} %add_convert_fusion.refs_11_.refs_1_, bf16[768,1024]{1,0:T(8,128)(2,1)S(1)} %collective-permute-done.60.refs_2_, bf16[512,1024]{1,0:T(8,128)(2,1)S(1)} %copy-done, ...), custom_call_target="tpu_custom_call" | custom-call | flops 15728640 | bytes 6291456 | tf_op jit(solution)/shard_map/final_norm/pallas_call | solution.py:93
  273.7 8.2 %collective-permute-done.63 = f32[8,1024]{1,0:T(8,128)S(1)} collective-permute-done((f32[8,1024]{1,0:T(8,128)S(1)}, f32[8,1024]{1,0:T(8,128)S(1)}, u32[]{:S(2)}, u32[]{:S(2)}) %collective-permute-start.63) | collective-permute-done | bytes 32800 | tf_op jit(solution)/shard_map/ppermute | solution.py:1448
  291.5 6.8 %collective-permute-done.66.refs_1_ = bf16[128,1024]{1,0:T(8,128)(2,1)S(1)} collective-permute-done((bf16[128,1024]{1,0:T(8,128)(2,1)S(1)}, bf16[128,1024]{1,0:T(8,128)(2,1)S(1)}, u32[]{:S(2)}, u32[]{:S(2)}) %collective-permute-start.66) | collective-permute-done | bytes 262176 | tf_op jit(solution)/shard_map/ppermute | solution.py:1116
  (214 shorter events, 109.5 us)
Async XLA Ops:
  0.7 15.2 %collective-permute-start = (bf16[256,1024]{1,0:T(8,128)(2,1)}, bf16[256,1024]{1,0:T(8,128)(2,1)S(1)}, u32[]{:S(2)}, u32[]{:S(2)}) collective-permute-start(bf16[256,1024]{1,0:T(8,128)(2,1)} %refs_3_.6), channel_id=1, source_target_pairs={{0,2},{1,3},{2,0},{3,1},{4,6},{5,7},{6,4},{7,5},{8,10},{9,11},{10,... | collective-permute-start | bytes 1572872 | tf_op jit(solution)/shard_map/ppermute | solution.py:1211
  30.8 16.1 %collective-permute-start.8 = (bf16[512,512]{1,0:T(8,128)(2,1)S(1)}, bf16[512,512]{1,0:T(8,128)(2,1)S(1)}, u32[]{:S(2)}, u32[]{:S(2)}) collective-permute-start(bf16[512,512]{1,0:T(8,128)(2,1)S(1)} %get-tuple-element.143.refs_3_.refs_6_.refs_2_), channel_id=1, source_target_pairs={{0,8},{4,12},{8,16},{12,20},{16,24},{20,28},{24,0},{28,4},{1,9},{5... | collective-permute-start | bytes 1572872 | tf_op jit(solution)/shard_map/ppermute | solution.py:1217
  34.2 16.6 %collective-permute-start.14 = (bf16[256,1024]{1,0:T(8,128)(2,1)S(1)}, bf16[256,1024]{1,0:T(8,128)(2,1)S(1)}, u32[]{:S(2)}, u32[]{:S(2)}) collective-permute-start(bf16[256,1024]{1,0:T(8,128)(2,1)S(1)} %copy-done.7), channel_id=1, source_target_pairs={{0,1},{1,0},{2,3},{3,2},{4,5},{5,4},{6,7},{7,6},{8,9},{9,8},{10,11... | collective-permute-start | bytes 1572872 | tf_op jit(solution)/shard_map/ppermute | solution.py:1211
  34.2 18.1 %collective-permute-start.7 = (bf16[512,512]{1,0:T(8,128)(2,1)S(1)}, bf16[512,512]{1,0:T(8,128)(2,1)S(1)}, u32[]{:S(2)}, u32[]{:S(2)}) collective-permute-start(bf16[512,512]{1,0:T(8,128)(2,1)S(1)} %get-tuple-element.143.refs_3_.refs_6_.refs_2_), channel_id=1, source_target_pairs={{0,4},{4,0},{8,12},{12,8},{16,20},{20,16},{24,28},{28,24},{1,5},{5... | collective-permute-start | bytes 1572872 | tf_op jit(solution)/shard_map/ppermute | solution.py:1217
  46.9 16.6 %collective-permute-start.10 = (bf16[512,512]{1,0:T(8,128)(2,1)S(1)}, bf16[512,512]{1,0:T(8,128)(2,1)S(1)}, u32[]{:S(2)}, u32[]{:S(2)}) collective-permute-start(bf16[512,512]{1,0:T(8,128)(2,1)S(1)} %collective-permute-done.8.refs_5_.refs_8_), channel_id=1, source_target_pairs={{0,8},{4,12},{8,16},{12,20},{16,24},{20,28},{24,0},{28,4},{1,9},{5... | collective-permute-start | bytes 1572872 | tf_op jit(solution)/shard_map/ppermute | solution.py:1217
  46.9 18.2 %collective-permute-start.16 = (bf16[256,1024]{1,0:T(8,128)(2,1)S(1)}, bf16[256,1024]{1,0:T(8,128)(2,1)S(1)}, u32[]{:S(2)}, u32[]{:S(2)}) collective-permute-start(bf16[256,1024]{1,0:T(8,128)(2,1)S(1)} %collective-permute-done.15.refs_13_.refs_7_), channel_id=1, source_target_pairs={{0,1},{1,0},{2,3},{3,2},{4,5},{5,4},{6,7},{7,6},{8,9},{9,8},{10,11... | collective-permute-start | bytes 1572872 | tf_op jit(solution)/shard_map/ppermute | solution.py:1211
  46.9 26.0 %collective-permute-start.9 = (bf16[512,512]{1,0:T(8,128)(2,1)S(1)}, bf16[512,512]{1,0:T(8,128)(2,1)S(1)}, u32[]{:S(2)}, u32[]{:S(2)}) collective-permute-start(bf16[512,512]{1,0:T(8,128)(2,1)S(1)} %get-tuple-element.143.refs_3_.refs_6_.refs_2_), channel_id=1, source_target_pairs={{0,24},{4,28},{8,0},{12,4},{16,8},{20,12},{24,16},{28,20},{1,25},{... | collective-permute-start | bytes 1572872 | tf_op jit(solution)/shard_map/ppermute | solution.py:1217
  50.8 23.3 %collective-permute-start.11 = (bf16[512,512]{1,0:T(8,128)(2,1)S(1)}, bf16[512,512]{1,0:T(8,128)(2,1)S(1)}, u32[]{:S(2)}, u32[]{:S(2)}) collective-permute-start(bf16[512,512]{1,0:T(8,128)(2,1)S(1)} %collective-permute-done.8.refs_5_.refs_8_), channel_id=1, source_target_pairs={{0,4},{4,0},{8,12},{12,8},{16,20},{20,16},{24,28},{28,24},{1,5},{5... | collective-permute-start | bytes 1572872 | tf_op jit(solution)/shard_map/ppermute | solution.py:1217
  52.3 31.9 %collective-permute-start.12 = (bf16[512,512]{1,0:T(8,128)(2,1)S(1)}, bf16[512,512]{1,0:T(8,128)(2,1)S(1)}, u32[]{:S(2)}, u32[]{:S(2)}) collective-permute-start(bf16[512,512]{1,0:T(8,128)(2,1)S(1)} %collective-permute-done.7.refs_4_.refs_7_), channel_id=1, source_target_pairs={{0,24},{4,28},{8,0},{12,4},{16,8},{20,12},{24,16},{28,20},{1,25},{... | collective-permute-start | bytes 1572872 | tf_op jit(solution)/shard_map/ppermute | solution.py:1217
  63.6 20.6 %collective-permute-start.13 = (bf16[512,512]{1,0:T(8,128)(2,1)S(1)}, bf16[512,512]{1,0:T(8,128)(2,1)S(1)}, u32[]{:S(2)}, u32[]{:S(2)}) collective-permute-start(bf16[512,512]{1,0:T(8,128)(2,1)S(1)} %collective-permute-done.10.refs_7_.refs_10_), channel_id=1, source_target_pairs={{0,4},{4,0},{8,12},{12,8},{16,20},{20,16},{24,28},{28,24},{1,5},{5... | collective-permute-start | bytes 1572872 | tf_op jit(solution)/shard_map/ppermute | solution.py:1217
  65.1 28.6 %collective-permute-start.22 = (bf16[512,256]{1,0:T(8,128)(2,1)S(1)}, bf16[512,256]{1,0:T(8,128)(2,1)S(1)}, u32[]{:S(2)}, u32[]{:S(2)}) collective-permute-start(bf16[512,256]{1,0:T(8,128)(2,1)S(1)} %get-tuple-element.142.refs_2_.refs_7_), channel_id=1, source_target_pairs={{0,24},{4,28},{8,0},{12,4},{16,8},{20,12},{24,16},{28,20},{1,25},{... | collective-permute-start | bytes 786440 | tf_op jit(solution)/shard_map/ppermute | solution.py:1217
  73.0 23.0 %collective-permute-start.21 = (bf16[512,256]{1,0:T(8,128)(2,1)S(1)}, bf16[512,256]{1,0:T(8,128)(2,1)S(1)}, u32[]{:S(2)}, u32[]{:S(2)}) collective-permute-start(bf16[512,256]{1,0:T(8,128)(2,1)S(1)} %get-tuple-element.142.refs_2_.refs_7_), channel_id=1, source_target_pairs={{0,8},{4,12},{8,16},{12,20},{16,24},{20,28},{24,0},{28,4},{1,9},{5... | collective-permute-start | bytes 786440 | tf_op jit(solution)/shard_map/ppermute | solution.py:1217
  74.1 21.9 %collective-permute-start.20 = (bf16[512,256]{1,0:T(8,128)(2,1)S(1)}, bf16[512,256]{1,0:T(8,128)(2,1)S(1)}, u32[]{:S(2)}, u32[]{:S(2)}) collective-permute-start(bf16[512,256]{1,0:T(8,128)(2,1)S(1)} %get-tuple-element.142.refs_2_.refs_7_), channel_id=1, source_target_pairs={{0,4},{4,0},{8,12},{12,8},{16,20},{20,16},{24,28},{28,24},{1,5},{5... | collective-permute-start | bytes 786440 | tf_op jit(solution)/shard_map/ppermute | solution.py:1217
  108.7 17.1 %collective-permute-start.28 = (bf16[256,1024]{1,0:T(8,128)(2,1)S(1)}, bf16[256,1024]{1,0:T(8,128)(2,1)S(1)}, u32[]{:S(2)}, u32[]{:S(2)}) collective-permute-start(bf16[256,1024]{1,0:T(8,128)(2,1)S(1)} %add_convert_fusion.3.refs_4_.refs_2_.refs_0_), channel_id=1, source_target_pairs={{0,2},{1,3},{2,0},{3,1},{4,6},{5,7},{6,4},{7,5},{8,10},{9,11},{10,... | collective-permute-start | bytes 1572872 | tf_op jit(solution)/shard_map/ppermute | solution.py:1211
  110.2 15.6 %collective-permute-start.30 = (bf16[512,256]{1,0:T(8,128)(2,1)S(1)}, bf16[512,256]{1,0:T(8,128)(2,1)S(1)}, u32[]{:S(2)}, u32[]{:S(2)}) collective-permute-start(bf16[512,256]{1,0:T(8,128)(2,1)S(1)} %collective-permute-done.21.refs_12_.refs_9_), channel_id=1, source_target_pairs={{0,4},{4,0},{8,12},{12,8},{16,20},{20,16},{24,28},{28,24},{1,5},{5... | collective-permute-start | bytes 786440 | tf_op jit(solution)/shard_map/ppermute | solution.py:1217
  141.5 25.2 %collective-permute-start.41 = (bf16[4,128,1024]{2,1,0:T(8,128)(2,1)S(1)}, bf16[4,128,1024]{2,1,0:T(8,128)(2,1)S(1)}, u32[]{:S(2)}, u32[]{:S(2)}) collective-permute-start(bf16[4,128,1024]{2,1,0:T(8,128)(2,1)S(1)} %get-tuple-element.176), channel_id=1, source_target_pairs={{0,4},{4,0},{8,12},{12,8},{16,20},{20,16},{24,28},{28,24},{1,5},{5... | collective-permute-start | bytes 3145736 | tf_op jit(solution)/shard_map/ppermute | solution.py:1108
  142.1 21.5 %collective-permute-start.39 = (bf16[544,256]{1,0:T(8,128)(2,1)S(1)}, bf16[544,256]{1,0:T(8,128)(2,1)S(1)}, u32[]{:S(2)}, u32[]{:S(2)}) collective-permute-start(bf16[544,256]{1,0:T(8,128)(2,1)S(1)} %collective-permute-done.34.refs_16_), channel_id=1, source_target_pairs={{0,8},{4,12},{8,16},{12,20},{16,24},{20,28},{24,0},{28,4},{1,9},{5... | collective-permute-start | bytes 835592 | tf_op jit(solution)/shard_map/ppermute | solution.py:1217
  144.5 19.0 %collective-permute-start.38 = (bf16[544,256]{1,0:T(8,128)(2,1)S(1)}, bf16[544,256]{1,0:T(8,128)(2,1)S(1)}, u32[]{:S(2)}, u32[]{:S(2)}) collective-permute-start(bf16[544,256]{1,0:T(8,128)(2,1)S(1)} %collective-permute-done.34.refs_16_), channel_id=1, source_target_pairs={{0,24},{4,28},{8,0},{12,4},{16,8},{20,12},{24,16},{28,20},{1,25},{... | collective-permute-start | bytes 835592 | tf_op jit(solution)/shard_map/ppermute | solution.py:1217
  145.9 17.6 %collective-permute-start.37 = (bf16[544,256]{1,0:T(8,128)(2,1)S(1)}, bf16[544,256]{1,0:T(8,128)(2,1)S(1)}, u32[]{:S(2)}, u32[]{:S(2)}) collective-permute-start(bf16[544,256]{1,0:T(8,128)(2,1)S(1)} %collective-permute-done.35.refs_17_), channel_id=1, source_target_pairs={{0,8},{4,12},{8,16},{12,20},{16,24},{20,28},{24,0},{28,4},{1,9},{5... | collective-permute-start | bytes 835592 | tf_op jit(solution)/shard_map/ppermute | solution.py:1217
  146.8 25.8 %collective-permute-start.26 = (bf16[256,1024]{1,0:T(8,128)(2,1)S(1)}, bf16[256,1024]{1,0:T(8,128)(2,1)S(1)}, u32[]{:S(2)}, u32[]{:S(2)}) collective-permute-start(bf16[256,1024]{1,0:T(8,128)(2,1)S(1)} %add_convert_fusion.2.refs_1_), channel_id=1, source_target_pairs={{0,2},{1,3},{2,0},{3,1},{4,6},{5,7},{6,4},{7,5},{8,10},{9,11},{10,... | collective-permute-start | bytes 1572872 | tf_op jit(solution)/shard_map/ppermute | solution.py:1211
  204.1 15.4 %collective-permute-start.48 = (bf16[4,128,512]{2,1,0:T(8,128)(2,1)S(1)}, bf16[4,128,512]{2,1,0:T(8,128)(2,1)S(1)}, u32[]{:S(2)}, u32[]{:S(2)}) collective-permute-start(bf16[4,128,512]{2,1,0:T(8,128)(2,1)S(1)} %get-tuple-element.209), channel_id=1, source_target_pairs={{0,4},{4,0},{8,12},{12,8},{16,20},{20,16},{24,28},{28,24},{1,5},{5... | collective-permute-start | bytes 1572872 | tf_op jit(solution)/shard_map/ppermute | solution.py:1108
  205.0 14.6 %collective-permute-start.49 = (bf16[128,1024]{1,0:T(8,128)(2,1)S(1)}, bf16[128,1024]{1,0:T(8,128)(2,1)S(1)}, u32[]{:S(2)}, u32[]{:S(2)}) collective-permute-start(bf16[128,1024]{1,0:T(8,128)(2,1)S(1)} %get-tuple-element.210.refs_4_), channel_id=1, source_target_pairs={{0,16},{4,20},{8,24},{12,28},{16,0},{20,4},{24,8},{28,12},{1,17},{... | collective-permute-start | bytes 786440 | tf_op jit(solution)/shard_map/ppermute | solution.py:1116
  219.6 14.3 %collective-permute-start.51 = (bf16[2,128,1024]{2,1,0:T(8,128)(2,1)S(1)}, bf16[2,128,1024]{2,1,0:T(8,128)(2,1)S(1)}, u32[]{:S(2)}, u32[]{:S(2)}) collective-permute-start(bf16[2,128,1024]{2,1,0:T(8,128)(2,1)S(1)} %get-tuple-element.214), channel_id=1, source_target_pairs={{0,8},{4,12},{8,0},{12,4},{16,24},{20,28},{24,16},{28,20},{1,9},{5... | collective-permute-start | bytes 1572872 | tf_op jit(solution)/shard_map/ppermute | solution.py:1112
  219.6 14.4 %collective-permute-start.52 = (bf16[4,128,512]{2,1,0:T(8,128)(2,1)S(1)}, bf16[4,128,512]{2,1,0:T(8,128)(2,1)S(1)}, u32[]{:S(2)}, u32[]{:S(2)}) collective-permute-start(bf16[4,128,512]{2,1,0:T(8,128)(2,1)S(1)} %get-tuple-element.217), channel_id=1, source_target_pairs={{0,4},{4,0},{8,12},{12,8},{16,20},{20,16},{24,28},{28,24},{1,5},{5... | collective-permute-start | bytes 1572872 | tf_op jit(solution)/shard_map/ppermute | solution.py:1108
  223.7 40.1 %collective-permute-start.60 = (bf16[768,1024]{1,0:T(8,128)(2,1)S(1)}, bf16[768,1024]{1,0:T(8,128)(2,1)S(1)}, u32[]{:S(2)}, u32[]{:S(2)}) collective-permute-start(bf16[768,1024]{1,0:T(8,128)(2,1)S(1)} %add_convert_fusion.refs_11_.refs_1_), channel_id=1, source_target_pairs={{0,2},{1,3},{2,0},{3,1},{4,6},{5,7},{6,4},{7,5},{8,10},{9,11},{10,... | collective-permute-start | bytes 4718600 | tf_op jit(solution)/shard_map/ppermute | solution.py:1211
  234.8 25.7 %collective-permute-start.53 = (bf16[4,128,1024]{2,1,0:T(8,128)(2,1)S(1)}, bf16[4,128,1024]{2,1,0:T(8,128)(2,1)S(1)}, u32[]{:S(2)}, u32[]{:S(2)}) collective-permute-start(bf16[4,128,1024]{2,1,0:T(8,128)(2,1)S(1)} %get-tuple-element.220.refs_10_), channel_id=1, source_target_pairs={{0,4},{4,0},{8,12},{12,8},{16,20},{20,16},{24,28},{28,24},{1,5},{5... | collective-permute-start | bytes 3145736 | tf_op jit(solution)/shard_map/ppermute | solution.py:1108
  236.1 24.3 %collective-permute-start.54 = (bf16[2,128,1024]{2,1,0:T(8,128)(2,1)S(1)}, bf16[2,128,1024]{2,1,0:T(8,128)(2,1)S(1)}, u32[]{:S(2)}, u32[]{:S(2)}) collective-permute-start(bf16[2,128,1024]{2,1,0:T(8,128)(2,1)S(1)} %get-tuple-element.222.refs_2_), channel_id=1, source_target_pairs={{0,8},{4,12},{8,0},{12,4},{16,24},{20,28},{24,16},{28,20},{1,9},{5... | collective-permute-start | bytes 1572872 | tf_op jit(solution)/shard_map/ppermute | solution.py:1112
  237.7 22.7 %collective-permute-start.55 = (bf16[128,1024]{1,0:T(8,128)(2,1)S(1)}, bf16[128,1024]{1,0:T(8,128)(2,1)S(1)}, u32[]{:S(2)}, u32[]{:S(2)}) collective-permute-start(bf16[128,1024]{1,0:T(8,128)(2,1)S(1)} %get-tuple-element.223), channel_id=1, source_target_pairs={{0,16},{4,20},{8,24},{12,28},{16,0},{20,4},{24,8},{28,12},{1,17},{... | collective-permute-start | bytes 786440 | tf_op jit(solution)/shard_map/ppermute | solution.py:1116
  245.1 15.3 %collective-permute-start.57 = (f32[8,1024]{1,0:T(8,128)S(1)}, f32[8,1024]{1,0:T(8,128)S(1)}, u32[]{:S(2)}, u32[]{:S(2)}) collective-permute-start(f32[8,1024]{1,0:T(8,128)S(1)} %add.39), channel_id=1, source_target_pairs={{0,4},{4,0},{8,12},{12,8},{16,20},{20,16},{24,28},{28,24},{1,5},{5... | collective-permute-start | bytes 98312 | tf_op jit(solution)/shard_map/ppermute | solution.py:1297
  261.4 20.5 %collective-permute-start.58 = (bf16[2,128,1024]{2,1,0:T(8,128)(2,1)S(1)}, bf16[2,128,1024]{2,1,0:T(8,128)(2,1)S(1)}, u32[]{:S(2)}, u32[]{:S(2)}) collective-permute-start(bf16[2,128,1024]{2,1,0:T(8,128)(2,1)S(1)} %get-tuple-element.230), channel_id=1, source_target_pairs={{0,8},{4,12},{8,0},{12,4},{16,24},{20,28},{24,16},{28,20},{1,9},{5... | collective-permute-start | bytes 1572872 | tf_op jit(solution)/shard_map/ppermute | solution.py:1112
  262.7 19.1 %collective-permute-start.59 = (bf16[128,1024]{1,0:T(8,128)(2,1)S(1)}, bf16[128,1024]{1,0:T(8,128)(2,1)S(1)}, u32[]{:S(2)}, u32[]{:S(2)}) collective-permute-start(bf16[128,1024]{1,0:T(8,128)(2,1)S(1)} %get-tuple-element.227.refs_3_), channel_id=1, source_target_pairs={{0,16},{4,20},{8,24},{12,28},{16,0},{20,4},{24,8},{28,12},{1,17},{... | collective-permute-start | bytes 786440 | tf_op jit(solution)/shard_map/ppermute | solution.py:1116
  283.1 15.2 %collective-permute-start.66 = (bf16[128,1024]{1,0:T(8,128)(2,1)S(1)}, bf16[128,1024]{1,0:T(8,128)(2,1)S(1)}, u32[]{:S(2)}, u32[]{:S(2)}) collective-permute-start(bf16[128,1024]{1,0:T(8,128)(2,1)S(1)} %get-tuple-element.244), channel_id=1, source_target_pairs={{0,16},{4,20},{8,24},{12,28},{16,0},{20,4},{24,8},{28,12},{1,17},{... | collective-permute-start | bytes 786440 | tf_op jit(solution)/shard_map/ppermute | solution.py:1116
  (68 other events, 647.5 us)

commit v6 on v5

--- a/solution.py
+++ b/solution.py
@@ -123,7 +123,7 @@
 
 def cross_forward_body(
     pos_ref, idx_ref, lat_ref, src_ref, gain_one_ref, gain_src_ref, wq_ref, wk_ref, wv_ref,
-    n1_ref, ns_ref, q_ref, kvp_ref, keep_ref, send_ref, kv_s, picks_s, *, steps,
+    n1_ref, ns_ref, q_ref, kvp_ref, keep_ref, send_ref, kv_s, picks_s, *, steps, groups,
 ):
     i = pl.program_id(0)
     width = wq_ref.shape[1]
@@ -136,22 +136,22 @@
     kv_s[pl.ds(row0, rows_src), width:] = dot(normed_src, wv_ref[...]).astype(bf16)
     norm_into(n1_ref, lat_ref, gain_one_ref)
     normed_one = n1_ref[...]
-    grp0 = pl.multiple_of(i * GROUP, GROUP)
-    q_ref[pl.ds(grp0, GROUP), :] = dot(normed_one, wq_ref[...]).astype(bf16)
+    rows_lat = lat_ref.shape[0]
+    q_ref[pl.ds(pl.multiple_of(i * rows_lat, rows_lat), rows_lat), :] = dot(normed_one, wq_ref[...]).astype(bf16)
 
     @pl.when(i == steps - 1)
     def _():
         count = kv_s.shape[0]
         lanes = lax.broadcasted_iota(jnp.int32, (128, count), 1).astype(f32)
-        for b in range(steps):
+        for b in range(groups):
             for part in range(SRC // 128):
-                row = index_row(idx_ref, pos_ref, b, steps, count)[:, part * 128 : (part + 1) * 128]
+                row = index_row(idx_ref, pos_ref, b, groups, count)[:, part * 128 : (part + 1) * 128]
                 column = jnp.transpose(jnp.broadcast_to(row, (128, 128)))
                 picks = jnp.where(jnp.tile(column, (1, count // 128)) == lanes, 1.0, 0.0).astype(bf16)
                 r0 = b * SRC + part * 128
                 picks_s[r0 : r0 + 128, :] = picks
         kvp_ref[...] = dot(picks_s[...], kv_s[...]).astype(bf16)
-        for b in range(steps):
+        for b in range(groups):
             for h in range(heads):
                 cols = slice(h * HEAD, (h + 1) * HEAD)
                 q = q_ref[b * GROUP : (b + 1) * GROUP, cols]
@@ -161,24 +161,25 @@
                 p = jnp.exp2(s - jnp.max(s, axis=-1, keepdims=True))
                 total = jnp.sum(p, axis=-1, keepdims=True)
                 mixed = (dot(p.astype(bf16), v) / total).astype(bf16)
-                if b < steps // 2:
+                if b < groups // 2:
                     keep_ref[b * GROUP : (b + 1) * GROUP, cols] = mixed
                 else:
-                    r0 = (b - steps // 2) * GROUP
+                    r0 = (b - groups // 2) * GROUP
                     send_ref[r0 : r0 + GROUP, cols] = mixed
 
 
 def cross_forward(pos, idx, latents, sources, gain_one, gain_src, wq, wk, wv):
     rows, width_d = latents.shape
-    steps = rows // GROUP
+    steps = 2
+    lat_blk = rows // steps
     count = sources.shape[0]
     blk = count // steps
     width = wq.shape[1]
     whole = lambda shape: pl.BlockSpec(shape, lambda i, c: (0,) * len(shape))
     return call(
-        functools.partial(cross_forward_body, steps=steps),
+        functools.partial(cross_forward_body, steps=steps, groups=rows // GROUP),
         [
-            (sds((rows, width_d), bf16), pl.BlockSpec((GROUP, width_d), lambda i, c: (i, 0))),
+            (sds((rows, width_d), bf16), pl.BlockSpec((lat_blk, width_d), lambda i, c: (i, 0))),
             (sds((count, width_d), bf16), pl.BlockSpec((blk, width_d), lambda i, c: (i, 0))),
             (sds((rows, width), bf16), whole((rows, width))),
             (sds((count, 2 * width), bf16), whole((count, 2 * width))),
@@ -187,7 +188,7 @@
         ],
         [
             whole(idx.shape),
-            pl.BlockSpec((GROUP, width_d), lambda i, c: ((i + c[0] * (steps // 2)) % steps, 0)),
+            pl.BlockSpec((lat_blk, width_d), lambda i, c: ((i + c[0] * (steps // 2)) % steps, 0)),
             pl.BlockSpec((blk, width_d), lambda i, c: (i, 0)),
             whole((1, width_d)),
             whole((1, width_d)),
@@ -1447,7 +1448,7 @@
         small, both_half = lax.optimization_barrier((small, both_half))
         near, far, both = [lax.ppermute(small, "seq", xor_pairs(bit, 8)) for bit in (2, 4, 6)]
         small = (small + near) + (far + both)
-        cross_own, cross_wsend = stage_two(cross_wkeep, cross_wgot, (self_wgot, small, mlp_outs[1]))
+        cross_own, cross_wsend = stage_two(cross_wkeep, cross_wgot, (self_wgot, small))
 
         cross_wsend, small, both_half = lax.optimization_barrier((cross_wsend, small, both_half))
         cross_wgot = far_z(cross_wsend)
@@ -1457,7 +1458,7 @@
             bit *= 2
         self_outs = stage_end(self_own, self_wgot, 4, (3,))
         latents_grad, sources_grad = place_both(pos, tensor_swap(both_half, 1), lat_whole, src_whole)
-        cross_outs = stage_end(cross_own, cross_wgot, 4, (3,), (latents_grad, self_outs[0]))
+        cross_outs = stage_end(cross_own, cross_wgot, 4, (3,), (latents_grad, self_outs[0], mlp_outs[1]))
     else:
         both_sum, both_got = half_sum(both_keep, both_send)
         small = gains_of((both_sum,))

time: 301 us -> 300 us (level)
  no operation moved by 1% of the time
where the time goes in v6:
time: 300 us; the launch traced here: 299 us
  waiting for transfers between devices  134 us (45%)
  Pallas kernels  89.1 us (30%)
  starting transfers between devices  68.5 us (23%)
  local copies, waits for them, and re-layouts  4.44 us (1%)
    pallas_call x35, Pallas kernels, call(): pl.pallas_call(run, out_shape=[shape for shape, ignored in outs], grid_sp...  89.1 us
    ppermute x21, waiting for transfers between devices, seq_gather(): move = lambda v, pairs: lax.ppermute(v, 'seq', pairs)  62.4 us
    ppermute x21, starting transfers between devices, seq_gather(): move = lambda v, pairs: lax.ppermute(v, 'seq', pairs)  29.4 us
    ppermute x26, waiting for transfers between devices, tensor_swap(): return lax.ppermute(x, 'tensor', xor_pairs(bit, lax.axis_size('tensor')))  23.1 us
    ppermute x26, starting transfers between devices, tensor_swap(): return lax.ppermute(x, 'tensor', xor_pairs(bit, lax.axis_size('tensor')))  16.7 us
    ppermute x3, waiting for transfers between devices, sum_over(): v = v + lax.ppermute(v, axis, xor_pairs(bit, size))  16.1 us
    ppermute x4, waiting for transfers between devices, far_z(): return lax.ppermute(v, 'seq', xor_pairs(4, 8))  12.8 us
    ppermute x3, waiting for transfers between devices, local(): lax.ppermute(small, 'seq', xor_pairs(bit, 8))  9.17 us
  transfers between devices with their start and end apart: 67, of which 33 were waited for; matrix products, arithmetic and copies ran while one was open for 1% of the time, Pallas kernels for 26%

profile of v6, /device:TPU:0, one launch (start us, length us, event | category | flops | bytes accessed | tf_op | source)
XLA Modules:
  0.0 299.3 jit_solution(8045850444634089893)
XLA Ops:
  0.7 3.0 %collective-permute-start = (bf16[256,1024]{1,0:T(8,128)(2,1)}, bf16[256,1024]{1,0:T(8,128)(2,1)S(1)}, u32[]{:S(2)}, u32[]{:S(2)}) collective-permute-start(bf16[256,1024]{1,0:T(8,128)(2,1)} %refs_3_.6), channel_id=1, source_target_pairs={{0,2},{1,3},{2,0},{3,1},{4,6},{5,7},{6,4},{7,5},{8,10},{9,11},{10,... | collective-permute-start | bytes 1572872 | tf_op jit(solution)/shard_map/ppermute | solution.py:1212
  4.3 9.2 %cross_forward.1 = (bf16[512,1024]{1,0:T(8,128)(2,1)}, bf16[1024,1024]{1,0:T(8,128)(2,1)}, bf16[512,256]{1,0:T(8,128)(2,1)}, bf16[1024,512]{1,0:T(8,128)(2,1)}, ...) custom-call(s32[3]{0:T(128)} %pad_add_fusion.refs_0_, s32[4,256]{1,0:T(4,128)} %refs_6_.6, bf16[512,1024]{1,0:T(8,128)(2,1)} %refs_3_.7, ...), custom_call_target="tpu_custom_call" | custom-call | flops 4000000000 | bytes 12000000 | tf_op jit(solution)/shard_map/cross_forward/pallas_call | solution.py:93
  18.5 3.6 %collective-permute-done.3.refs_4_ = bf16[256,256]{1,0:T(8,128)(2,1)S(1)} collective-permute-done((bf16[256,256]{1,0:T(8,128)(2,1)}, bf16[256,256]{1,0:T(8,128)(2,1)S(1)}, u32[]{:S(2)}, u32[]{:S(2)}) %collective-permute-start.3) | collective-permute-done | bytes 131104 | tf_op jit(solution)/shard_map/ppermute | solution.py:1212
  22.1 3.1 %collective-permute-done.2.refs_3_ = bf16[256,256]{1,0:T(8,128)(2,1)S(1)} collective-permute-done((bf16[256,256]{1,0:T(8,128)(2,1)}, bf16[256,256]{1,0:T(8,128)(2,1)S(1)}, u32[]{:S(2)}, u32[]{:S(2)}) %collective-permute-start.2) | collective-permute-done | bytes 131104 | tf_op jit(solution)/shard_map/ppermute | solution.py:1212
  35.7 11.2 %collective-permute-done.8.refs_5_.refs_8_ = bf16[512,512]{1,0:T(8,128)(2,1)S(1)} collective-permute-done((bf16[512,512]{1,0:T(8,128)(2,1)S(1)}, bf16[512,512]{1,0:T(8,128)(2,1)S(1)}, u32[]{:S(2)}, u32[]{:S(2)}) %collective-permute-start.8) | collective-permute-done | bytes 524320 | tf_op jit(solution)/shard_map/ppermute | solution.py:1218
  46.9 3.8 %collective-permute-start.9 = (bf16[512,512]{1,0:T(8,128)(2,1)S(1)}, bf16[512,512]{1,0:T(8,128)(2,1)S(1)}, u32[]{:S(2)}, u32[]{:S(2)}) collective-permute-start(bf16[512,512]{1,0:T(8,128)(2,1)S(1)} %get-tuple-element.143.refs_3_.refs_6_.refs_2_), channel_id=1, source_target_pairs={{0,24},{4,28},{8,0},{12,4},{16,8},{20,12},{24,16},{28,20},{1,25},{... | collective-permute-start | bytes 1572872 | tf_op jit(solution)/shard_map/ppermute | solution.py:1218
  52.3 11.2 %collective-permute-done.10.refs_7_.refs_10_ = bf16[512,512]{1,0:T(8,128)(2,1)S(1)} collective-permute-done((bf16[512,512]{1,0:T(8,128)(2,1)S(1)}, bf16[512,512]{1,0:T(8,128)(2,1)S(1)}, u32[]{:S(2)}, u32[]{:S(2)}) %collective-permute-start.10) | collective-permute-done | bytes 524320 | tf_op jit(solution)/shard_map/ppermute | solution.py:1218
  65.1 3.9 %act_back.1 = (bf16[512,1024]{1,0:T(8,128)(2,1)S(1)}, f32[512,1024]{1,0:T(8,128)S(1)}) custom-call(s32[3]{0:T(128)S(1)} %copy-done.15, bf16[512,1024]{1,0:T(8,128)(2,1)S(1)} %copy-done.23, bf16[1024,1024]{1,0:T(8,128)(2,1)S(1)} %copy-done.6), custom_call_target="tpu_custom_call" | custom-call | flops 1073741824 | bytes 6000000 | tf_op jit(solution)/shard_map/act_back/pallas_call | solution.py:93
  69.0 3.9 %collective-permute-done.9.refs_6_.refs_9_ = bf16[512,512]{1,0:T(8,128)(2,1)S(1)} collective-permute-done((bf16[512,512]{1,0:T(8,128)(2,1)S(1)}, bf16[512,512]{1,0:T(8,128)(2,1)S(1)}, u32[]{:S(2)}, u32[]{:S(2)}) %collective-permute-start.9) | collective-permute-done | bytes 524320 | tf_op jit(solution)/shard_map/ppermute | solution.py:1218
  75.3 8.9 %collective-permute-done.12.refs_9_.refs_12_ = bf16[512,512]{1,0:T(8,128)(2,1)S(1)} collective-permute-done((bf16[512,512]{1,0:T(8,128)(2,1)S(1)}, bf16[512,512]{1,0:T(8,128)(2,1)S(1)}, u32[]{:S(2)}, u32[]{:S(2)}) %collective-permute-start.12) | collective-permute-done | bytes 524320 | tf_op jit(solution)/shard_map/ppermute | solution.py:1218
  84.2 7.9 %attend.1 = (bf16[256,256]{1,0:T(8,128)(2,1)S(1)}, bf16[256,256]{1,0:T(8,128)(2,1)S(1)}, bf16[16,256]{1,0:T(8,128)(2,1)S(1)}, f32[2,512,128]{2,1,0:T(8,128)S(1)}) custom-call(s32[3]{0:T(128)S(1)} %copy-done.15, s32[32]{0:T(128)S(1)} %copy-done.20, bf16[512,256]{1,0:T(8,128)(2,1)S(1)} %get-tuple-element.142.refs_2_.refs_7_, ...), custom_call_target="tpu_custom_call" | custom-call | flops 2000000000 | bytes 7000000 | tf_op jit(solution)/shard_map/attend/pallas_call | solution.py:93
  103.2 3.4 %mlp.1 = (bf16[512,1024]{1,0:T(8,128)(2,1)S(1)}, bf16[512,1024]{1,0:T(8,128)(2,1)S(1)}, bf16[256,1024]{1,0:T(8,128)(2,1)S(1)}, bf16[256,1024]{1,0:T(8,128)(2,1)S(1)}) custom-call(bf16[256,1024]{1,0:T(8,128)(2,1)S(1)} %get-tuple-element.149.refs_0_.refs_1_, bf16[256,1024]{1,0:T(8,128)(2,1)S(1)} %collective-permute-done.23.refs_1_.refs_2_, ...), custom_call_target="tpu_custom_call" | custom-call | flops 2147483648 | bytes 9000000 | tf_op jit(solution)/shard_map/mlp/pallas_call | solution.py:93
  114.0 3.9 %collective-permute-done.29.refs_6_.refs_11_ = bf16[512,256]{1,0:T(8,128)(2,1)S(1)} collective-permute-done((bf16[512,256]{1,0:T(8,128)(2,1)S(1)}, bf16[512,256]{1,0:T(8,128)(2,1)S(1)}, u32[]{:S(2)}, u32[]{:S(2)}) %collective-permute-start.29) | collective-permute-done | bytes 262176 | tf_op jit(solution)/shard_map/ppermute | solution.py:1218
  119.4 2.4 feature_grads.4
  121.8 2.4 feature_grads.5
  129.4 3.7 %collective-permute-start.35 = (bf16[544,256]{1,0:T(8,128)(2,1)S(1)}, bf16[544,256]{1,0:T(8,128)(2,1)S(1)}, u32[]{:S(2)}, u32[]{:S(2)}) collective-permute-start(bf16[544,256]{1,0:T(8,128)(2,1)S(1)} %get-tuple-element.165.refs_3_.refs_15_), channel_id=1, source_target_pairs={{0,8},{4,12},{8,16},{12,20},{16,24},{20,28},{24,0},{28,4},{1,9},{5... | collective-permute-start | bytes 835592 | tf_op jit(solution)/shard_map/ppermute | solution.py:1218
  133.7 5.7 %query_back.1.refs_3_ = bf16[512,256]{1,0:T(8,128)(2,1)S(1)} custom-call(s32[3]{0:T(128)S(1)} %copy-done.15, s32[32]{0:T(128)S(1)} %copy-done.20, bf16[512,256]{1,0:T(8,128)(2,1)S(1)} %get-tuple-element.142.refs_2_.refs_7_, bf16[544,256]{1,0:T(8,128)(2,1)S(1)} %get-tuple-element.165.refs_3_.refs_15_, f32[2,512,128]{2,1,0:T(8,128)S(1)} %get-tuple-element.166.refs_4_, ...), custom_call_target="tpu_custom_call" | custom-call | flops 2000000000 | bytes 7000000 | tf_op jit(solution)/shard_map/query_back/pallas_call | solution.py:93
  142.1 2.4 collective-permute-start.39
  148.2 15.4 %collective-permute-done.37.refs_19_ = bf16[544,256]{1,0:T(8,128)(2,1)S(1)} collective-permute-done((bf16[544,256]{1,0:T(8,128)(2,1)S(1)}, bf16[544,256]{1,0:T(8,128)(2,1)S(1)}, u32[]{:S(2)}, u32[]{:S(2)}) %collective-permute-start.37) | collective-permute-done | bytes 278560 | tf_op jit(solution)/shard_map/ppermute | solution.py:1218
  167.5 4.0 %collective-permute-done.40.refs_22_ = bf16[544,256]{1,0:T(8,128)(2,1)S(1)} collective-permute-done((bf16[544,256]{1,0:T(8,128)(2,1)S(1)}, bf16[544,256]{1,0:T(8,128)(2,1)S(1)}, u32[]{:S(2)}, u32[]{:S(2)}) %collective-permute-start.40) | collective-permute-done | bytes 278560 | tf_op jit(solution)/shard_map/ppermute | solution.py:1218
  174.0 8.5 %key_back.1 = (bf16[512,768]{1,0:T(8,128)(2,1)S(1)}, bf16[256,1024]{1,0:T(8,128)(2,1)S(1)}, bf16[256,1024]{1,0:T(8,128)(2,1)S(1)}) custom-call(s32[3]{0:T(128)S(1)} %copy-done.15, s32[32]{0:T(128)S(1)} %copy-done.20, bf16[512,512]{1,0:T(8,128)(2,1)S(1)} %get-tuple-element.143.refs_3_.refs_6_.refs_2_, bf16[512,256]{1,0:T(8,128)(2,1)S(1)} %query_back.1.refs_3_, ...), custom_call_target="tpu_custom_call" | custom-call | flops 4000000000 | bytes 9000000 | tf_op jit(solution)/shard_map/key_back/pallas_call | solution.py:93
  190.8 3.5 %feature_grads.6 = (bf16[4,128,1024]{2,1,0:T(8,128)(2,1)S(1)}, bf16[4,128,512]{2,1,0:T(8,128)(2,1)S(1)}, bf16[4,128,512]{2,1,0:T(8,128)(2,1)S(1)}) custom-call(s32[3]{0:T(128)S(1)} %copy-done.15, bf16[256,1024]{1,0:T(8,128)(2,1)S(1)} %get-tuple-element.186.refs_0_.refs_1_, bf16[256,1024]{1,0:T(8,128)(2,1)S(1)} %collective-permute-done.6.refs_1_.refs_2_, ...), custom_call_target="tpu_custom_call" | custom-call | flops 1073741824 | bytes 5242880 | tf_op jit(solution)/shard_map/feature_grads/pallas_call | solution.py:93
  194.3 4.2 %collective-permute-done.45.refs_1_ = bf16[2,128,1024]{2,1,0:T(8,128)(2,1)S(1)} collective-permute-done((bf16[2,128,1024]{2,1,0:T(8,128)(2,1)S(1)}, bf16[2,128,1024]{2,1,0:T(8,128)(2,1)S(1)}, u32[]{:S(2)}, u32[]{:S(2)}) %collective-permute-start.45) | collective-permute-done | bytes 524320 | tf_op jit(solution)/shard_map/ppermute | solution.py:1113
  206.2 7.4 %cross_back.1 = (bf16[512,256]{1,0:T(8,128)(2,1)S(1)}, bf16[1024,256]{1,0:T(8,128)(2,1)S(1)}, bf16[1024,256]{1,0:T(8,128)(2,1)S(1)}, bf16[768,1024]{1,0:T(8,128)(2,1)S(1)}, bf16[768,1024]{1,0:T(8,128)(2,1)S(1)}) custom-call(s32[3]{0:T(128)S(1)} %copy-done.15, bf16[256,1024]{1,0:T(8,128)(2,1)S(1)} %get-tuple-element.196.refs_1_.refs_7_, ...), custom_call_target="tpu_custom_call" | custom-call | flops 4000000000 | bytes 12000000 | tf_op jit(solution)/shard_map/cross_back/pallas_call | solution.py:93
  213.6 6.0 %collective-permute-done.49.refs_1_ = bf16[128,1024]{1,0:T(8,128)(2,1)S(1)} collective-permute-done((bf16[128,1024]{1,0:T(8,128)(2,1)S(1)}, bf16[128,1024]{1,0:T(8,128)(2,1)S(1)}, u32[]{:S(2)}, u32[]{:S(2)}) %collective-permute-start.49) | collective-permute-done | bytes 262176 | tf_op jit(solution)/shard_map/ppermute | solution.py:1117
  225.2 6.4 %feature_grads.7 = (bf16[4,128,1024]{2,1,0:T(8,128)(2,1)S(1)}, bf16[4,128,1024]{2,1,0:T(8,128)(2,1)S(1)}) custom-call(s32[3]{0:T(128)S(1)} %copy-done.15, bf16[512,1024]{1,0:T(8,128)(2,1)S(1)} %copy-done.9, bf16[512,256]{1,0:T(8,128)(2,1)S(1)} %get-tuple-element.201.refs_2_, bf16[1024,1024]{1,0:T(8,128)(2,1)S(1)} %copy-done.1, ...), custom_call_target="tpu_custom_call" | custom-call | flops 1610612736 | bytes 9961472 | tf_op jit(solution)/shard_map/feature_grads/pallas_call | solution.py:93
  231.5 2.4 collective-permute-done.51.refs_1_
  240.0 3.8 %gains.1 = f32[8,1024]{1,0:T(8,128)S(1)} custom-call(s32[3]{0:T(128)S(1)} %copy-done.15, s32[32]{0:T(128)S(1)} %copy-done.20, s32[3]{0:T(128)S(1)} %copy-done.21, bf16[768,1024]{1,0:T(8,128)(2,1)S(1)} %get-tuple-element.205.refs_3_, bf16[768,1024]{1,0:T(8,128)(2,1)S(1)} %get-tuple-element.211.refs_4_, bf16[512,1024]{1,0:T(8,128)(2,1)S(1)} %copy-done, ...), custom_call_target="tpu_custom_call" | custom-call | flops 31457280 | bytes 6291456 | tf_op jit(solution)/shard_map/gains/pallas_call | solution.py:93
  246.2 14.2 %collective-permute-done.57 = f32[8,1024]{1,0:T(8,128)S(1)} collective-permute-done((f32[8,1024]{1,0:T(8,128)S(1)}, f32[8,1024]{1,0:T(8,128)S(1)}, u32[]{:S(2)}, u32[]{:S(2)}) %collective-permute-start.57) | collective-permute-done | bytes 32800 | tf_op jit(solution)/shard_map/ppermute | solution.py:1298
  263.8 4.5 %final_norm.1 = (bf16[768,1024]{1,0:T(8,128)(2,1)S(1)}, bf16[512,1024]{1,0:T(8,128)(2,1)}, bf16[1024,1024]{1,0:T(8,128)(2,1)}) custom-call(s32[3]{0:T(128)S(1)} %copy-done.15, bf16[768,1024]{1,0:T(8,128)(2,1)S(1)} %add_convert_fusion.refs_11_.refs_1_, bf16[768,1024]{1,0:T(8,128)(2,1)S(1)} %collective-permute-done.60.refs_2_, bf16[512,1024]{1,0:T(8,128)(2,1)S(1)} %copy-done, ...), custom_call_target="tpu_custom_call" | custom-call | flops 15728640 | bytes 6291456 | tf_op jit(solution)/shard_map/final_norm/pallas_call | solution.py:93
  272.7 9.2 %collective-permute-done.63 = f32[8,1024]{1,0:T(8,128)S(1)} collective-permute-done((f32[8,1024]{1,0:T(8,128)S(1)}, f32[8,1024]{1,0:T(8,128)S(1)}, u32[]{:S(2)}, u32[]{:S(2)}) %collective-permute-start.63) | collective-permute-done | bytes 32800 | tf_op jit(solution)/shard_map/ppermute | solution.py:1449
  290.5 6.8 %collective-permute-done.66.refs_1_ = bf16[128,1024]{1,0:T(8,128)(2,1)S(1)} collective-permute-done((bf16[128,1024]{1,0:T(8,128)(2,1)S(1)}, bf16[128,1024]{1,0:T(8,128)(2,1)S(1)}, u32[]{:S(2)}, u32[]{:S(2)}) %collective-permute-start.66) | collective-permute-done | bytes 262176 | tf_op jit(solution)/shard_map/ppermute | solution.py:1117
  (214 shorter events, 108.1 us)
Async XLA Ops:
  0.7 15.2 %collective-permute-start = (bf16[256,1024]{1,0:T(8,128)(2,1)}, bf16[256,1024]{1,0:T(8,128)(2,1)S(1)}, u32[]{:S(2)}, u32[]{:S(2)}) collective-permute-start(bf16[256,1024]{1,0:T(8,128)(2,1)} %refs_3_.6), channel_id=1, source_target_pairs={{0,2},{1,3},{2,0},{3,1},{4,6},{5,7},{6,4},{7,5},{8,10},{9,11},{10,... | collective-permute-start | bytes 1572872 | tf_op jit(solution)/shard_map/ppermute | solution.py:1212
  30.8 16.1 %collective-permute-start.8 = (bf16[512,512]{1,0:T(8,128)(2,1)S(1)}, bf16[512,512]{1,0:T(8,128)(2,1)S(1)}, u32[]{:S(2)}, u32[]{:S(2)}) collective-permute-start(bf16[512,512]{1,0:T(8,128)(2,1)S(1)} %get-tuple-element.143.refs_3_.refs_6_.refs_2_), channel_id=1, source_target_pairs={{0,8},{4,12},{8,16},{12,20},{16,24},{20,28},{24,0},{28,4},{1,9},{5... | collective-permute-start | bytes 1572872 | tf_op jit(solution)/shard_map/ppermute | solution.py:1218
  34.2 16.6 %collective-permute-start.14 = (bf16[256,1024]{1,0:T(8,128)(2,1)S(1)}, bf16[256,1024]{1,0:T(8,128)(2,1)S(1)}, u32[]{:S(2)}, u32[]{:S(2)}) collective-permute-start(bf16[256,1024]{1,0:T(8,128)(2,1)S(1)} %copy-done.8), channel_id=1, source_target_pairs={{0,1},{1,0},{2,3},{3,2},{4,5},{5,4},{6,7},{7,6},{8,9},{9,8},{10,11... | collective-permute-start | bytes 1572872 | tf_op jit(solution)/shard_map/ppermute | solution.py:1212
  34.2 18.1 %collective-permute-start.7 = (bf16[512,512]{1,0:T(8,128)(2,1)S(1)}, bf16[512,512]{1,0:T(8,128)(2,1)S(1)}, u32[]{:S(2)}, u32[]{:S(2)}) collective-permute-start(bf16[512,512]{1,0:T(8,128)(2,1)S(1)} %get-tuple-element.143.refs_3_.refs_6_.refs_2_), channel_id=1, source_target_pairs={{0,4},{4,0},{8,12},{12,8},{16,20},{20,16},{24,28},{28,24},{1,5},{5... | collective-permute-start | bytes 1572872 | tf_op jit(solution)/shard_map/ppermute | solution.py:1218
  46.9 16.6 %collective-permute-start.10 = (bf16[512,512]{1,0:T(8,128)(2,1)S(1)}, bf16[512,512]{1,0:T(8,128)(2,1)S(1)}, u32[]{:S(2)}, u32[]{:S(2)}) collective-permute-start(bf16[512,512]{1,0:T(8,128)(2,1)S(1)} %collective-permute-done.8.refs_5_.refs_8_), channel_id=1, source_target_pairs={{0,8},{4,12},{8,16},{12,20},{16,24},{20,28},{24,0},{28,4},{1,9},{5... | collective-permute-start | bytes 1572872 | tf_op jit(solution)/shard_map/ppermute | solution.py:1218
  46.9 18.2 %collective-permute-start.16 = (bf16[256,1024]{1,0:T(8,128)(2,1)S(1)}, bf16[256,1024]{1,0:T(8,128)(2,1)S(1)}, u32[]{:S(2)}, u32[]{:S(2)}) collective-permute-start(bf16[256,1024]{1,0:T(8,128)(2,1)S(1)} %collective-permute-done.15.refs_13_.refs_7_), channel_id=1, source_target_pairs={{0,1},{1,0},{2,3},{3,2},{4,5},{5,4},{6,7},{7,6},{8,9},{9,8},{10,11... | collective-permute-start | bytes 1572872 | tf_op jit(solution)/shard_map/ppermute | solution.py:1212
  46.9 26.0 %collective-permute-start.9 = (bf16[512,512]{1,0:T(8,128)(2,1)S(1)}, bf16[512,512]{1,0:T(8,128)(2,1)S(1)}, u32[]{:S(2)}, u32[]{:S(2)}) collective-permute-start(bf16[512,512]{1,0:T(8,128)(2,1)S(1)} %get-tuple-element.143.refs_3_.refs_6_.refs_2_), channel_id=1, source_target_pairs={{0,24},{4,28},{8,0},{12,4},{16,8},{20,12},{24,16},{28,20},{1,25},{... | collective-permute-start | bytes 1572872 | tf_op jit(solution)/shard_map/ppermute | solution.py:1218
  50.8 23.3 %collective-permute-start.11 = (bf16[512,512]{1,0:T(8,128)(2,1)S(1)}, bf16[512,512]{1,0:T(8,128)(2,1)S(1)}, u32[]{:S(2)}, u32[]{:S(2)}) collective-permute-start(bf16[512,512]{1,0:T(8,128)(2,1)S(1)} %collective-permute-done.8.refs_5_.refs_8_), channel_id=1, source_target_pairs={{0,4},{4,0},{8,12},{12,8},{16,20},{20,16},{24,28},{28,24},{1,5},{5... | collective-permute-start | bytes 1572872 | tf_op jit(solution)/shard_map/ppermute | solution.py:1218
  52.3 31.9 %collective-permute-start.12 = (bf16[512,512]{1,0:T(8,128)(2,1)S(1)}, bf16[512,512]{1,0:T(8,128)(2,1)S(1)}, u32[]{:S(2)}, u32[]{:S(2)}) collective-permute-start(bf16[512,512]{1,0:T(8,128)(2,1)S(1)} %collective-permute-done.7.refs_4_.refs_7_), channel_id=1, source_target_pairs={{0,24},{4,28},{8,0},{12,4},{16,8},{20,12},{24,16},{28,20},{1,25},{... | collective-permute-start | bytes 1572872 | tf_op jit(solution)/shard_map/ppermute | solution.py:1218
  63.6 20.6 %collective-permute-start.13 = (bf16[512,512]{1,0:T(8,128)(2,1)S(1)}, bf16[512,512]{1,0:T(8,128)(2,1)S(1)}, u32[]{:S(2)}, u32[]{:S(2)}) collective-permute-start(bf16[512,512]{1,0:T(8,128)(2,1)S(1)} %collective-permute-done.10.refs_7_.refs_10_), channel_id=1, source_target_pairs={{0,4},{4,0},{8,12},{12,8},{16,20},{20,16},{24,28},{28,24},{1,5},{5... | collective-permute-start | bytes 1572872 | tf_op jit(solution)/shard_map/ppermute | solution.py:1218
  65.1 28.6 %collective-permute-start.22 = (bf16[512,256]{1,0:T(8,128)(2,1)S(1)}, bf16[512,256]{1,0:T(8,128)(2,1)S(1)}, u32[]{:S(2)}, u32[]{:S(2)}) collective-permute-start(bf16[512,256]{1,0:T(8,128)(2,1)S(1)} %get-tuple-element.142.refs_2_.refs_7_), channel_id=1, source_target_pairs={{0,24},{4,28},{8,0},{12,4},{16,8},{20,12},{24,16},{28,20},{1,25},{... | collective-permute-start | bytes 786440 | tf_op jit(solution)/shard_map/ppermute | solution.py:1218
  73.0 23.0 %collective-permute-start.21 = (bf16[512,256]{1,0:T(8,128)(2,1)S(1)}, bf16[512,256]{1,0:T(8,128)(2,1)S(1)}, u32[]{:S(2)}, u32[]{:S(2)}) collective-permute-start(bf16[512,256]{1,0:T(8,128)(2,1)S(1)} %get-tuple-element.142.refs_2_.refs_7_), channel_id=1, source_target_pairs={{0,8},{4,12},{8,16},{12,20},{16,24},{20,28},{24,0},{28,4},{1,9},{5... | collective-permute-start | bytes 786440 | tf_op jit(solution)/shard_map/ppermute | solution.py:1218
  74.1 21.9 %collective-permute-start.20 = (bf16[512,256]{1,0:T(8,128)(2,1)S(1)}, bf16[512,256]{1,0:T(8,128)(2,1)S(1)}, u32[]{:S(2)}, u32[]{:S(2)}) collective-permute-start(bf16[512,256]{1,0:T(8,128)(2,1)S(1)} %get-tuple-element.142.refs_2_.refs_7_), channel_id=1, source_target_pairs={{0,4},{4,0},{8,12},{12,8},{16,20},{20,16},{24,28},{28,24},{1,5},{5... | collective-permute-start | bytes 786440 | tf_op jit(solution)/shard_map/ppermute | solution.py:1218
  108.7 17.1 %collective-permute-start.28 = (bf16[256,1024]{1,0:T(8,128)(2,1)S(1)}, bf16[256,1024]{1,0:T(8,128)(2,1)S(1)}, u32[]{:S(2)}, u32[]{:S(2)}) collective-permute-start(bf16[256,1024]{1,0:T(8,128)(2,1)S(1)} %add_convert_fusion.3.refs_4_.refs_2_.refs_0_), channel_id=1, source_target_pairs={{0,2},{1,3},{2,0},{3,1},{4,6},{5,7},{6,4},{7,5},{8,10},{9,11},{10,... | collective-permute-start | bytes 1572872 | tf_op jit(solution)/shard_map/ppermute | solution.py:1212
  110.2 15.6 %collective-permute-start.30 = (bf16[512,256]{1,0:T(8,128)(2,1)S(1)}, bf16[512,256]{1,0:T(8,128)(2,1)S(1)}, u32[]{:S(2)}, u32[]{:S(2)}) collective-permute-start(bf16[512,256]{1,0:T(8,128)(2,1)S(1)} %collective-permute-done.21.refs_12_.refs_9_), channel_id=1, source_target_pairs={{0,4},{4,0},{8,12},{12,8},{16,20},{20,16},{24,28},{28,24},{1,5},{5... | collective-permute-start | bytes 786440 | tf_op jit(solution)/shard_map/ppermute | solution.py:1218
  141.5 25.2 %collective-permute-start.41 = (bf16[4,128,1024]{2,1,0:T(8,128)(2,1)S(1)}, bf16[4,128,1024]{2,1,0:T(8,128)(2,1)S(1)}, u32[]{:S(2)}, u32[]{:S(2)}) collective-permute-start(bf16[4,128,1024]{2,1,0:T(8,128)(2,1)S(1)} %get-tuple-element.176), channel_id=1, source_target_pairs={{0,4},{4,0},{8,12},{12,8},{16,20},{20,16},{24,28},{28,24},{1,5},{5... | collective-permute-start | bytes 3145736 | tf_op jit(solution)/shard_map/ppermute | solution.py:1109
  142.1 21.5 %collective-permute-start.39 = (bf16[544,256]{1,0:T(8,128)(2,1)S(1)}, bf16[544,256]{1,0:T(8,128)(2,1)S(1)}, u32[]{:S(2)}, u32[]{:S(2)}) collective-permute-start(bf16[544,256]{1,0:T(8,128)(2,1)S(1)} %collective-permute-done.34.refs_16_), channel_id=1, source_target_pairs={{0,8},{4,12},{8,16},{12,20},{16,24},{20,28},{24,0},{28,4},{1,9},{5... | collective-permute-start | bytes 835592 | tf_op jit(solution)/shard_map/ppermute | solution.py:1218
  144.5 19.0 %collective-permute-start.38 = (bf16[544,256]{1,0:T(8,128)(2,1)S(1)}, bf16[544,256]{1,0:T(8,128)(2,1)S(1)}, u32[]{:S(2)}, u32[]{:S(2)}) collective-permute-start(bf16[544,256]{1,0:T(8,128)(2,1)S(1)} %collective-permute-done.34.refs_16_), channel_id=1, source_target_pairs={{0,24},{4,28},{8,0},{12,4},{16,8},{20,12},{24,16},{28,20},{1,25},{... | collective-permute-start | bytes 835592 | tf_op jit(solution)/shard_map/ppermute | solution.py:1218
  145.9 17.6 %collective-permute-start.37 = (bf16[544,256]{1,0:T(8,128)(2,1)S(1)}, bf16[544,256]{1,0:T(8,128)(2,1)S(1)}, u32[]{:S(2)}, u32[]{:S(2)}) collective-permute-start(bf16[544,256]{1,0:T(8,128)(2,1)S(1)} %collective-permute-done.35.refs_17_), channel_id=1, source_target_pairs={{0,8},{4,12},{8,16},{12,20},{16,24},{20,28},{24,0},{28,4},{1,9},{5... | collective-permute-start | bytes 835592 | tf_op jit(solution)/shard_map/ppermute | solution.py:1218
  146.8 25.8 %collective-permute-start.26 = (bf16[256,1024]{1,0:T(8,128)(2,1)S(1)}, bf16[256,1024]{1,0:T(8,128)(2,1)S(1)}, u32[]{:S(2)}, u32[]{:S(2)}) collective-permute-start(bf16[256,1024]{1,0:T(8,128)(2,1)S(1)} %add_convert_fusion.2.refs_1_), channel_id=1, source_target_pairs={{0,2},{1,3},{2,0},{3,1},{4,6},{5,7},{6,4},{7,5},{8,10},{9,11},{10,... | collective-permute-start | bytes 1572872 | tf_op jit(solution)/shard_map/ppermute | solution.py:1212
  204.1 15.4 %collective-permute-start.48 = (bf16[4,128,512]{2,1,0:T(8,128)(2,1)S(1)}, bf16[4,128,512]{2,1,0:T(8,128)(2,1)S(1)}, u32[]{:S(2)}, u32[]{:S(2)}) collective-permute-start(bf16[4,128,512]{2,1,0:T(8,128)(2,1)S(1)} %get-tuple-element.209), channel_id=1, source_target_pairs={{0,4},{4,0},{8,12},{12,8},{16,20},{20,16},{24,28},{28,24},{1,5},{5... | collective-permute-start | bytes 1572872 | tf_op jit(solution)/shard_map/ppermute | solution.py:1109
  205.0 14.6 %collective-permute-start.49 = (bf16[128,1024]{1,0:T(8,128)(2,1)S(1)}, bf16[128,1024]{1,0:T(8,128)(2,1)S(1)}, u32[]{:S(2)}, u32[]{:S(2)}) collective-permute-start(bf16[128,1024]{1,0:T(8,128)(2,1)S(1)} %get-tuple-element.210.refs_4_), channel_id=1, source_target_pairs={{0,16},{4,20},{8,24},{12,28},{16,0},{20,4},{24,8},{28,12},{1,17},{... | collective-permute-start | bytes 786440 | tf_op jit(solution)/shard_map/ppermute | solution.py:1117
  219.6 14.3 %collective-permute-start.51 = (bf16[2,128,1024]{2,1,0:T(8,128)(2,1)S(1)}, bf16[2,128,1024]{2,1,0:T(8,128)(2,1)S(1)}, u32[]{:S(2)}, u32[]{:S(2)}) collective-permute-start(bf16[2,128,1024]{2,1,0:T(8,128)(2,1)S(1)} %get-tuple-element.214), channel_id=1, source_target_pairs={{0,8},{4,12},{8,0},{12,4},{16,24},{20,28},{24,16},{28,20},{1,9},{5... | collective-permute-start | bytes 1572872 | tf_op jit(solution)/shard_map/ppermute | solution.py:1113
  219.6 14.4 %collective-permute-start.52 = (bf16[4,128,512]{2,1,0:T(8,128)(2,1)S(1)}, bf16[4,128,512]{2,1,0:T(8,128)(2,1)S(1)}, u32[]{:S(2)}, u32[]{:S(2)}) collective-permute-start(bf16[4,128,512]{2,1,0:T(8,128)(2,1)S(1)} %get-tuple-element.217), channel_id=1, source_target_pairs={{0,4},{4,0},{8,12},{12,8},{16,20},{20,16},{24,28},{28,24},{1,5},{5... | collective-permute-start | bytes 1572872 | tf_op jit(solution)/shard_map/ppermute | solution.py:1109
  223.7 40.1 %collective-permute-start.60 = (bf16[768,1024]{1,0:T(8,128)(2,1)S(1)}, bf16[768,1024]{1,0:T(8,128)(2,1)S(1)}, u32[]{:S(2)}, u32[]{:S(2)}) collective-permute-start(bf16[768,1024]{1,0:T(8,128)(2,1)S(1)} %add_convert_fusion.refs_11_.refs_1_), channel_id=1, source_target_pairs={{0,2},{1,3},{2,0},{3,1},{4,6},{5,7},{6,4},{7,5},{8,10},{9,11},{10,... | collective-permute-start | bytes 4718600 | tf_op jit(solution)/shard_map/ppermute | solution.py:1212
  234.8 25.7 %collective-permute-start.53 = (bf16[4,128,1024]{2,1,0:T(8,128)(2,1)S(1)}, bf16[4,128,1024]{2,1,0:T(8,128)(2,1)S(1)}, u32[]{:S(2)}, u32[]{:S(2)}) collective-permute-start(bf16[4,128,1024]{2,1,0:T(8,128)(2,1)S(1)} %get-tuple-element.220.refs_10_), channel_id=1, source_target_pairs={{0,4},{4,0},{8,12},{12,8},{16,20},{20,16},{24,28},{28,24},{1,5},{5... | collective-permute-start | bytes 3145736 | tf_op jit(solution)/shard_map/ppermute | solution.py:1109
  236.1 24.3 %collective-permute-start.54 = (bf16[2,128,1024]{2,1,0:T(8,128)(2,1)S(1)}, bf16[2,128,1024]{2,1,0:T(8,128)(2,1)S(1)}, u32[]{:S(2)}, u32[]{:S(2)}) collective-permute-start(bf16[2,128,1024]{2,1,0:T(8,128)(2,1)S(1)} %get-tuple-element.222.refs_2_), channel_id=1, source_target_pairs={{0,8},{4,12},{8,0},{12,4},{16,24},{20,28},{24,16},{28,20},{1,9},{5... | collective-permute-start | bytes 1572872 | tf_op jit(solution)/shard_map/ppermute | solution.py:1113
  237.7 22.7 %collective-permute-start.55 = (bf16[128,1024]{1,0:T(8,128)(2,1)S(1)}, bf16[128,1024]{1,0:T(8,128)(2,1)S(1)}, u32[]{:S(2)}, u32[]{:S(2)}) collective-permute-start(bf16[128,1024]{1,0:T(8,128)(2,1)S(1)} %get-tuple-element.223), channel_id=1, source_target_pairs={{0,16},{4,20},{8,24},{12,28},{16,0},{20,4},{24,8},{28,12},{1,17},{... | collective-permute-start | bytes 786440 | tf_op jit(solution)/shard_map/ppermute | solution.py:1117
  245.1 15.3 %collective-permute-start.57 = (f32[8,1024]{1,0:T(8,128)S(1)}, f32[8,1024]{1,0:T(8,128)S(1)}, u32[]{:S(2)}, u32[]{:S(2)}) collective-permute-start(f32[8,1024]{1,0:T(8,128)S(1)} %add.39), channel_id=1, source_target_pairs={{0,4},{4,0},{8,12},{12,8},{16,20},{20,16},{24,28},{28,24},{1,5},{5... | collective-permute-start | bytes 98312 | tf_op jit(solution)/shard_map/ppermute | solution.py:1298
  261.4 20.5 %collective-permute-start.58 = (bf16[2,128,1024]{2,1,0:T(8,128)(2,1)S(1)}, bf16[2,128,1024]{2,1,0:T(8,128)(2,1)S(1)}, u32[]{:S(2)}, u32[]{:S(2)}) collective-permute-start(bf16[2,128,1024]{2,1,0:T(8,128)(2,1)S(1)} %get-tuple-element.230), channel_id=1, source_target_pairs={{0,8},{4,12},{8,0},{12,4},{16,24},{20,28},{24,16},{28,20},{1,9},{5... | collective-permute-start | bytes 1572872 | tf_op jit(solution)/shard_map/ppermute | solution.py:1113
  262.7 19.1 %collective-permute-start.59 = (bf16[128,1024]{1,0:T(8,128)(2,1)S(1)}, bf16[128,1024]{1,0:T(8,128)(2,1)S(1)}, u32[]{:S(2)}, u32[]{:S(2)}) collective-permute-start(bf16[128,1024]{1,0:T(8,128)(2,1)S(1)} %get-tuple-element.227.refs_3_), channel_id=1, source_target_pairs={{0,16},{4,20},{8,24},{12,28},{16,0},{20,4},{24,8},{28,12},{1,17},{... | collective-permute-start | bytes 786440 | tf_op jit(solution)/shard_map/ppermute | solution.py:1117
  282.0 15.2 %collective-permute-start.66 = (bf16[128,1024]{1,0:T(8,128)(2,1)S(1)}, bf16[128,1024]{1,0:T(8,128)(2,1)S(1)}, u32[]{:S(2)}, u32[]{:S(2)}) collective-permute-start(bf16[128,1024]{1,0:T(8,128)(2,1)S(1)} %get-tuple-element.244), channel_id=1, source_target_pairs={{0,16},{4,20},{8,24},{12,28},{16,0},{20,4},{24,8},{28,12},{1,17},{... | collective-permute-start | bytes 786440 | tf_op jit(solution)/shard_map/ppermute | solution.py:1117
  (68 other events, 655.0 us)
